TPU v7x, 32 devices: a whole 2x2x4 slice. The times are simulated.
32 devices in a mesh: slab: 2 (over y), tile: 4 (over z), view: 4 (over x, core).
Axes of the slice: x: 2, y: 2, z: 4, core: 2. Of those that a mesh axis runs over, the one named last changes fastest.
Arguments:
- recorded: float32 [4, 96, 32, 1024], P('view', 'tile', 'slab'), parts along dimension 2, may hold values from 0.5 to 2
- psf_taps: float32 [4, 3, 15], P('view'), may hold values from 0.2 to 1
- estimate: float32 [96, 32, 1024], P('tile', 'slab'), parts along dimension 1, may hold values from 0.5 to 2
Outputs:
- joined: float32 [96, 32, 1024], P('tile', 'slab'), parts along dimension 1
There are 2 independent parts, one for each index of `slab`. A program takes and returns all parts, laid end to end along the dimension named above; an argument that names none is the same for every part. Nothing has to cross between parts.
All inputs are finite; a program needn't handle non-finite values.
Results may differ from a plain program's by a relative error of at most 0.00002.
Values sent between devices are 32-bit elements; how exact they have to be, the bound alone decides.
No kernel may reach another device: no remote copies, remote signals or barrier semaphores. Data moves between devices by JAX's collectives and lax.ppermute only.
A program may use at most 64 MiB of HBM per device.

v0:
```python
import jax
import jax.numpy as jnp
from jax import lax
from jax.sharding import PartitionSpec as P

RADIUS = 7
ITERS = 2


def with_halo(shard, sides, width):
    for axis, dim in sides:
        devices, length = (lax.axis_size(axis), shard.shape[dim])
        up = [(i, (i + 1) % devices) for i in range(devices - 1)]
        down = [(j, i) for i, j in up]
        last = lax.slice_in_dim(shard, length - width, length, axis=dim)
        initial = lax.slice_in_dim(shard, 0, width, axis=dim)
        before = lax.ppermute(last, axis, up)
        after = lax.ppermute(initial, axis, down)
        shard = jnp.concatenate([before, shard, after], axis=dim)
    return shard


def valid_along(padded, kernel_row, axis_num, mirrored):
    length_out = padded.shape[axis_num] - 2 * RADIUS
    summed = jnp.zeros(
        padded.shape[:axis_num] + (length_out,) + padded.shape[axis_num + 1 :], jnp.float32
    )
    for offset in range(2 * RADIUS + 1):
        weight = kernel_row[2 * RADIUS - offset] if mirrored else kernel_row[offset]
        summed = summed + weight * lax.slice_in_dim(
            padded, offset, offset + length_out, axis=axis_num
        )
    return summed


def along(values_in, kernel_row, axis_num, mirrored):
    widths = [(0, 0)] * values_in.ndim
    widths[axis_num] = (RADIUS, RADIUS)
    return valid_along(jnp.pad(values_in, widths), kernel_row, axis_num, mirrored)


def finish_zy(values_in, kernel_view, mirrored):
    result = along(values_in, kernel_view[1], 1, mirrored)
    return along(result, kernel_view[2], 2, mirrored)


def local(recorded, psf_taps, estimate):
    kernel = psf_taps / jnp.sum(psf_taps, axis=2, keepdims=True)
    local_views = recorded.shape[0]
    view_total = lax.axis_size("view") * local_views
    for iteration in range(ITERS):
        extended = with_halo(estimate, (("tile", 0),), RADIUS)
        kernel_view = kernel[0]
        blurred = finish_zy(valid_along(extended, kernel_view[0], 0, False), kernel_view, False)
        quotient = recorded[0] / blurred
        quotient_wide = with_halo(quotient, (("tile", 0),), RADIUS)
        correction = finish_zy(
            valid_along(quotient_wide, kernel_view[0], 0, True), kernel_view, True
        )
        log_terms = jnp.log(correction)
        log_total = lax.psum(log_terms, "view")
        estimate = estimate * jnp.exp(log_total / view_total)
    return estimate


def solution(mesh):
    in_specs = (P("view", "tile", "slab", None), P("view", None, None), P("tile", "slab", None))
    out_specs = P("tile", "slab", None)
    return jax.shard_map(local, mesh=mesh, in_specs=in_specs, out_specs=out_specs, check_vma=False)
```

profile of v0, /device:TPU:0, one launch (start us, length us, event | category | flops | bytes accessed | tf_op | source)
XLA Modules:
  0.0 333.5 jit_solution(3361568924771776846)
XLA Ops:
  7.9 5.0 %collective-permute-start = (f32[7,16,1024]{2,1,0:T(8,128)S(1)}, f32[7,16,1024]{2,1,0:T(8,128)S(1)}, u32[]{:S(2)}, u32[]{:S(2)}) collective-permute-start(f32[7,16,1024]{2,1,0:T(8,128)S(1)} %get-tuple-element.13), channel_id=1, source_target_pairs={{0,4},{4,8},{8,12},{1,5},{5,9},{9,13},{2,6},{6,10},{10,14},{3,7},{... | collective-permute-start | bytes 1376264 | tf_op jit(solution)/shard_map/ppermute | solution.py:17
  16.5 6.1 %collective-permute-done = f32[7,16,1024]{2,1,0:T(8,128)S(1)} collective-permute-done((f32[7,16,1024]{2,1,0:T(8,128)S(1)}, f32[7,16,1024]{2,1,0:T(8,128)S(1)}, u32[]{:S(2)}, u32[]{:S(2)}) %collective-permute-start) | collective-permute-done | bytes 458784 | tf_op jit(solution)/shard_map/ppermute | solution.py:17
  23.0 3.7 %collective-permute-done.1 = f32[7,16,1024]{2,1,0:T(8,128)S(1)} collective-permute-done((f32[7,16,1024]{2,1,0:T(8,128)S(1)}, f32[7,16,1024]{2,1,0:T(8,128)S(1)}, u32[]{:S(2)}, u32[]{:S(2)}) %collective-permute-start.1) | collective-permute-done | bytes 458784 | tf_op jit(solution)/shard_map/ppermute | solution.py:18
  26.8 12.1 %fusion.346 = f32[24,16,1024]{2,1,0:T(8,128)S(1)} fusion(f32[31,16,1024]{2,1,0:T(8,128)S(1)} %constant_dynamic-update-slice_fusion.2, f32[31,16,1024]{2,1,0:T(8,128)S(1)} %get-tuple-element.11, f32[24,16,1024]{2,1,0:T(8,128)S(1)} %copy-done, f32[]{:T(128)} %bitcast.19, f32[]{:T(128)} %bitcast.18, f32[]{:T(128)} %bitcast.17, f32[]{:T(128)} %bitcast.16, ...), kind=kLoop, calls=%fused_computation.537 | loop fusion | flops 11403264 | bytes 25165884 | tf_op jit(solution)/shard_map/add | solution.py:30
  38.9 12.4 %fusion.242 = f32[24,16,1024]{2,1,0:T(8,128)S(1)} fusion(f32[24,16,1024]{2,1,0:T(8,128)S(1)} %fusion.346, f32[]{:T(128)} %bitcast.32, f32[]{:T(128)} %bitcast.31, f32[]{:T(128)} %bitcast.30, f32[]{:T(128)} %bitcast.29, f32[]{:T(128)} %bitcast.28, f32[]{:T(128)} %bitcast.27, f32[]{:T(128)} %bitcast.26, f32[]{:T(128)} %bitcast.25, f32[]{:T(128)} %bitcast.24, ...), kind=kLoop, calls=%fused_computation.426 | loop fusion | flops 11403264 | bytes 3145788 | tf_op jit(solution)/shard_map/add | solution.py:30
  51.2 15.3 %fusion.15 = f32[24,16,1024]{2,1,0:T(8,128)S(1)} fusion(f32[24,16,1024]{2,1,0:T(8,128)S(1)} %fusion.242, f32[1,24,16,1024]{3,2,1,0:T(8,128)S(1)} %copy-done.1, f32[]{:T(128)} %bitcast.45, f32[]{:T(128)} %bitcast.44, f32[]{:T(128)} %bitcast.43, f32[]{:T(128)} %bitcast.42, f32[]{:T(128)} %bitcast.41, f32[]{:T(128)} %bitcast.40, f32[]{:T(128)} %bitcast.39, ...), kind=kLoop, calls=%fused_computation.199 | loop fusion | flops 11796480 | bytes 4718652 | tf_op jit(solution)/shard_map/div | solution.py:55
  68.0 4.8 %collective-permute-start.2 = (f32[7,16,1024]{2,1,0:T(8,128)S(1)}, f32[7,16,1024]{2,1,0:T(8,128)S(1)}, u32[]{:S(2)}, u32[]{:S(2)}) collective-permute-start(f32[7,16,1024]{2,1,0:T(8,128)S(1)} %get-tuple-element.9), channel_id=1, source_target_pairs={{0,4},{4,8},{8,12},{1,5},{5,9},{9,13},{2,6},{6,10},{10,14},{3,7},{... | collective-permute-start | bytes 1376264 | tf_op jit(solution)/shard_map/ppermute | solution.py:17
  72.7 7.0 %collective-permute-done.3 = f32[7,16,1024]{2,1,0:T(8,128)S(1)} collective-permute-done((f32[7,16,1024]{2,1,0:T(8,128)S(1)}, f32[7,16,1024]{2,1,0:T(8,128)S(1)}, u32[]{:S(2)}, u32[]{:S(2)}) %collective-permute-start.3) | collective-permute-done | bytes 458784 | tf_op jit(solution)/shard_map/ppermute | solution.py:18
  80.9 12.3 %fusion.193 = f32[24,16,1024]{2,1,0:T(8,128)S(1)} fusion(f32[24,16,1024]{2,1,0:T(8,128)S(1)} %fusion.15, f32[7,16,1024]{2,1,0:T(8,128)S(1)} %collective-permute-done.3, f32[7,16,1024]{2,1,0:T(8,128)S(1)} %collective-permute-done.2, f32[]{:T(128)} %bitcast.19, f32[]{:T(128)} %bitcast.18, f32[]{:T(128)} %bitcast.17, f32[]{:T(128)} %bitcast.16, f32[]{:T(128)} %bitcast.15, ...), kind=kLoop, calls=%fused_computation.377 | loop fusion | flops 16908288 | bytes 4063292 | tf_op jit(solution)/shard_map/add | solution.py:30
  93.1 12.2 %fusion.270 = f32[24,16,1024]{2,1,0:T(8,128)S(1)} fusion(f32[24,16,1024]{2,1,0:T(8,128)S(1)} %fusion.193, f32[]{:T(128)} %bitcast.32, f32[]{:T(128)} %bitcast.31, f32[]{:T(128)} %bitcast.30, f32[]{:T(128)} %bitcast.29, f32[]{:T(128)} %bitcast.28, f32[]{:T(128)} %bitcast.27, f32[]{:T(128)} %bitcast.26, f32[]{:T(128)} %bitcast.25, f32[]{:T(128)} %bitcast.24, ...), kind=kLoop, calls=%fused_computation.454 | loop fusion | flops 11403264 | bytes 3145788 | tf_op jit(solution)/shard_map/add | solution.py:30
  105.4 16.2 %fusion.361 = f32[24,16,1024]{2,1,0:T(8,128)} fusion(f32[24,16,1024]{2,1,0:T(8,128)S(1)} %fusion.270, f32[]{:T(128)} %bitcast.45, f32[]{:T(128)} %bitcast.44, f32[]{:T(128)} %bitcast.43, f32[]{:T(128)} %bitcast.42, f32[]{:T(128)} %bitcast.41, f32[]{:T(128)} %bitcast.40, f32[]{:T(128)} %bitcast.39, f32[]{:T(128)} %bitcast.38, f32[]{:T(128)} %bitcast.37, ...), kind=kLoop, calls=%fused_computation.567 | loop fusion | flops 11403264 | bytes 3145788 | tf_op jit(solution)/shard_map/log | solution.py:60
  121.7 45.1 %all-reduce.11.cloned.1.call-done = f32[24,16,1024]{2,1,0:T(8,128)} async-done(((f32[24,16,1024]{2,1,0:T(8,128)}), f32[24,16,1024]{2,1,0:T(8,128)}) %all-reduce.11.cloned.1.call-update) | async-done | bytes 1572880 | tf_op jit(solution)/shard_map/psum | solution.py:61
  169.8 4.6 %collective-permute-start.4 = (f32[7,16,1024]{2,1,0:T(8,128)S(1)}, f32[7,16,1024]{2,1,0:T(8,128)S(1)}, u32[]{:S(2)}, u32[]{:S(2)}) collective-permute-start(f32[7,16,1024]{2,1,0:T(8,128)S(1)} %get-tuple-element.7), channel_id=1, source_target_pairs={{0,4},{4,8},{8,12},{1,5},{5,9},{9,13},{2,6},{6,10},{10,14},{3,7},{... | collective-permute-start | bytes 1376264 | tf_op jit(solution)/shard_map/ppermute | solution.py:17
  174.4 8.2 %collective-permute-done.5 = f32[7,16,1024]{2,1,0:T(8,128)S(1)} collective-permute-done((f32[7,16,1024]{2,1,0:T(8,128)S(1)}, f32[7,16,1024]{2,1,0:T(8,128)S(1)}, u32[]{:S(2)}, u32[]{:S(2)}) %collective-permute-start.5) | collective-permute-done | bytes 458784 | tf_op jit(solution)/shard_map/ppermute | solution.py:18
  183.8 12.2 %fusion.155 = f32[24,16,1024]{2,1,0:T(8,128)S(1)} fusion(f32[24,16,1024]{2,1,0:T(8,128)S(1)} %exponential_multiply_fusion.1, f32[7,16,1024]{2,1,0:T(8,128)S(1)} %collective-permute-done.5, f32[7,16,1024]{2,1,0:T(8,128)S(1)} %collective-permute-done.4, f32[]{:T(128)} %bitcast.19, f32[]{:T(128)} %bitcast.18, f32[]{:T(128)} %bitcast.17, f32[]{:T(128)} %bitcast.16, ...), kind=kLoop, calls=%fused_computation.339 | loop fusion | flops 16908288 | bytes 4063292 | tf_op jit(solution)/shard_map/add | solution.py:30
  195.9 12.4 %fusion.298 = f32[24,16,1024]{2,1,0:T(8,128)S(1)} fusion(f32[24,16,1024]{2,1,0:T(8,128)S(1)} %fusion.155, f32[]{:T(128)} %bitcast.32, f32[]{:T(128)} %bitcast.31, f32[]{:T(128)} %bitcast.30, f32[]{:T(128)} %bitcast.29, f32[]{:T(128)} %bitcast.28, f32[]{:T(128)} %bitcast.27, f32[]{:T(128)} %bitcast.26, f32[]{:T(128)} %bitcast.25, f32[]{:T(128)} %bitcast.24, ...), kind=kLoop, calls=%fused_computation.482 | loop fusion | flops 11403264 | bytes 3145788 | tf_op jit(solution)/shard_map/add | solution.py:30
  208.3 15.3 %fusion.72 = f32[24,16,1024]{2,1,0:T(8,128)S(1)} fusion(f32[24,16,1024]{2,1,0:T(8,128)S(1)} %fusion.298, f32[1,24,16,1024]{3,2,1,0:T(8,128)S(1)} %copy-done.2, f32[]{:T(128)} %bitcast.45, f32[]{:T(128)} %bitcast.44, f32[]{:T(128)} %bitcast.43, f32[]{:T(128)} %bitcast.42, f32[]{:T(128)} %bitcast.41, f32[]{:T(128)} %bitcast.40, f32[]{:T(128)} %bitcast.39, ...), kind=kLoop, calls=%fused_computation.256 | loop fusion | flops 11796480 | bytes 4718652 | tf_op jit(solution)/shard_map/div | solution.py:55
  225.3 5.0 %collective-permute-start.6 = (f32[7,16,1024]{2,1,0:T(8,128)S(1)}, f32[7,16,1024]{2,1,0:T(8,128)S(1)}, u32[]{:S(2)}, u32[]{:S(2)}) collective-permute-start(f32[7,16,1024]{2,1,0:T(8,128)S(1)} %get-tuple-element.5), channel_id=1, source_target_pairs={{0,4},{4,8},{8,12},{1,5},{5,9},{9,13},{2,6},{6,10},{10,14},{3,7},{... | collective-permute-start | bytes 1376264 | tf_op jit(solution)/shard_map/ppermute | solution.py:17
  230.3 7.1 %collective-permute-done.7 = f32[7,16,1024]{2,1,0:T(8,128)S(1)} collective-permute-done((f32[7,16,1024]{2,1,0:T(8,128)S(1)}, f32[7,16,1024]{2,1,0:T(8,128)S(1)}, u32[]{:S(2)}, u32[]{:S(2)}) %collective-permute-start.7) | collective-permute-done | bytes 458784 | tf_op jit(solution)/shard_map/ppermute | solution.py:18
  238.8 12.2 %fusion.117 = f32[24,16,1024]{2,1,0:T(8,128)S(1)} fusion(f32[24,16,1024]{2,1,0:T(8,128)S(1)} %fusion.72, f32[7,16,1024]{2,1,0:T(8,128)S(1)} %collective-permute-done.7, f32[7,16,1024]{2,1,0:T(8,128)S(1)} %collective-permute-done.6, f32[]{:T(128)} %bitcast.19, f32[]{:T(128)} %bitcast.18, f32[]{:T(128)} %bitcast.17, f32[]{:T(128)} %bitcast.16, f32[]{:T(128)} %bitcast.15, ...), kind=kLoop, calls=%fused_computation.301 | loop fusion | flops 16908288 | bytes 4063292 | tf_op jit(solution)/shard_map/add | solution.py:30
  251.0 12.2 %fusion.326 = f32[24,16,1024]{2,1,0:T(8,128)S(1)} fusion(f32[24,16,1024]{2,1,0:T(8,128)S(1)} %fusion.117, f32[]{:T(128)} %bitcast.32, f32[]{:T(128)} %bitcast.31, f32[]{:T(128)} %bitcast.30, f32[]{:T(128)} %bitcast.29, f32[]{:T(128)} %bitcast.28, f32[]{:T(128)} %bitcast.27, f32[]{:T(128)} %bitcast.26, f32[]{:T(128)} %bitcast.25, f32[]{:T(128)} %bitcast.24, ...), kind=kLoop, calls=%fused_computation.510 | loop fusion | flops 11403264 | bytes 3145788 | tf_op jit(solution)/shard_map/add | solution.py:30
  263.2 16.2 %fusion.360 = f32[24,16,1024]{2,1,0:T(8,128)} fusion(f32[24,16,1024]{2,1,0:T(8,128)S(1)} %fusion.326, f32[]{:T(128)} %bitcast.45, f32[]{:T(128)} %bitcast.44, f32[]{:T(128)} %bitcast.43, f32[]{:T(128)} %bitcast.42, f32[]{:T(128)} %bitcast.41, f32[]{:T(128)} %bitcast.40, f32[]{:T(128)} %bitcast.39, f32[]{:T(128)} %bitcast.38, f32[]{:T(128)} %bitcast.37, ...), kind=kLoop, calls=%fused_computation.566 | loop fusion | flops 11403264 | bytes 3145788 | tf_op jit(solution)/shard_map/log | solution.py:60
  279.4 44.4 %all-reduce.13.cloned.1.call-done = f32[24,16,1024]{2,1,0:T(8,128)} async-done(((f32[24,16,1024]{2,1,0:T(8,128)}), f32[24,16,1024]{2,1,0:T(8,128)}) %all-reduce.13.cloned.1.call-update) | async-done | bytes 1572880 | tf_op jit(solution)/shard_map/psum | solution.py:61
  323.8 2.8 exponential_multiply_fusion
  (32 shorter events, 15.2 us)
Async XLA Ops:
  6.5 16.1 %copy-start = (f32[24,16,1024]{2,1,0:T(8,128)S(1)}, f32[24,16,1024]{2,1,0:T(8,128)}, u32[]{:S(2)}) copy-start(f32[24,16,1024]{2,1,0:T(8,128)} %param.5) | copy-start | bytes 4718596
  6.5 7.7 %copy-start.3 = (f32[1,3,15]{2,0,1:T(1,128)S(1)}, f32[1,3,15]{2,0,1:T(1,128)}, u32[]{:S(2)}) copy-start(f32[1,3,15]{2,0,1:T(1,128)} %param.4) | copy-start | bytes 544
  6.5 160.2 %all-reduce.11.cloned.1.call-start = ((), (), s32[]{:S(2)}) async-start(), calls=%async_computation | async-start | bytes 3145728 | tf_op jit(solution)/shard_map/psum | solution.py:61
  7.9 14.7 %collective-permute-start = (f32[7,16,1024]{2,1,0:T(8,128)S(1)}, f32[7,16,1024]{2,1,0:T(8,128)S(1)}, u32[]{:S(2)}, u32[]{:S(2)}) collective-permute-start(f32[7,16,1024]{2,1,0:T(8,128)S(1)} %get-tuple-element.13), channel_id=1, source_target_pairs={{0,4},{4,8},{8,12},{1,5},{5,9},{9,13},{2,6},{6,10},{10,14},{3,7},{... | collective-permute-start | bytes 1376264 | tf_op jit(solution)/shard_map/ppermute | solution.py:17
  12.9 13.9 %collective-permute-start.1 = (f32[7,16,1024]{2,1,0:T(8,128)S(1)}, f32[7,16,1024]{2,1,0:T(8,128)S(1)}, u32[]{:S(2)}, u32[]{:S(2)}) collective-permute-start(f32[7,16,1024]{2,1,0:T(8,128)S(1)} %get-tuple-element.14), channel_id=1, source_target_pairs={{4,0},{8,4},{12,8},{5,1},{9,5},{13,9},{6,2},{10,6},{14,10},{7,3},{... | collective-permute-start | bytes 1376264 | tf_op jit(solution)/shard_map/ppermute | solution.py:18
  38.9 12.4 %copy-start.1 = (f32[1,24,16,1024]{3,2,1,0:T(8,128)S(1)}, f32[1,24,16,1024]{3,2,1,0:T(8,128)}, u32[]{:S(2)}) copy-start(f32[1,24,16,1024]{3,2,1,0:T(8,128)} %param.3) | copy-start | bytes 4718596
  66.7 13.0 %collective-permute-start.3 = (f32[7,16,1024]{2,1,0:T(8,128)S(1)}, f32[7,16,1024]{2,1,0:T(8,128)S(1)}, u32[]{:S(2)}, u32[]{:S(2)}) collective-permute-start(f32[7,16,1024]{2,1,0:T(8,128)S(1)} %get-tuple-element.10), channel_id=1, source_target_pairs={{4,0},{8,4},{12,8},{5,1},{9,5},{13,9},{6,2},{10,6},{14,10},{7,3},{... | collective-permute-start | bytes 1376264 | tf_op jit(solution)/shard_map/ppermute | solution.py:18
  68.0 12.9 %collective-permute-start.2 = (f32[7,16,1024]{2,1,0:T(8,128)S(1)}, f32[7,16,1024]{2,1,0:T(8,128)S(1)}, u32[]{:S(2)}, u32[]{:S(2)}) collective-permute-start(f32[7,16,1024]{2,1,0:T(8,128)S(1)} %get-tuple-element.9), channel_id=1, source_target_pairs={{0,4},{4,8},{8,12},{1,5},{5,9},{9,13},{2,6},{6,10},{10,14},{3,7},{... | collective-permute-start | bytes 1376264 | tf_op jit(solution)/shard_map/ppermute | solution.py:17
  121.6 202.2 %all-reduce.13.cloned.1.call-start = ((), (), s32[]{:S(2)}) async-start(), calls=%async_computation.1 | async-start | bytes 3145728 | tf_op jit(solution)/shard_map/psum | solution.py:61
  168.5 14.0 %collective-permute-start.5 = (f32[7,16,1024]{2,1,0:T(8,128)S(1)}, f32[7,16,1024]{2,1,0:T(8,128)S(1)}, u32[]{:S(2)}, u32[]{:S(2)}) collective-permute-start(f32[7,16,1024]{2,1,0:T(8,128)S(1)} %get-tuple-element.8), channel_id=1, source_target_pairs={{4,0},{8,4},{12,8},{5,1},{9,5},{13,9},{6,2},{10,6},{14,10},{7,3},{... | collective-permute-start | bytes 1376264 | tf_op jit(solution)/shard_map/ppermute | solution.py:18
  169.8 13.9 %collective-permute-start.4 = (f32[7,16,1024]{2,1,0:T(8,128)S(1)}, f32[7,16,1024]{2,1,0:T(8,128)S(1)}, u32[]{:S(2)}, u32[]{:S(2)}) collective-permute-start(f32[7,16,1024]{2,1,0:T(8,128)S(1)} %get-tuple-element.7), channel_id=1, source_target_pairs={{0,4},{4,8},{8,12},{1,5},{5,9},{9,13},{2,6},{6,10},{10,14},{3,7},{... | collective-permute-start | bytes 1376264 | tf_op jit(solution)/shard_map/ppermute | solution.py:17
  195.9 12.4 %copy-start.2 = (f32[1,24,16,1024]{3,2,1,0:T(8,128)S(1)}, f32[1,24,16,1024]{3,2,1,0:T(8,128)}, u32[]{:S(2)}) copy-start(f32[1,24,16,1024]{3,2,1,0:T(8,128)} %param.3) | copy-start | bytes 4718596
  223.7 13.7 %collective-permute-start.7 = (f32[7,16,1024]{2,1,0:T(8,128)S(1)}, f32[7,16,1024]{2,1,0:T(8,128)S(1)}, u32[]{:S(2)}, u32[]{:S(2)}) collective-permute-start(f32[7,16,1024]{2,1,0:T(8,128)S(1)} %get-tuple-element.6), channel_id=1, source_target_pairs={{4,0},{8,4},{12,8},{5,1},{9,5},{13,9},{6,2},{10,6},{14,10},{7,3},{... | collective-permute-start | bytes 1376264 | tf_op jit(solution)/shard_map/ppermute | solution.py:18
  225.3 13.5 %collective-permute-start.6 = (f32[7,16,1024]{2,1,0:T(8,128)S(1)}, f32[7,16,1024]{2,1,0:T(8,128)S(1)}, u32[]{:S(2)}, u32[]{:S(2)}) collective-permute-start(f32[7,16,1024]{2,1,0:T(8,128)S(1)} %get-tuple-element.5), channel_id=1, source_target_pairs={{0,4},{4,8},{8,12},{1,5},{5,9},{9,13},{2,6},{6,10},{10,14},{3,7},{... | collective-permute-start | bytes 1376264 | tf_op jit(solution)/shard_map/ppermute | solution.py:17
Sparse Core Ops, SparseCore 0:
  121.7 44.9 all-reduce.10
  279.6 44.1 all-reduce.12
where the time goes:
time: 335 us; the launch traced here: 333 us
  other arithmetic  166 us (50%)
  waiting for transfers between devices  125 us (37%)
  starting transfers between devices  24.8 us (7%)
  between operations  13.7 us (4%)
  local copies, waits for them, and re-layouts  4.11 us (1%)
    add x8, other arithmetic, valid_along(): summed + weight * lax.slice_in_dim(padded, offset, offset + length_out, a...  97.8 us
    psum x2, waiting for transfers between devices, local(): log_total = lax.psum(log_terms, 'view')  89.5 us
    log x2, other arithmetic, local(): log_terms = jnp.log(correction)  32.4 us
    div x2, other arithmetic, local(): quotient = recorded[0] / blurred  30.7 us
    ppermute x4, waiting for transfers between devices, with_halo(): after = lax.ppermute(initial, axis, down)  25.9 us
    ppermute x4, starting transfers between devices, with_halo(): before = lax.ppermute(last, axis, up)  19.4 us
    ppermute x4, waiting for transfers between devices, with_halo(): before = lax.ppermute(last, axis, up)  9.9 us
  transfers between devices with their start and end apart: 10, of which 10 were waited for; matrix products, arithmetic and copies ran while one was open for 1% of the time, Pallas kernels for 0%

commit v1 on v0

v1 whole, which is shorter than its diff:
```python
import functools

import jax
import jax.numpy as jnp
from jax import lax
from jax.experimental import pallas as pl
from jax.experimental.pallas import tpu as pltpu
from jax.sharding import PartitionSpec as P

RADIUS = 7
ITERS = 2
TAPS = 2 * RADIUS + 1
LANES = 128
ROWS = 256
BF = jnp.bfloat16
F32 = jnp.float32
VMEM = pl.BlockSpec(memory_space=pltpu.VMEM)
SMEM = pl.BlockSpec(memory_space=pltpu.SMEM)
PARAMS = pltpu.CompilerParams(vmem_limit_bytes=60 * 1024 * 1024)


def halves(value):
    high = value.astype(BF)
    return high, (value - high.astype(F32)).astype(BF)


def dot(a, b):
    return jnp.dot(a, b, preferred_element_type=F32)


def dot3(a, b):
    return dot(a[0], b[0]) + (dot(a[1], b[0]) + dot(a[0], b[1]))


def operators_kernel(nz, kern, th, tl, wh, wl):
    planes = ROWS // nz
    i = lax.broadcasted_iota(jnp.int32, (2 * ROWS, ROWS), 0)
    o = lax.broadcasted_iota(jnp.int32, (2 * ROWS, ROWS), 1)
    shift_y = i - o - (LANES - RADIUS)
    row = lax.broadcasted_iota(jnp.int32, (ROWS, 2 * ROWS), 0)
    col = lax.broadcasted_iota(jnp.int32, (ROWS, 2 * ROWS), 1)
    shift_x = col // nz - row // nz
    shift_z = col % nz - row % nz + RADIUS
    for mirrored in range(2):
        ty = jnp.zeros((2 * ROWS, ROWS), F32)
        kx = jnp.zeros((ROWS, 2 * ROWS), F32)
        kz = jnp.zeros((ROWS, 2 * ROWS), F32)
        for k in range(TAPS):
            tap = TAPS - 1 - k if mirrored else k
            kx = jnp.where(shift_x == k, kern[0, tap], kx)
            kz = jnp.where(shift_z == k, kern[1, tap], kz)
            ty = jnp.where(shift_y == k, kern[2, tap], ty)
        th[mirrored], tl[mirrored] = halves(ty)
        wh[mirrored], wl[mirrored] = halves(kx * kz)


def operators(kern, nz):
    t = jax.ShapeDtypeStruct((2, 2 * ROWS, ROWS), BF)
    w = jax.ShapeDtypeStruct((2, ROWS, 2 * ROWS), BF)
    return pl.pallas_call(
        functools.partial(operators_kernel, nz),
        out_shape=(t, t, w, w),
        in_specs=[SMEM],
        out_specs=(VMEM,) * 4,
        compiler_params=PARAMS,
        name="operators",
    )(kern)


def blur_y(x, th, tl, store):
    width = x.shape[1]
    xh, xl = halves(x)
    for o0 in range(0, width, ROWS):
        size = min(ROWS, width - o0)
        k0, k1 = max(0, o0 - LANES), min(width, o0 + size + LANES)
        t0 = k0 - (o0 - LANES)
        rows = slice(t0, t0 + k1 - k0)
        t = (th[rows, :size], tl[rows, :size])
        store(o0, size, dot3((xh[:, k0:k1], xl[:, k0:k1]), t))


def blur_xz(dh, dl, wh, wl, nz, planes_out, store):
    width = dh.shape[1]
    step = ROWS // nz
    for p0 in range(0, planes_out, step):
        planes = min(step, planes_out - p0)
        m = planes * nz
        k = min(2 * ROWS, (planes_out + 2 * RADIUS - p0) * nz)
        for o0 in range(0, width, ROWS):
            size = min(ROWS, width - o0)
            d = (
                dh[p0 * nz : p0 * nz + k, o0 : o0 + size],
                dl[p0 * nz : p0 * nz + k, o0 : o0 + size],
            )
            store(p0 * nz, m, o0, size, dot3((wh[:m, :k], wl[:m, :k]), d))


def to_halves(dh, dl, r0, n):
    def store(o0, size, value):
        h, l = halves(value)
        dh[r0 : r0 + n, o0 : o0 + size] = h
        dl[r0 : r0 + n, o0 : o0 + size] = l

    return store


def chunks(rows, step=128):
    return [(r, min(step, rows - r)) for r in range(0, rows, step)]


def own_kernel(est, th, tl, dh, dl):
    for r0, n in chunks(est.shape[0]):
        blur_y(est[r0 : r0 + n, :], th.at[0], tl.at[0], to_halves(dh, dl, r0, n))


def own_blur_y(est, ops):
    out = jax.ShapeDtypeStruct(est.shape, BF)
    return pl.pallas_call(
        own_kernel,
        out_shape=(out, out),
        in_specs=[VMEM] * 3,
        out_specs=(VMEM, VMEM),
        compiler_params=PARAMS,
        name="own_blur_y",
    )(est, ops[0], ops[1])


def forward_kernel(nz, core, mine, other, oh, ol, th, tl, wh, wl, blurred, rims, dh, dl):
    width = oh.shape[1]
    half = nz // 2
    rim = mine.shape[1]
    c = core[0]
    a = pl.multiple_of(c * half, half)
    b = pl.multiple_of((1 - c) * half, half)
    for side in range(2):
        rims[side, :, pl.ds(a, half), :] = mine[side]
        rims[side, :, pl.ds(b, half), :] = other[side]
    own = oh.shape[0]
    for side in range(2):
        base = 0 if side == 0 else rim * nz + own
        flat = rims[side].reshape(rim * nz, width)
        for r0, n in chunks(rim * nz, 112):
            blur_y(flat[r0 : r0 + n, :], th.at[0], tl.at[0], to_halves(dh, dl, base + r0, n))
    dh[rim * nz : rim * nz + own, :] = oh[...]
    dl[rim * nz : rim * nz + own, :] = ol[...]

    def store(r0, m, o0, size, value):
        blurred[r0 : r0 + m, o0 : o0 + size] = value

    blur_xz(dh, dl, wh.at[0], wl.at[0], nz, blurred.shape[0] // nz, store)


def forward(core, mine, other, own, ops, nz):
    rim = mine.shape[1]
    rows, width = own[0].shape
    total = rows + 2 * rim * nz
    return pl.pallas_call(
        functools.partial(forward_kernel, nz),
        out_shape=jax.ShapeDtypeStruct((total - 2 * RADIUS * nz, width), F32),
        in_specs=[SMEM] + [VMEM] * 8,
        out_specs=VMEM,
        scratch_shapes=[
            pltpu.VMEM((2, rim, nz, width), F32),
            pltpu.VMEM((total, width), BF),
            pltpu.VMEM((total, width), BF),
        ],
        compiler_params=PARAMS,
        name="forward",
    )(core, mine, other, own[0], own[1], *ops)


def adjoint_kernel(nz, rim_rows, blurred, before, own, after, th, tl, wh, wl, added, out, dh, dl):
    rows = own.shape[0]
    parts = ((before, 0, rim_rows), (own, rim_rows, rows), (after, rim_rows + rows, rim_rows))
    for ref, base, count in parts:
        for r0, n in chunks(count):
            q = ref[r0 : r0 + n, :] / blurred[base + r0 : base + r0 + n, :]
            blur_y(q, th.at[1], tl.at[1], to_halves(dh, dl, base + r0, n))

    def store(r0, m, o0, size, value):
        log = jnp.log(value)
        if added is not None:
            log = log + added[r0 : r0 + m, o0 : o0 + size]
        out[r0 : r0 + m, o0 : o0 + size] = log

    blur_xz(dh, dl, wh.at[1], wl.at[1], nz, rows // nz, store)


def adjoint(blurred, before, own, after, ops, added, nz):
    rows, width = own.shape
    args = [blurred, before, own, after, *ops]
    kernel = functools.partial(adjoint_kernel, nz, before.shape[0])
    if added is None:
        body = lambda *refs: kernel(*refs[:8], None, *refs[8:])
    else:
        body = kernel
        args.append(added)
    return pl.pallas_call(
        body,
        out_shape=jax.ShapeDtypeStruct((rows, width), F32),
        in_specs=[VMEM] * len(args),
        out_specs=VMEM,
        scratch_shapes=[pltpu.VMEM(blurred.shape, BF), pltpu.VMEM(blurred.shape, BF)],
        compiler_params=PARAMS,
        name="adjoint",
    )(*args)


def local(recorded, psf_taps, estimate):
    views = lax.axis_size("view")
    cores = 2
    chips = views // cores
    tiles = lax.axis_size("tile")
    nx, nz, ny = estimate.shape
    half = nz // 2
    place = lax.axis_index("view")
    chip, core = place // cores, place % cores
    core_arr = core.astype(jnp.int32).reshape(1)

    part = ny // chips
    width = min(ny, part + (LANES if chips <= 2 else 2 * LANES))

    def start_of(c):
        return jnp.clip(c * part - LANES, 0, ny - width)

    start = start_of(chip)

    def window(values, of):
        return lax.dynamic_slice_in_dim(values, start_of(of), width, axis=2)

    def swap_core(values):
        pairs = [(v, v ^ 1) for v in range(views)]
        return lax.ppermute(values, "view", pairs)

    def to_chip(values, r):
        pairs = [(v, (v + r * cores) % views) for v in range(views)]
        return lax.ppermute(values, "view", pairs)

    up = [(t, t + 1) for t in range(tiles - 1)]
    down = [(t + 1, t) for t in range(tiles - 1)]

    def rims(first, last):
        return lax.ppermute(last, "tile", up), lax.ppermute(first, "tile", down)

    def estimate_rims(est):
        sel = lax.dynamic_slice_in_dim(est, core * half, half, axis=1)
        mine = jnp.stack(rims(sel[: 2 * RADIUS], sel[nx - 2 * RADIUS :]))
        return mine, swap_core(mine)

    recorded = recorded[0]
    est = window(estimate, chip)
    est_rims = estimate_rims(est)

    kern = psf_taps[0] / jnp.sum(psf_taps[0], axis=1, keepdims=True)
    kerns = [kern] + [to_chip(kern, r) for r in range(1, chips)]

    own = window(recorded, chip)
    record = [(own, *rims(own[:RADIUS], own[nx - RADIUS :]))]
    for r in range(1, chips):
        sent = window(recorded, (chip + r) % chips)
        edges = to_chip(jnp.concatenate([sent[:RADIUS], sent[nx - RADIUS :]]), r)
        middle = to_chip(sent[RADIUS : nx - RADIUS], r)
        first, last = edges[:RADIUS], edges[RADIUS:]
        record.append((jnp.concatenate([first, middle, last]), *rims(first, last)))

    ops = [operators(k, nz) for k in kerns]
    flat = lambda a: a.reshape(-1, a.shape[-1])

    for iteration in range(ITERS):
        if iteration:
            est_rims = estimate_rims(est)
        total = None
        owns = [own_blur_y(flat(est), op[:2]) for op in ops]
        for rec, op, done in zip(record, ops, owns):
            blurred = forward(core_arr, *est_rims, done, op, nz)
            total = adjoint(blurred, flat(rec[1]), flat(rec[0]), flat(rec[2]), op, total, nz)
        if iteration < ITERS - 1:
            total = (total + swap_core(total)).reshape(est.shape)
            est = est * jnp.exp(total / views)

    offset = chip * part - start
    total = lax.dynamic_slice_in_dim(total.reshape(est.shape), offset, part, axis=2)
    est = lax.dynamic_slice_in_dim(est, offset, part, axis=2)
    pick = lambda a, c: lax.dynamic_slice_in_dim(a, c * half, half, axis=1)
    total = pick(total, core) + swap_core(pick(total, 1 - core))
    est = pick(est, core) * jnp.exp(total / views)
    parts = jnp.stack([est] + [to_chip(est, r) for r in range(1, chips)])
    others = swap_core(parts)
    joined = jnp.where(
        core == 0, jnp.concatenate([parts, others], 2), jnp.concatenate([others, parts], 2)
    )
    out = jnp.zeros((nx, nz, ny), F32)
    for r in range(chips):
        at = ((chip - r) % chips) * part
        out = lax.dynamic_update_slice_in_dim(out, joined[r], at, axis=2)
    return out


def solution(mesh):
    in_specs = (P("view", "tile", "slab", None), P("view", None, None), P("tile", "slab", None))
    out_specs = P("tile", "slab", None)
    return jax.shard_map(local, mesh=mesh, in_specs=in_specs, out_specs=out_specs, check_vma=False)
```

time: 335 us -> 150 us (0.45)
  other arithmetic: 166 us -> 7.92 us
  waiting for transfers between devices: 125 us -> 29.7 us
  Pallas kernels: 0 us -> 69.2 us
  between operations: 13.7 us -> 0.31 us
  local copies, waits for them, and re-layouts: 4.11 us -> 14.3 us
  starting transfers between devices: 24.8 us -> 28.4 us
    add x8 -> x0, other arithmetic: 97.8 us -> none  [valid_along(): summed + weight * lax.slice_in_dim(padded, offset, offset + length_out, a...]
    psum x2 -> x0, waiting for transfers between devices: 89.5 us -> none  [local(): log_total = lax.psum(log_terms, 'view')]
    pallas_call x0 -> x14, Pallas kernels: none -> 69.2 us  [the longest x4 24.1 us: forward(): pl.pallas_call(functools.partial(forward_kernel, nz), out_shape=jax.Shape...]
    log x2 -> x0, other arithmetic: 32.4 us -> none  [local(): log_terms = jnp.log(correction)]
    div x3 -> x1, other arithmetic: 30.7 us -> 0.07 us  [local(): kern = psf_taps[0] / jnp.sum(psf_taps[0], axis=1, keepdims=True)]
    ppermute x8 -> x17, waiting for transfers between devices: 35.8 us -> 29.7 us  [the longest x4 13.4 us: to_chip(): return lax.ppermute(values, 'view', pairs)]
    dynamic_slice x0 -> x3, local copies, waits for them, and re-layouts: none -> 3.74 us  [the longest x2 2.54 us: window(): return lax.dynamic_slice_in_dim(values, start_of(of), width, axis=2)]
    ppermute x8 -> x17, starting transfers between devices: 24.7 us -> 28.4 us  [the longest x8 21.8 us: rims(): return (lax.ppermute(last, 'tile', up), lax.ppermute(first, 'tile', down))]
  transfers between devices with their start and end apart: 10 -> 17, of which waited for: 10 -> 8; matrix products, arithmetic and copies ran while one was open for 1% -> 7% of each run, Pallas kernels for 0% -> 26%
where the time goes in v1:
time: 150 us
  Pallas kernels  69.2 us (46%)
  waiting for transfers between devices  29.7 us (20%)
  starting transfers between devices  28.4 us (19%)
  local copies, waits for them, and re-layouts  14.3 us (10%)
  other arithmetic  7.92 us (5%)
    pallas_call x4, Pallas kernels, forward(): pl.pallas_call(functools.partial(forward_kernel, nz), out_shape=jax.Shape...  24.1 us
    pallas_call x4, Pallas kernels, adjoint(): pl.pallas_call(body, out_shape=jax.ShapeDtypeStruct((rows, width), F32),...  23.7 us
    ppermute x8, starting transfers between devices, rims(): return (lax.ppermute(last, 'tile', up), lax.ppermute(first, 'tile', down))  21.8 us
    pallas_call x4, Pallas kernels, own_blur_y(): pl.pallas_call(own_kernel, out_shape=(out, out), in_specs=[VMEM] * 3, out...  13.6 us
    ppermute x4, waiting for transfers between devices, to_chip(): return lax.ppermute(values, 'view', pairs)  13.4 us
    ppermute x8, waiting for transfers between devices, rims(): return (lax.ppermute(last, 'tile', up), lax.ppermute(first, 'tile', down))  9.89 us
    pallas_call x2, Pallas kernels, operators(): pl.pallas_call(functools.partial(operators_kernel, nz), out_shape=(t, t,...  7.79 us
    ppermute x5, waiting for transfers between devices, swap_core(): return lax.ppermute(values, 'view', pairs)  6.35 us
  transfers between devices with their start and end apart: 17, of which 8 were waited for; matrix products, arithmetic and copies ran while one was open for 7% of the time, Pallas kernels for 26%

profile of v1, /device:TPU:0, one launch (start us, length us, event | category | flops | bytes accessed | tf_op | source)
XLA Modules:
  0.0 149.8 jit_solution(2950867488777464391)
XLA Ops:
  3.4 3.0 %collective-permute-start.4 = (f32[14,16,640]{2,1,0:T(8,128)}, f32[14,16,640]{2,1,0:T(8,128)}, u32[]{:S(2)}, u32[]{:S(2)}) collective-permute-start(f32[14,16,640]{2,1,0:T(8,128)} %pad_maximum_fusion.3), channel_id=1, source_target_pairs={{0,2},{1,3},{2,0},{3,1},{4,6},{5,7},{6,4},{7,5},{8,10},{9,11},{10,... | collective-permute-start | bytes 1720328 | tf_op jit(solution)/shard_map/ppermute | solution.py:237
  7.4 3.5 %collective-permute-start = (f32[14,8,640]{2,1,0:T(8,128)}, f32[14,8,640]{2,1,0:T(8,128)S(1)}, u32[]{:S(2)}, u32[]{:S(2)}) collective-permute-start(f32[14,8,640]{2,1,0:T(8,128)} %get-tuple-element.41), channel_id=1, source_target_pairs={{0,4},{4,8},{8,12},{1,5},{5,9},{9,13},{2,6},{6,10},{10,14},{3,7},{... | collective-permute-start | bytes 860168 | tf_op jit(solution)/shard_map/ppermute | solution.py:243
  12.2 5.3 %collective-permute-start.8 = (f32[7,16,640]{2,1,0:T(8,128)}, f32[7,16,640]{2,1,0:T(8,128)}, u32[]{:S(2)}, u32[]{:S(2)}) collective-permute-start(f32[7,16,640]{2,1,0:T(8,128)} %get-tuple-element.38), channel_id=1, source_target_pairs={{0,4},{4,8},{8,12},{1,5},{5,9},{9,13},{2,6},{6,10},{10,14},{3,7},{... | collective-permute-start | bytes 860168 | tf_op jit(solution)/shard_map/ppermute | solution.py:243
  25.2 3.7 %collective-permute-done.3.kern = f32[3,15]{1,0:T(4,128)S(1)} collective-permute-done((f32[3,15]{1,0:T(4,128)S(1)}, f32[3,15]{1,0:T(4,128)S(1)}, u32[]{:S(2)}, u32[]{:S(2)}) %collective-permute-start.3) | collective-permute-done | bytes 212 | tf_op jit(solution)/shard_map/ppermute | solution.py:237
  28.9 3.4 %collective-permute-start.5 = (f32[7,16,640]{2,1,0:T(8,128)}, f32[7,16,640]{2,1,0:T(8,128)S(1)}, u32[]{:S(2)}, u32[]{:S(2)}) collective-permute-start(f32[7,16,640]{2,1,0:T(8,128)} %get-tuple-element.46), channel_id=1, source_target_pairs={{0,4},{4,8},{8,12},{1,5},{5,9},{9,13},{2,6},{6,10},{10,14},{3,7},{... | collective-permute-start | bytes 860168 | tf_op jit(solution)/shard_map/ppermute | solution.py:243
  34.8 3.9 %operators.3 = (bf16[2,512,256]{2,1,0:T(8,128)(2,1)}, bf16[2,512,256]{2,1,0:T(8,128)(2,1)}, bf16[2,256,512]{2,1,0:T(8,128)(2,1)}, bf16[2,256,512]{2,1,0:T(8,128)(2,1)}) custom-call(f32[3,15]{1,0:T(4,128)} %copy-done.8), custom_call_target="tpu_custom_call" | custom-call | tf_op jit(solution)/shard_map/operators/pallas_call | solution.py:60
  38.7 3.4 %own_blur_y.5 = (bf16[384,640]{1,0:T(8,128)(2,1)}, bf16[384,640]{1,0:T(8,128)(2,1)}) custom-call(f32[384,640]{1,0:T(8,128)} %bitcast.43, bf16[2,512,256]{2,1,0:T(8,128)(2,1)} %get-tuple-element.27.th.refs_4_, bf16[2,512,256]{2,1,0:T(8,128)(2,1)} %get-tuple-element.28.tl.refs_5_), custom_call_target="tpu_custom_call" | custom-call | tf_op jit(solution)/shard_map/own_blur_y/pallas_call | solution.py:118
  43.4 3.9 %operators.2 = (bf16[2,512,256]{2,1,0:T(8,128)(2,1)}, bf16[2,512,256]{2,1,0:T(8,128)(2,1)}, bf16[2,256,512]{2,1,0:T(8,128)(2,1)}, bf16[2,256,512]{2,1,0:T(8,128)(2,1)}) custom-call(f32[3,15]{1,0:T(4,128)} %copy-done.10), custom_call_target="tpu_custom_call" | custom-call | tf_op jit(solution)/shard_map/operators/pallas_call | solution.py:60
  47.2 3.4 %own_blur_y.4 = (bf16[384,640]{1,0:T(8,128)(2,1)}, bf16[384,640]{1,0:T(8,128)(2,1)}) custom-call(f32[384,640]{1,0:T(8,128)} %bitcast.44, bf16[2,512,256]{2,1,0:T(8,128)(2,1)} %get-tuple-element.21.th, bf16[2,512,256]{2,1,0:T(8,128)(2,1)} %get-tuple-element.22.tl), custom_call_target="tpu_custom_call" | custom-call | tf_op jit(solution)/shard_map/own_blur_y/pallas_call | solution.py:118
  52.8 6.0 %forward.5.refs_0_ = f32[608,640]{1,0:T(8,128)} custom-call(s32[1]{0:T(128)} %bitcast.core, f32[2,14,8,640]{3,2,1,0:T(8,128)} %copy-done.1, f32[2,14,8,640]{3,2,1,0:T(8,128)} %collective-permute-done.2.other, bf16[384,640]{1,0:T(8,128)(2,1)} %get-tuple-element.29.oh, bf16[384,640]{1,0:T(8,128)(2,1)} %get-tuple-element.30.ol, ...), custom_call_target="tpu_custom_call" | custom-call | tf_op jit(solution)/shard_map/forward/pallas_call | solution.py:157
  58.8 5.8 %adjoint.4.added = f32[384,640]{1,0:T(8,128)} custom-call(f32[608,640]{1,0:T(8,128)} %forward.5.refs_0_, f32[112,640]{1,0:T(8,128)} %bitcast.11.refs_1_, f32[384,640]{1,0:T(8,128)} %bitcast.41, f32[112,640]{1,0:T(8,128)} %bitcast.14.refs_3_, bf16[2,512,256]{2,1,0:T(8,128)(2,1)} %get-tuple-element.27.th.refs_4_, ...), custom_call_target="tpu_custom_call" | custom-call | tf_op jit(solution)/shard_map/adjoint/pallas_call | solution.py:198
  64.6 6.1 %forward.4.blurred = f32[608,640]{1,0:T(8,128)} custom-call(s32[1]{0:T(128)} %bitcast.core, f32[2,14,8,640]{3,2,1,0:T(8,128)} %copy-done.1, f32[2,14,8,640]{3,2,1,0:T(8,128)} %collective-permute-done.2.other, bf16[384,640]{1,0:T(8,128)(2,1)} %get-tuple-element.23.oh, bf16[384,640]{1,0:T(8,128)(2,1)} %get-tuple-element.24.ol, ...), custom_call_target="tpu_custom_call" | custom-call | tf_op jit(solution)/shard_map/forward/pallas_call | solution.py:157
  71.5 6.1 %adjoint.5 = f32[384,640]{1,0:T(8,128)} custom-call(f32[608,640]{1,0:T(8,128)} %forward.4.blurred, f32[112,640]{1,0:T(8,128)} %bitcast.52, f32[384,640]{1,0:T(8,128)} %bitcast.39, f32[112,640]{1,0:T(8,128)} %bitcast.9.after, bf16[2,512,256]{2,1,0:T(8,128)(2,1)} %get-tuple-element.21.th, bf16[2,512,256]{2,1,0:T(8,128)(2,1)} %get-tuple-element.22.tl, ...), custom_call_target="tpu_custom_call" | custom-call | tf_op jit(solution)/shard_map/adjoint/pallas_call | solution.py:198
  77.6 2.8 %collective-permute-done.10 = f32[384,640]{1,0:T(8,128)S(1)} collective-permute-done((f32[384,640]{1,0:T(8,128)}, f32[384,640]{1,0:T(8,128)S(1)}, u32[]{:S(2)}, u32[]{:S(2)}) %collective-permute-start.10) | collective-permute-done | bytes 983072 | tf_op jit(solution)/shard_map/ppermute | solution.py:233
  82.1 4.6 %collective-permute-start.11 = (f32[14,8,640]{2,1,0:T(8,128)S(1)}, f32[14,8,640]{2,1,0:T(8,128)S(1)}, u32[]{:S(2)}, u32[]{:S(2)}) collective-permute-start(f32[14,8,640]{2,1,0:T(8,128)S(1)} %get-tuple-element.43), channel_id=1, source_target_pairs={{0,4},{4,8},{8,12},{1,5},{5,9},{9,13},{2,6},{6,10},{10,14},{3,7},{... | collective-permute-start | bytes 860168 | tf_op jit(solution)/shard_map/ppermute | solution.py:243
  88.0 5.1 %collective-permute-done.11 = f32[14,8,640]{2,1,0:T(8,128)S(1)} collective-permute-done((f32[14,8,640]{2,1,0:T(8,128)S(1)}, f32[14,8,640]{2,1,0:T(8,128)S(1)}, u32[]{:S(2)}, u32[]{:S(2)}) %collective-permute-start.11) | collective-permute-done | bytes 286752 | tf_op jit(solution)/shard_map/ppermute | solution.py:243
  93.0 4.1 %collective-permute-done.12 = f32[14,8,640]{2,1,0:T(8,128)S(1)} collective-permute-done((f32[14,8,640]{2,1,0:T(8,128)S(1)}, f32[14,8,640]{2,1,0:T(8,128)S(1)}, u32[]{:S(2)}, u32[]{:S(2)}) %collective-permute-start.12) | collective-permute-done | bytes 286752 | tf_op jit(solution)/shard_map/ppermute | solution.py:243
  97.3 3.5 %own_blur_y.7 = (bf16[384,640]{1,0:T(8,128)(2,1)}, bf16[384,640]{1,0:T(8,128)(2,1)}) custom-call(f32[384,640]{1,0:T(8,128)} %bitcast.37, bf16[2,512,256]{2,1,0:T(8,128)(2,1)} %get-tuple-element.27.th.refs_4_, bf16[2,512,256]{2,1,0:T(8,128)(2,1)} %get-tuple-element.28.tl.refs_5_), custom_call_target="tpu_custom_call" | custom-call | tf_op jit(solution)/shard_map/own_blur_y/pallas_call | solution.py:118
  100.8 3.4 %own_blur_y.6 = (bf16[384,640]{1,0:T(8,128)(2,1)}, bf16[384,640]{1,0:T(8,128)(2,1)}) custom-call(f32[384,640]{1,0:T(8,128)} %bitcast.38, bf16[2,512,256]{2,1,0:T(8,128)(2,1)} %get-tuple-element.21.th, bf16[2,512,256]{2,1,0:T(8,128)(2,1)} %get-tuple-element.22.tl), custom_call_target="tpu_custom_call" | custom-call | tf_op jit(solution)/shard_map/own_blur_y/pallas_call | solution.py:118
  105.0 6.0 %forward.7.refs_0_ = f32[608,640]{1,0:T(8,128)} custom-call(s32[1]{0:T(128)} %bitcast.core, f32[2,14,8,640]{3,2,1,0:T(8,128)} %copy-done.2, f32[2,14,8,640]{3,2,1,0:T(8,128)} %copy-done.5, bf16[384,640]{1,0:T(8,128)(2,1)} %get-tuple-element.35.oh, bf16[384,640]{1,0:T(8,128)(2,1)} %get-tuple-element.36.ol, bf16[2,512,256]{2,1,0:T(8,128)(2,1)} %get-tuple-element.27.th.refs_4_, ...), custom_call_target="tpu_custom_call" | custom-call | tf_op jit(solution)/shard_map/forward/pallas_call | solution.py:157
  111.0 5.7 %adjoint.6.added = f32[384,640]{1,0:T(8,128)} custom-call(f32[608,640]{1,0:T(8,128)} %forward.7.refs_0_, f32[112,640]{1,0:T(8,128)} %bitcast.11.refs_1_, f32[384,640]{1,0:T(8,128)} %bitcast.42, f32[112,640]{1,0:T(8,128)} %bitcast.14.refs_3_, bf16[2,512,256]{2,1,0:T(8,128)(2,1)} %get-tuple-element.27.th.refs_4_, ...), custom_call_target="tpu_custom_call" | custom-call | tf_op jit(solution)/shard_map/adjoint/pallas_call | solution.py:198
  116.7 6.0 %forward.6.blurred = f32[608,640]{1,0:T(8,128)} custom-call(s32[1]{0:T(128)} %bitcast.core, f32[2,14,8,640]{3,2,1,0:T(8,128)} %copy-done.2, f32[2,14,8,640]{3,2,1,0:T(8,128)} %copy-done.5, bf16[384,640]{1,0:T(8,128)(2,1)} %get-tuple-element.33.oh, bf16[384,640]{1,0:T(8,128)(2,1)} %get-tuple-element.34.ol, bf16[2,512,256]{2,1,0:T(8,128)(2,1)} %get-tuple-element.21.th, ...), custom_call_target="tpu_custom_call" | custom-call | tf_op jit(solution)/shard_map/forward/pallas_call | solution.py:157
  122.7 6.1 %adjoint.7 = f32[384,640]{1,0:T(8,128)} custom-call(f32[608,640]{1,0:T(8,128)} %forward.6.blurred, f32[112,640]{1,0:T(8,128)} %bitcast.53, f32[384,640]{1,0:T(8,128)} %bitcast.40, f32[112,640]{1,0:T(8,128)} %bitcast.9.after, bf16[2,512,256]{2,1,0:T(8,128)(2,1)} %get-tuple-element.21.th, bf16[2,512,256]{2,1,0:T(8,128)(2,1)} %get-tuple-element.22.tl, ...), custom_call_target="tpu_custom_call" | custom-call | tf_op jit(solution)/shard_map/adjoint/pallas_call | solution.py:198
  135.1 9.8 %collective-permute-done.15 = f32[24,8,512]{2,1,0:T(8,128)S(1)} collective-permute-done((f32[24,8,512]{2,1,0:T(8,128)S(1)}, f32[24,8,512]{2,1,0:T(8,128)S(1)}, u32[]{:S(2)}, u32[]{:S(2)}) %collective-permute-start.15) | collective-permute-done | bytes 393248 | tf_op jit(solution)/shard_map/ppermute | solution.py:237
  (68 shorter events, 35.2 us)
Async XLA Ops:
  2.6 14.9 %copy-start.3 = (f32[1,24,16,1024]{3,2,1,0:T(8,128)S(1)}, f32[1,24,16,1024]{3,2,1,0:T(8,128)}, u32[]{:S(2)}) copy-start(f32[1,24,16,1024]{3,2,1,0:T(8,128)} %param.3) | copy-start | bytes 4718596
  2.6 16.4 %copy-start.9 = (f32[1,3,15]{2,0,1:T(1,128)S(1)}, f32[1,3,15]{2,0,1:T(1,128)}, u32[]{:S(2)}) copy-start(f32[1,3,15]{2,0,1:T(1,128)} %param.4) | copy-start | bytes 544
  3.4 19.6 %collective-permute-start.4 = (f32[14,16,640]{2,1,0:T(8,128)}, f32[14,16,640]{2,1,0:T(8,128)}, u32[]{:S(2)}, u32[]{:S(2)}) collective-permute-start(f32[14,16,640]{2,1,0:T(8,128)} %pad_maximum_fusion.3), channel_id=1, source_target_pairs={{0,2},{1,3},{2,0},{3,1},{4,6},{5,7},{6,4},{7,5},{8,10},{9,11},{10,... | collective-permute-start | bytes 1720328 | tf_op jit(solution)/shard_map/ppermute | solution.py:237
  7.4 11.7 %collective-permute-start = (f32[14,8,640]{2,1,0:T(8,128)}, f32[14,8,640]{2,1,0:T(8,128)S(1)}, u32[]{:S(2)}, u32[]{:S(2)}) collective-permute-start(f32[14,8,640]{2,1,0:T(8,128)} %get-tuple-element.41), channel_id=1, source_target_pairs={{0,4},{4,8},{8,12},{1,5},{5,9},{9,13},{2,6},{6,10},{10,14},{3,7},{... | collective-permute-start | bytes 860168 | tf_op jit(solution)/shard_map/ppermute | solution.py:243
  10.9 10.2 %collective-permute-start.1 = (f32[14,8,640]{2,1,0:T(8,128)}, f32[14,8,640]{2,1,0:T(8,128)}, u32[]{:S(2)}, u32[]{:S(2)}) collective-permute-start(f32[14,8,640]{2,1,0:T(8,128)} %get-tuple-element.42), channel_id=1, source_target_pairs={{4,0},{8,4},{12,8},{5,1},{9,5},{13,9},{6,2},{10,6},{14,10},{7,3},{... | collective-permute-start | bytes 860168 | tf_op jit(solution)/shard_map/ppermute | solution.py:243
  12.2 46.6 %collective-permute-start.8 = (f32[7,16,640]{2,1,0:T(8,128)}, f32[7,16,640]{2,1,0:T(8,128)}, u32[]{:S(2)}, u32[]{:S(2)}) collective-permute-start(f32[7,16,640]{2,1,0:T(8,128)} %get-tuple-element.38), channel_id=1, source_target_pairs={{0,4},{4,8},{8,12},{1,5},{5,9},{9,13},{2,6},{6,10},{10,14},{3,7},{... | collective-permute-start | bytes 860168 | tf_op jit(solution)/shard_map/ppermute | solution.py:243
  18.4 13.8 %collective-permute-start.6 = (f32[10,16,640]{2,1,0:T(8,128)}, f32[10,16,640]{2,1,0:T(8,128)}, u32[]{:S(2)}, u32[]{:S(2)}) collective-permute-start(f32[10,16,640]{2,1,0:T(8,128)} %dynamic-slice_bitcast_fusion), channel_id=1, source_target_pairs={{0,2},{1,3},{2,0},{3,1},{4,6},{5,7},{6,4},{7,5},{8,10},{9,11},{10,... | collective-permute-start | bytes 1228808 | tf_op jit(solution)/shard_map/ppermute | solution.py:237
  19.1 15.7 %copy-start.8 = (f32[3,15]{1,0:T(4,128)}, f32[3,15]{1,0:T(4,128)S(1)}, u32[]{:S(2)}) copy-start(f32[3,15]{1,0:T(4,128)S(1)} %bitcast_divide_fusion.kern) | copy-start | bytes 544
  19.1 39.7 %collective-permute-start.9 = (f32[7,16,640]{2,1,0:T(8,128)}, f32[7,16,640]{2,1,0:T(8,128)}, u32[]{:S(2)}, u32[]{:S(2)}) collective-permute-start(f32[7,16,640]{2,1,0:T(8,128)} %get-tuple-element.37), channel_id=1, source_target_pairs={{4,0},{8,4},{12,8},{5,1},{9,5},{13,9},{6,2},{10,6},{14,10},{7,3},{... | collective-permute-start | bytes 860168 | tf_op jit(solution)/shard_map/ppermute | solution.py:243
  21.1 7.7 %collective-permute-start.3 = (f32[3,15]{1,0:T(4,128)S(1)}, f32[3,15]{1,0:T(4,128)S(1)}, u32[]{:S(2)}, u32[]{:S(2)}) collective-permute-start(f32[3,15]{1,0:T(4,128)S(1)} %bitcast_divide_fusion.kern), channel_id=1, source_target_pairs={{0,2},{1,3},{2,0},{3,1},{4,6},{5,7},{6,4},{7,5},{8,10},{9,11},{10,... | collective-permute-start | bytes 548 | tf_op jit(solution)/shard_map/ppermute | solution.py:237
  23.0 19.1 %copy-start.1 = (f32[2,14,8,640]{3,2,1,0:T(8,128)}, f32[2,14,8,640]{3,2,1,0:T(8,128)S(1)}, u32[]{:S(2)}) copy-start(f32[2,14,8,640]{3,2,1,0:T(8,128)S(1)} %pad_maximum_fusion.2.mine) | copy-start | bytes 1720324
  23.0 29.8 %collective-permute-start.2 = (f32[2,14,8,640]{3,2,1,0:T(8,128)S(1)}, f32[2,14,8,640]{3,2,1,0:T(8,128)}, u32[]{:S(2)}, u32[]{:S(2)}) collective-permute-start(f32[2,14,8,640]{3,2,1,0:T(8,128)S(1)} %pad_maximum_fusion.2.mine), channel_id=1, source_target_pairs={{0,1},{1,0},{2,3},{3,2},{4,5},{5,4},{6,7},{7,6},{8,9},{9,8},{10,11... | collective-permute-start | bytes 1720328 | tf_op jit(solution)/shard_map/ppermute | solution.py:233
  28.8 13.2 %copy-start.10 = (f32[3,15]{1,0:T(4,128)}, f32[3,15]{1,0:T(4,128)S(1)}, u32[]{:S(2)}) copy-start(f32[3,15]{1,0:T(4,128)S(1)} %collective-permute-done.3.kern) | copy-start | bytes 544
  28.9 41.9 %collective-permute-start.5 = (f32[7,16,640]{2,1,0:T(8,128)}, f32[7,16,640]{2,1,0:T(8,128)S(1)}, u32[]{:S(2)}, u32[]{:S(2)}) collective-permute-start(f32[7,16,640]{2,1,0:T(8,128)} %get-tuple-element.46), channel_id=1, source_target_pairs={{0,4},{4,8},{8,12},{1,5},{5,9},{9,13},{2,6},{6,10},{10,14},{3,7},{... | collective-permute-start | bytes 860168 | tf_op jit(solution)/shard_map/ppermute | solution.py:243
  32.2 38.5 %collective-permute-start.7 = (f32[7,16,640]{2,1,0:T(8,128)}, f32[7,16,640]{2,1,0:T(8,128)}, u32[]{:S(2)}, u32[]{:S(2)}) collective-permute-start(f32[7,16,640]{2,1,0:T(8,128)} %get-tuple-element.45), channel_id=1, source_target_pairs={{4,0},{8,4},{12,8},{5,1},{9,5},{13,9},{6,2},{10,6},{14,10},{7,3},{... | collective-permute-start | bytes 860168 | tf_op jit(solution)/shard_map/ppermute | solution.py:243
  77.6 2.8 %collective-permute-start.10 = (f32[384,640]{1,0:T(8,128)}, f32[384,640]{1,0:T(8,128)S(1)}, u32[]{:S(2)}, u32[]{:S(2)}) collective-permute-start(f32[384,640]{1,0:T(8,128)} %adjoint.5), channel_id=1, source_target_pairs={{0,1},{1,0},{2,3},{3,2},{4,5},{5,4},{6,7},{7,6},{8,9},{9,8},{10,11... | collective-permute-start | bytes 2949128 | tf_op jit(solution)/shard_map/ppermute | solution.py:233
  82.0 15.3 %copy-start = (f32[24,16,640]{2,1,0:T(8,128)}, f32[24,16,640]{2,1,0:T(8,128)S(1)}, u32[]{:S(2)}) copy-start(f32[24,16,640]{2,1,0:T(8,128)S(1)} %fusion.4) | copy-start | bytes 2949124
  82.1 10.9 %collective-permute-start.11 = (f32[14,8,640]{2,1,0:T(8,128)S(1)}, f32[14,8,640]{2,1,0:T(8,128)S(1)}, u32[]{:S(2)}, u32[]{:S(2)}) collective-permute-start(f32[14,8,640]{2,1,0:T(8,128)S(1)} %get-tuple-element.43), channel_id=1, source_target_pairs={{0,4},{4,8},{8,12},{1,5},{5,9},{9,13},{2,6},{6,10},{10,14},{3,7},{... | collective-permute-start | bytes 860168 | tf_op jit(solution)/shard_map/ppermute | solution.py:243
  86.7 10.5 %collective-permute-start.12 = (f32[14,8,640]{2,1,0:T(8,128)S(1)}, f32[14,8,640]{2,1,0:T(8,128)S(1)}, u32[]{:S(2)}, u32[]{:S(2)}) collective-permute-start(f32[14,8,640]{2,1,0:T(8,128)S(1)} %get-tuple-element.44), channel_id=1, source_target_pairs={{4,0},{8,4},{12,8},{5,1},{9,5},{13,9},{6,2},{10,6},{14,10},{7,3},{... | collective-permute-start | bytes 860168 | tf_op jit(solution)/shard_map/ppermute | solution.py:243
  97.2 7.0 %copy-start.2 = (f32[2,14,8,640]{3,2,1,0:T(8,128)}, f32[2,14,8,640]{3,2,1,0:T(8,128)S(1)}, u32[]{:S(2)}) copy-start(f32[2,14,8,640]{3,2,1,0:T(8,128)S(1)} %pad_maximum_fusion.4.mine) | copy-start | bytes 1720324
  97.2 7.0 %collective-permute-start.13 = (f32[2,14,8,640]{3,2,1,0:T(8,128)S(1)}, f32[2,14,8,640]{3,2,1,0:T(8,128)S(1)}, u32[]{:S(2)}, u32[]{:S(2)}) collective-permute-start(f32[2,14,8,640]{3,2,1,0:T(8,128)S(1)} %pad_maximum_fusion.4.mine), channel_id=1, source_target_pairs={{0,1},{1,0},{2,3},{3,2},{4,5},{5,4},{6,7},{7,6},{8,9},{9,8},{10,11... | collective-permute-start | bytes 1720328 | tf_op jit(solution)/shard_map/ppermute | solution.py:233
  129.9 1.9 %collective-permute-start.14 = (f32[24,8,512]{2,1,0:T(8,128)S(1)}, f32[24,8,512]{2,1,0:T(8,128)S(1)}, u32[]{:S(2)}, u32[]{:S(2)}) collective-permute-start(f32[24,8,512]{2,1,0:T(8,128)S(1)} %constant_dynamic-slice_fusion.1), channel_id=1, source_target_pairs={{0,1},{1,0},{2,3},{3,2},{4,5},{5,4},{6,7},{7,6},{8,9},{9,8},{10,11... | collective-permute-start | bytes 1179656 | tf_op jit(solution)/shard_map/ppermute | solution.py:233
  133.7 11.1 %collective-permute-start.15 = (f32[24,8,512]{2,1,0:T(8,128)S(1)}, f32[24,8,512]{2,1,0:T(8,128)S(1)}, u32[]{:S(2)}, u32[]{:S(2)}) collective-permute-start(f32[24,8,512]{2,1,0:T(8,128)S(1)} %exponential_multiply_fusion), channel_id=1, source_target_pairs={{0,2},{1,3},{2,0},{3,1},{4,6},{5,7},{6,4},{7,5},{8,10},{9,11},{10,... | collective-permute-start | bytes 1179656 | tf_op jit(solution)/shard_map/ppermute | solution.py:237
  144.9 2.4 %collective-permute-start.16 = (f32[2,24,8,512]{3,2,1,0:T(8,128)S(1)}, f32[2,24,8,512]{3,2,1,0:T(8,128)S(1)}, u32[]{:S(2)}, u32[]{:S(2)}) collective-permute-start(f32[2,24,8,512]{3,2,1,0:T(8,128)S(1)} %pad_maximum_fusion.1), channel_id=1, source_target_pairs={{0,1},{1,0},{2,3},{3,2},{4,5},{5,4},{6,7},{7,6},{8,9},{9,8},{10,11... | collective-permute-start | bytes 2359304 | tf_op jit(solution)/shard_map/ppermute | solution.py:233
  (4 other events, 9.1 us)

commit v2 on v1

--- a/solution.py
+++ b/solution.py
@@ -16,7 +16,7 @@
 F32 = jnp.float32
 VMEM = pl.BlockSpec(memory_space=pltpu.VMEM)
 SMEM = pl.BlockSpec(memory_space=pltpu.SMEM)
-PARAMS = pltpu.CompilerParams(vmem_limit_bytes=60 * 1024 * 1024)
+PARAMS = pltpu.CompilerParams(vmem_limit_bytes=20 * 1024 * 1024)
 
 
 def halves(value):

time: 150 us -> 107 us (0.71)
  Pallas kernels: 69.2 us -> 32.6 us
  local copies, waits for them, and re-layouts: 14.3 us -> 8.85 us
  other arithmetic: 7.92 us -> 4.18 us
  waiting for transfers between devices: 29.7 us -> 32.9 us
    pallas_call x4, Pallas kernels: 23.7 us -> 9.45 us  [adjoint(): pl.pallas_call(body, out_shape=jax.ShapeDtypeStruct((rows, width), F32),...]
    pallas_call x4, Pallas kernels: 24.1 us -> 13.6 us  [forward(): pl.pallas_call(functools.partial(forward_kernel, nz), out_shape=jax.Shape...]
    pallas_call x4, Pallas kernels: 13.6 us -> 3.79 us  [own_blur_y(): pl.pallas_call(own_kernel, out_shape=(out, out), in_specs=[VMEM] * 3, out...]
    ppermute x4, waiting for transfers between devices: 13.4 us -> 16.3 us  [to_chip(): return lax.ppermute(values, 'view', pairs)]
    pallas_call x2, Pallas kernels: 7.79 us -> 5.68 us  [operators(): pl.pallas_call(functools.partial(operators_kernel, nz), out_shape=(t, t,...]
    slice x1, local copies, waits for them, and re-layouts: 2.08 us -> 0.04 us  [local(): first, last = (edges[:RADIUS], edges[RADIUS:])]
    dynamic_slice x2, local copies, waits for them, and re-layouts: 2.54 us -> 0.65 us  [window(): return lax.dynamic_slice_in_dim(values, start_of(of), width, axis=2)]
  transfers between devices with their start and end apart: 17 -> 17, of which waited for: 8 -> 9; matrix products, arithmetic and copies ran while one was open for 7% -> 6% of each run, Pallas kernels for 26% -> 16%
where the time goes in v2:
time: 107 us
  waiting for transfers between devices  32.9 us (31%)
  Pallas kernels  32.6 us (30%)
  starting transfers between devices  27.4 us (26%)
  local copies, waits for them, and re-layouts  8.85 us (8%)
  other arithmetic  4.18 us (4%)
    ppermute x8, starting transfers between devices, rims(): return (lax.ppermute(last, 'tile', up), lax.ppermute(first, 'tile', down))  21.6 us
    ppermute x4, waiting for transfers between devices, to_chip(): return lax.ppermute(values, 'view', pairs)  16.3 us
    pallas_call x4, Pallas kernels, forward(): pl.pallas_call(functools.partial(forward_kernel, nz), out_shape=jax.Shape...  13.6 us
    ppermute x8, waiting for transfers between devices, rims(): return (lax.ppermute(last, 'tile', up), lax.ppermute(first, 'tile', down))  9.83 us
    pallas_call x4, Pallas kernels, adjoint(): pl.pallas_call(body, out_shape=jax.ShapeDtypeStruct((rows, width), F32),...  9.45 us
    ppermute x5, waiting for transfers between devices, swap_core(): return lax.ppermute(values, 'view', pairs)  6.8 us
    pallas_call x2, Pallas kernels, operators(): pl.pallas_call(functools.partial(operators_kernel, nz), out_shape=(t, t,...  5.68 us
    ppermute x4, starting transfers between devices, to_chip(): return lax.ppermute(values, 'view', pairs)  5.39 us
  transfers between devices with their start and end apart: 17, of which 9 were waited for; matrix products, arithmetic and copies ran while one was open for 6% of the time, Pallas kernels for 16%

profile of v2, /device:TPU:0, one launch (start us, length us, event | category | flops | bytes accessed | tf_op | source)
XLA Modules:
  0.0 106.6 jit_solution(7445473531051182435)
XLA Ops:
  0.0 2.5 %dynamic-slice_bitcast_fusion.1 = (f32[7,16,640]{2,1,0:T(8,128)}, f32[7,16,640]{2,1,0:T(8,128)}, f32[7,16,640]{2,1,0:T(8,128)S(1)}, f32[7,16,640]{2,1,0:T(8,128)S(1)}) fusion(f32[1,24,16,1024]{3,2,1,0:T(8,128)} %param.3, s32[]{:T(128)S(6)} %min.11, s32[]{:T(128)S(6)} %add.73, s32[]{:T(128)S(6)} %min.13), kind=kLoop, calls=%fused_computation.13 | loop fusion | bytes 2293772 | tf_op jit(solution)/shard_map/slice | solution.py:258
  2.6 3.0 %collective-permute-start.4 = (f32[14,16,640]{2,1,0:T(8,128)S(1)}, f32[14,16,640]{2,1,0:T(8,128)S(1)}, u32[]{:S(2)}, u32[]{:S(2)}) collective-permute-start(f32[14,16,640]{2,1,0:T(8,128)S(1)} %pad_maximum_fusion.3), channel_id=1, source_target_pairs={{0,2},{1,3},{2,0},{3,1},{4,6},{5,7},{6,4},{7,5},{8,10},{9,11},{10,... | collective-permute-start | bytes 1720328 | tf_op jit(solution)/shard_map/ppermute | solution.py:237
  6.7 3.5 %collective-permute-start = (f32[14,8,640]{2,1,0:T(8,128)}, f32[14,8,640]{2,1,0:T(8,128)S(1)}, u32[]{:S(2)}, u32[]{:S(2)}) collective-permute-start(f32[14,8,640]{2,1,0:T(8,128)} %get-tuple-element.41), channel_id=1, source_target_pairs={{0,4},{4,8},{8,12},{1,5},{5,9},{9,13},{2,6},{6,10},{10,14},{3,7},{... | collective-permute-start | bytes 860168 | tf_op jit(solution)/shard_map/ppermute | solution.py:243
  11.5 4.6 %collective-permute-start.8 = (f32[7,16,640]{2,1,0:T(8,128)}, f32[7,16,640]{2,1,0:T(8,128)S(1)}, u32[]{:S(2)}, u32[]{:S(2)}) collective-permute-start(f32[7,16,640]{2,1,0:T(8,128)} %get-tuple-element.38), channel_id=1, source_target_pairs={{0,4},{4,8},{8,12},{1,5},{5,9},{9,13},{2,6},{6,10},{10,14},{3,7},{... | collective-permute-start | bytes 860168 | tf_op jit(solution)/shard_map/ppermute | solution.py:243
  16.0 1.9 %dynamic-slice_bitcast_fusion = f32[10,16,640]{2,1,0:T(8,128)} fusion(f32[1,24,16,1024]{3,2,1,0:T(8,128)} %param.3, s32[]{:T(128)S(6)} %add.74, s32[]{:T(128)S(6)} %min.13), kind=kLoop, calls=%fused_computation.11 | loop fusion | bytes 819208 | tf_op jit(solution)/shard_map/slice | solution.py:262
  22.7 5.7 %collective-permute-done.3.kern = f32[3,15]{1,0:T(4,128)S(1)} collective-permute-done((f32[3,15]{1,0:T(4,128)S(1)}, f32[3,15]{1,0:T(4,128)S(1)}, u32[]{:S(2)}, u32[]{:S(2)}) %collective-permute-start.3) | collective-permute-done | bytes 212 | tf_op jit(solution)/shard_map/ppermute | solution.py:237
  28.4 3.5 %collective-permute-start.5 = (f32[7,16,640]{2,1,0:T(8,128)S(1)}, f32[7,16,640]{2,1,0:T(8,128)S(1)}, u32[]{:S(2)}, u32[]{:S(2)}) collective-permute-start(f32[7,16,640]{2,1,0:T(8,128)S(1)} %get-tuple-element.46), channel_id=1, source_target_pairs={{0,4},{4,8},{8,12},{1,5},{5,9},{9,13},{2,6},{6,10},{10,14},{3,7},{... | collective-permute-start | bytes 860168 | tf_op jit(solution)/shard_map/ppermute | solution.py:243
  33.6 2.8 %operators.3 = (bf16[2,512,256]{2,1,0:T(8,128)(2,1)S(1)}, bf16[2,512,256]{2,1,0:T(8,128)(2,1)S(1)}, bf16[2,256,512]{2,1,0:T(8,128)(2,1)S(1)}, bf16[2,256,512]{2,1,0:T(8,128)(2,1)S(1)}) custom-call(f32[3,15]{1,0:T(4,128)S(1)} %bitcast_divide_fusion.kern), custom_call_target="tpu_custom_call" | custom-call | tf_op jit(solution)/shard_map/operators/pallas_call | solution.py:60
  37.8 2.8 %operators.2 = (bf16[2,512,256]{2,1,0:T(8,128)(2,1)S(1)}, bf16[2,512,256]{2,1,0:T(8,128)(2,1)S(1)}, bf16[2,256,512]{2,1,0:T(8,128)(2,1)S(1)}, bf16[2,256,512]{2,1,0:T(8,128)(2,1)S(1)}) custom-call(f32[3,15]{1,0:T(4,128)S(1)} %collective-permute-done.3.kern), custom_call_target="tpu_custom_call" | custom-call | tf_op jit(solution)/shard_map/operators/pallas_call | solution.py:60
  42.8 2.7 %forward.5.refs_0_ = f32[608,640]{1,0:T(8,128)S(1)} custom-call(s32[1]{0:T(128)} %bitcast.core, f32[2,14,8,640]{3,2,1,0:T(8,128)S(1)} %pad_maximum_fusion.2.mine, f32[2,14,8,640]{3,2,1,0:T(8,128)S(1)} %collective-permute-done.2.other, bf16[384,640]{1,0:T(8,128)(2,1)S(1)} %get-tuple-element.29.oh, bf16[384,640]{1,0:T(8,128)(2,1)S(1)} %get-tuple-element.30.ol, ...), custom_call_target="tpu_custom_call" | custom-call | tf_op jit(solution)/shard_map/forward/pallas_call | solution.py:157
  45.5 2.4 %adjoint.4.added = f32[384,640]{1,0:T(8,128)S(1)} custom-call(f32[608,640]{1,0:T(8,128)S(1)} %forward.5.refs_0_, f32[112,640]{1,0:T(8,128)S(1)} %bitcast.51, f32[384,640]{1,0:T(8,128)S(1)} %bitcast.41, f32[112,640]{1,0:T(8,128)S(1)} %bitcast.53, bf16[2,512,256]{2,1,0:T(8,128)(2,1)S(1)} %get-tuple-element.27.th.refs_4_, ...), custom_call_target="tpu_custom_call" | custom-call | tf_op jit(solution)/shard_map/adjoint/pallas_call | solution.py:198
  47.9 2.8 %forward.4.blurred = f32[608,640]{1,0:T(8,128)S(1)} custom-call(s32[1]{0:T(128)} %bitcast.core, f32[2,14,8,640]{3,2,1,0:T(8,128)S(1)} %pad_maximum_fusion.2.mine, f32[2,14,8,640]{3,2,1,0:T(8,128)S(1)} %collective-permute-done.2.other, bf16[384,640]{1,0:T(8,128)(2,1)S(1)} %get-tuple-element.23.oh, bf16[384,640]{1,0:T(8,128)(2,1)S(1)} %get-tuple-element.24.ol, ...), custom_call_target="tpu_custom_call" | custom-call | tf_op jit(solution)/shard_map/forward/pallas_call | solution.py:157
  50.8 2.3 %adjoint.5 = f32[384,640]{1,0:T(8,128)S(1)} custom-call(f32[608,640]{1,0:T(8,128)S(1)} %forward.4.blurred, f32[112,640]{1,0:T(8,128)S(1)} %bitcast.47, f32[384,640]{1,0:T(8,128)S(1)} %bitcast.39, f32[112,640]{1,0:T(8,128)S(1)} %bitcast.49, bf16[2,512,256]{2,1,0:T(8,128)(2,1)S(1)} %get-tuple-element.21.th, bf16[2,512,256]{2,1,0:T(8,128)(2,1)S(1)} %get-tuple-element.22.tl, ...), custom_call_target="tpu_custom_call" | custom-call | tf_op jit(solution)/shard_map/adjoint/pallas_call | solution.py:198
  53.3 2.6 %collective-permute-done.10 = f32[384,640]{1,0:T(8,128)S(1)} collective-permute-done((f32[384,640]{1,0:T(8,128)S(1)}, f32[384,640]{1,0:T(8,128)S(1)}, u32[]{:S(2)}, u32[]{:S(2)}) %collective-permute-start.10) | collective-permute-done | bytes 983072 | tf_op jit(solution)/shard_map/ppermute | solution.py:233
  56.4 4.8 %collective-permute-start.11 = (f32[14,8,640]{2,1,0:T(8,128)S(1)}, f32[14,8,640]{2,1,0:T(8,128)S(1)}, u32[]{:S(2)}, u32[]{:S(2)}) collective-permute-start(f32[14,8,640]{2,1,0:T(8,128)S(1)} %get-tuple-element.43), channel_id=1, source_target_pairs={{0,4},{4,8},{8,12},{1,5},{5,9},{9,13},{2,6},{6,10},{10,14},{3,7},{... | collective-permute-start | bytes 860168 | tf_op jit(solution)/shard_map/ppermute | solution.py:243
  62.5 5.1 %collective-permute-done.11 = f32[14,8,640]{2,1,0:T(8,128)S(1)} collective-permute-done((f32[14,8,640]{2,1,0:T(8,128)S(1)}, f32[14,8,640]{2,1,0:T(8,128)S(1)}, u32[]{:S(2)}, u32[]{:S(2)}) %collective-permute-start.11) | collective-permute-done | bytes 286752 | tf_op jit(solution)/shard_map/ppermute | solution.py:243
  67.6 4.4 %collective-permute-done.12 = f32[14,8,640]{2,1,0:T(8,128)S(1)} collective-permute-done((f32[14,8,640]{2,1,0:T(8,128)S(1)}, f32[14,8,640]{2,1,0:T(8,128)S(1)}, u32[]{:S(2)}, u32[]{:S(2)}) %collective-permute-start.12) | collective-permute-done | bytes 286752 | tf_op jit(solution)/shard_map/ppermute | solution.py:243
  75.2 4.1 %forward.7.refs_0_ = f32[608,640]{1,0:T(8,128)S(1)} custom-call(s32[1]{0:T(128)} %bitcast.core, f32[2,14,8,640]{3,2,1,0:T(8,128)} %pad_maximum_fusion.4.mine, f32[2,14,8,640]{3,2,1,0:T(8,128)} %collective-permute-done.13.other, bf16[384,640]{1,0:T(8,128)(2,1)S(1)} %get-tuple-element.35.oh, bf16[384,640]{1,0:T(8,128)(2,1)S(1)} %get-tuple-element.36.ol, ...), custom_call_target="tpu_custom_call" | custom-call | tf_op jit(solution)/shard_map/forward/pallas_call | solution.py:157
  79.3 2.4 %adjoint.6.added = f32[384,640]{1,0:T(8,128)S(1)} custom-call(f32[608,640]{1,0:T(8,128)S(1)} %forward.7.refs_0_, f32[112,640]{1,0:T(8,128)S(1)} %bitcast.52, f32[384,640]{1,0:T(8,128)S(1)} %bitcast.42, f32[112,640]{1,0:T(8,128)S(1)} %bitcast.54, bf16[2,512,256]{2,1,0:T(8,128)(2,1)S(1)} %get-tuple-element.27.th.refs_4_, ...), custom_call_target="tpu_custom_call" | custom-call | tf_op jit(solution)/shard_map/adjoint/pallas_call | solution.py:198
  81.7 4.0 %forward.6.blurred = f32[608,640]{1,0:T(8,128)S(1)} custom-call(s32[1]{0:T(128)} %bitcast.core, f32[2,14,8,640]{3,2,1,0:T(8,128)} %pad_maximum_fusion.4.mine, f32[2,14,8,640]{3,2,1,0:T(8,128)} %collective-permute-done.13.other, bf16[384,640]{1,0:T(8,128)(2,1)S(1)} %get-tuple-element.33.oh, bf16[384,640]{1,0:T(8,128)(2,1)S(1)} %get-tuple-element.34.ol, ...), custom_call_target="tpu_custom_call" | custom-call | tf_op jit(solution)/shard_map/forward/pallas_call | solution.py:157
  85.8 2.4 %adjoint.7 = f32[384,640]{1,0:T(8,128)S(1)} custom-call(f32[608,640]{1,0:T(8,128)S(1)} %forward.6.blurred, f32[112,640]{1,0:T(8,128)S(1)} %bitcast.48, f32[384,640]{1,0:T(8,128)S(1)} %bitcast.40, f32[112,640]{1,0:T(8,128)S(1)} %bitcast.50, bf16[2,512,256]{2,1,0:T(8,128)(2,1)S(1)} %get-tuple-element.21.th, bf16[2,512,256]{2,1,0:T(8,128)(2,1)S(1)} %get-tuple-element.22.tl, ...), custom_call_target="tpu_custom_call" | custom-call | tf_op jit(solution)/shard_map/adjoint/pallas_call | solution.py:198
  88.5 1.6 %collective-permute-done.14 = f32[24,8,512]{2,1,0:T(8,128)S(1)} collective-permute-done((f32[24,8,512]{2,1,0:T(8,128)S(1)}, f32[24,8,512]{2,1,0:T(8,128)S(1)}, u32[]{:S(2)}, u32[]{:S(2)}) %collective-permute-start.14) | collective-permute-done | bytes 393248 | tf_op jit(solution)/shard_map/ppermute | solution.py:233
  91.0 10.6 %collective-permute-done.15 = f32[24,8,512]{2,1,0:T(8,128)S(1)} collective-permute-done((f32[24,8,512]{2,1,0:T(8,128)S(1)}, f32[24,8,512]{2,1,0:T(8,128)S(1)}, u32[]{:S(2)}, u32[]{:S(2)}) %collective-permute-start.15) | collective-permute-done | bytes 393248 | tf_op jit(solution)/shard_map/ppermute | solution.py:237
  101.8 2.2 %collective-permute-done.16 = f32[2,24,8,512]{3,2,1,0:T(8,128)S(1)} collective-permute-done((f32[2,24,8,512]{3,2,1,0:T(8,128)S(1)}, f32[2,24,8,512]{3,2,1,0:T(8,128)S(1)}, u32[]{:S(2)}, u32[]{:S(2)}) %collective-permute-start.16) | collective-permute-done | bytes 786464 | tf_op jit(solution)/shard_map/ppermute | solution.py:233
  (92 shorter events, 21.2 us)
Async XLA Ops:
  2.6 16.0 %copy-start.22 = (f32[1,3,15]{2,0,1:T(1,128)S(1)}, f32[1,3,15]{2,0,1:T(1,128)}, u32[]{:S(2)}) copy-start(f32[1,3,15]{2,0,1:T(1,128)} %param.4) | copy-start | bytes 544
  2.6 20.0 %collective-permute-start.4 = (f32[14,16,640]{2,1,0:T(8,128)S(1)}, f32[14,16,640]{2,1,0:T(8,128)S(1)}, u32[]{:S(2)}, u32[]{:S(2)}) collective-permute-start(f32[14,16,640]{2,1,0:T(8,128)S(1)} %pad_maximum_fusion.3), channel_id=1, source_target_pairs={{0,2},{1,3},{2,0},{3,1},{4,6},{5,7},{6,4},{7,5},{8,10},{9,11},{10,... | collective-permute-start | bytes 1720328 | tf_op jit(solution)/shard_map/ppermute | solution.py:237
  6.7 12.1 %collective-permute-start = (f32[14,8,640]{2,1,0:T(8,128)}, f32[14,8,640]{2,1,0:T(8,128)S(1)}, u32[]{:S(2)}, u32[]{:S(2)}) collective-permute-start(f32[14,8,640]{2,1,0:T(8,128)} %get-tuple-element.41), channel_id=1, source_target_pairs={{0,4},{4,8},{8,12},{1,5},{5,9},{9,13},{2,6},{6,10},{10,14},{3,7},{... | collective-permute-start | bytes 860168 | tf_op jit(solution)/shard_map/ppermute | solution.py:243
  10.2 10.2 %collective-permute-start.1 = (f32[14,8,640]{2,1,0:T(8,128)}, f32[14,8,640]{2,1,0:T(8,128)}, u32[]{:S(2)}, u32[]{:S(2)}) collective-permute-start(f32[14,8,640]{2,1,0:T(8,128)} %get-tuple-element.42), channel_id=1, source_target_pairs={{4,0},{8,4},{12,8},{5,1},{9,5},{13,9},{6,2},{10,6},{14,10},{7,3},{... | collective-permute-start | bytes 860168 | tf_op jit(solution)/shard_map/ppermute | solution.py:243
  11.5 34.0 %collective-permute-start.8 = (f32[7,16,640]{2,1,0:T(8,128)}, f32[7,16,640]{2,1,0:T(8,128)S(1)}, u32[]{:S(2)}, u32[]{:S(2)}) collective-permute-start(f32[7,16,640]{2,1,0:T(8,128)} %get-tuple-element.38), channel_id=1, source_target_pairs={{0,4},{4,8},{8,12},{1,5},{5,9},{9,13},{2,6},{6,10},{10,14},{3,7},{... | collective-permute-start | bytes 860168 | tf_op jit(solution)/shard_map/ppermute | solution.py:243
  18.0 13.9 %collective-permute-start.6 = (f32[10,16,640]{2,1,0:T(8,128)}, f32[10,16,640]{2,1,0:T(8,128)}, u32[]{:S(2)}, u32[]{:S(2)}) collective-permute-start(f32[10,16,640]{2,1,0:T(8,128)} %dynamic-slice_bitcast_fusion), channel_id=1, source_target_pairs={{0,2},{1,3},{2,0},{3,1},{4,6},{5,7},{6,4},{7,5},{8,10},{9,11},{10,... | collective-permute-start | bytes 1228808 | tf_op jit(solution)/shard_map/ppermute | solution.py:237
  18.7 26.8 %collective-permute-start.9 = (f32[7,16,640]{2,1,0:T(8,128)}, f32[7,16,640]{2,1,0:T(8,128)S(1)}, u32[]{:S(2)}, u32[]{:S(2)}) collective-permute-start(f32[7,16,640]{2,1,0:T(8,128)} %get-tuple-element.37), channel_id=1, source_target_pairs={{4,0},{8,4},{12,8},{5,1},{9,5},{13,9},{6,2},{10,6},{14,10},{7,3},{... | collective-permute-start | bytes 860168 | tf_op jit(solution)/shard_map/ppermute | solution.py:243
  20.4 8.0 %collective-permute-start.3 = (f32[3,15]{1,0:T(4,128)S(1)}, f32[3,15]{1,0:T(4,128)S(1)}, u32[]{:S(2)}, u32[]{:S(2)}) collective-permute-start(f32[3,15]{1,0:T(4,128)S(1)} %bitcast_divide_fusion.kern), channel_id=1, source_target_pairs={{0,2},{1,3},{2,0},{3,1},{4,6},{5,7},{6,4},{7,5},{8,10},{9,11},{10,... | collective-permute-start | bytes 548 | tf_op jit(solution)/shard_map/ppermute | solution.py:237
  22.6 20.2 %collective-permute-start.2 = (f32[2,14,8,640]{3,2,1,0:T(8,128)S(1)}, f32[2,14,8,640]{3,2,1,0:T(8,128)S(1)}, u32[]{:S(2)}, u32[]{:S(2)}) collective-permute-start(f32[2,14,8,640]{3,2,1,0:T(8,128)S(1)} %pad_maximum_fusion.2.mine), channel_id=1, source_target_pairs={{0,1},{1,0},{2,3},{3,2},{4,5},{5,4},{6,7},{7,6},{8,9},{9,8},{10,11... | collective-permute-start | bytes 1720328 | tf_op jit(solution)/shard_map/ppermute | solution.py:233
  28.4 22.4 %collective-permute-start.5 = (f32[7,16,640]{2,1,0:T(8,128)S(1)}, f32[7,16,640]{2,1,0:T(8,128)S(1)}, u32[]{:S(2)}, u32[]{:S(2)}) collective-permute-start(f32[7,16,640]{2,1,0:T(8,128)S(1)} %get-tuple-element.46), channel_id=1, source_target_pairs={{0,4},{4,8},{8,12},{1,5},{5,9},{9,13},{2,6},{6,10},{10,14},{3,7},{... | collective-permute-start | bytes 860168 | tf_op jit(solution)/shard_map/ppermute | solution.py:243
  31.9 18.9 %collective-permute-start.7 = (f32[7,16,640]{2,1,0:T(8,128)S(1)}, f32[7,16,640]{2,1,0:T(8,128)S(1)}, u32[]{:S(2)}, u32[]{:S(2)}) collective-permute-start(f32[7,16,640]{2,1,0:T(8,128)S(1)} %get-tuple-element.45), channel_id=1, source_target_pairs={{4,0},{8,4},{12,8},{5,1},{9,5},{13,9},{6,2},{10,6},{14,10},{7,3},{... | collective-permute-start | bytes 860168 | tf_op jit(solution)/shard_map/ppermute | solution.py:243
  36.5 9.0 %copy-start.8 = (bf16[2,256,512]{2,1,0:T(8,128)(2,1)}, bf16[2,256,512]{2,1,0:T(8,128)(2,1)S(1)}, u32[]{:S(2)}) copy-start(bf16[2,256,512]{2,1,0:T(8,128)(2,1)S(1)} %get-tuple-element.31.wh.refs_6_) | copy-start | bytes 1572868
  36.5 9.0 %copy-start.10 = (bf16[2,256,512]{2,1,0:T(8,128)(2,1)}, bf16[2,256,512]{2,1,0:T(8,128)(2,1)S(1)}, u32[]{:S(2)}) copy-start(bf16[2,256,512]{2,1,0:T(8,128)(2,1)S(1)} %get-tuple-element.32.wl.refs_7_) | copy-start | bytes 1572868
  37.8 7.7 %copy-start.2 = (f32[1,24,16,640]{3,2,1,0:T(8,128)}, f32[1,24,16,640]{3,2,1,0:T(8,128)S(1)}, u32[]{:S(2)}) copy-start(f32[1,24,16,640]{3,2,1,0:T(8,128)S(1)} %constant_dynamic-slice_fusion.3) | copy-start | bytes 2949124
  40.7 10.1 %copy-start.4 = (bf16[2,256,512]{2,1,0:T(8,128)(2,1)}, bf16[2,256,512]{2,1,0:T(8,128)(2,1)S(1)}, u32[]{:S(2)}) copy-start(bf16[2,256,512]{2,1,0:T(8,128)(2,1)S(1)} %get-tuple-element.25.wh) | copy-start | bytes 1572868
  40.7 10.1 %copy-start.6 = (bf16[2,256,512]{2,1,0:T(8,128)(2,1)}, bf16[2,256,512]{2,1,0:T(8,128)(2,1)S(1)}, u32[]{:S(2)}) copy-start(bf16[2,256,512]{2,1,0:T(8,128)(2,1)S(1)} %get-tuple-element.26.wl) | copy-start | bytes 1572868
  42.7 8.1 %copy-start = (f32[24,16,640]{2,1,0:T(8,128)}, f32[24,16,640]{2,1,0:T(8,128)S(1)}, u32[]{:S(2)}) copy-start(f32[24,16,640]{2,1,0:T(8,128)S(1)} %pad_maximum_fusion) | copy-start | bytes 2949124
  53.2 2.6 %collective-permute-start.10 = (f32[384,640]{1,0:T(8,128)S(1)}, f32[384,640]{1,0:T(8,128)S(1)}, u32[]{:S(2)}, u32[]{:S(2)}) collective-permute-start(f32[384,640]{1,0:T(8,128)S(1)} %adjoint.5), channel_id=1, source_target_pairs={{0,1},{1,0},{2,3},{3,2},{4,5},{5,4},{6,7},{7,6},{8,9},{9,8},{10,11... | collective-permute-start | bytes 2949128 | tf_op jit(solution)/shard_map/ppermute | solution.py:233
  56.4 11.2 %collective-permute-start.11 = (f32[14,8,640]{2,1,0:T(8,128)S(1)}, f32[14,8,640]{2,1,0:T(8,128)S(1)}, u32[]{:S(2)}, u32[]{:S(2)}) collective-permute-start(f32[14,8,640]{2,1,0:T(8,128)S(1)} %get-tuple-element.43), channel_id=1, source_target_pairs={{0,4},{4,8},{8,12},{1,5},{5,9},{9,13},{2,6},{6,10},{10,14},{3,7},{... | collective-permute-start | bytes 860168 | tf_op jit(solution)/shard_map/ppermute | solution.py:243
  61.2 10.8 %collective-permute-start.12 = (f32[14,8,640]{2,1,0:T(8,128)S(1)}, f32[14,8,640]{2,1,0:T(8,128)S(1)}, u32[]{:S(2)}, u32[]{:S(2)}) collective-permute-start(f32[14,8,640]{2,1,0:T(8,128)S(1)} %get-tuple-element.44), channel_id=1, source_target_pairs={{4,0},{8,4},{12,8},{5,1},{9,5},{13,9},{6,2},{10,6},{14,10},{7,3},{... | collective-permute-start | bytes 860168 | tf_op jit(solution)/shard_map/ppermute | solution.py:243
  72.8 2.3 %collective-permute-start.13 = (f32[2,14,8,640]{3,2,1,0:T(8,128)}, f32[2,14,8,640]{3,2,1,0:T(8,128)}, u32[]{:S(2)}, u32[]{:S(2)}) collective-permute-start(f32[2,14,8,640]{3,2,1,0:T(8,128)} %pad_maximum_fusion.4.mine), channel_id=1, source_target_pairs={{0,1},{1,0},{2,3},{3,2},{4,5},{5,4},{6,7},{7,6},{8,9},{9,8},{10,11... | collective-permute-start | bytes 1720328 | tf_op jit(solution)/shard_map/ppermute | solution.py:233
  88.3 1.8 %collective-permute-start.14 = (f32[24,8,512]{2,1,0:T(8,128)S(1)}, f32[24,8,512]{2,1,0:T(8,128)S(1)}, u32[]{:S(2)}, u32[]{:S(2)}) collective-permute-start(f32[24,8,512]{2,1,0:T(8,128)S(1)} %constant_dynamic-slice_fusion.1), channel_id=1, source_target_pairs={{0,1},{1,0},{2,3},{3,2},{4,5},{5,4},{6,7},{7,6},{8,9},{9,8},{10,11... | collective-permute-start | bytes 1179656 | tf_op jit(solution)/shard_map/ppermute | solution.py:233
  90.4 11.2 %collective-permute-start.15 = (f32[24,8,512]{2,1,0:T(8,128)S(1)}, f32[24,8,512]{2,1,0:T(8,128)S(1)}, u32[]{:S(2)}, u32[]{:S(2)}) collective-permute-start(f32[24,8,512]{2,1,0:T(8,128)S(1)} %exponential_multiply_fusion), channel_id=1, source_target_pairs={{0,2},{1,3},{2,0},{3,1},{4,6},{5,7},{6,4},{7,5},{8,10},{9,11},{10,... | collective-permute-start | bytes 1179656 | tf_op jit(solution)/shard_map/ppermute | solution.py:237
  101.7 2.4 %collective-permute-start.16 = (f32[2,24,8,512]{3,2,1,0:T(8,128)S(1)}, f32[2,24,8,512]{3,2,1,0:T(8,128)S(1)}, u32[]{:S(2)}, u32[]{:S(2)}) collective-permute-start(f32[2,24,8,512]{3,2,1,0:T(8,128)S(1)} %pad_maximum_fusion.1), channel_id=1, source_target_pairs={{0,1},{1,0},{2,3},{3,2},{4,5},{5,4},{6,7},{7,6},{8,9},{9,8},{10,11... | collective-permute-start | bytes 2359304 | tf_op jit(solution)/shard_map/ppermute | solution.py:233
  (16 other events, 52.4 us)

commit v3 on v2

v3 whole, which is shorter than its diff:
```python
import functools
from typing import NamedTuple

import jax
import jax.numpy as jnp
from jax import lax
from jax.experimental import pallas as pl
from jax.experimental.pallas import tpu as pltpu
from jax.sharding import PartitionSpec as P


RADIUS = 7
ITERS = 2
TAPS = 2 * RADIUS + 1
LANES = 128
ROWS = 256
BF = jnp.bfloat16
F32 = jnp.float32
VMEM = pl.BlockSpec(memory_space=pltpu.VMEM)
SMEM = pl.BlockSpec(memory_space=pltpu.SMEM)
ANY = pl.BlockSpec(memory_space=pl.ANY)
PARAMS = pltpu.CompilerParams(vmem_limit_bytes=20 * 1024 * 1024)


def halves(value):
    high = value.astype(BF)
    return high, (value - high.astype(F32)).astype(BF)


def dot(a, b):
    return jnp.dot(a, b, preferred_element_type=F32)


def dot3(a, b):
    return dot(a[0], b[0]) + (dot(a[1], b[0]) + dot(a[0], b[1]))


class Split(NamedTuple):
    chips: int
    cores: int
    part: int
    width: int
    ny: int
    half: int

    def start(self, chip):
        place = jnp.clip(chip * self.part - LANES, 0, self.ny - self.width)
        return pl.multiple_of(place, LANES)

    def here(self):
        place = lax.axis_index("view")
        return place // self.cores, lax.rem(place, self.cores)

    def inner(self):
        chip, _ = self.here()
        return pl.multiple_of(chip * self.part - self.start(chip), LANES)

    def rows(self, core):
        return pl.ds(pl.multiple_of(core * self.half, self.half), self.half)


def cut_kernel(split, moves, ahead, *refs):
    source, outs, sem = refs[0], refs[1:-1], refs[-1]
    chip, core = split.here()
    lanes = pl.ds(split.start(lax.rem(chip + ahead, split.chips)), split.width)
    copies = []
    for out, (x0, at, n, by_core) in moves:
        z = split.rows(core) if by_core else slice(None)
        copies.append(
            pltpu.make_async_copy(
                source.at[x0 : x0 + n, z, lanes], outs[out].at[at : at + n], sem.at[len(copies)]
            )
        )
        copies[-1].start()
    for copy in copies:
        copy.wait()


def cut(source, split, ahead, outs):
    moves, shapes = [], []
    for index, ranges in enumerate(outs):
        at = 0
        for x0, n, by_core in ranges:
            moves.append((index, (x0, at, n, by_core)))
            at += n
        nz = split.half if ranges[0][2] else source.shape[1]
        shapes.append(jax.ShapeDtypeStruct((at, nz, split.width), F32))
    return pl.pallas_call(
        functools.partial(cut_kernel, split, tuple(moves), ahead),
        out_shape=tuple(shapes),
        in_specs=[ANY],
        out_specs=(VMEM,) * len(shapes),
        scratch_shapes=[pltpu.SemaphoreType.DMA((len(moves),))],
        compiler_params=PARAMS,
        name="cut",
    )(source)


def update_kernel(split, views, mine, sibling, est, out, first, last):
    _, core = split.here()
    out[...] = est[...] * jnp.exp((mine[...] + sibling[...]) / views)
    rim = first.shape[0]
    first[...] = out[:rim, split.rows(core), :]
    last[...] = out[out.shape[0] - rim :, split.rows(core), :]


def update(split, views, mine, sibling, est):
    rim = jax.ShapeDtypeStruct((2 * RADIUS, split.half, split.width), F32)
    return pl.pallas_call(
        functools.partial(update_kernel, split, views),
        out_shape=(jax.ShapeDtypeStruct(est.shape, F32), rim, rim),
        in_specs=[VMEM] * 3,
        out_specs=(VMEM,) * 3,
        compiler_params=PARAMS,
        name="update",
    )(mine, sibling, est)


def finish_kernel(split, views, mine, sibling, est, out):
    _, core = split.here()
    old = est[:, split.rows(core), pl.ds(split.inner(), split.part)]
    out[...] = old * jnp.exp((mine[...] + sibling[...]) / views)


def finish(split, views, mine, sibling, est):
    return pl.pallas_call(
        functools.partial(finish_kernel, split, views),
        out_shape=jax.ShapeDtypeStruct(mine.shape, F32),
        in_specs=[VMEM] * 3,
        out_specs=VMEM,
        compiler_params=PARAMS,
        name="finish",
    )(mine, sibling, est)


def operators_kernel(nz, kern, th, tl, wh, wl):
    planes = ROWS // nz
    band = LANES + 3 * 8
    first = LANES - 8
    i = lax.broadcasted_iota(jnp.int32, (band, LANES), 0) + first
    o = lax.broadcasted_iota(jnp.int32, (band, LANES), 1)
    shift_y = i - o - (LANES - RADIUS)
    row = lax.broadcasted_iota(jnp.int32, (nz, 2 * ROWS), 0)
    col = lax.broadcasted_iota(jnp.int32, (nz, 2 * ROWS), 1)
    shift_x = col // nz
    shift_z = col % nz - row + RADIUS
    th[...] = jnp.zeros_like(th)
    tl[...] = jnp.zeros_like(tl)
    for mirrored in range(2):
        ty = jnp.zeros((band, LANES), F32)
        kx = jnp.zeros((nz, 2 * ROWS), F32)
        kz = jnp.zeros((nz, 2 * ROWS), F32)
        for k in range(TAPS):
            tap = TAPS - 1 - k if mirrored else k
            kx = jnp.where(shift_x == k, kern[0, tap], kx)
            kz = jnp.where(shift_z == k, kern[1, tap], kz)
            ty = jnp.where(shift_y == k, kern[2, tap], ty)
        high, low = halves(ty)
        for c0 in range(0, ROWS, LANES):
            rows = slice(first + c0, first + c0 + band)
            th[mirrored, rows, c0 : c0 + LANES] = high
            tl[mirrored, rows, c0 : c0 + LANES] = low
        strip = kx * kz
        for p in range(planes):
            moved = pltpu.roll(strip, p * nz, 1) if p else strip
            rows = slice(p * nz, (p + 1) * nz)
            wh[mirrored, rows, :], wl[mirrored, rows, :] = halves(moved)


def operators(kern, nz):
    t = jax.ShapeDtypeStruct((2, 2 * ROWS, ROWS), BF)
    w = jax.ShapeDtypeStruct((2, ROWS, 2 * ROWS), BF)
    return pl.pallas_call(
        functools.partial(operators_kernel, nz),
        out_shape=(t, t, w, w),
        in_specs=[SMEM],
        out_specs=(VMEM,) * 4,
        compiler_params=PARAMS,
        name="operators",
    )(kern)


def blur_y(x, th, tl, store):
    width = x.shape[1]
    xh, xl = halves(x)
    for o0 in range(0, width, ROWS):
        size = min(ROWS, width - o0)
        k0, k1 = max(0, o0 - LANES), min(width, o0 + size + LANES)
        t0 = k0 - (o0 - LANES)
        rows = slice(t0, t0 + k1 - k0)
        t = (th[rows, :size], tl[rows, :size])
        store(o0, size, dot3((xh[:, k0:k1], xl[:, k0:k1]), t))


def blur_xz(dh, dl, wh, wl, nz, planes_out, store):
    width = dh.shape[1]
    step = ROWS // nz
    for p0 in range(0, planes_out, step):
        planes = min(step, planes_out - p0)
        m = planes * nz
        k = min(2 * ROWS, (planes_out + 2 * RADIUS - p0) * nz)
        for o0 in range(0, width, ROWS):
            size = min(ROWS, width - o0)
            d = (
                dh[p0 * nz : p0 * nz + k, o0 : o0 + size],
                dl[p0 * nz : p0 * nz + k, o0 : o0 + size],
            )
            store(p0 * nz, m, o0, size, dot3((wh[:m, :k], wl[:m, :k]), d))


def to_halves(dh, dl, r0, n):
    def store(o0, size, value):
        h, l = halves(value)
        dh[r0 : r0 + n, o0 : o0 + size] = h
        dl[r0 : r0 + n, o0 : o0 + size] = l

    return store


def chunks(rows, step=128):
    return [(r, min(step, rows - r)) for r in range(0, rows, step)]


def own_kernel(est, th, tl, dh, dl):
    for r0, n in chunks(est.shape[0]):
        blur_y(est[r0 : r0 + n, :], th.at[0], tl.at[0], to_halves(dh, dl, r0, n))


def own_blur_y(est, ops):
    out = jax.ShapeDtypeStruct(est.shape, BF)
    return pl.pallas_call(
        own_kernel,
        out_shape=(out, out),
        in_specs=[VMEM] * 3,
        out_specs=(VMEM, VMEM),
        compiler_params=PARAMS,
        name="own_blur_y",
    )(est, ops[0], ops[1])


def forward_kernel(nz, split, m0, s0, m1, s1, oh, ol, th, tl, wh, wl, blurred, rims, dh, dl):
    width = oh.shape[1]
    rim = m0.shape[0]
    own = oh.shape[0]
    _, core = split.here()
    for side, (mine, sibling) in enumerate(((m0, s0), (m1, s1))):
        rims[side, :, split.rows(core), :] = mine[...]
        rims[side, :, split.rows(1 - core), :] = sibling[...]
    for side in range(2):
        base = 0 if side == 0 else rim * nz + own
        flat = rims[side].reshape(rim * nz, width)
        for r0, n in chunks(rim * nz, 112):
            blur_y(flat[r0 : r0 + n, :], th.at[0], tl.at[0], to_halves(dh, dl, base + r0, n))
    dh[rim * nz : rim * nz + own, :] = oh[...]
    dl[rim * nz : rim * nz + own, :] = ol[...]

    def store(r0, m, o0, size, value):
        blurred[r0 : r0 + m, o0 : o0 + size] = value

    blur_xz(dh, dl, wh.at[0], wl.at[0], nz, blurred.shape[0] // nz, store)


def forward(split, rims, own, ops, nz):
    rim = rims[0].shape[0]
    rows, width = own[0].shape
    total = rows + 2 * rim * nz
    return pl.pallas_call(
        functools.partial(forward_kernel, nz, split),
        out_shape=jax.ShapeDtypeStruct((total - 2 * RADIUS * nz, width), F32),
        in_specs=[VMEM] * 10,
        out_specs=VMEM,
        scratch_shapes=[
            pltpu.VMEM((2, rim, nz, width), F32),
            pltpu.VMEM((total, width), BF),
            pltpu.VMEM((total, width), BF),
        ],
        compiler_params=PARAMS,
        name="forward",
    )(*rims, own[0], own[1], *ops)


def adjoint_kernel(nz, pieces, inputs, has_added, last, *refs):
    blurred, refs = refs[0], refs[1:]
    record, refs = refs[:inputs], refs[inputs:]
    th, tl, wh, wl = refs[:4]
    refs = refs[4:]
    if has_added:
        added, refs = refs[0], refs[1:]
    if last is not None:
        keep, send, refs = refs[0], refs[1], refs[2:]
    out, dh, dl = refs
    base = 0
    for which, start, count in pieces:
        for r0, n in chunks(count):
            rows = slice(base + r0, base + r0 + n)
            q = record[which][start + r0 : start + r0 + n, :] / blurred[rows, :]
            blur_y(q, th.at[1], tl.at[1], to_halves(dh, dl, base + r0, n))
        base += count

    def store(r0, m, o0, size, value):
        log = jnp.log(value)
        planes = slice(r0 // nz, (r0 + m) // nz)
        log = log.reshape(m // nz, nz, size)
        if has_added:
            log = log + added[planes, :, o0 : o0 + size]
        out[planes, :, o0 : o0 + size] = log

    blur_xz(dh, dl, wh.at[1], wl.at[1], nz, out.shape[0], store)
    if last is not None:
        _, core = last.here()
        lanes = pl.ds(last.inner(), last.part)
        keep[...] = out[:, last.rows(core), lanes]
        send[...] = out[:, last.rows(1 - core), lanes]


def adjoint(blurred, record, pieces, ops, added, nz, last=None):
    rows, width = blurred.shape
    args = [blurred, *record, *ops] + ([] if added is None else [added])
    full = (rows // nz - 2 * RADIUS, nz, width)
    shape = jax.ShapeDtypeStruct(full, F32)
    scratch = [pltpu.VMEM(blurred.shape, BF), pltpu.VMEM(blurred.shape, BF)]
    if last is not None:
        shape = (jax.ShapeDtypeStruct((full[0], last.half, last.part), F32),) * 2
        scratch = [pltpu.VMEM(full, F32)] + scratch
    return pl.pallas_call(
        functools.partial(adjoint_kernel, nz, pieces, len(record), added is not None, last),
        out_shape=shape,
        in_specs=[VMEM] * len(args),
        out_specs=VMEM if last is None else (VMEM, VMEM),
        scratch_shapes=scratch,
        compiler_params=PARAMS,
        name="adjoint",
    )(*args)


def join_kernel(split, *refs):
    mine, out = refs[:-1], refs[-1]
    chip, core = split.here()
    for r in range(split.chips):
        owner = lax.rem(chip + split.chips - r, split.chips)
        lanes = pl.ds(pl.multiple_of(owner * split.part, LANES), split.part)
        out[:, split.rows(core), lanes] = mine[r][...]
        out[:, split.rows(1 - core), lanes] = mine[split.chips + r][...]


def join(split, mine, others, nz):
    return pl.pallas_call(
        functools.partial(join_kernel, split),
        out_shape=jax.ShapeDtypeStruct((mine[0].shape[0], nz, split.ny), F32),
        in_specs=[VMEM] * (2 * len(mine)),
        out_specs=VMEM,
        compiler_params=PARAMS,
        name="join",
    )(*mine, *others)


def steps(recorded, psf_taps, estimate):
    views = lax.axis_size("view")
    tiles = lax.axis_size("tile")
    nx, nz, ny = estimate.shape
    cores = 2
    chips = views // cores
    part = ny // chips
    width = min(ny, part + (LANES if chips <= 2 else 2 * LANES))
    split = Split(chips, cores, part, width, ny, nz // cores)
    assert 2 * RADIUS * ITERS <= LANES and nx >= 2 * RADIUS
    flat = lambda a: a.reshape(-1, a.shape[-1])

    def swap_core(values):
        pairs = [(v, v ^ 1) for v in range(views)]
        return lax.ppermute(values, "view", pairs)

    def to_chip(values, r):
        pairs = [(v, (v + r * cores) % views) for v in range(views)]
        return lax.ppermute(values, "view", pairs)

    up = [(t, t + 1) for t in range(tiles - 1)]
    down = [(t + 1, t) for t in range(tiles - 1)]

    def rims(first, last):
        before = lax.ppermute(last, "tile", up)
        after = lax.ppermute(first, "tile", down)
        return before, after

    def estimate_rims(first, last):
        before, after = rims(first, last)
        return (before, swap_core(before), after, swap_core(after))

    recorded = recorded[0]
    kern = psf_taps[0] / jnp.sum(psf_taps[0], axis=1, keepdims=True)
    kerns = [kern] + [to_chip(kern, r) for r in range(1, chips)]

    rim, body = RADIUS * nz, (nx - 2 * RADIUS) * nz
    edges, middles = [None], [None]
    for r in range(1, chips):
        (both,) = cut(
            recorded, split, r, [((0, RADIUS, False), (nx - RADIUS, RADIUS, False))]
        )
        edges.append(to_chip(both, r))
        (inside,) = cut(recorded, split, r, [((RADIUS, nx - 2 * RADIUS, False),)])
        middles.append(to_chip(inside, r))

    est, first, last = cut(
        estimate,
        split,
        0,
        [
            ((0, nx, False),),
            ((0, 2 * RADIUS, True),),
            ((nx - 2 * RADIUS, 2 * RADIUS, True),),
        ],
    )
    est_rims = estimate_rims(first, last)

    own, first, last = cut(
        recorded,
        split,
        0,
        [((0, nx, False),), ((0, RADIUS, False),), ((nx - RADIUS, RADIUS, False),)],
    )
    before, after = rims(first, last)
    record = [tuple(flat(a) for a in (before, own, after))]
    pieces = [((0, 0, rim), (1, 0, 2 * rim + body), (2, 0, rim))]
    for r in range(1, chips):
        before, after = rims(edges[r][:RADIUS], edges[r][RADIUS:])
        record.append(tuple(flat(a) for a in (before, edges[r], middles[r], after)))
        pieces.append(((0, 0, rim), (1, 0, rim), (2, 0, body), (1, rim, rim), (3, 0, rim)))

    ops = []
    for k in kerns:
        ops.append(operators(k, nz))

    for iteration in range(ITERS):
        final = iteration == ITERS - 1
        total = None
        owns = []
        for r in range(chips):
            owns.append(own_blur_y(flat(est), ops[r][:2]))
        for r in range(chips):
            blurred = forward(split, est_rims, owns[r], ops[r], nz)
            end = split if final and r == chips - 1 else None
            total = adjoint(blurred, record[r], pieces[r], ops[r], total, nz, end)
        if not final:
            sibling = swap_core(total)
            est, first, last = update(split, views, total, sibling, est)
            est_rims = estimate_rims(first, last)

    keep, send = total
    est = finish(split, views, keep, swap_core(send), est)
    parts = [est] + [to_chip(est, r) for r in range(1, chips)]
    others = [swap_core(p) for p in parts]
    return join(split, parts, others, nz)


def solution(mesh):
    in_specs = (P("view", "tile", "slab", None), P("view", None, None), P("tile", "slab", None))
    out_specs = P("tile", "slab", None)
    return jax.shard_map(steps, mesh=mesh, in_specs=in_specs, out_specs=out_specs, check_vma=False)
```

time: 107 us -> 98.4 us (0.920)
  local copies, waits for them, and re-layouts: 8.85 us -> 2.86 us
  other arithmetic: 4.18 us -> 0.18 us
  waiting for transfers between devices: 32.9 us -> 34.4 us
    ppermute x8, waiting for transfers between devices: 9.83 us -> 18 us  [the longest x4 9.74 us: rims(): before = lax.ppermute(last, 'tile', up)]
    slice x5 -> x1, local copies, waits for them, and re-layouts: 5.6 us -> 0.04 us  [steps(): before, after = rims(edges[r][:RADIUS], edges[r][RADIUS:])]
    ppermute x4, waiting for transfers between devices: 16.3 us -> 10.8 us  [to_chip(): return lax.ppermute(values, 'view', pairs)]
    pallas_call x8 -> x15, Pallas kernels: 23.1 us -> 26.6 us  [the longest x4 12.7 us: forward(): pl.pallas_call(functools.partial(forward_kernel, nz, split), out_shape=ja...]
    pallas_call x2, Pallas kernels: 5.68 us -> 2.15 us  [operators(): pl.pallas_call(functools.partial(operators_kernel, nz), out_shape=(t, t,...]
    another operation x3 -> x0, other arithmetic: 1.9 us -> none  [the longest x2 1.85 us: estimate_rims(): mine = jnp.stack(rims(sel[:2 * RADIUS], sel[nx - 2 * RADIUS:]))]
    unnamed x46 -> x8, local copies, waits for them, and re-layouts: 1.24 us -> 2.82 us
    ppermute x5 -> x8, waiting for transfers between devices: 6.8 us -> 5.63 us  [swap_core(): return lax.ppermute(values, 'view', pairs)]
  transfers between devices with their start and end apart: 17 -> 20, of which waited for: 9 -> 8; matrix products, arithmetic and copies ran while one was open for 6% -> 0% of each run, Pallas kernels for 16% -> 17%
where the time goes in v3:
time: 98.4 us; the launch traced here: 98 us
  waiting for transfers between devices  34.4 us (35%)
  Pallas kernels  32.5 us (33%)
  starting transfers between devices  27.8 us (28%)
  local copies, waits for them, and re-layouts  2.86 us (3%)
    ppermute x4, starting transfers between devices, rims(): before = lax.ppermute(last, 'tile', up)  16.1 us
    pallas_call x4, Pallas kernels, forward(): pl.pallas_call(functools.partial(forward_kernel, nz, split), out_shape=ja...  12.7 us
    ppermute x4, waiting for transfers between devices, to_chip(): return lax.ppermute(values, 'view', pairs)  10.8 us
    pallas_call x4, Pallas kernels, adjoint(): pl.pallas_call(functools.partial(adjoint_kernel, nz, pieces, len(record),...  9.99 us
    ppermute x4, waiting for transfers between devices, rims(): before = lax.ppermute(last, 'tile', up)  9.74 us
    ppermute x4, waiting for transfers between devices, rims(): after = lax.ppermute(first, 'tile', down)  8.26 us
    ppermute x4, starting transfers between devices, to_chip(): return lax.ppermute(values, 'view', pairs)  5.76 us
    ppermute x8, waiting for transfers between devices, swap_core(): return lax.ppermute(values, 'view', pairs)  5.63 us
  transfers between devices with their start and end apart: 20, of which 8 were waited for; matrix products, arithmetic and copies ran while one was open for 0% of the time, Pallas kernels for 17%

profile of v3, /device:TPU:0, one launch (start us, length us, event | category | flops | bytes accessed | tf_op | source)
XLA Modules:
  0.0 98.0 jit_solution(9842053171010324689)
XLA Ops:
  0.0 1.4 %copy-done = f32[1,24,16,1024]{3,2,1,0:T(8,128)S(1)} copy-done((f32[1,24,16,1024]{3,2,1,0:T(8,128)S(1)}, f32[1,24,16,1024]{3,2,1,0:T(8,128)}, u32[]{:S(2)}) %copy-start) | copy-done | bytes 1572888
  2.3 3.0 %collective-permute-start.5 = (f32[14,16,640]{2,1,0:T(8,128)}, f32[14,16,640]{2,1,0:T(8,128)S(1)}, u32[]{:S(2)}, u32[]{:S(2)}) collective-permute-start(f32[14,16,640]{2,1,0:T(8,128)} %cut.5), channel_id=1, source_target_pairs={{0,2},{1,3},{2,0},{3,1},{4,6},{5,7},{6,4},{7,5},{8,10},{9,11},{10,... | collective-permute-start | bytes 1720328 | tf_op jit(solution)/shard_map/ppermute | solution.py:375
  5.4 1.4 %copy-done.2 = f32[24,16,1024]{2,1,0:T(8,128)S(1)} copy-done((f32[24,16,1024]{2,1,0:T(8,128)S(1)}, f32[24,16,1024]{2,1,0:T(8,128)}, u32[]{:S(2)}) %copy-start.2) | copy-done | bytes 1572888
  7.8 3.5 %collective-permute-start = (f32[14,8,640]{2,1,0:T(8,128)}, f32[14,8,640]{2,1,0:T(8,128)S(1)}, u32[]{:S(2)}, u32[]{:S(2)}) collective-permute-start(f32[14,8,640]{2,1,0:T(8,128)} %get-tuple-element.32), channel_id=1, source_target_pairs={{0,4},{4,8},{8,12},{1,5},{5,9},{9,13},{2,6},{6,10},{10,14},{3,7},{... | collective-permute-start | bytes 860168 | tf_op jit(solution)/shard_map/ppermute | solution.py:381
  12.7 4.7 %collective-permute-done.m0 = f32[14,8,640]{2,1,0:T(8,128)S(1)} collective-permute-done((f32[14,8,640]{2,1,0:T(8,128)}, f32[14,8,640]{2,1,0:T(8,128)S(1)}, u32[]{:S(2)}, u32[]{:S(2)}) %collective-permute-start) | collective-permute-done | bytes 286752 | tf_op jit(solution)/shard_map/ppermute | solution.py:381
  17.4 4.1 %collective-permute-done.2.m1 = f32[14,8,640]{2,1,0:T(8,128)} collective-permute-done((f32[14,8,640]{2,1,0:T(8,128)}, f32[14,8,640]{2,1,0:T(8,128)}, u32[]{:S(2)}, u32[]{:S(2)}) %collective-permute-start.2) | collective-permute-done | bytes 286752 | tf_op jit(solution)/shard_map/ppermute | solution.py:382
  22.3 3.5 %collective-permute-start.9 = (f32[7,16,640]{2,1,0:T(8,128)S(1)}, f32[7,16,640]{2,1,0:T(8,128)S(1)}, u32[]{:S(2)}, u32[]{:S(2)}) collective-permute-start(f32[7,16,640]{2,1,0:T(8,128)S(1)} %get-tuple-element.47), channel_id=1, source_target_pairs={{0,4},{4,8},{8,12},{1,5},{5,9},{9,13},{2,6},{6,10},{10,14},{3,7},{... | collective-permute-start | bytes 860168 | tf_op jit(solution)/shard_map/ppermute | solution.py:381
  27.2 1.6 %collective-permute-start.7 = (f32[10,16,640]{2,1,0:T(8,128)S(1)}, f32[10,16,640]{2,1,0:T(8,128)S(1)}, u32[]{:S(2)}, u32[]{:S(2)}) collective-permute-start(f32[10,16,640]{2,1,0:T(8,128)S(1)} %cut.6), channel_id=1, source_target_pairs={{0,2},{1,3},{2,0},{3,1},{4,6},{5,7},{6,4},{7,5},{8,10},{9,11},{10,... | collective-permute-start | bytes 1228808 | tf_op jit(solution)/shard_map/ppermute | solution.py:375
  28.8 4.6 %collective-permute-start.6 = (f32[7,16,640]{2,1,0:T(8,128)S(1)}, f32[7,16,640]{2,1,0:T(8,128)S(1)}, u32[]{:S(2)}, u32[]{:S(2)}) collective-permute-start(f32[7,16,640]{2,1,0:T(8,128)S(1)} %get-tuple-element.60), channel_id=1, source_target_pairs={{0,4},{4,8},{8,12},{1,5},{5,9},{9,13},{2,6},{6,10},{10,14},{3,7},{... | collective-permute-start | bytes 860168 | tf_op jit(solution)/shard_map/ppermute | solution.py:381
  38.8 3.7 %forward.5.refs_0_ = f32[608,640]{1,0:T(8,128)S(1)} custom-call(f32[14,8,640]{2,1,0:T(8,128)S(1)} %collective-permute-done.m0, f32[14,8,640]{2,1,0:T(8,128)S(1)} %collective-permute-done.1.s0, f32[14,8,640]{2,1,0:T(8,128)} %collective-permute-done.2.m1, f32[14,8,640]{2,1,0:T(8,128)S(1)} %collective-permute-done.3.s1, ...), custom_call_target="tpu_custom_call" | custom-call | tf_op jit(solution)/shard_map/forward/pallas_call | solution.py:267
  42.4 2.3 %adjoint.4.refs_9_ = f32[24,16,640]{2,1,0:T(8,128)S(1)} custom-call(f32[608,640]{1,0:T(8,128)S(1)} %forward.5.refs_0_, f32[112,640]{1,0:T(8,128)S(1)} %bitcast.29, f32[384,640]{1,0:T(8,128)S(1)} %bitcast.21, f32[112,640]{1,0:T(8,128)S(1)} %bitcast.31, bf16[2,512,256]{2,1,0:T(8,128)(2,1)S(1)} %get-tuple-element.41.th.refs_4_, ...), custom_call_target="tpu_custom_call" | custom-call | tf_op jit(solution)/shard_map/adjoint/pallas_call | solution.py:325
  44.8 3.7 %forward.4.refs_0_ = f32[608,640]{1,0:T(8,128)S(1)} custom-call(f32[14,8,640]{2,1,0:T(8,128)S(1)} %collective-permute-done.m0, f32[14,8,640]{2,1,0:T(8,128)S(1)} %collective-permute-done.1.s0, f32[14,8,640]{2,1,0:T(8,128)} %collective-permute-done.2.m1, f32[14,8,640]{2,1,0:T(8,128)S(1)} %collective-permute-done.3.s1, ...), custom_call_target="tpu_custom_call" | custom-call | tf_op jit(solution)/shard_map/forward/pallas_call | solution.py:267
  48.5 2.7 %adjoint.5.mine = f32[24,16,640]{2,1,0:T(8,128)S(1)} custom-call(f32[608,640]{1,0:T(8,128)S(1)} %forward.4.refs_0_, f32[112,640]{1,0:T(8,128)S(1)} %bitcast.25, f32[224,640]{1,0:T(8,128)S(1)} %bitcast.19, f32[160,640]{1,0:T(8,128)S(1)} %bitcast.23, f32[112,640]{1,0:T(8,128)S(1)} %bitcast.27, bf16[2,512,256]{2,1,0:T(8,128)(2,1)S(1)} %get-tuple-element.35.th.refs_5_, ...), custom_call_target="tpu_custom_call" | custom-call | tf_op jit(solution)/shard_map/adjoint/pallas_call | solution.py:325
  51.3 2.6 %collective-permute-done.11.sibling = f32[24,16,640]{2,1,0:T(8,128)S(1)} collective-permute-done((f32[24,16,640]{2,1,0:T(8,128)S(1)}, f32[24,16,640]{2,1,0:T(8,128)S(1)}, u32[]{:S(2)}, u32[]{:S(2)}) %collective-permute-start.11) | collective-permute-done | bytes 983072 | tf_op jit(solution)/shard_map/ppermute | solution.py:371
  54.3 4.6 %collective-permute-start.12 = (f32[14,8,640]{2,1,0:T(8,128)S(1)}, f32[14,8,640]{2,1,0:T(8,128)S(1)}, u32[]{:S(2)}, u32[]{:S(2)}) collective-permute-start(f32[14,8,640]{2,1,0:T(8,128)S(1)} %get-tuple-element.50), channel_id=1, source_target_pairs={{0,4},{4,8},{8,12},{1,5},{5,9},{9,13},{2,6},{6,10},{10,14},{3,7},{... | collective-permute-start | bytes 860168 | tf_op jit(solution)/shard_map/ppermute | solution.py:381
  60.1 5.1 %collective-permute-done.12.m0 = f32[14,8,640]{2,1,0:T(8,128)S(1)} collective-permute-done((f32[14,8,640]{2,1,0:T(8,128)S(1)}, f32[14,8,640]{2,1,0:T(8,128)S(1)}, u32[]{:S(2)}, u32[]{:S(2)}) %collective-permute-start.12) | collective-permute-done | bytes 286752 | tf_op jit(solution)/shard_map/ppermute | solution.py:381
  65.2 4.1 %collective-permute-done.14.m1 = f32[14,8,640]{2,1,0:T(8,128)S(1)} collective-permute-done((f32[14,8,640]{2,1,0:T(8,128)S(1)}, f32[14,8,640]{2,1,0:T(8,128)S(1)}, u32[]{:S(2)}, u32[]{:S(2)}) %collective-permute-start.14) | collective-permute-done | bytes 286752 | tf_op jit(solution)/shard_map/ppermute | solution.py:382
  71.2 2.7 %forward.7.refs_0_ = f32[608,640]{1,0:T(8,128)S(1)} custom-call(f32[14,8,640]{2,1,0:T(8,128)S(1)} %collective-permute-done.12.m0, f32[14,8,640]{2,1,0:T(8,128)S(1)} %collective-permute-done.13.s0, f32[14,8,640]{2,1,0:T(8,128)S(1)} %collective-permute-done.14.m1, f32[14,8,640]{2,1,0:T(8,128)S(1)} %collective-permute-done.15.s1, ...), custom_call_target="tpu_custom_call" | custom-call | tf_op jit(solution)/shard_map/forward/pallas_call | solution.py:267
  73.9 2.3 %adjoint.6.refs_9_ = f32[24,16,640]{2,1,0:T(8,128)S(1)} custom-call(f32[608,640]{1,0:T(8,128)S(1)} %forward.7.refs_0_, f32[112,640]{1,0:T(8,128)S(1)} %bitcast.30, f32[384,640]{1,0:T(8,128)S(1)} %bitcast.22, f32[112,640]{1,0:T(8,128)S(1)} %bitcast.32, bf16[2,512,256]{2,1,0:T(8,128)(2,1)S(1)} %get-tuple-element.41.th.refs_4_, ...), custom_call_target="tpu_custom_call" | custom-call | tf_op jit(solution)/shard_map/adjoint/pallas_call | solution.py:325
  76.3 2.7 %forward.6.refs_0_ = f32[608,640]{1,0:T(8,128)S(1)} custom-call(f32[14,8,640]{2,1,0:T(8,128)S(1)} %collective-permute-done.12.m0, f32[14,8,640]{2,1,0:T(8,128)S(1)} %collective-permute-done.13.s0, f32[14,8,640]{2,1,0:T(8,128)S(1)} %collective-permute-done.14.m1, f32[14,8,640]{2,1,0:T(8,128)S(1)} %collective-permute-done.15.s1, ...), custom_call_target="tpu_custom_call" | custom-call | tf_op jit(solution)/shard_map/forward/pallas_call | solution.py:267
  79.0 2.6 %adjoint.7 = (f32[24,8,512]{2,1,0:T(8,128)S(1)}, f32[24,8,512]{2,1,0:T(8,128)S(1)}) custom-call(f32[608,640]{1,0:T(8,128)S(1)} %forward.6.refs_0_, f32[112,640]{1,0:T(8,128)S(1)} %bitcast.26, f32[224,640]{1,0:T(8,128)S(1)} %bitcast.20, f32[160,640]{1,0:T(8,128)S(1)} %bitcast.24, f32[112,640]{1,0:T(8,128)S(1)} %bitcast.28, ...), custom_call_target="tpu_custom_call" | custom-call | tf_op jit(solution)/shard_map/adjoint/pallas_call | solution.py:325
  82.1 1.3 %collective-permute-done.16.sibling = f32[24,8,512]{2,1,0:T(8,128)S(1)} collective-permute-done((f32[24,8,512]{2,1,0:T(8,128)S(1)}, f32[24,8,512]{2,1,0:T(8,128)S(1)}, u32[]{:S(2)}, u32[]{:S(2)}) %collective-permute-start.16) | collective-permute-done | bytes 393248 | tf_op jit(solution)/shard_map/ppermute | solution.py:371
  84.3 10.7 %collective-permute-done.17.refs_1_ = f32[24,8,512]{2,1,0:T(8,128)S(1)} collective-permute-done((f32[24,8,512]{2,1,0:T(8,128)S(1)}, f32[24,8,512]{2,1,0:T(8,128)S(1)}, u32[]{:S(2)}, u32[]{:S(2)}) %collective-permute-start.17) | collective-permute-done | bytes 393248 | tf_op jit(solution)/shard_map/ppermute | solution.py:375
  95.0 1.7 %collective-permute-done.19.refs_3_ = f32[24,8,512]{2,1,0:T(8,128)S(1)} collective-permute-done((f32[24,8,512]{2,1,0:T(8,128)S(1)}, f32[24,8,512]{2,1,0:T(8,128)S(1)}, u32[]{:S(2)}, u32[]{:S(2)}) %collective-permute-start.19) | collective-permute-done | bytes 393248 | tf_op jit(solution)/shard_map/ppermute | solution.py:371
  (48 shorter events, 17.1 us)
Async XLA Ops:
  0.0 1.4 %copy-start = (f32[1,24,16,1024]{3,2,1,0:T(8,128)S(1)}, f32[1,24,16,1024]{3,2,1,0:T(8,128)}, u32[]{:S(2)}) copy-start(f32[1,24,16,1024]{3,2,1,0:T(8,128)} %param.3) | copy-start | bytes 4718596
  1.4 11.2 %copy-start.3 = (f32[1,3,15]{2,0,1:T(1,128)S(1)}, f32[1,3,15]{2,0,1:T(1,128)}, u32[]{:S(2)}) copy-start(f32[1,3,15]{2,0,1:T(1,128)} %param.4) | copy-start | bytes 544
  1.4 20.7 %copy-start.1 = (f32[1,24,16,1024]{3,2,1,0:T(8,128)S(1)}, f32[1,24,16,1024]{3,2,1,0:T(8,128)}, u32[]{:S(2)}) copy-start(f32[1,24,16,1024]{3,2,1,0:T(8,128)} %param.3) | copy-start | bytes 4718596
  2.3 24.9 %collective-permute-start.5 = (f32[14,16,640]{2,1,0:T(8,128)}, f32[14,16,640]{2,1,0:T(8,128)S(1)}, u32[]{:S(2)}, u32[]{:S(2)}) collective-permute-start(f32[14,16,640]{2,1,0:T(8,128)} %cut.5), channel_id=1, source_target_pairs={{0,2},{1,3},{2,0},{3,1},{4,6},{5,7},{6,4},{7,5},{8,10},{9,11},{10,... | collective-permute-start | bytes 1720328 | tf_op jit(solution)/shard_map/ppermute | solution.py:375
  5.4 1.4 %copy-start.2 = (f32[24,16,1024]{2,1,0:T(8,128)S(1)}, f32[24,16,1024]{2,1,0:T(8,128)}, u32[]{:S(2)}) copy-start(f32[24,16,1024]{2,1,0:T(8,128)} %refs_0_.1) | copy-start | bytes 4718596
  7.8 9.6 %collective-permute-start = (f32[14,8,640]{2,1,0:T(8,128)}, f32[14,8,640]{2,1,0:T(8,128)S(1)}, u32[]{:S(2)}, u32[]{:S(2)}) collective-permute-start(f32[14,8,640]{2,1,0:T(8,128)} %get-tuple-element.32), channel_id=1, source_target_pairs={{0,4},{4,8},{8,12},{1,5},{5,9},{9,13},{2,6},{6,10},{10,14},{3,7},{... | collective-permute-start | bytes 860168 | tf_op jit(solution)/shard_map/ppermute | solution.py:381
  11.3 10.2 %collective-permute-start.2 = (f32[14,8,640]{2,1,0:T(8,128)}, f32[14,8,640]{2,1,0:T(8,128)}, u32[]{:S(2)}, u32[]{:S(2)}) collective-permute-start(f32[14,8,640]{2,1,0:T(8,128)} %get-tuple-element.33), channel_id=1, source_target_pairs={{4,0},{8,4},{12,8},{5,1},{9,5},{13,9},{6,2},{10,6},{14,10},{7,3},{... | collective-permute-start | bytes 860168 | tf_op jit(solution)/shard_map/ppermute | solution.py:382
  17.4 11.4 %collective-permute-start.1 = (f32[14,8,640]{2,1,0:T(8,128)S(1)}, f32[14,8,640]{2,1,0:T(8,128)S(1)}, u32[]{:S(2)}, u32[]{:S(2)}) collective-permute-start(f32[14,8,640]{2,1,0:T(8,128)S(1)} %collective-permute-done.m0), channel_id=1, source_target_pairs={{0,1},{1,0},{2,3},{3,2},{4,5},{5,4},{6,7},{7,6},{8,9},{9,8},{10,11... | collective-permute-start | bytes 860168 | tf_op jit(solution)/shard_map/ppermute | solution.py:371
  21.5 11.9 %collective-permute-start.3 = (f32[14,8,640]{2,1,0:T(8,128)}, f32[14,8,640]{2,1,0:T(8,128)S(1)}, u32[]{:S(2)}, u32[]{:S(2)}) collective-permute-start(f32[14,8,640]{2,1,0:T(8,128)} %collective-permute-done.2.m1), channel_id=1, source_target_pairs={{0,1},{1,0},{2,3},{3,2},{4,5},{5,4},{6,7},{7,6},{8,9},{9,8},{10,11... | collective-permute-start | bytes 860168 | tf_op jit(solution)/shard_map/ppermute | solution.py:371
  21.6 4.3 %collective-permute-start.4 = (f32[3,15]{1,0:T(4,128)S(1)}, f32[3,15]{1,0:T(4,128)S(1)}, u32[]{:S(2)}, u32[]{:S(2)}) collective-permute-start(f32[3,15]{1,0:T(4,128)S(1)} %bitcast_divide_fusion.kern), channel_id=1, source_target_pairs={{0,2},{1,3},{2,0},{3,1},{4,6},{5,7},{6,4},{7,5},{8,10},{9,11},{10,... | collective-permute-start | bytes 548 | tf_op jit(solution)/shard_map/ppermute | solution.py:375
  22.3 20.1 %collective-permute-start.9 = (f32[7,16,640]{2,1,0:T(8,128)S(1)}, f32[7,16,640]{2,1,0:T(8,128)S(1)}, u32[]{:S(2)}, u32[]{:S(2)}) collective-permute-start(f32[7,16,640]{2,1,0:T(8,128)S(1)} %get-tuple-element.47), channel_id=1, source_target_pairs={{0,4},{4,8},{8,12},{1,5},{5,9},{9,13},{2,6},{6,10},{10,14},{3,7},{... | collective-permute-start | bytes 860168 | tf_op jit(solution)/shard_map/ppermute | solution.py:381
  25.9 16.5 %collective-permute-start.10 = (f32[7,16,640]{2,1,0:T(8,128)S(1)}, f32[7,16,640]{2,1,0:T(8,128)S(1)}, u32[]{:S(2)}, u32[]{:S(2)}) collective-permute-start(f32[7,16,640]{2,1,0:T(8,128)S(1)} %get-tuple-element.49), channel_id=1, source_target_pairs={{4,0},{8,4},{12,8},{5,1},{9,5},{13,9},{6,2},{10,6},{14,10},{7,3},{... | collective-permute-start | bytes 860168 | tf_op jit(solution)/shard_map/ppermute | solution.py:382
  27.2 21.2 %collective-permute-start.7 = (f32[10,16,640]{2,1,0:T(8,128)S(1)}, f32[10,16,640]{2,1,0:T(8,128)S(1)}, u32[]{:S(2)}, u32[]{:S(2)}) collective-permute-start(f32[10,16,640]{2,1,0:T(8,128)S(1)} %cut.6), channel_id=1, source_target_pairs={{0,2},{1,3},{2,0},{3,1},{4,6},{5,7},{6,4},{7,5},{8,10},{9,11},{10,... | collective-permute-start | bytes 1228808 | tf_op jit(solution)/shard_map/ppermute | solution.py:375
  28.8 19.6 %collective-permute-start.6 = (f32[7,16,640]{2,1,0:T(8,128)S(1)}, f32[7,16,640]{2,1,0:T(8,128)S(1)}, u32[]{:S(2)}, u32[]{:S(2)}) collective-permute-start(f32[7,16,640]{2,1,0:T(8,128)S(1)} %get-tuple-element.60), channel_id=1, source_target_pairs={{0,4},{4,8},{8,12},{1,5},{5,9},{9,13},{2,6},{6,10},{10,14},{3,7},{... | collective-permute-start | bytes 860168 | tf_op jit(solution)/shard_map/ppermute | solution.py:381
  33.4 15.1 %collective-permute-start.8 = (f32[7,16,640]{2,1,0:T(8,128)S(1)}, f32[7,16,640]{2,1,0:T(8,128)S(1)}, u32[]{:S(2)}, u32[]{:S(2)}) collective-permute-start(f32[7,16,640]{2,1,0:T(8,128)S(1)} %get-tuple-element.59), channel_id=1, source_target_pairs={{4,0},{8,4},{12,8},{5,1},{9,5},{13,9},{6,2},{10,6},{14,10},{7,3},{... | collective-permute-start | bytes 860168 | tf_op jit(solution)/shard_map/ppermute | solution.py:382
  51.2 2.6 %collective-permute-start.11 = (f32[24,16,640]{2,1,0:T(8,128)S(1)}, f32[24,16,640]{2,1,0:T(8,128)S(1)}, u32[]{:S(2)}, u32[]{:S(2)}) collective-permute-start(f32[24,16,640]{2,1,0:T(8,128)S(1)} %adjoint.5.mine), channel_id=1, source_target_pairs={{0,1},{1,0},{2,3},{3,2},{4,5},{5,4},{6,7},{7,6},{8,9},{9,8},{10,11... | collective-permute-start | bytes 2949128 | tf_op jit(solution)/shard_map/ppermute | solution.py:371
  54.3 10.9 %collective-permute-start.12 = (f32[14,8,640]{2,1,0:T(8,128)S(1)}, f32[14,8,640]{2,1,0:T(8,128)S(1)}, u32[]{:S(2)}, u32[]{:S(2)}) collective-permute-start(f32[14,8,640]{2,1,0:T(8,128)S(1)} %get-tuple-element.50), channel_id=1, source_target_pairs={{0,4},{4,8},{8,12},{1,5},{5,9},{9,13},{2,6},{6,10},{10,14},{3,7},{... | collective-permute-start | bytes 860168 | tf_op jit(solution)/shard_map/ppermute | solution.py:381
  58.8 10.5 %collective-permute-start.14 = (f32[14,8,640]{2,1,0:T(8,128)S(1)}, f32[14,8,640]{2,1,0:T(8,128)S(1)}, u32[]{:S(2)}, u32[]{:S(2)}) collective-permute-start(f32[14,8,640]{2,1,0:T(8,128)S(1)} %get-tuple-element.51), channel_id=1, source_target_pairs={{4,0},{8,4},{12,8},{5,1},{9,5},{13,9},{6,2},{10,6},{14,10},{7,3},{... | collective-permute-start | bytes 860168 | tf_op jit(solution)/shard_map/ppermute | solution.py:382
  65.2 6.0 %collective-permute-start.13 = (f32[14,8,640]{2,1,0:T(8,128)S(1)}, f32[14,8,640]{2,1,0:T(8,128)S(1)}, u32[]{:S(2)}, u32[]{:S(2)}) collective-permute-start(f32[14,8,640]{2,1,0:T(8,128)S(1)} %collective-permute-done.12.m0), channel_id=1, source_target_pairs={{0,1},{1,0},{2,3},{3,2},{4,5},{5,4},{6,7},{7,6},{8,9},{9,8},{10,11... | collective-permute-start | bytes 860168 | tf_op jit(solution)/shard_map/ppermute | solution.py:371
  69.3 1.9 %collective-permute-start.15 = (f32[14,8,640]{2,1,0:T(8,128)S(1)}, f32[14,8,640]{2,1,0:T(8,128)S(1)}, u32[]{:S(2)}, u32[]{:S(2)}) collective-permute-start(f32[14,8,640]{2,1,0:T(8,128)S(1)} %collective-permute-done.14.m1), channel_id=1, source_target_pairs={{0,1},{1,0},{2,3},{3,2},{4,5},{5,4},{6,7},{7,6},{8,9},{9,8},{10,11... | collective-permute-start | bytes 860168 | tf_op jit(solution)/shard_map/ppermute | solution.py:371
  81.6 1.9 %collective-permute-start.16 = (f32[24,8,512]{2,1,0:T(8,128)S(1)}, f32[24,8,512]{2,1,0:T(8,128)S(1)}, u32[]{:S(2)}, u32[]{:S(2)}) collective-permute-start(f32[24,8,512]{2,1,0:T(8,128)S(1)} %get-tuple-element.58), channel_id=1, source_target_pairs={{0,1},{1,0},{2,3},{3,2},{4,5},{5,4},{6,7},{7,6},{8,9},{9,8},{10,11... | collective-permute-start | bytes 1179656 | tf_op jit(solution)/shard_map/ppermute | solution.py:371
  83.6 11.5 %collective-permute-start.17 = (f32[24,8,512]{2,1,0:T(8,128)S(1)}, f32[24,8,512]{2,1,0:T(8,128)S(1)}, u32[]{:S(2)}, u32[]{:S(2)}) collective-permute-start(f32[24,8,512]{2,1,0:T(8,128)S(1)} %finish.1.refs_0_), channel_id=1, source_target_pairs={{0,2},{1,3},{2,0},{3,1},{4,6},{5,7},{6,4},{7,5},{8,10},{9,11},{10,... | collective-permute-start | bytes 1179656 | tf_op jit(solution)/shard_map/ppermute | solution.py:375
  84.2 10.8 %collective-permute-start.18 = (f32[24,8,512]{2,1,0:T(8,128)S(1)}, f32[24,8,512]{2,1,0:T(8,128)S(1)}, u32[]{:S(2)}, u32[]{:S(2)}) collective-permute-start(f32[24,8,512]{2,1,0:T(8,128)S(1)} %finish.1.refs_0_), channel_id=1, source_target_pairs={{0,1},{1,0},{2,3},{3,2},{4,5},{5,4},{6,7},{7,6},{8,9},{9,8},{10,11... | collective-permute-start | bytes 1179656 | tf_op jit(solution)/shard_map/ppermute | solution.py:371
  95.0 1.7 %collective-permute-start.19 = (f32[24,8,512]{2,1,0:T(8,128)S(1)}, f32[24,8,512]{2,1,0:T(8,128)S(1)}, u32[]{:S(2)}, u32[]{:S(2)}) collective-permute-start(f32[24,8,512]{2,1,0:T(8,128)S(1)} %collective-permute-done.17.refs_1_), channel_id=1, source_target_pairs={{0,1},{1,0},{2,3},{3,2},{4,5},{5,4},{6,7},{7,6},{8,9},{9,8},{10,11... | collective-permute-start | bytes 1179656 | tf_op jit(solution)/shard_map/ppermute | solution.py:371

commit v4 on v3

v4 whole, which is shorter than its diff:
```python
import functools
from typing import NamedTuple

import jax
import jax.numpy as jnp
from jax import lax
from jax.experimental import pallas as pl
from jax.experimental.pallas import tpu as pltpu
from jax.sharding import PartitionSpec as P


RADIUS = 7
ITERS = 2
TAPS = 2 * RADIUS + 1
LANES = 128
ROWS = 256
BF = jnp.bfloat16
F32 = jnp.float32
VMEM = pl.BlockSpec(memory_space=pltpu.VMEM)
SMEM = pl.BlockSpec(memory_space=pltpu.SMEM)
ANY = pl.BlockSpec(memory_space=pltpu.HBM)
PARAMS = pltpu.CompilerParams(vmem_limit_bytes=20 * 1024 * 1024)


def halves(value):
    high = value.astype(BF)
    return high, (value - high.astype(F32)).astype(BF)


def dot(a, b):
    return jnp.dot(a, b, preferred_element_type=F32)


class Split(NamedTuple):
    chips: int
    cores: int
    part: int
    width: int
    ny: int
    half: int

    def start(self, chip):
        place = jnp.clip(chip * self.part - LANES, 0, self.ny - self.width)
        return pl.multiple_of(place, LANES)

    def here(self):
        place = lax.axis_index("view")
        return place // self.cores, lax.rem(place, self.cores)

    def inner(self):
        chip, _ = self.here()
        return pl.multiple_of(chip * self.part - self.start(chip), LANES)

    def odd(self):
        return lax.rem(lax.axis_index("tile"), 2)

    def rows(self, core):
        return pl.ds(pl.multiple_of(core * self.half, self.half), self.half)


def cut_kernel(split, moves, ahead, *refs):
    source, outs, sem = refs[0], refs[1:-1], refs[-1]
    chip, core = split.here()
    lanes = pl.ds(split.start(lax.rem(chip + ahead, split.chips)), split.width)
    copies = []
    for out, at, even, odd, n, whose in moves:
        x0 = even if even == odd else jnp.where(split.odd() == 1, odd, even)
        z = slice(None) if whose is None else split.rows(core if whose == 0 else 1 - core)
        copies.append(
            pltpu.make_async_copy(
                source.at[pl.ds(x0, n), z, lanes],
                outs[out].at[pl.ds(at, n)],
                sem.at[len(copies)],
            )
        )
        copies[-1].start()
    for copy in copies:
        copy.wait()


def cut(source, split, ahead, outs):
    moves, shapes = [], []
    for index, ranges in enumerate(outs):
        at = 0
        for even, odd, n, whose in ranges:
            moves.append((index, at, even, odd, n, whose))
            at += n
        nz = source.shape[1] if ranges[0][3] is None else split.half
        shapes.append(jax.ShapeDtypeStruct((at, nz, split.width), F32))
    return pl.pallas_call(
        functools.partial(cut_kernel, split, tuple(moves), ahead),
        out_shape=tuple(shapes),
        in_specs=[ANY],
        out_specs=(VMEM,) * len(shapes),
        scratch_shapes=[pltpu.SemaphoreType.DMA((len(moves),))],
        compiler_params=PARAMS,
        name="cut",
    )(source)


def update_kernel(split, views, mine, sibling, est, out, pair_a, pair_b):
    out[...] = est[...] * jnp.exp((mine[...] + sibling[...]) / views)
    rim = pair_a.shape[0]
    top = out.shape[0] - rim
    odd = split.odd()
    pair_a[...] = out[pl.ds((1 - odd) * top, rim)]
    pair_b[...] = out[pl.ds(odd * top, rim)]


def update(split, views, mine, sibling, est):
    rim = jax.ShapeDtypeStruct((2 * RADIUS, split.half, split.width), F32)
    return pl.pallas_call(
        functools.partial(update_kernel, split, views),
        out_shape=(jax.ShapeDtypeStruct(est.shape, F32), rim, rim),
        in_specs=[VMEM] * 3,
        out_specs=(VMEM,) * 3,
        compiler_params=PARAMS,
        name="update",
    )(mine, sibling, est)


def finish_kernel(split, views, mine, sibling, est, out):
    old = est[:, :, pl.ds(split.inner(), split.part)]
    out[...] = old * jnp.exp((mine[...] + sibling[...]) / views)


def finish(split, views, mine, sibling, est):
    return pl.pallas_call(
        functools.partial(finish_kernel, split, views),
        out_shape=jax.ShapeDtypeStruct(mine.shape, F32),
        in_specs=[VMEM] * 3,
        out_specs=VMEM,
        compiler_params=PARAMS,
        name="finish",
    )(mine, sibling, est)


def operators_kernel(nz, taps, t, w, th, tl):
    planes = ROWS // nz
    band = LANES + 3 * 8
    first = LANES - 8
    i = lax.broadcasted_iota(jnp.int32, (band, LANES), 0) + first
    o = lax.broadcasted_iota(jnp.int32, (band, LANES), 1)
    shift_y = i - o - (LANES - RADIUS)
    row = lax.broadcasted_iota(jnp.int32, (nz, 2 * ROWS), 0)
    col = lax.broadcasted_iota(jnp.int32, (nz, 2 * ROWS), 1)
    shift_x = col // nz
    shift_z = col % nz - row + RADIUS
    sums = []
    for d in range(3):
        value = taps[d, 0]
        for k in range(1, TAPS):
            value = value + taps[d, k]
        sums.append(value)
    th[...] = jnp.zeros_like(th)
    tl[...] = jnp.zeros_like(tl)
    half = LANES // 2
    for mirrored in range(2):
        ty = jnp.zeros((band, LANES), F32)
        kx = jnp.zeros((nz, 2 * ROWS), F32)
        kz = jnp.zeros((nz, 2 * ROWS), F32)
        for k in range(TAPS):
            tap = TAPS - 1 - k if mirrored else k
            kx = jnp.where(shift_x == k, taps[0, tap], kx)
            kz = jnp.where(shift_z == k, taps[1, tap], kz)
            ty = jnp.where(shift_y == k, taps[2, tap], ty)
        kx = kx / sums[0]
        kz = kz / sums[1]
        ty = ty / sums[2]
        high, low = halves(ty)
        for c0 in range(0, ROWS, LANES):
            rows = slice(first + c0, first + c0 + band)
            th[rows, c0 : c0 + LANES] = high
            tl[rows, c0 : c0 + LANES] = low
        inside = slice(LANES, LANES + ROWS)
        right, left = slice(LANES + ROWS, LANES + ROWS + half), slice(half, LANES)
        t[mirrored, 0] = th[inside, :]
        t[mirrored, 1] = tl[inside, :]
        for at in (0, LANES):
            t[mirrored, 2, at : at + half] = th[right, :]
            t[mirrored, 2, at + half : at + LANES] = th[left, :]
        t[mirrored, 3, :half] = tl[right, :]
        t[mirrored, 3, half:LANES] = tl[left, :]
        t[mirrored, 3, LANES:] = jnp.zeros((ROWS - LANES, ROWS), BF)
        t[mirrored, 4, :, :LANES] = th[:ROWS, :LANES]
        t[mirrored, 4, :, LANES:] = tl[:ROWS, :LANES]
        strip = kx * kz
        for p in range(planes):
            moved = pltpu.roll(strip, p * nz, 1) if p else strip
            rows = slice(p * nz, (p + 1) * nz)
            w[mirrored, 0, rows, :], w[mirrored, 1, rows, :] = halves(moved)


def operators(taps, nz):
    return pl.pallas_call(
        functools.partial(operators_kernel, nz),
        out_shape=(
            jax.ShapeDtypeStruct((2, 5, ROWS, ROWS), BF),
            jax.ShapeDtypeStruct((2, 2, ROWS, 2 * ROWS), BF),
        ),
        in_specs=[SMEM],
        out_specs=(VMEM,) * 2,
        scratch_shapes=[pltpu.VMEM((2 * ROWS, ROWS), BF)] * 2,
        compiler_params=PARAMS,
        name="operators",
    )(taps)


def blur_y(x, t, store):
    n, width = x.shape
    xh, xl = halves(x)
    right = lax.broadcasted_iota(jnp.int32, (n, LANES), 1) < LANES // 2
    for o0 in range(0, width, ROWS):
        size = min(ROWS, width - o0)
        if size == ROWS:
            end = o0 + ROWS
            at = slice(o0, end)
            out = dot(xh[:, at], t[0]) + (dot(xl[:, at], t[0]) + dot(xh[:, at], t[1]))
            none = jnp.zeros((n, LANES), F32)
            corner = jnp.where(
                right,
                x[:, end : end + LANES] if end < width else none,
                x[:, o0 - LANES : o0] if o0 else none,
            )
            ch, cl = halves(corner)
            out = out + (dot(jnp.concatenate([ch, cl], 1), t[2]) + dot(ch, t[3, :LANES]))
        else:
            at = slice(o0 - LANES, o0 + LANES)
            both = dot(xh[:, at], t[4])
            out = both[:, :LANES] + (both[:, LANES:] + dot(xl[:, at], t[4, :, :LANES]))
        store(o0, size, out)


def blur_xz(dh, dl, w, nz, planes_out, store):
    width = dh.shape[1]
    step = ROWS // nz
    for p0 in range(0, planes_out, step):
        planes = min(step, planes_out - p0)
        m = planes * nz
        k = min(2 * ROWS, (planes_out + 2 * RADIUS - p0) * nz)
        rows = slice(p0 * nz, p0 * nz + k)
        wh, wl = w[0, :m, :k], w[1, :m, :k]
        for o0 in range(0, width, ROWS):
            size = min(ROWS, width - o0)
            at = slice(o0, o0 + size)
            if size == ROWS:
                out = dot(wh, dh[rows, at]) + (dot(wl, dh[rows, at]) + dot(wh, dl[rows, at]))
            else:
                both = dot(wh, jnp.concatenate([dh[rows, at], dl[rows, at]], 1))
                out = both[:, :size] + (both[:, size:] + dot(wl, dh[rows, at]))
            store(p0 * nz, m, o0, size, out)


def to_halves(dh, dl, rows):
    def store(o0, size, value):
        h, l = halves(value)
        dh[rows, o0 : o0 + size] = h
        dl[rows, o0 : o0 + size] = l

    return store


def chunks(rows, step=128):
    return [(r, min(step, rows - r)) for r in range(0, rows, step)]


def own_kernel(split, mine, sibling, t, dh, dl, est):
    _, core = split.here()
    est[:, split.rows(core), :] = mine[...]
    est[:, split.rows(1 - core), :] = sibling[...]
    planes, nz, width = est.shape
    step = LANES // nz
    for p in range(0, planes, step):
        n = min(step, planes - p)
        rows = slice(p * nz, (p + n) * nz)
        x = est[p : p + n].reshape(n * nz, width)
        blur_y(x, t.at[0], to_halves(dh, dl, rows))


def own_blur_y(split, mine, sibling, t):
    planes, half, width = mine.shape
    nz = half * split.cores
    out = jax.ShapeDtypeStruct((planes * nz, width), BF)
    return pl.pallas_call(
        functools.partial(own_kernel, split),
        out_shape=(out, out),
        in_specs=[VMEM] * 3,
        out_specs=(VMEM, VMEM),
        scratch_shapes=[pltpu.VMEM((planes, nz, width), F32)],
        compiler_params=PARAMS,
        name="own_blur_y",
    )(mine, sibling, t)


def forward_kernel(nz, split, ma, sa, mb, sb, oh, ol, t, w, blurred, rims, dh, dl):
    width = oh.shape[1]
    rim = ma.shape[0]
    own = oh.shape[0]
    _, core = split.here()
    odd = split.odd()
    for side, mine, sibling in ((1 - odd, ma, sa), (odd, mb, sb)):
        rims[side, :, split.rows(core), :] = mine[...]
        rims[side, :, split.rows(1 - core), :] = sibling[...]
    for side in range(2):
        base = 0 if side == 0 else rim * nz + own
        flat = rims[side].reshape(rim * nz, width)
        for r0, n in chunks(rim * nz, 112):
            rows = slice(base + r0, base + r0 + n)
            blur_y(flat[r0 : r0 + n, :], t.at[0], to_halves(dh, dl, rows))
    dh[rim * nz : rim * nz + own, :] = oh[...]
    dl[rim * nz : rim * nz + own, :] = ol[...]

    def store(r0, m, o0, size, value):
        blurred[r0 : r0 + m, o0 : o0 + size] = value

    blur_xz(dh, dl, w.at[0], nz, blurred.shape[0] // nz, store)


def forward(split, rims, own, ops, nz):
    rim = rims[0].shape[0]
    rows, width = own[0].shape
    total = rows + 2 * rim * nz
    return pl.pallas_call(
        functools.partial(forward_kernel, nz, split),
        out_shape=jax.ShapeDtypeStruct((total - 2 * RADIUS * nz, width), F32),
        in_specs=[VMEM] * 8,
        out_specs=VMEM,
        scratch_shapes=[
            pltpu.VMEM((2, rim, nz, width), F32),
            pltpu.VMEM((total, width), BF),
            pltpu.VMEM((total, width), BF),
        ],
        compiler_params=PARAMS,
        name="forward",
    )(*rims, own[0], own[1], *ops)


def adjoint_kernel(nz, split, pieces, inputs, has_added, ends, *refs):
    blurred, refs = refs[0], refs[1:]
    record, refs = refs[:inputs], refs[inputs:]
    t, w, refs = refs[0], refs[1], refs[2:]
    if has_added:
        added, refs = refs[0], refs[1:]
    if ends is not None:
        keep, send, refs = refs[0], refs[1], refs[2:]
    out, dh, dl = refs
    odd = split.odd()
    for which, start, count, even_base, odd_base in pieces:
        if even_base == odd_base:
            base = even_base
        else:
            base = pl.multiple_of(jnp.where(odd == 1, odd_base, even_base), nz)
        for r0, n in chunks(count):
            rows = pl.ds(base + r0, n)
            q = record[which][start + r0 : start + r0 + n, :] / blurred[rows, :]
            blur_y(q, t.at[1], to_halves(dh, dl, rows))

    def store(r0, m, o0, size, value):
        log = jnp.log(value)
        planes = slice(r0 // nz, (r0 + m) // nz)
        log = log.reshape(m // nz, nz, size)
        if has_added:
            log = log + added[planes, :, o0 : o0 + size]
        out[planes, :, o0 : o0 + size] = log

    blur_xz(dh, dl, w.at[1], nz, out.shape[0], store)
    if ends is not None:
        _, core = split.here()
        lanes = slice(None) if ends == split.width else pl.ds(split.inner(), ends)
        keep[...] = out[:, split.rows(core), lanes]
        send[...] = out[:, split.rows(1 - core), lanes]


def adjoint(split, blurred, record, pieces, ops, added, nz, ends=None):
    rows, width = blurred.shape
    args = [blurred, *record, *ops] + ([] if added is None else [added])
    full = (rows // nz - 2 * RADIUS, nz, width)
    shape = jax.ShapeDtypeStruct(full, F32)
    scratch = [pltpu.VMEM(blurred.shape, BF), pltpu.VMEM(blurred.shape, BF)]
    if ends is not None:
        shape = (jax.ShapeDtypeStruct((full[0], split.half, ends), F32),) * 2
        scratch = [pltpu.VMEM(full, F32)] + scratch
    kernel = functools.partial(
        adjoint_kernel, nz, split, pieces, len(record), added is not None, ends
    )
    return pl.pallas_call(
        kernel,
        out_shape=shape,
        in_specs=[VMEM] * len(args),
        out_specs=VMEM if ends is None else (VMEM, VMEM),
        scratch_shapes=scratch,
        compiler_params=PARAMS,
        name="adjoint",
    )(*args)


def join_kernel(split, *refs):
    mine, out = refs[:-1], refs[-1]
    chip, core = split.here()
    for r in range(split.chips):
        owner = lax.rem(chip + split.chips - r, split.chips)
        lanes = pl.ds(pl.multiple_of(owner * split.part, LANES), split.part)
        out[:, split.rows(core), lanes] = mine[r][...]
        out[:, split.rows(1 - core), lanes] = mine[split.chips + r][...]


def join(split, mine, others, nz):
    return pl.pallas_call(
        functools.partial(join_kernel, split),
        out_shape=jax.ShapeDtypeStruct((mine[0].shape[0], nz, split.ny), F32),
        in_specs=[VMEM] * (2 * len(mine)),
        out_specs=VMEM,
        compiler_params=PARAMS,
        name="join",
    )(*mine, *others)


def steps(recorded, psf_taps, estimate):
    views = lax.axis_size("view")
    tiles = lax.axis_size("tile")
    nx, nz, ny = estimate.shape
    cores = 2
    chips = views // cores
    part = ny // chips
    width = min(ny, part + (LANES if chips <= 2 else 2 * LANES))
    split = Split(chips, cores, part, width, ny, nz // cores)
    assert 2 * RADIUS * ITERS <= LANES and nx >= 2 * RADIUS
    flat = lambda a: a.reshape(-1, a.shape[-1])

    def swap_core(values):
        pairs = [(v, v ^ 1) for v in range(views)]
        return lax.ppermute(values, "view", pairs)

    def to_chip(values, r):
        pairs = [(v, (v + r * cores) % views) for v in range(views)]
        return lax.ppermute(values, "view", pairs)

    next_a = [(t, t ^ 1) for t in range(tiles) if t ^ 1 < tiles]
    next_b = [(t, ((t + 1) ^ 1) - 1) for t in range(1, tiles)]
    next_b = [(t, u) for t, u in next_b if u < tiles]

    def pair_up(a, b):
        b = lax.ppermute(b, "tile", next_b)
        a = lax.ppermute(a, "tile", next_a)
        return a, b

    def estimate_rims(a, b):
        a, b = pair_up(a, b)
        return a, swap_core(a), b, swap_core(b)

    recorded = recorded[0]
    taps = [psf_taps[0]] + [to_chip(psf_taps[0], r) for r in range(1, chips)]

    def to_a(n, whose=None):
        return (nx - n, 0, n, whose)

    def to_b(n, whose=None):
        return (0, nx - n, n, whose)

    rim, body = RADIUS * nz, (nx - 2 * RADIUS) * nz
    end = 2 * rim + body
    edges, middles = [None], [None]
    for r in range(1, chips):
        (both,) = cut(recorded, split, r, [(to_a(RADIUS), to_b(RADIUS))])
        edges.append(to_chip(both, r))
        inside = (RADIUS, RADIUS, nx - 2 * RADIUS, None)
        (inside,) = cut(recorded, split, r, [(inside,)])
        middles.append(to_chip(inside, r))

    est, est_sibling, pair_a, pair_b = cut(
        estimate,
        split,
        0,
        [
            ((0, 0, nx, 0),),
            ((0, 0, nx, 1),),
            (to_a(2 * RADIUS, 0),),
            (to_b(2 * RADIUS, 0),),
        ],
    )
    est_rims = estimate_rims(pair_a, pair_b)

    own, pair_a, pair_b = cut(
        recorded, split, 0, [((0, 0, nx, None),), (to_a(RADIUS),), (to_b(RADIUS),)]
    )
    pair_a, pair_b = pair_up(pair_a, pair_b)
    record = [tuple(flat(a) for a in (pair_a, own, pair_b))]
    outer_a, outer_b = (0, 0, rim, rim + end, 0), (2, 0, rim, 0, rim + end)
    pieces = [((1, 0, end, rim, rim), outer_a, outer_b)]
    for r in range(1, chips):
        pair_a, pair_b = pair_up(edges[r][:RADIUS], edges[r][RADIUS:])
        record.append(tuple(flat(a) for a in (pair_a, edges[r], pair_b, middles[r])))
        inner_a = (1, 0, rim, end, rim)
        inner_b = (1, rim, rim, rim, end)
        pieces.append((inner_a, inner_b, (3, 0, body, 2 * rim, 2 * rim), outer_a, outer_b))

    ops = []
    for k in taps:
        ops.append(operators(k, nz))

    for iteration in range(ITERS):
        final = iteration == ITERS - 1
        total = None
        owns = []
        for r in range(chips):
            owns.append(own_blur_y(split, est, est_sibling, ops[r][0]))
        for r in range(chips):
            blurred = forward(split, est_rims, owns[r], ops[r], nz)
            ends = (part if final else width) if r == chips - 1 else None
            total = adjoint(split, blurred, record[r], pieces[r], ops[r], total, nz, ends)
        keep, send = total
        sibling = swap_core(send)
        if not final:
            est, pair_a, pair_b = update(split, views, keep, sibling, est)
            est_rims = estimate_rims(pair_a, pair_b)
            est_sibling = swap_core(est)

    est = finish(split, views, keep, sibling, est)
    parts = [est] + [to_chip(est, r) for r in range(1, chips)]
    others = [swap_core(p) for p in parts]
    return join(split, parts, others, nz)


def solution(mesh):
    in_specs = (P("view", "tile", "slab", None), P("view", None, None), P("tile", "slab", None))
    out_specs = P("tile", "slab", None)
    return jax.shard_map(steps, mesh=mesh, in_specs=in_specs, out_specs=out_specs, check_vma=False)
```

time: 98.4 us -> 81.3 us (0.83)
  waiting for transfers between devices: 34.4 us -> 27.4 us
  Pallas kernels: 32.5 us -> 26.7 us
  starting transfers between devices: 27.8 us -> 23 us
    ppermute x8, starting transfers between devices: 21.3 us -> 15.3 us  [the longest x4 12.5 us: pair_up(): a = lax.ppermute(a, 'tile', next_a)]
    ppermute x8, waiting for transfers between devices: 18 us -> 12.4 us  [the longest x4 12.4 us: pair_up(): a = lax.ppermute(a, 'tile', next_a)]
    pallas_call x4, Pallas kernels: 12.7 us -> 9.45 us  [forward(): pl.pallas_call(functools.partial(forward_kernel, nz, split), out_shape=ja...]
    pallas_call x4, Pallas kernels: 2.19 us -> 0.58 us  [cut(): pl.pallas_call(functools.partial(cut_kernel, split, tuple(moves), ahead),...]
    ppermute x4, waiting for transfers between devices: 10.8 us -> 9.71 us  [to_chip(): return lax.ppermute(values, 'view', pairs)]
    ppermute x8 -> x9, waiting for transfers between devices: 5.63 us -> 5.29 us  [swap_core(): return lax.ppermute(values, 'view', pairs)]
    unnamed x8 -> x9, local copies, waits for them, and re-layouts: 2.82 us -> 2.82 us
  transfers between devices with their start and end apart: 20 -> 21, of which waited for: 8 -> 6; matrix products, arithmetic and copies ran while one was open for 0% -> 0% of each run, Pallas kernels for 17% -> 16%
where the time goes in v4:
time: 81.3 us; the launch traced here: 80.3 us
  waiting for transfers between devices  27.4 us (34%)
  Pallas kernels  26.7 us (33%)
  starting transfers between devices  23 us (28%)
  local copies, waits for them, and re-layouts  2.86 us (4%)
    ppermute x4, starting transfers between devices, pair_up(): a = lax.ppermute(a, 'tile', next_a)  12.5 us
    ppermute x4, waiting for transfers between devices, pair_up(): a = lax.ppermute(a, 'tile', next_a)  12.4 us
    ppermute x4, waiting for transfers between devices, to_chip(): return lax.ppermute(values, 'view', pairs)  9.71 us
    pallas_call x4, Pallas kernels, adjoint(): pl.pallas_call(kernel, out_shape=shape, in_specs=[VMEM] * len(args), out_...  9.57 us
    pallas_call x4, Pallas kernels, forward(): pl.pallas_call(functools.partial(forward_kernel, nz, split), out_shape=ja...  9.45 us
    ppermute x4, starting transfers between devices, to_chip(): return lax.ppermute(values, 'view', pairs)  6.47 us
    ppermute x9, waiting for transfers between devices, swap_core(): return lax.ppermute(values, 'view', pairs)  5.29 us
    pallas_call x4, Pallas kernels, own_blur_y(): pl.pallas_call(functools.partial(own_kernel, split), out_shape=(out, out)...  3.34 us
  transfers between devices with their start and end apart: 21, of which 6 were waited for; matrix products, arithmetic and copies ran while one was open for 0% of the time, Pallas kernels for 16%

profile of v4, /device:TPU:0, one launch (start us, length us, event | category | flops | bytes accessed | tf_op | source)
XLA Modules:
  0.0 80.3 jit_solution(13477760760914998329)
XLA Ops:
  0.0 1.4 %copy-done = f32[1,24,16,1024]{3,2,1,0:T(8,128)S(1)} copy-done((f32[1,24,16,1024]{3,2,1,0:T(8,128)S(1)}, f32[1,24,16,1024]{3,2,1,0:T(8,128)}, u32[]{:S(2)}) %copy-start) | copy-done | bytes 1572888
  1.5 3.0 %collective-permute-start.5 = (f32[14,16,640]{2,1,0:T(8,128)S(1)}, f32[14,16,640]{2,1,0:T(8,128)S(1)}, u32[]{:S(2)}, u32[]{:S(2)}) collective-permute-start(f32[14,16,640]{2,1,0:T(8,128)S(1)} %cut.5), channel_id=1, source_target_pairs={{0,2},{1,3},{2,0},{3,1},{4,6},{5,7},{6,4},{7,5},{8,10},{9,11},{10,... | collective-permute-start | bytes 1720328 | tf_op jit(solution)/shard_map/ppermute | solution.py:436
  4.6 1.4 %copy-done.2 = f32[24,16,1024]{2,1,0:T(8,128)S(1)} copy-done((f32[24,16,1024]{2,1,0:T(8,128)S(1)}, f32[24,16,1024]{2,1,0:T(8,128)}, u32[]{:S(2)}) %copy-start.2) | copy-done | bytes 1572888
  6.2 1.6 %collective-permute-start = (f32[14,8,640]{2,1,0:T(8,128)S(1)}, f32[14,8,640]{2,1,0:T(8,128)S(1)}, u32[]{:S(2)}, u32[]{:S(2)}) collective-permute-start(f32[14,8,640]{2,1,0:T(8,128)S(1)} %get-tuple-element.31), channel_id=1, source_target_pairs={{0,4},{4,0},{8,12},{12,8},{1,5},{5,1},{9,13},{13,9},{2,6},{6,2},{1... | collective-permute-start | bytes 860168 | tf_op jit(solution)/shard_map/ppermute | solution.py:444
  8.5 6.0 %collective-permute-done.ma = f32[14,8,640]{2,1,0:T(8,128)S(1)} collective-permute-done((f32[14,8,640]{2,1,0:T(8,128)S(1)}, f32[14,8,640]{2,1,0:T(8,128)S(1)}, u32[]{:S(2)}, u32[]{:S(2)}) %collective-permute-start) | collective-permute-done | bytes 286752 | tf_op jit(solution)/shard_map/ppermute | solution.py:444
  15.7 4.4 %collective-permute-start.9 = (f32[7,16,640]{2,1,0:T(8,128)S(1)}, f32[7,16,640]{2,1,0:T(8,128)S(1)}, u32[]{:S(2)}, u32[]{:S(2)}) collective-permute-start(f32[7,16,640]{2,1,0:T(8,128)S(1)} %get-tuple-element.43), channel_id=1, source_target_pairs={{0,4},{4,0},{8,12},{12,8},{1,5},{5,1},{9,13},{13,9},{2,6},{6,2},{1... | collective-permute-start | bytes 860168 | tf_op jit(solution)/shard_map/ppermute | solution.py:444
  20.9 1.5 %collective-permute-start.8 = (f32[10,16,640]{2,1,0:T(8,128)S(1)}, f32[10,16,640]{2,1,0:T(8,128)S(1)}, u32[]{:S(2)}, u32[]{:S(2)}) collective-permute-start(f32[10,16,640]{2,1,0:T(8,128)S(1)} %cut.6), channel_id=1, source_target_pairs={{0,2},{1,3},{2,0},{3,1},{4,6},{5,7},{6,4},{7,5},{8,10},{9,11},{10,... | collective-permute-start | bytes 1228808 | tf_op jit(solution)/shard_map/ppermute | solution.py:436
  22.4 4.8 %collective-permute-start.6 = (f32[7,16,640]{2,1,0:T(8,128)S(1)}, f32[7,16,640]{2,1,0:T(8,128)S(1)}, u32[]{:S(2)}, u32[]{:S(2)}) collective-permute-start(f32[7,16,640]{2,1,0:T(8,128)S(1)} %get-tuple-element.58), channel_id=1, source_target_pairs={{0,4},{4,0},{8,12},{12,8},{1,5},{5,1},{9,13},{13,9},{2,6},{6,2},{1... | collective-permute-start | bytes 860168 | tf_op jit(solution)/shard_map/ppermute | solution.py:444
  31.8 2.4 %forward.5.refs_0_ = f32[608,640]{1,0:T(8,128)S(1)} custom-call(f32[14,8,640]{2,1,0:T(8,128)S(1)} %collective-permute-done.ma, f32[14,8,640]{2,1,0:T(8,128)S(1)} %collective-permute-done.1.sa, f32[14,8,640]{2,1,0:T(8,128)S(1)} %collective-permute-done.2.mb, f32[14,8,640]{2,1,0:T(8,128)S(1)} %collective-permute-done.3.sb, ...), custom_call_target="tpu_custom_call" | custom-call | tf_op jit(solution)/shard_map/forward/pallas_call | solution.py:323
  34.2 2.2 %adjoint.4.refs_7_ = f32[24,16,640]{2,1,0:T(8,128)S(1)} custom-call(f32[608,640]{1,0:T(8,128)S(1)} %forward.5.refs_0_, f32[112,640]{1,0:T(8,128)S(1)} %bitcast.20, f32[384,640]{1,0:T(8,128)S(1)} %bitcast.16, f32[112,640]{1,0:T(8,128)S(1)} %bitcast.22, bf16[2,5,256,256]{3,2,1,0:T(8,128)(2,1)S(1)} %get-tuple-element.39.t.refs_4_, ...), custom_call_target="tpu_custom_call" | custom-call | tf_op jit(solution)/shard_map/adjoint/pallas_call | solution.py:386
  36.4 2.4 %forward.4.refs_0_ = f32[608,640]{1,0:T(8,128)S(1)} custom-call(f32[14,8,640]{2,1,0:T(8,128)S(1)} %collective-permute-done.ma, f32[14,8,640]{2,1,0:T(8,128)S(1)} %collective-permute-done.1.sa, f32[14,8,640]{2,1,0:T(8,128)S(1)} %collective-permute-done.2.mb, f32[14,8,640]{2,1,0:T(8,128)S(1)} %collective-permute-done.3.sb, ...), custom_call_target="tpu_custom_call" | custom-call | tf_op jit(solution)/shard_map/forward/pallas_call | solution.py:323
  38.8 2.8 %adjoint.5 = (f32[24,8,640]{2,1,0:T(8,128)S(1)}, f32[24,8,640]{2,1,0:T(8,128)S(1)}) custom-call(f32[608,640]{1,0:T(8,128)S(1)} %forward.4.refs_0_, f32[112,640]{1,0:T(8,128)S(1)} %bitcast.24, f32[224,640]{1,0:T(8,128)S(1)} %bitcast.14, f32[112,640]{1,0:T(8,128)S(1)} %bitcast.26, f32[160,640]{1,0:T(8,128)S(1)} %bitcast.18, ...), custom_call_target="tpu_custom_call" | custom-call | tf_op jit(solution)/shard_map/adjoint/pallas_call | solution.py:386
  41.6 1.9 %collective-permute-done.11.sibling = f32[24,8,640]{2,1,0:T(8,128)S(1)} collective-permute-done((f32[24,8,640]{2,1,0:T(8,128)S(1)}, f32[24,8,640]{2,1,0:T(8,128)S(1)}, u32[]{:S(2)}, u32[]{:S(2)}) %collective-permute-start.11) | collective-permute-done | bytes 491552 | tf_op jit(solution)/shard_map/ppermute | solution.py:432
  43.7 1.6 %collective-permute-start.12 = (f32[14,8,640]{2,1,0:T(8,128)S(1)}, f32[14,8,640]{2,1,0:T(8,128)S(1)}, u32[]{:S(2)}, u32[]{:S(2)}) collective-permute-start(f32[14,8,640]{2,1,0:T(8,128)S(1)} %get-tuple-element.48), channel_id=1, source_target_pairs={{0,4},{4,0},{8,12},{12,8},{1,5},{5,1},{9,13},{13,9},{2,6},{6,2},{1... | collective-permute-start | bytes 860168 | tf_op jit(solution)/shard_map/ppermute | solution.py:444
  46.3 6.4 %collective-permute-done.12.ma = f32[14,8,640]{2,1,0:T(8,128)S(1)} collective-permute-done((f32[14,8,640]{2,1,0:T(8,128)S(1)}, f32[14,8,640]{2,1,0:T(8,128)S(1)}, u32[]{:S(2)}, u32[]{:S(2)}) %collective-permute-start.12) | collective-permute-done | bytes 286752 | tf_op jit(solution)/shard_map/ppermute | solution.py:444
  54.9 2.4 %forward.7.refs_0_ = f32[608,640]{1,0:T(8,128)S(1)} custom-call(f32[14,8,640]{2,1,0:T(8,128)S(1)} %collective-permute-done.12.ma, f32[14,8,640]{2,1,0:T(8,128)S(1)} %collective-permute-done.13.sa, f32[14,8,640]{2,1,0:T(8,128)S(1)} %collective-permute-done.14.mb, f32[14,8,640]{2,1,0:T(8,128)S(1)} %collective-permute-done.15.sb, ...), custom_call_target="tpu_custom_call" | custom-call | tf_op jit(solution)/shard_map/forward/pallas_call | solution.py:323
  57.2 2.2 %adjoint.6.refs_7_ = f32[24,16,640]{2,1,0:T(8,128)S(1)} custom-call(f32[608,640]{1,0:T(8,128)S(1)} %forward.7.refs_0_, f32[112,640]{1,0:T(8,128)S(1)} %bitcast.21, f32[384,640]{1,0:T(8,128)S(1)} %bitcast.17, f32[112,640]{1,0:T(8,128)S(1)} %bitcast.23, bf16[2,5,256,256]{3,2,1,0:T(8,128)(2,1)S(1)} %get-tuple-element.39.t.refs_4_, ...), custom_call_target="tpu_custom_call" | custom-call | tf_op jit(solution)/shard_map/adjoint/pallas_call | solution.py:386
  59.4 2.4 %forward.6.refs_0_ = f32[608,640]{1,0:T(8,128)S(1)} custom-call(f32[14,8,640]{2,1,0:T(8,128)S(1)} %collective-permute-done.12.ma, f32[14,8,640]{2,1,0:T(8,128)S(1)} %collective-permute-done.13.sa, f32[14,8,640]{2,1,0:T(8,128)S(1)} %collective-permute-done.14.mb, f32[14,8,640]{2,1,0:T(8,128)S(1)} %collective-permute-done.15.sb, ...), custom_call_target="tpu_custom_call" | custom-call | tf_op jit(solution)/shard_map/forward/pallas_call | solution.py:323
  61.8 2.5 %adjoint.7 = (f32[24,8,512]{2,1,0:T(8,128)S(1)}, f32[24,8,512]{2,1,0:T(8,128)S(1)}) custom-call(f32[608,640]{1,0:T(8,128)S(1)} %forward.6.refs_0_, f32[112,640]{1,0:T(8,128)S(1)} %bitcast.25, f32[224,640]{1,0:T(8,128)S(1)} %bitcast.15, f32[112,640]{1,0:T(8,128)S(1)} %bitcast.27, f32[160,640]{1,0:T(8,128)S(1)} %bitcast.19, ...), custom_call_target="tpu_custom_call" | custom-call | tf_op jit(solution)/shard_map/adjoint/pallas_call | solution.py:386
  64.3 1.7 %collective-permute-done.17.sibling = f32[24,8,512]{2,1,0:T(8,128)S(1)} collective-permute-done((f32[24,8,512]{2,1,0:T(8,128)S(1)}, f32[24,8,512]{2,1,0:T(8,128)S(1)}, u32[]{:S(2)}, u32[]{:S(2)}) %collective-permute-start.17) | collective-permute-done | bytes 393248 | tf_op jit(solution)/shard_map/ppermute | solution.py:432
  66.1 1.5 %collective-permute-start.18 = (f32[24,8,512]{2,1,0:T(8,128)S(1)}, f32[24,8,512]{2,1,0:T(8,128)S(1)}, u32[]{:S(2)}, u32[]{:S(2)}) collective-permute-start(f32[24,8,512]{2,1,0:T(8,128)S(1)} %finish.1.refs_0_), channel_id=1, source_target_pairs={{0,2},{1,3},{2,0},{3,1},{4,6},{5,7},{6,4},{7,5},{8,10},{9,11},{10,... | collective-permute-start | bytes 1179656 | tf_op jit(solution)/shard_map/ppermute | solution.py:436
  67.6 9.7 %collective-permute-done.18.refs_1_ = f32[24,8,512]{2,1,0:T(8,128)S(1)} collective-permute-done((f32[24,8,512]{2,1,0:T(8,128)S(1)}, f32[24,8,512]{2,1,0:T(8,128)S(1)}, u32[]{:S(2)}, u32[]{:S(2)}) %collective-permute-start.18) | collective-permute-done | bytes 393248 | tf_op jit(solution)/shard_map/ppermute | solution.py:436
  77.4 1.7 %collective-permute-done.20.refs_3_ = f32[24,8,512]{2,1,0:T(8,128)S(1)} collective-permute-done((f32[24,8,512]{2,1,0:T(8,128)S(1)}, f32[24,8,512]{2,1,0:T(8,128)S(1)}, u32[]{:S(2)}, u32[]{:S(2)}) %collective-permute-start.20) | collective-permute-done | bytes 393248 | tf_op jit(solution)/shard_map/ppermute | solution.py:432
  79.1 1.3 %join.1 = f32[24,16,1024]{2,1,0:T(8,128)} custom-call(f32[24,8,512]{2,1,0:T(8,128)S(1)} %finish.1.refs_0_, f32[24,8,512]{2,1,0:T(8,128)S(1)} %collective-permute-done.18.refs_1_, f32[24,8,512]{2,1,0:T(8,128)S(1)} %collective-permute-done.19.refs_2_, f32[24,8,512]{2,1,0:T(8,128)S(1)} %collective-permute-done.20.refs_3_), custom_call_target="tpu_custom_call" | custom-call | tf_op jit(solution)/shard_map/join/pallas_call | solution.py:408
  (49 shorter events, 11.0 us)
Async XLA Ops:
  0.0 1.4 %copy-start = (f32[1,24,16,1024]{3,2,1,0:T(8,128)S(1)}, f32[1,24,16,1024]{3,2,1,0:T(8,128)}, u32[]{:S(2)}) copy-start(f32[1,24,16,1024]{3,2,1,0:T(8,128)} %param.3) | copy-start | bytes 4718596
  1.4 13.7 %copy-start.3 = (f32[1,3,15]{2,0,1:T(1,128)S(1)}, f32[1,3,15]{2,0,1:T(1,128)}, u32[]{:S(2)}) copy-start(f32[1,3,15]{2,0,1:T(1,128)} %param.4) | copy-start | bytes 544
  1.4 14.1 %copy-start.1 = (f32[1,24,16,1024]{3,2,1,0:T(8,128)S(1)}, f32[1,24,16,1024]{3,2,1,0:T(8,128)}, u32[]{:S(2)}) copy-start(f32[1,24,16,1024]{3,2,1,0:T(8,128)} %param.3) | copy-start | bytes 4718596
  1.5 19.3 %collective-permute-start.5 = (f32[14,16,640]{2,1,0:T(8,128)S(1)}, f32[14,16,640]{2,1,0:T(8,128)S(1)}, u32[]{:S(2)}, u32[]{:S(2)}) collective-permute-start(f32[14,16,640]{2,1,0:T(8,128)S(1)} %cut.5), channel_id=1, source_target_pairs={{0,2},{1,3},{2,0},{3,1},{4,6},{5,7},{6,4},{7,5},{8,10},{9,11},{10,... | collective-permute-start | bytes 1720328 | tf_op jit(solution)/shard_map/ppermute | solution.py:436
  6.2 8.4 %collective-permute-start = (f32[14,8,640]{2,1,0:T(8,128)S(1)}, f32[14,8,640]{2,1,0:T(8,128)S(1)}, u32[]{:S(2)}, u32[]{:S(2)}) collective-permute-start(f32[14,8,640]{2,1,0:T(8,128)S(1)} %get-tuple-element.31), channel_id=1, source_target_pairs={{0,4},{4,0},{8,12},{12,8},{1,5},{5,1},{9,13},{13,9},{2,6},{6,2},{1... | collective-permute-start | bytes 860168 | tf_op jit(solution)/shard_map/ppermute | solution.py:444
  7.8 6.7 %collective-permute-start.2 = (f32[14,8,640]{2,1,0:T(8,128)S(1)}, f32[14,8,640]{2,1,0:T(8,128)S(1)}, u32[]{:S(2)}, u32[]{:S(2)}) collective-permute-start(f32[14,8,640]{2,1,0:T(8,128)S(1)} %get-tuple-element.32), channel_id=1, source_target_pairs={{4,8},{8,4},{5,9},{9,5},{6,10},{10,6},{7,11},{11,7},{20,24},{24,20... | collective-permute-start | bytes 860168 | tf_op jit(solution)/shard_map/ppermute | solution.py:443
  14.6 7.9 %collective-permute-start.1 = (f32[14,8,640]{2,1,0:T(8,128)S(1)}, f32[14,8,640]{2,1,0:T(8,128)S(1)}, u32[]{:S(2)}, u32[]{:S(2)}) collective-permute-start(f32[14,8,640]{2,1,0:T(8,128)S(1)} %collective-permute-done.ma), channel_id=1, source_target_pairs={{0,1},{1,0},{2,3},{3,2},{4,5},{5,4},{6,7},{7,6},{8,9},{9,8},{10,11... | collective-permute-start | bytes 860168 | tf_op jit(solution)/shard_map/ppermute | solution.py:432
  14.6 12.7 %collective-permute-start.3 = (f32[14,8,640]{2,1,0:T(8,128)S(1)}, f32[14,8,640]{2,1,0:T(8,128)S(1)}, u32[]{:S(2)}, u32[]{:S(2)}) collective-permute-start(f32[14,8,640]{2,1,0:T(8,128)S(1)} %collective-permute-done.2.mb), channel_id=1, source_target_pairs={{0,1},{1,0},{2,3},{3,2},{4,5},{5,4},{6,7},{7,6},{8,9},{9,8},{10,11... | collective-permute-start | bytes 860168 | tf_op jit(solution)/shard_map/ppermute | solution.py:432
  15.1 5.1 %collective-permute-start.4 = (f32[3,15]{1,0:T(4,128)S(1)}, f32[3,15]{1,0:T(4,128)S(1)}, u32[]{:S(2)}, u32[]{:S(2)}) collective-permute-start(f32[3,15]{1,0:T(4,128)S(1)} %bitcast.28), channel_id=1, source_target_pairs={{0,2},{1,3},{2,0},{3,1},{4,6},{5,7},{6,4},{7,5},{8,10},{9,11},{10,... | collective-permute-start | bytes 548 | tf_op jit(solution)/shard_map/ppermute | solution.py:436
  15.7 18.5 %collective-permute-start.9 = (f32[7,16,640]{2,1,0:T(8,128)S(1)}, f32[7,16,640]{2,1,0:T(8,128)S(1)}, u32[]{:S(2)}, u32[]{:S(2)}) collective-permute-start(f32[7,16,640]{2,1,0:T(8,128)S(1)} %get-tuple-element.43), channel_id=1, source_target_pairs={{0,4},{4,0},{8,12},{12,8},{1,5},{5,1},{9,13},{13,9},{2,6},{6,2},{1... | collective-permute-start | bytes 860168 | tf_op jit(solution)/shard_map/ppermute | solution.py:444
  20.2 14.0 %collective-permute-start.10 = (f32[7,16,640]{2,1,0:T(8,128)S(1)}, f32[7,16,640]{2,1,0:T(8,128)S(1)}, u32[]{:S(2)}, u32[]{:S(2)}) collective-permute-start(f32[7,16,640]{2,1,0:T(8,128)S(1)} %get-tuple-element.45), channel_id=1, source_target_pairs={{4,8},{8,4},{5,9},{9,5},{6,10},{10,6},{7,11},{11,7},{20,24},{24,20... | collective-permute-start | bytes 860168 | tf_op jit(solution)/shard_map/ppermute | solution.py:443
  20.9 17.9 %collective-permute-start.8 = (f32[10,16,640]{2,1,0:T(8,128)S(1)}, f32[10,16,640]{2,1,0:T(8,128)S(1)}, u32[]{:S(2)}, u32[]{:S(2)}) collective-permute-start(f32[10,16,640]{2,1,0:T(8,128)S(1)} %cut.6), channel_id=1, source_target_pairs={{0,2},{1,3},{2,0},{3,1},{4,6},{5,7},{6,4},{7,5},{8,10},{9,11},{10,... | collective-permute-start | bytes 1228808 | tf_op jit(solution)/shard_map/ppermute | solution.py:436
  22.4 16.4 %collective-permute-start.6 = (f32[7,16,640]{2,1,0:T(8,128)S(1)}, f32[7,16,640]{2,1,0:T(8,128)S(1)}, u32[]{:S(2)}, u32[]{:S(2)}) collective-permute-start(f32[7,16,640]{2,1,0:T(8,128)S(1)} %get-tuple-element.58), channel_id=1, source_target_pairs={{0,4},{4,0},{8,12},{12,8},{1,5},{5,1},{9,13},{13,9},{2,6},{6,2},{1... | collective-permute-start | bytes 860168 | tf_op jit(solution)/shard_map/ppermute | solution.py:444
  27.2 11.6 %collective-permute-start.7 = (f32[7,16,640]{2,1,0:T(8,128)S(1)}, f32[7,16,640]{2,1,0:T(8,128)S(1)}, u32[]{:S(2)}, u32[]{:S(2)}) collective-permute-start(f32[7,16,640]{2,1,0:T(8,128)S(1)} %get-tuple-element.57), channel_id=1, source_target_pairs={{4,8},{8,4},{5,9},{9,5},{6,10},{10,6},{7,11},{11,7},{20,24},{24,20... | collective-permute-start | bytes 860168 | tf_op jit(solution)/shard_map/ppermute | solution.py:443
  41.6 1.9 %collective-permute-start.11 = (f32[24,8,640]{2,1,0:T(8,128)S(1)}, f32[24,8,640]{2,1,0:T(8,128)S(1)}, u32[]{:S(2)}, u32[]{:S(2)}) collective-permute-start(f32[24,8,640]{2,1,0:T(8,128)S(1)} %get-tuple-element.47), channel_id=1, source_target_pairs={{0,1},{1,0},{2,3},{3,2},{4,5},{5,4},{6,7},{7,6},{8,9},{9,8},{10,11... | collective-permute-start | bytes 1474568 | tf_op jit(solution)/shard_map/ppermute | solution.py:432
  43.7 8.9 %collective-permute-start.12 = (f32[14,8,640]{2,1,0:T(8,128)S(1)}, f32[14,8,640]{2,1,0:T(8,128)S(1)}, u32[]{:S(2)}, u32[]{:S(2)}) collective-permute-start(f32[14,8,640]{2,1,0:T(8,128)S(1)} %get-tuple-element.48), channel_id=1, source_target_pairs={{0,4},{4,0},{8,12},{12,8},{1,5},{5,1},{9,13},{13,9},{2,6},{6,2},{1... | collective-permute-start | bytes 860168 | tf_op jit(solution)/shard_map/ppermute | solution.py:444
  45.3 7.3 %collective-permute-start.14 = (f32[14,8,640]{2,1,0:T(8,128)S(1)}, f32[14,8,640]{2,1,0:T(8,128)S(1)}, u32[]{:S(2)}, u32[]{:S(2)}) collective-permute-start(f32[14,8,640]{2,1,0:T(8,128)S(1)} %get-tuple-element.49), channel_id=1, source_target_pairs={{4,8},{8,4},{5,9},{9,5},{6,10},{10,6},{7,11},{11,7},{20,24},{24,20... | collective-permute-start | bytes 860168 | tf_op jit(solution)/shard_map/ppermute | solution.py:443
  46.2 7.0 %collective-permute-start.16 = (f32[24,8,640]{2,1,0:T(8,128)S(1)}, f32[24,8,640]{2,1,0:T(8,128)S(1)}, u32[]{:S(2)}, u32[]{:S(2)}) collective-permute-start(f32[24,8,640]{2,1,0:T(8,128)S(1)} %get-tuple-element.50.mine.est), channel_id=1, source_target_pairs={{0,1},{1,0},{2,3},{3,2},{4,5},{5,4},{6,7},{7,6},{8,9},{9,8},{10,11... | collective-permute-start | bytes 1474568 | tf_op jit(solution)/shard_map/ppermute | solution.py:432
  52.7 2.2 %collective-permute-start.13 = (f32[14,8,640]{2,1,0:T(8,128)S(1)}, f32[14,8,640]{2,1,0:T(8,128)S(1)}, u32[]{:S(2)}, u32[]{:S(2)}) collective-permute-start(f32[14,8,640]{2,1,0:T(8,128)S(1)} %collective-permute-done.12.ma), channel_id=1, source_target_pairs={{0,1},{1,0},{2,3},{3,2},{4,5},{5,4},{6,7},{7,6},{8,9},{9,8},{10,11... | collective-permute-start | bytes 860168 | tf_op jit(solution)/shard_map/ppermute | solution.py:432
  52.7 2.2 %collective-permute-start.15 = (f32[14,8,640]{2,1,0:T(8,128)S(1)}, f32[14,8,640]{2,1,0:T(8,128)S(1)}, u32[]{:S(2)}, u32[]{:S(2)}) collective-permute-start(f32[14,8,640]{2,1,0:T(8,128)S(1)} %collective-permute-done.14.mb), channel_id=1, source_target_pairs={{0,1},{1,0},{2,3},{3,2},{4,5},{5,4},{6,7},{7,6},{8,9},{9,8},{10,11... | collective-permute-start | bytes 860168 | tf_op jit(solution)/shard_map/ppermute | solution.py:432
  64.3 1.8 %collective-permute-start.17 = (f32[24,8,512]{2,1,0:T(8,128)S(1)}, f32[24,8,512]{2,1,0:T(8,128)S(1)}, u32[]{:S(2)}, u32[]{:S(2)}) collective-permute-start(f32[24,8,512]{2,1,0:T(8,128)S(1)} %get-tuple-element.56), channel_id=1, source_target_pairs={{0,1},{1,0},{2,3},{3,2},{4,5},{5,4},{6,7},{7,6},{8,9},{9,8},{10,11... | collective-permute-start | bytes 1179656 | tf_op jit(solution)/shard_map/ppermute | solution.py:432
  66.1 11.2 %collective-permute-start.18 = (f32[24,8,512]{2,1,0:T(8,128)S(1)}, f32[24,8,512]{2,1,0:T(8,128)S(1)}, u32[]{:S(2)}, u32[]{:S(2)}) collective-permute-start(f32[24,8,512]{2,1,0:T(8,128)S(1)} %finish.1.refs_0_), channel_id=1, source_target_pairs={{0,2},{1,3},{2,0},{3,1},{4,6},{5,7},{6,4},{7,5},{8,10},{9,11},{10,... | collective-permute-start | bytes 1179656 | tf_op jit(solution)/shard_map/ppermute | solution.py:436
  67.6 9.7 %collective-permute-start.19 = (f32[24,8,512]{2,1,0:T(8,128)S(1)}, f32[24,8,512]{2,1,0:T(8,128)S(1)}, u32[]{:S(2)}, u32[]{:S(2)}) collective-permute-start(f32[24,8,512]{2,1,0:T(8,128)S(1)} %finish.1.refs_0_), channel_id=1, source_target_pairs={{0,1},{1,0},{2,3},{3,2},{4,5},{5,4},{6,7},{7,6},{8,9},{9,8},{10,11... | collective-permute-start | bytes 1179656 | tf_op jit(solution)/shard_map/ppermute | solution.py:432
  77.3 1.7 %collective-permute-start.20 = (f32[24,8,512]{2,1,0:T(8,128)S(1)}, f32[24,8,512]{2,1,0:T(8,128)S(1)}, u32[]{:S(2)}, u32[]{:S(2)}) collective-permute-start(f32[24,8,512]{2,1,0:T(8,128)S(1)} %collective-permute-done.18.refs_1_), channel_id=1, source_target_pairs={{0,1},{1,0},{2,3},{3,2},{4,5},{5,4},{6,7},{7,6},{8,9},{9,8},{10,11... | collective-permute-start | bytes 1179656 | tf_op jit(solution)/shard_map/ppermute | solution.py:432
  (1 other events, 1.4 us)

commit v5 on v4

v5 whole, which is shorter than its diff:
```python
import functools
from typing import NamedTuple

import jax
import jax.numpy as jnp
from jax import lax
from jax.experimental import pallas as pl
from jax.experimental.pallas import tpu as pltpu
from jax.sharding import PartitionSpec as P


RADIUS = 7
ITERS = 2
TAPS = 2 * RADIUS + 1
LANES = 128
ROWS = 256
BF = jnp.bfloat16
F32 = jnp.float32
VMEM = pl.BlockSpec(memory_space=pltpu.VMEM)
SMEM = pl.BlockSpec(memory_space=pltpu.SMEM)
ANY = pl.BlockSpec(memory_space=pltpu.HBM)
PARAMS = pltpu.CompilerParams(vmem_limit_bytes=20 * 1024 * 1024)


def halves(value):
    high = value.astype(BF)
    return high, (value - high.astype(F32)).astype(BF)


def dot(a, b):
    return jnp.dot(a, b, preferred_element_type=F32)


class Split(NamedTuple):
    chips: int
    cores: int
    part: int
    width: int
    ny: int
    half: int

    def start(self, chip):
        place = jnp.clip(chip * self.part - LANES, 0, self.ny - self.width)
        return pl.multiple_of(place, LANES)

    def here(self):
        place = lax.axis_index("view")
        return place // self.cores, lax.rem(place, self.cores)

    def inner(self):
        chip, _ = self.here()
        return pl.multiple_of(chip * self.part - self.start(chip), LANES)

    def odd(self):
        return lax.rem(lax.axis_index("tile"), 2)

    def side(self, mine):
        _, core = self.here()
        own = 1 - lax.rem(self.odd() + core, 2)
        return own if mine else 1 - own

    def rows(self, core):
        return pl.ds(pl.multiple_of(core * self.half, self.half), self.half)


def cut_kernel(split, sources, moves, *refs):
    outs, sem = refs[sources:-1], refs[-1]
    chip, _ = split.here()
    copies = []
    for source, ahead, out, at, even, odd, n, by_core in moves:
        lanes = pl.ds(split.start(lax.rem(chip + ahead, split.chips)), split.width)
        which = 1 - split.side(True) if by_core else split.odd()
        x0 = even if even == odd else jnp.where(which == 1, odd, even)
        copies.append(
            pltpu.make_async_copy(
                refs[source].at[pl.ds(x0, n), :, lanes],
                outs[out].at[pl.ds(at, n)],
                sem.at[len(copies)],
            )
        )
        copies[-1].start()
    for copy in copies:
        copy.wait()


def cut(sources, split, outs):
    moves, shapes = [], []
    for index, (source, ahead, ranges) in enumerate(outs):
        at = 0
        for even, odd, n, by_core in ranges:
            moves.append((source, ahead, index, at, even, odd, n, by_core))
            at += n
        shapes.append(jax.ShapeDtypeStruct((at, sources[source].shape[1], split.width), F32))
    return pl.pallas_call(
        functools.partial(cut_kernel, split, len(sources), tuple(moves)),
        out_shape=tuple(shapes),
        in_specs=[ANY] * len(sources),
        out_specs=(VMEM,) * len(shapes),
        scratch_shapes=[pltpu.SemaphoreType.DMA((len(moves),))],
        compiler_params=PARAMS,
        name="cut",
    )(*sources)


def update_kernel(split, views, planes, *refs):
    est, out, rim = refs[-3:]
    for c, (p0, p1) in enumerate(planes):
        total = refs[2 * c][...] + refs[2 * c + 1][...]
        out[p0:p1] = est[p0:p1] * jnp.exp(total / views)
    n = rim.shape[0]
    rim[...] = out[pl.ds(split.side(True) * (out.shape[0] - n), n)]


def update(split, views, planes, sums, est):
    return pl.pallas_call(
        functools.partial(update_kernel, split, views, planes),
        out_shape=(
            jax.ShapeDtypeStruct(est.shape, F32),
            jax.ShapeDtypeStruct((2 * RADIUS, *est.shape[1:]), F32),
        ),
        in_specs=[VMEM] * (len(sums) + 1),
        out_specs=(VMEM,) * 2,
        compiler_params=PARAMS,
        name="update",
    )(*sums, est)


def finish_kernel(split, views, planes, mine, sibling, est, out):
    _, core = split.here()
    old = est[planes[0] : planes[1], split.rows(core), pl.ds(split.inner(), split.part)]
    out[...] = old * jnp.exp((mine[...] + sibling[...]) / views)


def finish(split, views, planes, mine, sibling, est):
    return pl.pallas_call(
        functools.partial(finish_kernel, split, views, planes),
        out_shape=jax.ShapeDtypeStruct(mine.shape, F32),
        in_specs=[VMEM] * 3,
        out_specs=VMEM,
        compiler_params=PARAMS,
        name="finish",
    )(mine, sibling, est)


def operators_kernel(nz, taps, t, w, wr, th, tl):
    planes = ROWS // nz
    band = LANES + 3 * 8
    first = LANES - 8
    i = lax.broadcasted_iota(jnp.int32, (band, LANES), 0) + first
    o = lax.broadcasted_iota(jnp.int32, (band, LANES), 1)
    shift_y = i - o - (LANES - RADIUS)
    row = lax.broadcasted_iota(jnp.int32, (nz, 2 * ROWS), 0)
    col = lax.broadcasted_iota(jnp.int32, (nz, 2 * ROWS), 1)
    shift_x = col // nz
    shift_z = col % nz - row + RADIUS
    sums = []
    for d in range(3):
        value = taps[0, d, 0]
        for k in range(1, TAPS):
            value = value + taps[0, d, k]
        sums.append(value)
    th[...] = jnp.zeros_like(th)
    tl[...] = jnp.zeros_like(tl)
    half = LANES // 2
    for mirrored in range(2):
        ty = jnp.zeros((band, LANES), F32)
        kx = jnp.zeros((nz, 2 * ROWS), F32)
        kz = jnp.zeros((nz, 2 * ROWS), F32)
        for k in range(TAPS):
            tap = TAPS - 1 - k if mirrored else k
            kx = jnp.where(shift_x == k, taps[0, 0, tap], kx)
            kz = jnp.where(shift_z == k, taps[0, 1, tap], kz)
            ty = jnp.where(shift_y == k, taps[0, 2, tap], ty)
        kx = kx / sums[0]
        kz = kz / sums[1]
        ty = ty / sums[2]
        high, low = halves(ty)
        for c0 in range(0, ROWS, LANES):
            rows = slice(first + c0, first + c0 + band)
            th[rows, c0 : c0 + LANES] = high
            tl[rows, c0 : c0 + LANES] = low
        inside = slice(LANES, LANES + ROWS)
        right, left = slice(LANES + ROWS, LANES + ROWS + half), slice(half, LANES)
        t[mirrored, 0] = th[inside, :]
        t[mirrored, 1] = tl[inside, :]
        for at in (0, LANES):
            t[mirrored, 2, at : at + half] = th[right, :]
            t[mirrored, 2, at + half : at + LANES] = th[left, :]
        t[mirrored, 3, :half] = tl[right, :]
        t[mirrored, 3, half:LANES] = tl[left, :]
        t[mirrored, 3, LANES:] = jnp.zeros((ROWS - LANES, ROWS), BF)
        t[mirrored, 4, :, :LANES] = th[:ROWS, :LANES]
        t[mirrored, 4, :, LANES:] = tl[:ROWS, :LANES]
        strip = kx * kz
        for p in range(planes):
            moved = pltpu.roll(strip, p * nz, 1) if p else strip
            rows = slice(p * nz, (p + 1) * nz)
            w[mirrored, 0, rows, :], w[mirrored, 1, rows, :] = halves(moved)
            if not mirrored:
                wr[0, 0, rows, :], wr[0, 1, rows, :] = halves(moved[:, :ROWS])
                back = (p - 2 * RADIUS) * nz % (2 * ROWS)
                moved = pltpu.roll(strip, back, 1)[:, :ROWS] if back else strip[:, :ROWS]
                wr[1, 0, rows, :], wr[1, 1, rows, :] = halves(moved)


def operators(taps, nz):
    return pl.pallas_call(
        functools.partial(operators_kernel, nz),
        out_shape=(
            jax.ShapeDtypeStruct((2, 5, ROWS, ROWS), BF),
            jax.ShapeDtypeStruct((2, 2, ROWS, 2 * ROWS), BF),
            jax.ShapeDtypeStruct((2, 2, ROWS, ROWS), BF),
        ),
        in_specs=[SMEM],
        out_specs=(VMEM,) * 3,
        scratch_shapes=[pltpu.VMEM((2 * ROWS, ROWS), BF)] * 2,
        compiler_params=PARAMS,
        name="operators",
    )(taps)


def blur_y(x, t, store):
    n, width = x.shape
    xh, xl = halves(x)
    right = lax.broadcasted_iota(jnp.int32, (n, LANES), 1) < LANES // 2
    for o0 in range(0, width, ROWS):
        size = min(ROWS, width - o0)
        if size == ROWS:
            end = o0 + ROWS
            at = slice(o0, end)
            out = dot(xh[:, at], t[0]) + (dot(xl[:, at], t[0]) + dot(xh[:, at], t[1]))
            none = jnp.zeros((n, LANES), F32)
            corner = jnp.where(
                right,
                x[:, end : end + LANES] if end < width else none,
                x[:, o0 - LANES : o0] if o0 else none,
            )
            ch, cl = halves(corner)
            out = out + (dot(jnp.concatenate([ch, cl], 1), t[2]) + dot(ch, t[3, :LANES]))
        else:
            at = slice(o0 - LANES, o0 + LANES)
            both = dot(xh[:, at], t[4])
            out = both[:, :LANES] + (both[:, LANES:] + dot(xl[:, at], t[4, :, :LANES]))
        store(o0, size, out)


def product(w, dh, dl, rows, store):
    wh, wl = w
    width = dh.shape[1]
    for o0 in range(0, width, ROWS):
        size = min(ROWS, width - o0)
        at = slice(o0, o0 + size)
        if size == ROWS:
            out = dot(wh, dh[rows, at]) + (dot(wl, dh[rows, at]) + dot(wh, dl[rows, at]))
        else:
            both = dot(wh, jnp.concatenate([dh[rows, at], dl[rows, at]], 1))
            out = both[:, :size] + (both[:, size:] + dot(wl, dh[rows, at]))
        store(o0, size, out)


def blur_xz(dh, dl, w, nz, planes_out, store):
    step = ROWS // nz
    for p0 in range(0, planes_out, step):
        m = min(step, planes_out - p0) * nz
        k = min(2 * ROWS, (planes_out + 2 * RADIUS - p0) * nz)
        rows = slice(p0 * nz, p0 * nz + k)
        put = functools.partial(store, p0 * nz, m)
        product((w[0, :m, :k], w[1, :m, :k]), dh, dl, rows, put)


def to_halves(dh, dl, rows):
    def store(o0, size, value):
        h, l = halves(value)
        dh[rows, o0 : o0 + size] = h
        dl[rows, o0 : o0 + size] = l

    return store


def chunks(rows, step=128):
    return [(r, min(step, rows - r)) for r in range(0, rows, step)]


def own_kernel(est, t, w, wr, blurred, dh, dl):
    planes, nz, width = est.shape
    step = LANES // nz
    for p in range(0, planes, step):
        n = min(step, planes - p)
        x = est[p : p + n].reshape(n * nz, width)
        blur_y(x, t.at[0], to_halves(dh, dl, slice(p * nz, (p + n) * nz)))
    total = planes + 2 * RADIUS
    step = ROWS // nz
    for p0 in range(0, total, step):
        out = min(step, total - p0)
        first = max(0, p0 - 2 * RADIUS)
        last = min(planes, p0 + out)
        k = (last - first) * nz
        m = out * nz
        if p0 < 2 * RADIUS:
            assert p0 == 0
            block = wr[1, 0, :m, :k], wr[1, 1, :m, :k]
        else:
            first = p0 - 2 * RADIUS
            block = w[0, 0, :m, :k], w[0, 1, :m, :k]

        def store(o0, size, value):
            blurred[p0 * nz : p0 * nz + m, o0 : o0 + size] = value

        product(block, dh, dl, slice(first * nz, last * nz), store)


def own_share(est, ops):
    planes, nz, width = est.shape
    t, w, wr = ops
    half = pltpu.VMEM((planes * nz, width), BF)
    return pl.pallas_call(
        own_kernel,
        out_shape=jax.ShapeDtypeStruct(((planes + 2 * RADIUS) * nz, width), F32),
        in_specs=[VMEM] * 4,
        out_specs=VMEM,
        scratch_shapes=[half, half],
        compiler_params=PARAMS,
        name="own_share",
    )(est, t, w, wr)


def rim_kernel(split, mine, before, rim, t, wr, blurred, dh, dl):
    planes, nz, width = rim.shape
    n = planes * nz
    side = split.side(mine)
    flat = rim[...].reshape(n, width)
    for r0, count in chunks(n, 112):
        blur_y(flat[r0 : r0 + count, :], t.at[0], to_halves(dh, dl, slice(r0, r0 + count)))
    rows = pl.ds(pl.multiple_of(side * (blurred.shape[0] - n), nz), n)

    def store(o0, size, value):
        blurred[rows, o0 : o0 + size] = before[rows, o0 : o0 + size] + value

    product((wr[side, 0, :n, :n], wr[side, 1, :n, :n]), dh, dl, slice(0, n), store)


def rim_share(split, mine, before, rim, ops):
    planes, nz, width = rim.shape
    half = pltpu.VMEM((planes * nz, width), BF)
    return pl.pallas_call(
        functools.partial(rim_kernel, split, mine),
        out_shape=jax.ShapeDtypeStruct(before.shape, F32),
        in_specs=[VMEM] * 4,
        out_specs=VMEM,
        scratch_shapes=[half, half],
        input_output_aliases={0: 0},
        compiler_params=PARAMS,
        name="rim_share",
    )(before, rim, ops[0], ops[2])


class Piece(NamedTuple):
    at: int
    rows: int
    odd: int
    odd_start: int
    even: int
    even_start: int

    def load(self, refs, odd, r0, n):
        if self.odd != self.even:
            a = refs[self.odd][self.odd_start + r0 : self.odd_start + r0 + n, :]
            b = refs[self.even][self.even_start + r0 : self.even_start + r0 + n, :]
            return jnp.where(odd == 1, a, b)
        start = self.even_start
        if self.odd_start != self.even_start:
            start = jnp.where(odd == 1, self.odd_start, self.even_start)
            start = pl.multiple_of(start, 8)
        return refs[self.odd][pl.ds(start + r0, n), :]


class Span(NamedTuple):
    planes: tuple
    blurred: tuple
    handed: bool
    hands_on: bool


def adjoint_kernel(nz, split, pieces, inputs, span, has_added, ends, *refs):
    refs = list(refs)
    take = lambda n: [refs.pop(0) for _ in range(n)]
    (blurred,), record, (t, w) = take(1), take(inputs), take(2)
    (added,) = take(1) if has_added else (None,)
    handed = take(2) if span.handed else None
    keep, send = take(2) if ends is not None else (None, None)
    (out,) = take(1) if ends is None else (None,)
    hands_on = take(2) if span.hands_on else None
    (out,) = take(1) if ends is not None else (out,)
    dh, dl = refs
    odd = split.odd()
    p0, p1 = span.planes
    base = p0 * nz
    q0, q1 = span.blurred[0] * nz, span.blurred[1] * nz
    if handed is not None:
        dh[: q0 - base, :] = handed[0][...]
        dl[: q0 - base, :] = handed[1][...]
    for piece in pieces:
        lo, hi = max(q0, piece.at), min(q1, piece.at + piece.rows)
        for r0, n in chunks(max(0, hi - lo)):
            at = lo + r0
            q = piece.load(record, odd, at - piece.at, n) / blurred[at : at + n, :]
            blur_y(q, t.at[1], to_halves(dh, dl, slice(at - base, at - base + n)))
    if hands_on is not None:
        hands_on[0][...] = dh[(p1 - p0) * nz :, :]
        hands_on[1][...] = dl[(p1 - p0) * nz :, :]

    def store(r0, m, o0, size, value):
        log = jnp.log(value)
        planes = slice(r0 // nz, (r0 + m) // nz)
        log = log.reshape(m // nz, nz, size)
        if has_added:
            log = log + added[planes, :, o0 : o0 + size]
        out[planes, :, o0 : o0 + size] = log

    blur_xz(dh, dl, w.at[1], nz, p1 - p0, store)
    if ends is not None:
        _, core = split.here()
        lanes = slice(None) if ends == split.width else pl.ds(split.inner(), ends)
        keep[...] = out[:, split.rows(core), lanes]
        send[...] = out[:, split.rows(1 - core), lanes]


def adjoint(split, blurred, record, pieces, ops, span, added, handed, nz, ends=None):
    width = blurred.shape[1]
    planes = span.planes[1] - span.planes[0]
    args = [blurred, *record, *ops[:2]] + ([] if added is None else [added])
    args += [] if handed is None else list(handed)
    rows = (planes + 2 * RADIUS) * nz
    full = (planes, nz, width)
    shapes = [jax.ShapeDtypeStruct(full, F32)]
    scratch = [pltpu.VMEM((rows, width), BF), pltpu.VMEM((rows, width), BF)]
    if ends is not None:
        shapes = [jax.ShapeDtypeStruct((planes, split.half, ends), F32)] * 2
        scratch = [pltpu.VMEM(full, F32)] + scratch
    if span.hands_on:
        shapes += [jax.ShapeDtypeStruct((2 * RADIUS * nz, width), BF)] * 2
    kernel = functools.partial(
        adjoint_kernel, nz, split, pieces, len(record), span, added is not None, ends
    )
    out = pl.pallas_call(
        kernel,
        out_shape=tuple(shapes),
        in_specs=[VMEM] * len(args),
        out_specs=(VMEM,) * len(shapes),
        scratch_shapes=scratch,
        compiler_params=PARAMS,
        name="adjoint",
    )(*args)
    total = out[0] if ends is None else out[:2]
    return total, (out[-2:] if span.hands_on else None)


def spans(nx, count):
    out, done = [], 0
    for c in range(count):
        p0, p1 = c * nx // count, (c + 1) * nx // count
        q1 = p1 + 2 * RADIUS
        out.append(Span((p0, p1), (done, q1), c > 0, c < count - 1))
        done = q1
    return out


def join_kernel(split, planes, *refs):
    parts, out = refs[:-1], refs[-1]
    chip, core = split.here()
    for c, (p0, p1) in enumerate(planes):
        for r in range(split.chips):
            owner = lax.rem(chip + split.chips - r, split.chips)
            lanes = pl.ds(pl.multiple_of(owner * split.part, LANES), split.part)
            mine, sibling = parts[2 * (c * split.chips + r) : 2 * (c * split.chips + r) + 2]
            out[p0:p1, split.rows(core), lanes] = mine[...]
            out[p0:p1, split.rows(1 - core), lanes] = sibling[...]


def join(split, planes, parts, nx, nz):
    return pl.pallas_call(
        functools.partial(join_kernel, split, planes),
        out_shape=jax.ShapeDtypeStruct((nx, nz, split.ny), F32),
        in_specs=[VMEM] * len(parts),
        out_specs=VMEM,
        compiler_params=PARAMS,
        name="join",
    )(*parts)


def steps(recorded, psf_taps, estimate):
    views = lax.axis_size("view")
    tiles = lax.axis_size("tile")
    nx, nz, ny = estimate.shape
    cores = 2
    chips = views // cores
    part = ny // chips
    width = min(ny, part + (LANES if chips <= 2 else 2 * LANES))
    split = Split(chips, cores, part, width, ny, nz // cores)
    assert 2 * RADIUS * ITERS <= LANES and nx >= 2 * RADIUS
    flat = lambda a: a.reshape(-1, a.shape[-1])

    def swap_core(values):
        pairs = [(v, v ^ 1) for v in range(views)]
        return lax.ppermute(values, "view", pairs)

    def to_chip(values, r):
        pairs = [(v, (v + r * cores) % views) for v in range(views)]
        return lax.ppermute(values, "view", pairs)

    next_a = [(t, t ^ 1) for t in range(tiles) if t ^ 1 < tiles]
    next_b = [(t, ((t + 1) ^ 1) - 1) for t in range(1, tiles)]
    next_b = [(t, u) for t, u in next_b if u < tiles]

    def pair_up(a, b):
        b = lax.ppermute(b, "tile", next_b)
        a = lax.ppermute(a, "tile", next_a)
        return a, b

    both = []
    for v in range(views):
        both += [(t * views + v, u * views + v) for t, u in (next_b if v % cores else next_a)]

    def estimate_rims(values):
        mine = lax.ppermute(values, ("tile", "view"), both)
        return mine, swap_core(mine)

    recorded = recorded[0]
    taps = [psf_taps] + [to_chip(psf_taps, r) for r in range(1, chips)]

    def to_a(n, by_core=False):
        return (nx - n, 0, n, by_core)

    def to_b(n):
        return (0, nx - n, n, False)

    rim, body = RADIUS * nz, (nx - 2 * RADIUS) * nz
    end = 2 * rim + body
    outs = []
    for r in range(1, chips):
        outs.append((0, r, (to_a(RADIUS), to_b(RADIUS))))
        outs.append((0, r, ((RADIUS, RADIUS, nx - 2 * RADIUS, False),)))
    outs += [(0, 0, ((0, 0, nx, False),)), (0, 0, (to_a(RADIUS),)), (0, 0, (to_b(RADIUS),))]
    outs += [(1, 0, ((0, 0, nx, False),)), (1, 0, (to_a(2 * RADIUS, True),))]
    cuts = cut((recorded, estimate), split, outs)
    own, own_a, own_b, est, est_rim = cuts[2 * (chips - 1) :]

    edges, middles = [None], [None]
    for r in range(1, chips):
        edges.append(to_chip(cuts[2 * r - 2], r))
        middles.append(to_chip(cuts[2 * r - 1], r))
    rims = estimate_rims(est_rim)
    own_a, own_b = pair_up(own_a, own_b)

    record = [tuple(flat(a) for a in (own_a, own_b, own))]
    before, after = Piece(0, rim, 0, 0, 1, 0), Piece(rim + end, rim, 1, 0, 0, 0)
    pieces = [(before, Piece(rim, end, 2, 0, 2, 0), after)]
    for r in range(1, chips):
        pair_a, pair_b = pair_up(edges[r][:RADIUS], edges[r][RADIUS:])
        record.append(tuple(flat(a) for a in (pair_a, pair_b, edges[r], middles[r])))
        first = Piece(rim, rim, 2, 0, 2, rim)
        inner = Piece(2 * rim, body, 3, 0, 3, 0)
        last = Piece(2 * rim + body, rim, 2, rim, 2, 0)
        pieces.append((before, first, inner, last, after))

    ops = []
    for k in taps:
        ops.append(operators(k, nz))

    for iteration in range(ITERS):
        final = iteration == ITERS - 1
        blurred = []
        for r in range(chips):
            blurred.append(own_share(est, ops[r]))
        for mine in (True, False):
            for r in range(chips):
                rim_planes = rims[0] if mine else rims[1]
                blurred[r] = rim_share(split, mine, blurred[r], rim_planes, ops[r])
        plan = spans(nx, 2)
        handed = [None] * chips
        sums = []
        for span in plan:
            total = None
            for r in range(chips):
                ends = part if final and r == chips - 1 else None
                total, handed[r] = adjoint(
                    split,
                    blurred[r],
                    record[r],
                    pieces[r],
                    ops[r],
                    span,
                    total,
                    handed[r],
                    nz,
                    ends,
                )
            keep, send = total if final else (total, total)
            sums.append((keep, swap_core(send)))
        if not final:
            planes = [span.planes for span in plan]
            est, est_rim = update(split, views, planes, sum(sums, ()), est)
            rims = estimate_rims(est_rim)

    parts = []
    for span, pair in zip(plan, sums):
        done = finish(split, views, span.planes, *pair, est)
        for r in range(chips):
            mine = to_chip(done, r) if r else done
            parts += [mine, swap_core(mine)]
    return join(split, [span.planes for span in plan], parts, nx, nz)


def solution(mesh):
    in_specs = (P("view", "tile", "slab", None), P("view", None, None), P("tile", "slab", None))
    out_specs = P("tile", "slab", None)
    return jax.shard_map(steps, mesh=mesh, in_specs=in_specs, out_specs=out_specs, check_vma=False)
```

time: 81.3 us -> 85.7 us (1.054)
  Pallas kernels: 26.7 us -> 29.6 us
  starting transfers between devices: 23 us -> 24.4 us
  waiting for transfers between devices: 27.4 us -> 28.3 us
    ppermute x0 -> x2, waiting for transfers between devices: none -> 14.6 us  [estimate_rims(): mine = lax.ppermute(values, ('tile', 'view'), both)]
    ppermute x4 -> x2, waiting for transfers between devices: 12.4 us -> 0.01 us  [pair_up(): a = lax.ppermute(a, 'tile', next_a)]
    ppermute x0 -> x2, starting transfers between devices: none -> 8.1 us  [estimate_rims(): mine = lax.ppermute(values, ('tile', 'view'), both)]
    ppermute x4 -> x2, starting transfers between devices: 12.5 us -> 6.4 us  [pair_up(): a = lax.ppermute(a, 'tile', next_a)]
    pallas_call x19 -> x25, Pallas kernels: 24.5 us -> 27.4 us  [the longest x8 10.7 us: adjoint(): pl.pallas_call(kernel, out_shape=tuple(shapes), in_specs=[VMEM] * len(arg...]
    ppermute x4 -> x2, starting transfers between devices: 2.86 us -> 1.33 us  [pair_up(): b = lax.ppermute(b, 'tile', next_b)]
    ppermute x9 -> x10, waiting for transfers between devices: 5.29 us -> 4.48 us  [swap_core(): return lax.ppermute(values, 'view', pairs)]
    ppermute x9 -> x10, starting transfers between devices: 1.24 us -> 1.73 us  [swap_core(): return lax.ppermute(values, 'view', pairs)]
  transfers between devices with their start and end apart: 21 -> 21, of which waited for: 6 -> 9; matrix products, arithmetic and copies ran while one was open for 0% -> 0% of each run, Pallas kernels for 16% -> 20%
where the time goes in v5:
time: 85.7 us; the launch traced here: 85.5 us
  Pallas kernels  29.6 us (35%)
  waiting for transfers between devices  28.3 us (33%)
  starting transfers between devices  24.4 us (28%)
  local copies, waits for them, and re-layouts  2.86 us (3%)
    ppermute x2, waiting for transfers between devices, estimate_rims(): mine = lax.ppermute(values, ('tile', 'view'), both)  14.6 us
    pallas_call x8, Pallas kernels, adjoint(): pl.pallas_call(kernel, out_shape=tuple(shapes), in_specs=[VMEM] * len(arg...  10.7 us
    ppermute x5, waiting for transfers between devices, to_chip(): return lax.ppermute(values, 'view', pairs)  9.25 us
    ppermute x2, starting transfers between devices, estimate_rims(): mine = lax.ppermute(values, ('tile', 'view'), both)  8.1 us
    pallas_call x8, Pallas kernels, rim_share(): pl.pallas_call(functools.partial(rim_kernel, split, mine), out_shape=jax....  7.5 us
    ppermute x5, starting transfers between devices, to_chip(): return lax.ppermute(values, 'view', pairs)  6.81 us
    pallas_call x4, Pallas kernels, own_share(): pl.pallas_call(own_kernel, out_shape=jax.ShapeDtypeStruct(((planes + 2 *...  6.78 us
    ppermute x2, starting transfers between devices, pair_up(): a = lax.ppermute(a, 'tile', next_a)  6.4 us
  transfers between devices with their start and end apart: 21, of which 9 were waited for; matrix products, arithmetic and copies ran while one was open for 0% of the time, Pallas kernels for 20%

profile of v5, /device:TPU:0, one launch (start us, length us, event | category | flops | bytes accessed | tf_op | source)
XLA Modules:
  0.0 85.5 jit_solution(7047226868538511551)
XLA Ops:
  0.0 1.4 %copy-done = f32[1,24,16,1024]{3,2,1,0:T(8,128)S(1)} copy-done((f32[1,24,16,1024]{3,2,1,0:T(8,128)S(1)}, f32[1,24,16,1024]{3,2,1,0:T(8,128)}, u32[]{:S(2)}) %copy-start) | copy-done | bytes 1572888
  1.4 1.4 %copy-done.1 = f32[24,16,1024]{2,1,0:T(8,128)S(1)} copy-done((f32[24,16,1024]{2,1,0:T(8,128)S(1)}, f32[24,16,1024]{2,1,0:T(8,128)}, u32[]{:S(2)}) %copy-start.1) | copy-done | bytes 1572888
  3.3 5.0 %collective-permute-start.1 = (f32[14,16,640]{2,1,0:T(8,128)S(1)}, f32[14,16,640]{2,1,0:T(8,128)S(1)}, u32[]{:S(2)}, u32[]{:S(2)}) collective-permute-start(f32[14,16,640]{2,1,0:T(8,128)S(1)} %get-tuple-element.39), channel_id=1, source_target_pairs={{0,4},{4,0},{8,12},{12,8},{5,9},{9,5},{2,6},{6,2},{10,14},{14,10},... | collective-permute-start | bytes 1720328 | tf_op jit(solution)/shard_map/ppermute | solution.py:525
  8.3 1.6 %collective-permute-start.3 = (f32[14,16,640]{2,1,0:T(8,128)S(1)}, f32[14,16,640]{2,1,0:T(8,128)S(1)}, u32[]{:S(2)}, u32[]{:S(2)}) collective-permute-start(f32[14,16,640]{2,1,0:T(8,128)S(1)} %get-tuple-element.40), channel_id=1, source_target_pairs={{0,2},{1,3},{2,0},{3,1},{4,6},{5,7},{6,4},{7,5},{8,10},{9,11},{10,... | collective-permute-start | bytes 1720328 | tf_op jit(solution)/shard_map/ppermute | solution.py:509
  9.9 6.1 %collective-permute-done.1.rim = f32[14,16,640]{2,1,0:T(8,128)S(1)} collective-permute-done((f32[14,16,640]{2,1,0:T(8,128)S(1)}, f32[14,16,640]{2,1,0:T(8,128)S(1)}, u32[]{:S(2)}, u32[]{:S(2)}) %collective-permute-start.1) | collective-permute-done | bytes 573472 | tf_op jit(solution)/shard_map/ppermute | solution.py:525
  16.0 2.0 %collective-permute-start.7 = (f32[7,16,640]{2,1,0:T(8,128)S(1)}, f32[7,16,640]{2,1,0:T(8,128)S(1)}, u32[]{:S(2)}, u32[]{:S(2)}) collective-permute-start(f32[7,16,640]{2,1,0:T(8,128)S(1)} %get-tuple-element.45), channel_id=1, source_target_pairs={{0,4},{4,0},{8,12},{12,8},{1,5},{5,1},{9,13},{13,9},{2,6},{6,2},{1... | collective-permute-start | bytes 860168 | tf_op jit(solution)/shard_map/ppermute | solution.py:517
  18.7 1.6 %collective-permute-start = (f32[1,3,15]{2,1,0:T(4,128)S(1)}, f32[1,3,15]{2,1,0:T(4,128)S(1)}, u32[]{:S(2)}, u32[]{:S(2)}) collective-permute-start(f32[1,3,15]{2,1,0:T(4,128)S(1)} %copy.12.taps), channel_id=1, source_target_pairs={{0,2},{1,3},{2,0},{3,1},{4,6},{5,7},{6,4},{7,5},{8,10},{9,11},{10,... | collective-permute-start | bytes 548 | tf_op jit(solution)/shard_map/ppermute | solution.py:509
  20.3 1.5 %collective-permute-start.6 = (f32[10,16,640]{2,1,0:T(8,128)S(1)}, f32[10,16,640]{2,1,0:T(8,128)S(1)}, u32[]{:S(2)}, u32[]{:S(2)}) collective-permute-start(f32[10,16,640]{2,1,0:T(8,128)S(1)} %get-tuple-element.41), channel_id=1, source_target_pairs={{0,2},{1,3},{2,0},{3,1},{4,6},{5,7},{6,4},{7,5},{8,10},{9,11},{10,... | collective-permute-start | bytes 1228808 | tf_op jit(solution)/shard_map/ppermute | solution.py:509
  22.4 4.4 %collective-permute-start.4 = (f32[7,16,640]{2,1,0:T(8,128)S(1)}, f32[7,16,640]{2,1,0:T(8,128)S(1)}, u32[]{:S(2)}, u32[]{:S(2)}) collective-permute-start(f32[7,16,640]{2,1,0:T(8,128)S(1)} %get-tuple-element.66), channel_id=1, source_target_pairs={{0,4},{4,0},{8,12},{12,8},{1,5},{5,1},{9,13},{13,9},{2,6},{6,2},{1... | collective-permute-start | bytes 860168 | tf_op jit(solution)/shard_map/ppermute | solution.py:517
  28.5 1.7 %own_share.5.before = f32[608,640]{1,0:T(8,128)S(1)} custom-call(f32[24,16,640]{2,1,0:T(8,128)S(1)} %get-tuple-element.35.est.refs_4_, bf16[2,5,256,256]{3,2,1,0:T(8,128)(2,1)S(1)} %get-tuple-element.42.t.refs_4_, bf16[2,2,256,512]{3,2,1,0:T(8,128)(2,1)S(1)} %get-tuple-element.43.w.refs_5_, bf16[2,2,256,256]{3,2,1,0:T(8,128)(2,1)S(1)} %get-tuple-element.44.wr), custom_call_target="tpu_custom_call" | custom-call | tf_op jit(solution)/shard_map/own_share/pallas_call | solution.py:316
  31.4 1.7 %own_share.4.before = f32[608,640]{1,0:T(8,128)S(1)} custom-call(f32[24,16,640]{2,1,0:T(8,128)S(1)} %get-tuple-element.35.est.refs_4_, bf16[2,5,256,256]{3,2,1,0:T(8,128)(2,1)S(1)} %get-tuple-element.36.t.refs_5_, bf16[2,2,256,512]{3,2,1,0:T(8,128)(2,1)S(1)} %get-tuple-element.37.w.refs_6_, bf16[2,2,256,256]{3,2,1,0:T(8,128)(2,1)S(1)} %get-tuple-element.38.wr), custom_call_target="tpu_custom_call" | custom-call | tf_op jit(solution)/shard_map/own_share/pallas_call | solution.py:316
  35.9 1.5 %adjoint.8 = (f32[12,16,640]{2,1,0:T(8,128)S(1)}, bf16[224,640]{1,0:T(8,128)(2,1)S(1)}, bf16[224,640]{1,0:T(8,128)(2,1)S(1)}) custom-call(f32[608,640]{1,0:T(8,128)S(1)} %rim_share.11.refs_0_, f32[112,640]{1,0:T(8,128)S(1)} %bitcast.28, f32[112,640]{1,0:T(8,128)S(1)} %bitcast.32, f32[384,640]{1,0:T(8,128)S(1)} %bitcast.8, ...), custom_call_target="tpu_custom_call" | custom-call | tf_op jit(solution)/shard_map/adjoint/pallas_call | solution.py:445
  39.5 1.7 %adjoint.9 = (f32[12,16,640]{2,1,0:T(8,128)S(1)}, bf16[224,640]{1,0:T(8,128)(2,1)S(1)}, bf16[224,640]{1,0:T(8,128)(2,1)S(1)}) custom-call(f32[608,640]{1,0:T(8,128)S(1)} %rim_share.9.refs_0_, f32[112,640]{1,0:T(8,128)S(1)} %bitcast.20, f32[112,640]{1,0:T(8,128)S(1)} %bitcast.24, f32[224,640]{1,0:T(8,128)S(1)} %bitcast.12, f32[160,640]{1,0:T(8,128)S(1)} %bitcast.16, ...), custom_call_target="tpu_custom_call" | custom-call | tf_op jit(solution)/shard_map/adjoint/pallas_call | solution.py:445
  42.8 1.4 %collective-permute-done.10.refs_3_ = f32[12,16,640]{2,1,0:T(8,128)S(1)} collective-permute-done((f32[12,16,640]{2,1,0:T(8,128)S(1)}, f32[12,16,640]{2,1,0:T(8,128)S(1)}, u32[]{:S(2)}, u32[]{:S(2)}) %collective-permute-start.10) | collective-permute-done | bytes 491552 | tf_op jit(solution)/shard_map/ppermute | solution.py:505
  45.4 3.1 %collective-permute-start.11 = (f32[14,16,640]{2,1,0:T(8,128)S(1)}, f32[14,16,640]{2,1,0:T(8,128)S(1)}, u32[]{:S(2)}, u32[]{:S(2)}) collective-permute-start(f32[14,16,640]{2,1,0:T(8,128)S(1)} %get-tuple-element.55), channel_id=1, source_target_pairs={{0,4},{4,0},{8,12},{12,8},{5,9},{9,5},{2,6},{6,2},{10,14},{14,10},... | collective-permute-start | bytes 1720328 | tf_op jit(solution)/shard_map/ppermute | solution.py:525
  48.6 8.5 %collective-permute-done.11.rim = f32[14,16,640]{2,1,0:T(8,128)S(1)} collective-permute-done((f32[14,16,640]{2,1,0:T(8,128)S(1)}, f32[14,16,640]{2,1,0:T(8,128)S(1)}, u32[]{:S(2)}, u32[]{:S(2)}) %collective-permute-start.11) | collective-permute-done | bytes 573472 | tf_op jit(solution)/shard_map/ppermute | solution.py:525
  57.0 1.7 %own_share.7.before = f32[608,640]{1,0:T(8,128)S(1)} custom-call(f32[24,16,640]{2,1,0:T(8,128)S(1)} %get-tuple-element.54.est, bf16[2,5,256,256]{3,2,1,0:T(8,128)(2,1)S(1)} %get-tuple-element.42.t.refs_4_, bf16[2,2,256,512]{3,2,1,0:T(8,128)(2,1)S(1)} %get-tuple-element.43.w.refs_5_, bf16[2,2,256,256]{3,2,1,0:T(8,128)(2,1)S(1)} %get-tuple-element.44.wr), custom_call_target="tpu_custom_call" | custom-call | tf_op jit(solution)/shard_map/own_share/pallas_call | solution.py:316
  58.7 1.7 %own_share.6.before = f32[608,640]{1,0:T(8,128)S(1)} custom-call(f32[24,16,640]{2,1,0:T(8,128)S(1)} %get-tuple-element.54.est, bf16[2,5,256,256]{3,2,1,0:T(8,128)(2,1)S(1)} %get-tuple-element.36.t.refs_5_, bf16[2,2,256,512]{3,2,1,0:T(8,128)(2,1)S(1)} %get-tuple-element.37.w.refs_6_, bf16[2,2,256,256]{3,2,1,0:T(8,128)(2,1)S(1)} %get-tuple-element.38.wr), custom_call_target="tpu_custom_call" | custom-call | tf_op jit(solution)/shard_map/own_share/pallas_call | solution.py:316
  63.3 1.5 %adjoint.12 = (f32[12,16,640]{2,1,0:T(8,128)S(1)}, bf16[224,640]{1,0:T(8,128)(2,1)S(1)}, bf16[224,640]{1,0:T(8,128)(2,1)S(1)}) custom-call(f32[608,640]{1,0:T(8,128)S(1)} %rim_share.15.refs_0_, f32[112,640]{1,0:T(8,128)S(1)} %bitcast.30, f32[112,640]{1,0:T(8,128)S(1)} %bitcast.34, f32[384,640]{1,0:T(8,128)S(1)} %bitcast.10, ...), custom_call_target="tpu_custom_call" | custom-call | tf_op jit(solution)/shard_map/adjoint/pallas_call | solution.py:445
  66.8 1.7 %adjoint.13 = (f32[12,8,512]{2,1,0:T(8,128)S(1)}, f32[12,8,512]{2,1,0:T(8,128)S(1)}, bf16[224,640]{1,0:T(8,128)(2,1)S(1)}, bf16[224,640]{1,0:T(8,128)(2,1)S(1)}) custom-call(f32[608,640]{1,0:T(8,128)S(1)} %rim_share.13.refs_0_, f32[112,640]{1,0:T(8,128)S(1)} %bitcast.22, f32[112,640]{1,0:T(8,128)S(1)} %bitcast.26, f32[224,640]{1,0:T(8,128)S(1)} %bitcast.14, ...), custom_call_target="tpu_custom_call" | custom-call | tf_op jit(solution)/shard_map/adjoint/pallas_call | solution.py:445
  71.3 1.6 %collective-permute-start.19 = (f32[12,8,512]{2,1,0:T(8,128)S(1)}, f32[12,8,512]{2,1,0:T(8,128)S(1)}, u32[]{:S(2)}, u32[]{:S(2)}) collective-permute-start(f32[12,8,512]{2,1,0:T(8,128)S(1)} %finish.3.refs_4_), channel_id=1, source_target_pairs={{0,2},{1,3},{2,0},{3,1},{4,6},{5,7},{6,4},{7,5},{8,10},{9,11},{10,... | collective-permute-start | bytes 589832 | tf_op jit(solution)/shard_map/ppermute | solution.py:509
  74.0 5.1 %collective-permute-done.19.refs_6_ = f32[12,8,512]{2,1,0:T(8,128)S(1)} collective-permute-done((f32[12,8,512]{2,1,0:T(8,128)S(1)}, f32[12,8,512]{2,1,0:T(8,128)S(1)}, u32[]{:S(2)}, u32[]{:S(2)}) %collective-permute-start.19) | collective-permute-done | bytes 196640 | tf_op jit(solution)/shard_map/ppermute | solution.py:509
  79.1 3.6 %collective-permute-done.15.refs_2_ = f32[12,8,512]{2,1,0:T(8,128)S(1)} collective-permute-done((f32[12,8,512]{2,1,0:T(8,128)S(1)}, f32[12,8,512]{2,1,0:T(8,128)S(1)}, u32[]{:S(2)}, u32[]{:S(2)}) %collective-permute-start.15) | collective-permute-done | bytes 196640 | tf_op jit(solution)/shard_map/ppermute | solution.py:509
  82.8 1.4 %collective-permute-done.16.refs_3_ = f32[12,8,512]{2,1,0:T(8,128)S(1)} collective-permute-done((f32[12,8,512]{2,1,0:T(8,128)S(1)}, f32[12,8,512]{2,1,0:T(8,128)S(1)}, u32[]{:S(2)}, u32[]{:S(2)}) %collective-permute-start.16) | collective-permute-done | bytes 196640 | tf_op jit(solution)/shard_map/ppermute | solution.py:505
  (53 shorter events, 22.4 us)
Async XLA Ops:
  0.0 1.4 %copy-start = (f32[1,24,16,1024]{3,2,1,0:T(8,128)S(1)}, f32[1,24,16,1024]{3,2,1,0:T(8,128)}, u32[]{:S(2)}) copy-start(f32[1,24,16,1024]{3,2,1,0:T(8,128)} %param.3) | copy-start | bytes 4718596
  1.4 1.4 %copy-start.1 = (f32[24,16,1024]{2,1,0:T(8,128)S(1)}, f32[24,16,1024]{2,1,0:T(8,128)}, u32[]{:S(2)}) copy-start(f32[24,16,1024]{2,1,0:T(8,128)} %refs_1_.1) | copy-start | bytes 4718596
  2.8 15.9 %copy-start.2 = (f32[1,3,15]{2,0,1:T(1,128)S(1)}, f32[1,3,15]{2,0,1:T(1,128)}, u32[]{:S(2)}) copy-start(f32[1,3,15]{2,0,1:T(1,128)} %param.4) | copy-start | bytes 544
  3.3 12.6 %collective-permute-start.1 = (f32[14,16,640]{2,1,0:T(8,128)S(1)}, f32[14,16,640]{2,1,0:T(8,128)S(1)}, u32[]{:S(2)}, u32[]{:S(2)}) collective-permute-start(f32[14,16,640]{2,1,0:T(8,128)S(1)} %get-tuple-element.39), channel_id=1, source_target_pairs={{0,4},{4,0},{8,12},{12,8},{5,9},{9,5},{2,6},{6,2},{10,14},{14,10},... | collective-permute-start | bytes 1720328 | tf_op jit(solution)/shard_map/ppermute | solution.py:525
  8.3 11.9 %collective-permute-start.3 = (f32[14,16,640]{2,1,0:T(8,128)S(1)}, f32[14,16,640]{2,1,0:T(8,128)S(1)}, u32[]{:S(2)}, u32[]{:S(2)}) collective-permute-start(f32[14,16,640]{2,1,0:T(8,128)S(1)} %get-tuple-element.40), channel_id=1, source_target_pairs={{0,2},{1,3},{2,0},{3,1},{4,6},{5,7},{6,4},{7,5},{8,10},{9,11},{10,... | collective-permute-start | bytes 1720328 | tf_op jit(solution)/shard_map/ppermute | solution.py:509
  16.0 10.7 %collective-permute-start.2 = (f32[14,16,640]{2,1,0:T(8,128)S(1)}, f32[14,16,640]{2,1,0:T(8,128)S(1)}, u32[]{:S(2)}, u32[]{:S(2)}) collective-permute-start(f32[14,16,640]{2,1,0:T(8,128)S(1)} %collective-permute-done.1.rim), channel_id=1, source_target_pairs={{0,1},{1,0},{2,3},{3,2},{4,5},{5,4},{6,7},{7,6},{8,9},{9,8},{10,11... | collective-permute-start | bytes 1720328 | tf_op jit(solution)/shard_map/ppermute | solution.py:505
  16.0 19.9 %collective-permute-start.7 = (f32[7,16,640]{2,1,0:T(8,128)S(1)}, f32[7,16,640]{2,1,0:T(8,128)S(1)}, u32[]{:S(2)}, u32[]{:S(2)}) collective-permute-start(f32[7,16,640]{2,1,0:T(8,128)S(1)} %get-tuple-element.45), channel_id=1, source_target_pairs={{0,4},{4,0},{8,12},{12,8},{1,5},{5,1},{9,13},{13,9},{2,6},{6,2},{1... | collective-permute-start | bytes 860168 | tf_op jit(solution)/shard_map/ppermute | solution.py:517
  18.0 17.9 %collective-permute-start.8 = (f32[7,16,640]{2,1,0:T(8,128)S(1)}, f32[7,16,640]{2,1,0:T(8,128)S(1)}, u32[]{:S(2)}, u32[]{:S(2)}) collective-permute-start(f32[7,16,640]{2,1,0:T(8,128)S(1)} %get-tuple-element.46), channel_id=1, source_target_pairs={{4,8},{8,4},{5,9},{9,5},{6,10},{10,6},{7,11},{11,7},{20,24},{24,20... | collective-permute-start | bytes 860168 | tf_op jit(solution)/shard_map/ppermute | solution.py:516
  18.7 3.7 %collective-permute-start = (f32[1,3,15]{2,1,0:T(4,128)S(1)}, f32[1,3,15]{2,1,0:T(4,128)S(1)}, u32[]{:S(2)}, u32[]{:S(2)}) collective-permute-start(f32[1,3,15]{2,1,0:T(4,128)S(1)} %copy.12.taps), channel_id=1, source_target_pairs={{0,2},{1,3},{2,0},{3,1},{4,6},{5,7},{6,4},{7,5},{8,10},{9,11},{10,... | collective-permute-start | bytes 548 | tf_op jit(solution)/shard_map/ppermute | solution.py:509
  20.3 19.2 %collective-permute-start.6 = (f32[10,16,640]{2,1,0:T(8,128)S(1)}, f32[10,16,640]{2,1,0:T(8,128)S(1)}, u32[]{:S(2)}, u32[]{:S(2)}) collective-permute-start(f32[10,16,640]{2,1,0:T(8,128)S(1)} %get-tuple-element.41), channel_id=1, source_target_pairs={{0,2},{1,3},{2,0},{3,1},{4,6},{5,7},{6,4},{7,5},{8,10},{9,11},{10,... | collective-permute-start | bytes 1228808 | tf_op jit(solution)/shard_map/ppermute | solution.py:509
  22.4 17.1 %collective-permute-start.4 = (f32[7,16,640]{2,1,0:T(8,128)S(1)}, f32[7,16,640]{2,1,0:T(8,128)S(1)}, u32[]{:S(2)}, u32[]{:S(2)}) collective-permute-start(f32[7,16,640]{2,1,0:T(8,128)S(1)} %get-tuple-element.66), channel_id=1, source_target_pairs={{0,4},{4,0},{8,12},{12,8},{1,5},{5,1},{9,13},{13,9},{2,6},{6,2},{1... | collective-permute-start | bytes 860168 | tf_op jit(solution)/shard_map/ppermute | solution.py:517
  26.7 12.7 %collective-permute-start.5 = (f32[7,16,640]{2,1,0:T(8,128)S(1)}, f32[7,16,640]{2,1,0:T(8,128)S(1)}, u32[]{:S(2)}, u32[]{:S(2)}) collective-permute-start(f32[7,16,640]{2,1,0:T(8,128)S(1)} %get-tuple-element.65), channel_id=1, source_target_pairs={{4,8},{8,4},{5,9},{9,5},{6,10},{10,6},{7,11},{11,7},{20,24},{24,20... | collective-permute-start | bytes 860168 | tf_op jit(solution)/shard_map/ppermute | solution.py:516
  42.3 1.9 %collective-permute-start.10 = (f32[12,16,640]{2,1,0:T(8,128)S(1)}, f32[12,16,640]{2,1,0:T(8,128)S(1)}, u32[]{:S(2)}, u32[]{:S(2)}) collective-permute-start(f32[12,16,640]{2,1,0:T(8,128)S(1)} %adjoint.11.refs_2_), channel_id=1, source_target_pairs={{0,1},{1,0},{2,3},{3,2},{4,5},{5,4},{6,7},{7,6},{8,9},{9,8},{10,11... | collective-permute-start | bytes 1474568 | tf_op jit(solution)/shard_map/ppermute | solution.py:505
  42.3 2.6 %collective-permute-start.9 = (f32[12,16,640]{2,1,0:T(8,128)S(1)}, f32[12,16,640]{2,1,0:T(8,128)S(1)}, u32[]{:S(2)}, u32[]{:S(2)}) collective-permute-start(f32[12,16,640]{2,1,0:T(8,128)S(1)} %get-tuple-element.49.refs_0_), channel_id=1, source_target_pairs={{0,1},{1,0},{2,3},{3,2},{4,5},{5,4},{6,7},{7,6},{8,9},{9,8},{10,11... | collective-permute-start | bytes 1474568 | tf_op jit(solution)/shard_map/ppermute | solution.py:505
  45.4 11.6 %collective-permute-start.11 = (f32[14,16,640]{2,1,0:T(8,128)S(1)}, f32[14,16,640]{2,1,0:T(8,128)S(1)}, u32[]{:S(2)}, u32[]{:S(2)}) collective-permute-start(f32[14,16,640]{2,1,0:T(8,128)S(1)} %get-tuple-element.55), channel_id=1, source_target_pairs={{0,4},{4,0},{8,12},{12,8},{5,9},{9,5},{2,6},{6,2},{10,14},{14,10},... | collective-permute-start | bytes 1720328 | tf_op jit(solution)/shard_map/ppermute | solution.py:525
  57.0 5.3 %collective-permute-start.12 = (f32[14,16,640]{2,1,0:T(8,128)S(1)}, f32[14,16,640]{2,1,0:T(8,128)S(1)}, u32[]{:S(2)}, u32[]{:S(2)}) collective-permute-start(f32[14,16,640]{2,1,0:T(8,128)S(1)} %collective-permute-done.11.rim), channel_id=1, source_target_pairs={{0,1},{1,0},{2,3},{3,2},{4,5},{5,4},{6,7},{7,6},{8,9},{9,8},{10,11... | collective-permute-start | bytes 1720328 | tf_op jit(solution)/shard_map/ppermute | solution.py:505
  69.6 1.6 %collective-permute-start.17 = (f32[12,8,512]{2,1,0:T(8,128)S(1)}, f32[12,8,512]{2,1,0:T(8,128)S(1)}, u32[]{:S(2)}, u32[]{:S(2)}) collective-permute-start(f32[12,8,512]{2,1,0:T(8,128)S(1)} %get-tuple-element.64), channel_id=1, source_target_pairs={{0,1},{1,0},{2,3},{3,2},{4,5},{5,4},{6,7},{7,6},{8,9},{9,8},{10,11... | collective-permute-start | bytes 589832 | tf_op jit(solution)/shard_map/ppermute | solution.py:505
  70.2 2.7 %collective-permute-start.13 = (f32[12,8,512]{2,1,0:T(8,128)S(1)}, f32[12,8,512]{2,1,0:T(8,128)S(1)}, u32[]{:S(2)}, u32[]{:S(2)}) collective-permute-start(f32[12,8,512]{2,1,0:T(8,128)S(1)} %get-tuple-element.58), channel_id=1, source_target_pairs={{0,1},{1,0},{2,3},{3,2},{4,5},{5,4},{6,7},{7,6},{8,9},{9,8},{10,11... | collective-permute-start | bytes 589832 | tf_op jit(solution)/shard_map/ppermute | solution.py:505
  71.3 7.8 %collective-permute-start.19 = (f32[12,8,512]{2,1,0:T(8,128)S(1)}, f32[12,8,512]{2,1,0:T(8,128)S(1)}, u32[]{:S(2)}, u32[]{:S(2)}) collective-permute-start(f32[12,8,512]{2,1,0:T(8,128)S(1)} %finish.3.refs_4_), channel_id=1, source_target_pairs={{0,2},{1,3},{2,0},{3,1},{4,6},{5,7},{6,4},{7,5},{8,10},{9,11},{10,... | collective-permute-start | bytes 589832 | tf_op jit(solution)/shard_map/ppermute | solution.py:509
  72.9 9.9 %collective-permute-start.15 = (f32[12,8,512]{2,1,0:T(8,128)S(1)}, f32[12,8,512]{2,1,0:T(8,128)S(1)}, u32[]{:S(2)}, u32[]{:S(2)}) collective-permute-start(f32[12,8,512]{2,1,0:T(8,128)S(1)} %finish.2.refs_0_), channel_id=1, source_target_pairs={{0,2},{1,3},{2,0},{3,1},{4,6},{5,7},{6,4},{7,5},{8,10},{9,11},{10,... | collective-permute-start | bytes 589832 | tf_op jit(solution)/shard_map/ppermute | solution.py:509
  73.5 9.3 %collective-permute-start.18 = (f32[12,8,512]{2,1,0:T(8,128)S(1)}, f32[12,8,512]{2,1,0:T(8,128)S(1)}, u32[]{:S(2)}, u32[]{:S(2)}) collective-permute-start(f32[12,8,512]{2,1,0:T(8,128)S(1)} %finish.3.refs_4_), channel_id=1, source_target_pairs={{0,1},{1,0},{2,3},{3,2},{4,5},{5,4},{6,7},{7,6},{8,9},{9,8},{10,11... | collective-permute-start | bytes 589832 | tf_op jit(solution)/shard_map/ppermute | solution.py:505
  73.5 9.3 %collective-permute-start.14 = (f32[12,8,512]{2,1,0:T(8,128)S(1)}, f32[12,8,512]{2,1,0:T(8,128)S(1)}, u32[]{:S(2)}, u32[]{:S(2)}) collective-permute-start(f32[12,8,512]{2,1,0:T(8,128)S(1)} %finish.2.refs_0_), channel_id=1, source_target_pairs={{0,1},{1,0},{2,3},{3,2},{4,5},{5,4},{6,7},{7,6},{8,9},{9,8},{10,11... | collective-permute-start | bytes 589832 | tf_op jit(solution)/shard_map/ppermute | solution.py:505
  79.1 3.6 %collective-permute-start.20 = (f32[12,8,512]{2,1,0:T(8,128)S(1)}, f32[12,8,512]{2,1,0:T(8,128)S(1)}, u32[]{:S(2)}, u32[]{:S(2)}) collective-permute-start(f32[12,8,512]{2,1,0:T(8,128)S(1)} %collective-permute-done.19.refs_6_), channel_id=1, source_target_pairs={{0,1},{1,0},{2,3},{3,2},{4,5},{5,4},{6,7},{7,6},{8,9},{9,8},{10,11... | collective-permute-start | bytes 589832 | tf_op jit(solution)/shard_map/ppermute | solution.py:505
  82.8 1.4 %collective-permute-start.16 = (f32[12,8,512]{2,1,0:T(8,128)S(1)}, f32[12,8,512]{2,1,0:T(8,128)S(1)}, u32[]{:S(2)}, u32[]{:S(2)}) collective-permute-start(f32[12,8,512]{2,1,0:T(8,128)S(1)} %collective-permute-done.15.refs_2_), channel_id=1, source_target_pairs={{0,1},{1,0},{2,3},{3,2},{4,5},{5,4},{6,7},{7,6},{8,9},{9,8},{10,11... | collective-permute-start | bytes 589832 | tf_op jit(solution)/shard_map/ppermute | solution.py:505

commit v6 on v5

--- a/solution.py
+++ b/solution.py
@@ -99,7 +99,7 @@
         scratch_shapes=[pltpu.SemaphoreType.DMA((len(moves),))],
         compiler_params=PARAMS,
         name="cut",
-    )(*sources)
+    )(*[pltpu.with_memory_space_constraint(a, pltpu.HBM) for a in sources])
 
 
 def update_kernel(split, views, planes, *refs):
@@ -142,10 +142,13 @@
     )(mine, sibling, est)
 
 
-def operators_kernel(nz, taps, t, w, wr, th, tl):
+GROUP = 8
+
+
+def operators_kernel(nz, taps, t, last, w, wr, full):
     planes = ROWS // nz
-    band = LANES + 3 * 8
-    first = LANES - 8
+    band = LANES + 3 * GROUP
+    first = LANES - GROUP
     i = lax.broadcasted_iota(jnp.int32, (band, LANES), 0) + first
     o = lax.broadcasted_iota(jnp.int32, (band, LANES), 1)
     shift_y = i - o - (LANES - RADIUS)
@@ -159,9 +162,7 @@
         for k in range(1, TAPS):
             value = value + taps[0, d, k]
         sums.append(value)
-    th[...] = jnp.zeros_like(th)
-    tl[...] = jnp.zeros_like(tl)
-    half = LANES // 2
+    full[...] = jnp.zeros_like(full)
     for mirrored in range(2):
         ty = jnp.zeros((band, LANES), F32)
         kx = jnp.zeros((nz, 2 * ROWS), F32)
@@ -174,23 +175,33 @@
         kx = kx / sums[0]
         kz = kz / sums[1]
         ty = ty / sums[2]
-        high, low = halves(ty)
         for c0 in range(0, ROWS, LANES):
-            rows = slice(first + c0, first + c0 + band)
-            th[rows, c0 : c0 + LANES] = high
-            tl[rows, c0 : c0 + LANES] = low
-        inside = slice(LANES, LANES + ROWS)
-        right, left = slice(LANES + ROWS, LANES + ROWS + half), slice(half, LANES)
-        t[mirrored, 0] = th[inside, :]
-        t[mirrored, 1] = tl[inside, :]
-        for at in (0, LANES):
-            t[mirrored, 2, at : at + half] = th[right, :]
-            t[mirrored, 2, at + half : at + LANES] = th[left, :]
-        t[mirrored, 3, :half] = tl[right, :]
-        t[mirrored, 3, half:LANES] = tl[left, :]
-        t[mirrored, 3, LANES:] = jnp.zeros((ROWS - LANES, ROWS), BF)
-        t[mirrored, 4, :, :LANES] = th[:ROWS, :LANES]
-        t[mirrored, 4, :, LANES:] = tl[:ROWS, :LANES]
+            full[first + c0 : first + c0 + band, c0 : c0 + LANES] = ty
+        high, low = halves(full[LANES : LANES + ROWS, :])
+        t[mirrored, :ROWS] = high
+        t[mirrored, ROWS : 2 * ROWS] = high
+        t[mirrored, 2 * ROWS : 3 * ROWS] = low
+        right = full[LANES + ROWS : LANES + ROWS + GROUP, :]
+        left = full[LANES - GROUP : LANES, :]
+        right_high, left_high = right.astype(BF).astype(F32), left.astype(BF).astype(F32)
+        none = jnp.zeros((2 * GROUP, ROWS), F32)
+        corners = [
+            right_high,
+            none,
+            left_high,
+            right_high,
+            none,
+            left - left_high,
+            right - right_high,
+            none,
+            none,
+            none,
+            left_high,
+        ]
+        t[mirrored, 3 * ROWS :] = jnp.concatenate(corners, 0).astype(BF)
+        high, low = halves(full[:ROWS, :LANES])
+        last[mirrored, :, :LANES] = high
+        last[mirrored, :, LANES:] = low
         strip = kx * kz
         for p in range(planes):
             moved = pltpu.roll(strip, p * nz, 1) if p else strip
@@ -203,44 +214,53 @@
                 wr[1, 0, rows, :], wr[1, 1, rows, :] = halves(moved)
 
 
+class Operators(NamedTuple):
+    t: jax.Array
+    last: jax.Array
+    w: jax.Array
+    wr: jax.Array
+
+
 def operators(taps, nz):
-    return pl.pallas_call(
+    out = pl.pallas_call(
         functools.partial(operators_kernel, nz),
         out_shape=(
-            jax.ShapeDtypeStruct((2, 5, ROWS, ROWS), BF),
+            jax.ShapeDtypeStruct((2, 3 * ROWS + LANES, ROWS), BF),
+            jax.ShapeDtypeStruct((2, ROWS, ROWS), BF),
             jax.ShapeDtypeStruct((2, 2, ROWS, 2 * ROWS), BF),
             jax.ShapeDtypeStruct((2, 2, ROWS, ROWS), BF),
         ),
         in_specs=[SMEM],
-        out_specs=(VMEM,) * 3,
-        scratch_shapes=[pltpu.VMEM((2 * ROWS, ROWS), BF)] * 2,
+        out_specs=(VMEM,) * 4,
+        scratch_shapes=[pltpu.VMEM((2 * ROWS, ROWS), F32)],
         compiler_params=PARAMS,
         name="operators",
     )(taps)
-
-
-def blur_y(x, t, store):
+    return Operators(*out)
+
+
+def blur_y(x, t, last, store):
     n, width = x.shape
     xh, xl = halves(x)
-    right = lax.broadcasted_iota(jnp.int32, (n, LANES), 1) < LANES // 2
+    lane = lax.broadcasted_iota(jnp.int32, (n, LANES), 1)
     for o0 in range(0, width, ROWS):
         size = min(ROWS, width - o0)
         if size == ROWS:
             end = o0 + ROWS
             at = slice(o0, end)
-            out = dot(xh[:, at], t[0]) + (dot(xl[:, at], t[0]) + dot(xh[:, at], t[1]))
-            none = jnp.zeros((n, LANES), F32)
-            corner = jnp.where(
-                right,
-                x[:, end : end + LANES] if end < width else none,
-                x[:, o0 - LANES : o0] if o0 else none,
-            )
-            ch, cl = halves(corner)
-            out = out + (dot(jnp.concatenate([ch, cl], 1), t[2]) + dot(ch, t[3, :LANES]))
+            corner = jnp.zeros((n, LANES), F32)
+            if end < width:
+                corner = jnp.where(lane < GROUP, x[:, end : end + LANES], corner)
+            if o0:
+                corner = jnp.where(lane >= LANES - GROUP, x[:, o0 - LANES : o0], corner)
+            high = corner.astype(BF).astype(F32)
+            low = pltpu.roll(corner - high, LANES // 4, 1)
+            corner = (high + low + pltpu.roll(high, LANES // 2, 1)).astype(BF)
+            out = dot(jnp.concatenate([xh[:, at], xl[:, at], xh[:, at], corner], 1), t[...])
         else:
             at = slice(o0 - LANES, o0 + LANES)
-            both = dot(xh[:, at], t[4])
-            out = both[:, :LANES] + (both[:, LANES:] + dot(xl[:, at], t[4, :, :LANES]))
+            both = dot(xh[:, at], last[...])
+            out = both[:, :LANES] + (both[:, LANES:] + dot(xl[:, at], last[:, :LANES]))
         store(o0, size, out)
 
 
@@ -281,20 +301,20 @@
     return [(r, min(step, rows - r)) for r in range(0, rows, step)]
 
 
-def own_kernel(est, t, w, wr, blurred, dh, dl):
+def own_kernel(est, t, last, w, wr, blurred, dh, dl):
     planes, nz, width = est.shape
     step = LANES // nz
     for p in range(0, planes, step):
         n = min(step, planes - p)
         x = est[p : p + n].reshape(n * nz, width)
-        blur_y(x, t.at[0], to_halves(dh, dl, slice(p * nz, (p + n) * nz)))
+        blur_y(x, t.at[0], last.at[0], to_halves(dh, dl, slice(p * nz, (p + n) * nz)))
     total = planes + 2 * RADIUS
     step = ROWS // nz
     for p0 in range(0, total, step):
         out = min(step, total - p0)
         first = max(0, p0 - 2 * RADIUS)
-        last = min(planes, p0 + out)
-        k = (last - first) * nz
+        stop = min(planes, p0 + out)
+        k = (stop - first) * nz
         m = out * nz
         if p0 < 2 * RADIUS:
             assert p0 == 0
@@ -306,31 +326,31 @@
         def store(o0, size, value):
             blurred[p0 * nz : p0 * nz + m, o0 : o0 + size] = value
 
-        product(block, dh, dl, slice(first * nz, last * nz), store)
+        product(block, dh, dl, slice(first * nz, stop * nz), store)
 
 
 def own_share(est, ops):
     planes, nz, width = est.shape
-    t, w, wr = ops
     half = pltpu.VMEM((planes * nz, width), BF)
     return pl.pallas_call(
         own_kernel,
         out_shape=jax.ShapeDtypeStruct(((planes + 2 * RADIUS) * nz, width), F32),
-        in_specs=[VMEM] * 4,
+        in_specs=[VMEM] * 5,
         out_specs=VMEM,
         scratch_shapes=[half, half],
         compiler_params=PARAMS,
         name="own_share",
-    )(est, t, w, wr)
-
-
-def rim_kernel(split, mine, before, rim, t, wr, blurred, dh, dl):
+    )(est, *ops)
+
+
+def rim_kernel(split, mine, before, rim, t, last, wr, blurred, dh, dl):
     planes, nz, width = rim.shape
     n = planes * nz
     side = split.side(mine)
     flat = rim[...].reshape(n, width)
     for r0, count in chunks(n, 112):
-        blur_y(flat[r0 : r0 + count, :], t.at[0], to_halves(dh, dl, slice(r0, r0 + count)))
+        rows = slice(r0, r0 + count)
+        blur_y(flat[rows, :], t.at[0], last.at[0], to_halves(dh, dl, rows))
     rows = pl.ds(pl.multiple_of(side * (blurred.shape[0] - n), nz), n)
 
     def store(o0, size, value):
@@ -345,13 +365,13 @@
     return pl.pallas_call(
         functools.partial(rim_kernel, split, mine),
         out_shape=jax.ShapeDtypeStruct(before.shape, F32),
-        in_specs=[VMEM] * 4,
+        in_specs=[VMEM] * 5,
         out_specs=VMEM,
         scratch_shapes=[half, half],
         input_output_aliases={0: 0},
         compiler_params=PARAMS,
         name="rim_share",
-    )(before, rim, ops[0], ops[2])
+    )(before, rim, ops.t, ops.last, ops.wr)
 
 
 class Piece(NamedTuple):
@@ -384,7 +404,7 @@
 def adjoint_kernel(nz, split, pieces, inputs, span, has_added, ends, *refs):
     refs = list(refs)
     take = lambda n: [refs.pop(0) for _ in range(n)]
-    (blurred,), record, (t, w) = take(1), take(inputs), take(2)
+    (blurred,), record, (t, last, w) = take(1), take(inputs), take(3)
     (added,) = take(1) if has_added else (None,)
     handed = take(2) if span.handed else None
     keep, send = take(2) if ends is not None else (None, None)
@@ -404,7 +424,8 @@
         for r0, n in chunks(max(0, hi - lo)):
             at = lo + r0
             q = piece.load(record, odd, at - piece.at, n) / blurred[at : at + n, :]
-            blur_y(q, t.at[1], to_halves(dh, dl, slice(at - base, at - base + n)))
+            rows = slice(at - base, at - base + n)
+            blur_y(q, t.at[1], last.at[1], to_halves(dh, dl, rows))
     if hands_on is not None:
         hands_on[0][...] = dh[(p1 - p0) * nz :, :]
         hands_on[1][...] = dl[(p1 - p0) * nz :, :]
@@ -428,7 +449,7 @@
 def adjoint(split, blurred, record, pieces, ops, span, added, handed, nz, ends=None):
     width = blurred.shape[1]
     planes = span.planes[1] - span.planes[0]
-    args = [blurred, *record, *ops[:2]] + ([] if added is None else [added])
+    args = [blurred, *record, *ops[:3]] + ([] if added is None else [added])
     args += [] if handed is None else list(handed)
     rows = (planes + 2 * RADIUS) * nz
     full = (planes, nz, width)
@@ -466,15 +487,19 @@
 
 
 def join_kernel(split, planes, *refs):
-    parts, out = refs[:-1], refs[-1]
+    parts, out, sem = refs[:-2], refs[-2], refs[-1]
     chip, core = split.here()
-    for c, (p0, p1) in enumerate(planes):
+    copies = []
+    for p0, p1 in planes:
         for r in range(split.chips):
             owner = lax.rem(chip + split.chips - r, split.chips)
             lanes = pl.ds(pl.multiple_of(owner * split.part, LANES), split.part)
-            mine, sibling = parts[2 * (c * split.chips + r) : 2 * (c * split.chips + r) + 2]
-            out[p0:p1, split.rows(core), lanes] = mine[...]
-            out[p0:p1, split.rows(1 - core), lanes] = sibling[...]
+            for whose in (core, 1 - core):
+                to = out.at[p0:p1, split.rows(whose), lanes]
+                copies.append(pltpu.make_async_copy(parts[len(copies)], to, sem.at[len(copies)]))
+                copies[-1].start()
+    for copy in copies:
+        copy.wait()
 
 
 def join(split, planes, parts, nx, nz):
@@ -482,7 +507,8 @@
         functools.partial(join_kernel, split, planes),
         out_shape=jax.ShapeDtypeStruct((nx, nz, split.ny), F32),
         in_specs=[VMEM] * len(parts),
-        out_specs=VMEM,
+        out_specs=ANY,
+        scratch_shapes=[pltpu.SemaphoreType.DMA((len(parts),))],
         compiler_params=PARAMS,
         name="join",
     )(*parts)

time: 85.7 us -> 82.6 us (0.964)
  local copies, waits for them, and re-layouts: 2.86 us -> 0.04 us
    unnamed x7 -> x3, local copies, waits for them, and re-layouts: 2.82 us -> 0.01 us
    pallas_call x1, Pallas kernels: 0.52 us -> 2.26 us  [cut(): pl.pallas_call(functools.partial(cut_kernel, split, len(sources), tuple(m...]
    pallas_call x8, Pallas kernels: 10.7 us -> 9.75 us  [adjoint(): pl.pallas_call(kernel, out_shape=tuple(shapes), in_specs=[VMEM] * len(arg...]
where the time goes in v6:
time: 82.6 us; the launch traced here: 82.4 us
  Pallas kernels  29.1 us (35%)
  waiting for transfers between devices  28.1 us (34%)
  starting transfers between devices  24.6 us (30%)
    ppermute x2, waiting for transfers between devices, estimate_rims(): mine = lax.ppermute(values, ('tile', 'view'), both)  14.4 us
    pallas_call x8, Pallas kernels, adjoint(): pl.pallas_call(kernel, out_shape=tuple(shapes), in_specs=[VMEM] * len(arg...  9.75 us
    ppermute x5, waiting for transfers between devices, to_chip(): return lax.ppermute(values, 'view', pairs)  9.24 us
    ppermute x2, starting transfers between devices, estimate_rims(): mine = lax.ppermute(values, ('tile', 'view'), both)  8.31 us
    pallas_call x8, Pallas kernels, rim_share(): pl.pallas_call(functools.partial(rim_kernel, split, mine), out_shape=jax....  6.96 us
    ppermute x5, starting transfers between devices, to_chip(): return lax.ppermute(values, 'view', pairs)  6.83 us
    ppermute x2, starting transfers between devices, pair_up(): a = lax.ppermute(a, 'tile', next_a)  6.4 us
    pallas_call x4, Pallas kernels, own_share(): pl.pallas_call(own_kernel, out_shape=jax.ShapeDtypeStruct(((planes + 2 *...  6.37 us
  transfers between devices with their start and end apart: 21, of which 9 were waited for; matrix products, arithmetic and copies ran while one was open for 0% of the time, Pallas kernels for 20%

profile of v6, /device:TPU:0, one launch (start us, length us, event | category | flops | bytes accessed | tf_op | source)
XLA Modules:
  0.0 82.4 jit_solution(1061208029035128892)
XLA Ops:
  0.0 2.3 %cut.1 = (f32[14,16,640]{2,1,0:T(8,128)S(1)}, f32[10,16,640]{2,1,0:T(8,128)S(1)}, f32[24,16,640]{2,1,0:T(8,128)S(1)}, f32[7,16,640]{2,1,0:T(8,128)S(1)}, f32[7,1...) custom-call(f32[24,16,1024]{2,1,0:T(8,128)} %bitcast.36, f32[24,16,1024]{2,1,0:T(8,128)} %refs_1_.1), custom_call_target="tpu_custom_call" | custom-call | tf_op jit(solution)/shard_map/cut/pallas_call | solution.py:94
  2.3 5.0 %collective-permute-start.1 = (f32[14,16,640]{2,1,0:T(8,128)S(1)}, f32[14,16,640]{2,1,0:T(8,128)S(1)}, u32[]{:S(2)}, u32[]{:S(2)}) collective-permute-start(f32[14,16,640]{2,1,0:T(8,128)S(1)} %get-tuple-element.42), channel_id=1, source_target_pairs={{0,4},{4,0},{8,12},{12,8},{5,9},{9,5},{2,6},{6,2},{10,14},{14,10},... | collective-permute-start | bytes 1720328 | tf_op jit(solution)/shard_map/ppermute | solution.py:551
  7.3 1.6 %collective-permute-start.3 = (f32[14,16,640]{2,1,0:T(8,128)S(1)}, f32[14,16,640]{2,1,0:T(8,128)S(1)}, u32[]{:S(2)}, u32[]{:S(2)}) collective-permute-start(f32[14,16,640]{2,1,0:T(8,128)S(1)} %get-tuple-element.43), channel_id=1, source_target_pairs={{0,2},{1,3},{2,0},{3,1},{4,6},{5,7},{6,4},{7,5},{8,10},{9,11},{10,... | collective-permute-start | bytes 1720328 | tf_op jit(solution)/shard_map/ppermute | solution.py:535
  8.9 6.1 %collective-permute-done.1.rim = f32[14,16,640]{2,1,0:T(8,128)S(1)} collective-permute-done((f32[14,16,640]{2,1,0:T(8,128)S(1)}, f32[14,16,640]{2,1,0:T(8,128)S(1)}, u32[]{:S(2)}, u32[]{:S(2)}) %collective-permute-start.1) | collective-permute-done | bytes 573472 | tf_op jit(solution)/shard_map/ppermute | solution.py:551
  15.0 2.0 %collective-permute-start.7 = (f32[7,16,640]{2,1,0:T(8,128)S(1)}, f32[7,16,640]{2,1,0:T(8,128)S(1)}, u32[]{:S(2)}, u32[]{:S(2)}) collective-permute-start(f32[7,16,640]{2,1,0:T(8,128)S(1)} %get-tuple-element.49), channel_id=1, source_target_pairs={{0,4},{4,0},{8,12},{12,8},{1,5},{5,1},{9,13},{13,9},{2,6},{6,2},{1... | collective-permute-start | bytes 860168 | tf_op jit(solution)/shard_map/ppermute | solution.py:543
  17.7 1.6 %collective-permute-start = (f32[1,3,15]{2,1,0:T(4,128)S(1)}, f32[1,3,15]{2,1,0:T(4,128)S(1)}, u32[]{:S(2)}, u32[]{:S(2)}) collective-permute-start(f32[1,3,15]{2,1,0:T(4,128)S(1)} %copy.12.taps), channel_id=1, source_target_pairs={{0,2},{1,3},{2,0},{3,1},{4,6},{5,7},{6,4},{7,5},{8,10},{9,11},{10,... | collective-permute-start | bytes 548 | tf_op jit(solution)/shard_map/ppermute | solution.py:535
  19.3 1.5 %collective-permute-start.6 = (f32[10,16,640]{2,1,0:T(8,128)S(1)}, f32[10,16,640]{2,1,0:T(8,128)S(1)}, u32[]{:S(2)}, u32[]{:S(2)}) collective-permute-start(f32[10,16,640]{2,1,0:T(8,128)S(1)} %get-tuple-element.44), channel_id=1, source_target_pairs={{0,2},{1,3},{2,0},{3,1},{4,6},{5,7},{6,4},{7,5},{8,10},{9,11},{10,... | collective-permute-start | bytes 1228808 | tf_op jit(solution)/shard_map/ppermute | solution.py:535
  21.3 4.4 %collective-permute-start.4 = (f32[7,16,640]{2,1,0:T(8,128)S(1)}, f32[7,16,640]{2,1,0:T(8,128)S(1)}, u32[]{:S(2)}, u32[]{:S(2)}) collective-permute-start(f32[7,16,640]{2,1,0:T(8,128)S(1)} %get-tuple-element.70), channel_id=1, source_target_pairs={{0,4},{4,0},{8,12},{12,8},{1,5},{5,1},{9,13},{13,9},{2,6},{6,2},{1... | collective-permute-start | bytes 860168 | tf_op jit(solution)/shard_map/ppermute | solution.py:543
  27.5 1.6 %own_share.5.before = f32[608,640]{1,0:T(8,128)S(1)} custom-call(f32[24,16,640]{2,1,0:T(8,128)S(1)} %get-tuple-element.37.est.refs_4_, bf16[2,896,256]{2,1,0:T(8,128)(2,1)S(1)} %get-tuple-element.45.t.refs_4_, bf16[2,256,256]{2,1,0:T(8,128)(2,1)S(1)} %get-tuple-element.46.last.refs_5_, bf16[2,2,256,512]{3,2,1,0:T(8,128)(2,1)S(1)} %get-tuple-element.47.w.refs_6_, ...), custom_call_target="tpu_custom_call" | custom-call | tf_op jit(solution)/shard_map/own_share/pallas_call | solution.py:335
  30.2 1.6 %own_share.4.before = f32[608,640]{1,0:T(8,128)S(1)} custom-call(f32[24,16,640]{2,1,0:T(8,128)S(1)} %get-tuple-element.37.est.refs_4_, bf16[2,896,256]{2,1,0:T(8,128)(2,1)S(1)} %get-tuple-element.38.t.refs_5_, bf16[2,256,256]{2,1,0:T(8,128)(2,1)S(1)} %get-tuple-element.39.last.refs_6_, bf16[2,2,256,512]{3,2,1,0:T(8,128)(2,1)S(1)} %get-tuple-element.40.w.refs_7_, ...), custom_call_target="tpu_custom_call" | custom-call | tf_op jit(solution)/shard_map/own_share/pallas_call | solution.py:335
  34.4 1.3 %adjoint.8 = (f32[12,16,640]{2,1,0:T(8,128)S(1)}, bf16[224,640]{1,0:T(8,128)(2,1)S(1)}, bf16[224,640]{1,0:T(8,128)(2,1)S(1)}) custom-call(f32[608,640]{1,0:T(8,128)S(1)} %rim_share.11.refs_0_, f32[112,640]{1,0:T(8,128)S(1)} %bitcast.28, f32[112,640]{1,0:T(8,128)S(1)} %bitcast.32, f32[384,640]{1,0:T(8,128)S(1)} %bitcast.8, ...), custom_call_target="tpu_custom_call" | custom-call | tf_op jit(solution)/shard_map/adjoint/pallas_call | solution.py:466
  37.6 1.5 %adjoint.9 = (f32[12,16,640]{2,1,0:T(8,128)S(1)}, bf16[224,640]{1,0:T(8,128)(2,1)S(1)}, bf16[224,640]{1,0:T(8,128)(2,1)S(1)}) custom-call(f32[608,640]{1,0:T(8,128)S(1)} %rim_share.9.refs_0_, f32[112,640]{1,0:T(8,128)S(1)} %bitcast.20, f32[112,640]{1,0:T(8,128)S(1)} %bitcast.24, f32[224,640]{1,0:T(8,128)S(1)} %bitcast.12, f32[160,640]{1,0:T(8,128)S(1)} %bitcast.16, ...), custom_call_target="tpu_custom_call" | custom-call | tf_op jit(solution)/shard_map/adjoint/pallas_call | solution.py:466
  40.8 1.4 %collective-permute-done.10.refs_3_ = f32[12,16,640]{2,1,0:T(8,128)S(1)} collective-permute-done((f32[12,16,640]{2,1,0:T(8,128)S(1)}, f32[12,16,640]{2,1,0:T(8,128)S(1)}, u32[]{:S(2)}, u32[]{:S(2)}) %collective-permute-start.10) | collective-permute-done | bytes 491552 | tf_op jit(solution)/shard_map/ppermute | solution.py:531
  43.2 3.3 %collective-permute-start.11 = (f32[14,16,640]{2,1,0:T(8,128)S(1)}, f32[14,16,640]{2,1,0:T(8,128)S(1)}, u32[]{:S(2)}, u32[]{:S(2)}) collective-permute-start(f32[14,16,640]{2,1,0:T(8,128)S(1)} %get-tuple-element.59), channel_id=1, source_target_pairs={{0,4},{4,0},{8,12},{12,8},{5,9},{9,5},{2,6},{6,2},{10,14},{14,10},... | collective-permute-start | bytes 1720328 | tf_op jit(solution)/shard_map/ppermute | solution.py:551
  46.5 8.3 %collective-permute-done.11.rim = f32[14,16,640]{2,1,0:T(8,128)S(1)} collective-permute-done((f32[14,16,640]{2,1,0:T(8,128)S(1)}, f32[14,16,640]{2,1,0:T(8,128)S(1)}, u32[]{:S(2)}, u32[]{:S(2)}) %collective-permute-start.11) | collective-permute-done | bytes 573472 | tf_op jit(solution)/shard_map/ppermute | solution.py:551
  54.8 1.6 %own_share.7.before = f32[608,640]{1,0:T(8,128)S(1)} custom-call(f32[24,16,640]{2,1,0:T(8,128)S(1)} %get-tuple-element.58.est, bf16[2,896,256]{2,1,0:T(8,128)(2,1)S(1)} %get-tuple-element.45.t.refs_4_, bf16[2,256,256]{2,1,0:T(8,128)(2,1)S(1)} %get-tuple-element.46.last.refs_5_, bf16[2,2,256,512]{3,2,1,0:T(8,128)(2,1)S(1)} %get-tuple-element.47.w.refs_6_, ...), custom_call_target="tpu_custom_call" | custom-call | tf_op jit(solution)/shard_map/own_share/pallas_call | solution.py:335
  56.4 1.6 %own_share.6.before = f32[608,640]{1,0:T(8,128)S(1)} custom-call(f32[24,16,640]{2,1,0:T(8,128)S(1)} %get-tuple-element.58.est, bf16[2,896,256]{2,1,0:T(8,128)(2,1)S(1)} %get-tuple-element.38.t.refs_5_, bf16[2,256,256]{2,1,0:T(8,128)(2,1)S(1)} %get-tuple-element.39.last.refs_6_, bf16[2,2,256,512]{3,2,1,0:T(8,128)(2,1)S(1)} %get-tuple-element.40.w.refs_7_, ...), custom_call_target="tpu_custom_call" | custom-call | tf_op jit(solution)/shard_map/own_share/pallas_call | solution.py:335
  60.6 1.3 %adjoint.12 = (f32[12,16,640]{2,1,0:T(8,128)S(1)}, bf16[224,640]{1,0:T(8,128)(2,1)S(1)}, bf16[224,640]{1,0:T(8,128)(2,1)S(1)}) custom-call(f32[608,640]{1,0:T(8,128)S(1)} %rim_share.15.refs_0_, f32[112,640]{1,0:T(8,128)S(1)} %bitcast.30, f32[112,640]{1,0:T(8,128)S(1)} %bitcast.34, f32[384,640]{1,0:T(8,128)S(1)} %bitcast.10, ...), custom_call_target="tpu_custom_call" | custom-call | tf_op jit(solution)/shard_map/adjoint/pallas_call | solution.py:466
  63.8 1.6 %adjoint.13 = (f32[12,8,512]{2,1,0:T(8,128)S(1)}, f32[12,8,512]{2,1,0:T(8,128)S(1)}, bf16[224,640]{1,0:T(8,128)(2,1)S(1)}, bf16[224,640]{1,0:T(8,128)(2,1)S(1)}) custom-call(f32[608,640]{1,0:T(8,128)S(1)} %rim_share.13.refs_0_, f32[112,640]{1,0:T(8,128)S(1)} %bitcast.22, f32[112,640]{1,0:T(8,128)S(1)} %bitcast.26, f32[224,640]{1,0:T(8,128)S(1)} %bitcast.14, ...), custom_call_target="tpu_custom_call" | custom-call | tf_op jit(solution)/shard_map/adjoint/pallas_call | solution.py:466
  68.1 1.6 %collective-permute-start.19 = (f32[12,8,512]{2,1,0:T(8,128)S(1)}, f32[12,8,512]{2,1,0:T(8,128)S(1)}, u32[]{:S(2)}, u32[]{:S(2)}) collective-permute-start(f32[12,8,512]{2,1,0:T(8,128)S(1)} %finish.3.refs_4_), channel_id=1, source_target_pairs={{0,2},{1,3},{2,0},{3,1},{4,6},{5,7},{6,4},{7,5},{8,10},{9,11},{10,... | collective-permute-start | bytes 589832 | tf_op jit(solution)/shard_map/ppermute | solution.py:535
  70.8 5.1 %collective-permute-done.19.refs_6_ = f32[12,8,512]{2,1,0:T(8,128)S(1)} collective-permute-done((f32[12,8,512]{2,1,0:T(8,128)S(1)}, f32[12,8,512]{2,1,0:T(8,128)S(1)}, u32[]{:S(2)}, u32[]{:S(2)}) %collective-permute-start.19) | collective-permute-done | bytes 196640 | tf_op jit(solution)/shard_map/ppermute | solution.py:535
  75.9 3.6 %collective-permute-done.15.refs_2_ = f32[12,8,512]{2,1,0:T(8,128)S(1)} collective-permute-done((f32[12,8,512]{2,1,0:T(8,128)S(1)}, f32[12,8,512]{2,1,0:T(8,128)S(1)}, u32[]{:S(2)}, u32[]{:S(2)}) %collective-permute-start.15) | collective-permute-done | bytes 196640 | tf_op jit(solution)/shard_map/ppermute | solution.py:535
  79.6 1.4 %collective-permute-done.16.refs_3_ = f32[12,8,512]{2,1,0:T(8,128)S(1)} collective-permute-done((f32[12,8,512]{2,1,0:T(8,128)S(1)}, f32[12,8,512]{2,1,0:T(8,128)S(1)}, u32[]{:S(2)}, u32[]{:S(2)}) %collective-permute-start.16) | collective-permute-done | bytes 196640 | tf_op jit(solution)/shard_map/ppermute | solution.py:531
  81.0 1.2 %join.1 = f32[24,16,1024]{2,1,0:T(8,128)} custom-call(f32[12,8,512]{2,1,0:T(8,128)S(1)} %finish.2.refs_0_, f32[12,8,512]{2,1,0:T(8,128)S(1)} %collective-permute-done.14.refs_1_, f32[12,8,512]{2,1,0:T(8,128)S(1)} %collective-permute-done.15.refs_2_, f32[12,8,512]{2,1,0:T(8,128)S(1)} %collective-permute-done.16.refs_3_, f32[12,8,512]{2,1,0:T(8,128)S(1)} %finish.3.refs_4_, ...), custom_call_target="tpu_custom_call" | custom-call | tf_op jit(solution)/shard_map/join/pallas_call | solution.py:506
  (49 shorter events, 19.4 us)
Async XLA Ops:
  0.0 17.7 %copy-start = (f32[1,3,15]{2,0,1:T(1,128)S(1)}, f32[1,3,15]{2,0,1:T(1,128)}, u32[]{:S(2)}) copy-start(f32[1,3,15]{2,0,1:T(1,128)} %param.4) | copy-start | bytes 544
  2.3 12.7 %collective-permute-start.1 = (f32[14,16,640]{2,1,0:T(8,128)S(1)}, f32[14,16,640]{2,1,0:T(8,128)S(1)}, u32[]{:S(2)}, u32[]{:S(2)}) collective-permute-start(f32[14,16,640]{2,1,0:T(8,128)S(1)} %get-tuple-element.42), channel_id=1, source_target_pairs={{0,4},{4,0},{8,12},{12,8},{5,9},{9,5},{2,6},{6,2},{10,14},{14,10},... | collective-permute-start | bytes 1720328 | tf_op jit(solution)/shard_map/ppermute | solution.py:551
  7.3 12.0 %collective-permute-start.3 = (f32[14,16,640]{2,1,0:T(8,128)S(1)}, f32[14,16,640]{2,1,0:T(8,128)S(1)}, u32[]{:S(2)}, u32[]{:S(2)}) collective-permute-start(f32[14,16,640]{2,1,0:T(8,128)S(1)} %get-tuple-element.43), channel_id=1, source_target_pairs={{0,2},{1,3},{2,0},{3,1},{4,6},{5,7},{6,4},{7,5},{8,10},{9,11},{10,... | collective-permute-start | bytes 1720328 | tf_op jit(solution)/shard_map/ppermute | solution.py:535
  15.0 10.7 %collective-permute-start.2 = (f32[14,16,640]{2,1,0:T(8,128)S(1)}, f32[14,16,640]{2,1,0:T(8,128)S(1)}, u32[]{:S(2)}, u32[]{:S(2)}) collective-permute-start(f32[14,16,640]{2,1,0:T(8,128)S(1)} %collective-permute-done.1.rim), channel_id=1, source_target_pairs={{0,1},{1,0},{2,3},{3,2},{4,5},{5,4},{6,7},{7,6},{8,9},{9,8},{10,11... | collective-permute-start | bytes 1720328 | tf_op jit(solution)/shard_map/ppermute | solution.py:531
  15.0 19.4 %collective-permute-start.7 = (f32[7,16,640]{2,1,0:T(8,128)S(1)}, f32[7,16,640]{2,1,0:T(8,128)S(1)}, u32[]{:S(2)}, u32[]{:S(2)}) collective-permute-start(f32[7,16,640]{2,1,0:T(8,128)S(1)} %get-tuple-element.49), channel_id=1, source_target_pairs={{0,4},{4,0},{8,12},{12,8},{1,5},{5,1},{9,13},{13,9},{2,6},{6,2},{1... | collective-permute-start | bytes 860168 | tf_op jit(solution)/shard_map/ppermute | solution.py:543
  17.0 17.4 %collective-permute-start.8 = (f32[7,16,640]{2,1,0:T(8,128)S(1)}, f32[7,16,640]{2,1,0:T(8,128)S(1)}, u32[]{:S(2)}, u32[]{:S(2)}) collective-permute-start(f32[7,16,640]{2,1,0:T(8,128)S(1)} %get-tuple-element.50), channel_id=1, source_target_pairs={{4,8},{8,4},{5,9},{9,5},{6,10},{10,6},{7,11},{11,7},{20,24},{24,20... | collective-permute-start | bytes 860168 | tf_op jit(solution)/shard_map/ppermute | solution.py:542
  17.7 3.7 %collective-permute-start = (f32[1,3,15]{2,1,0:T(4,128)S(1)}, f32[1,3,15]{2,1,0:T(4,128)S(1)}, u32[]{:S(2)}, u32[]{:S(2)}) collective-permute-start(f32[1,3,15]{2,1,0:T(4,128)S(1)} %copy.12.taps), channel_id=1, source_target_pairs={{0,2},{1,3},{2,0},{3,1},{4,6},{5,7},{6,4},{7,5},{8,10},{9,11},{10,... | collective-permute-start | bytes 548 | tf_op jit(solution)/shard_map/ppermute | solution.py:535
  19.3 18.4 %collective-permute-start.6 = (f32[10,16,640]{2,1,0:T(8,128)S(1)}, f32[10,16,640]{2,1,0:T(8,128)S(1)}, u32[]{:S(2)}, u32[]{:S(2)}) collective-permute-start(f32[10,16,640]{2,1,0:T(8,128)S(1)} %get-tuple-element.44), channel_id=1, source_target_pairs={{0,2},{1,3},{2,0},{3,1},{4,6},{5,7},{6,4},{7,5},{8,10},{9,11},{10,... | collective-permute-start | bytes 1228808 | tf_op jit(solution)/shard_map/ppermute | solution.py:535
  21.3 16.3 %collective-permute-start.4 = (f32[7,16,640]{2,1,0:T(8,128)S(1)}, f32[7,16,640]{2,1,0:T(8,128)S(1)}, u32[]{:S(2)}, u32[]{:S(2)}) collective-permute-start(f32[7,16,640]{2,1,0:T(8,128)S(1)} %get-tuple-element.70), channel_id=1, source_target_pairs={{0,4},{4,0},{8,12},{12,8},{1,5},{5,1},{9,13},{13,9},{2,6},{6,2},{1... | collective-permute-start | bytes 860168 | tf_op jit(solution)/shard_map/ppermute | solution.py:543
  25.7 11.9 %collective-permute-start.5 = (f32[7,16,640]{2,1,0:T(8,128)S(1)}, f32[7,16,640]{2,1,0:T(8,128)S(1)}, u32[]{:S(2)}, u32[]{:S(2)}) collective-permute-start(f32[7,16,640]{2,1,0:T(8,128)S(1)} %get-tuple-element.69), channel_id=1, source_target_pairs={{4,8},{8,4},{5,9},{9,5},{6,10},{10,6},{7,11},{11,7},{20,24},{24,20... | collective-permute-start | bytes 860168 | tf_op jit(solution)/shard_map/ppermute | solution.py:542
  40.2 1.9 %collective-permute-start.10 = (f32[12,16,640]{2,1,0:T(8,128)S(1)}, f32[12,16,640]{2,1,0:T(8,128)S(1)}, u32[]{:S(2)}, u32[]{:S(2)}) collective-permute-start(f32[12,16,640]{2,1,0:T(8,128)S(1)} %adjoint.11.refs_2_), channel_id=1, source_target_pairs={{0,1},{1,0},{2,3},{3,2},{4,5},{5,4},{6,7},{7,6},{8,9},{9,8},{10,11... | collective-permute-start | bytes 1474568 | tf_op jit(solution)/shard_map/ppermute | solution.py:531
  40.3 2.6 %collective-permute-start.9 = (f32[12,16,640]{2,1,0:T(8,128)S(1)}, f32[12,16,640]{2,1,0:T(8,128)S(1)}, u32[]{:S(2)}, u32[]{:S(2)}) collective-permute-start(f32[12,16,640]{2,1,0:T(8,128)S(1)} %get-tuple-element.53.refs_0_), channel_id=1, source_target_pairs={{0,1},{1,0},{2,3},{3,2},{4,5},{5,4},{6,7},{7,6},{8,9},{9,8},{10,11... | collective-permute-start | bytes 1474568 | tf_op jit(solution)/shard_map/ppermute | solution.py:531
  43.2 11.6 %collective-permute-start.11 = (f32[14,16,640]{2,1,0:T(8,128)S(1)}, f32[14,16,640]{2,1,0:T(8,128)S(1)}, u32[]{:S(2)}, u32[]{:S(2)}) collective-permute-start(f32[14,16,640]{2,1,0:T(8,128)S(1)} %get-tuple-element.59), channel_id=1, source_target_pairs={{0,4},{4,0},{8,12},{12,8},{5,9},{9,5},{2,6},{6,2},{10,14},{14,10},... | collective-permute-start | bytes 1720328 | tf_op jit(solution)/shard_map/ppermute | solution.py:551
  54.8 5.0 %collective-permute-start.12 = (f32[14,16,640]{2,1,0:T(8,128)S(1)}, f32[14,16,640]{2,1,0:T(8,128)S(1)}, u32[]{:S(2)}, u32[]{:S(2)}) collective-permute-start(f32[14,16,640]{2,1,0:T(8,128)S(1)} %collective-permute-done.11.rim), channel_id=1, source_target_pairs={{0,1},{1,0},{2,3},{3,2},{4,5},{5,4},{6,7},{7,6},{8,9},{9,8},{10,11... | collective-permute-start | bytes 1720328 | tf_op jit(solution)/shard_map/ppermute | solution.py:531
  66.4 1.7 %collective-permute-start.17 = (f32[12,8,512]{2,1,0:T(8,128)S(1)}, f32[12,8,512]{2,1,0:T(8,128)S(1)}, u32[]{:S(2)}, u32[]{:S(2)}) collective-permute-start(f32[12,8,512]{2,1,0:T(8,128)S(1)} %get-tuple-element.68), channel_id=1, source_target_pairs={{0,1},{1,0},{2,3},{3,2},{4,5},{5,4},{6,7},{7,6},{8,9},{9,8},{10,11... | collective-permute-start | bytes 589832 | tf_op jit(solution)/shard_map/ppermute | solution.py:531
  67.0 2.7 %collective-permute-start.13 = (f32[12,8,512]{2,1,0:T(8,128)S(1)}, f32[12,8,512]{2,1,0:T(8,128)S(1)}, u32[]{:S(2)}, u32[]{:S(2)}) collective-permute-start(f32[12,8,512]{2,1,0:T(8,128)S(1)} %get-tuple-element.62), channel_id=1, source_target_pairs={{0,1},{1,0},{2,3},{3,2},{4,5},{5,4},{6,7},{7,6},{8,9},{9,8},{10,11... | collective-permute-start | bytes 589832 | tf_op jit(solution)/shard_map/ppermute | solution.py:531
  68.1 7.8 %collective-permute-start.19 = (f32[12,8,512]{2,1,0:T(8,128)S(1)}, f32[12,8,512]{2,1,0:T(8,128)S(1)}, u32[]{:S(2)}, u32[]{:S(2)}) collective-permute-start(f32[12,8,512]{2,1,0:T(8,128)S(1)} %finish.3.refs_4_), channel_id=1, source_target_pairs={{0,2},{1,3},{2,0},{3,1},{4,6},{5,7},{6,4},{7,5},{8,10},{9,11},{10,... | collective-permute-start | bytes 589832 | tf_op jit(solution)/shard_map/ppermute | solution.py:535
  69.7 9.8 %collective-permute-start.15 = (f32[12,8,512]{2,1,0:T(8,128)S(1)}, f32[12,8,512]{2,1,0:T(8,128)S(1)}, u32[]{:S(2)}, u32[]{:S(2)}) collective-permute-start(f32[12,8,512]{2,1,0:T(8,128)S(1)} %finish.2.refs_0_), channel_id=1, source_target_pairs={{0,2},{1,3},{2,0},{3,1},{4,6},{5,7},{6,4},{7,5},{8,10},{9,11},{10,... | collective-permute-start | bytes 589832 | tf_op jit(solution)/shard_map/ppermute | solution.py:535
  70.3 9.3 %collective-permute-start.18 = (f32[12,8,512]{2,1,0:T(8,128)S(1)}, f32[12,8,512]{2,1,0:T(8,128)S(1)}, u32[]{:S(2)}, u32[]{:S(2)}) collective-permute-start(f32[12,8,512]{2,1,0:T(8,128)S(1)} %finish.3.refs_4_), channel_id=1, source_target_pairs={{0,1},{1,0},{2,3},{3,2},{4,5},{5,4},{6,7},{7,6},{8,9},{9,8},{10,11... | collective-permute-start | bytes 589832 | tf_op jit(solution)/shard_map/ppermute | solution.py:531
  70.3 9.3 %collective-permute-start.14 = (f32[12,8,512]{2,1,0:T(8,128)S(1)}, f32[12,8,512]{2,1,0:T(8,128)S(1)}, u32[]{:S(2)}, u32[]{:S(2)}) collective-permute-start(f32[12,8,512]{2,1,0:T(8,128)S(1)} %finish.2.refs_0_), channel_id=1, source_target_pairs={{0,1},{1,0},{2,3},{3,2},{4,5},{5,4},{6,7},{7,6},{8,9},{9,8},{10,11... | collective-permute-start | bytes 589832 | tf_op jit(solution)/shard_map/ppermute | solution.py:531
  75.9 3.6 %collective-permute-start.20 = (f32[12,8,512]{2,1,0:T(8,128)S(1)}, f32[12,8,512]{2,1,0:T(8,128)S(1)}, u32[]{:S(2)}, u32[]{:S(2)}) collective-permute-start(f32[12,8,512]{2,1,0:T(8,128)S(1)} %collective-permute-done.19.refs_6_), channel_id=1, source_target_pairs={{0,1},{1,0},{2,3},{3,2},{4,5},{5,4},{6,7},{7,6},{8,9},{9,8},{10,11... | collective-permute-start | bytes 589832 | tf_op jit(solution)/shard_map/ppermute | solution.py:531
  79.6 1.4 %collective-permute-start.16 = (f32[12,8,512]{2,1,0:T(8,128)S(1)}, f32[12,8,512]{2,1,0:T(8,128)S(1)}, u32[]{:S(2)}, u32[]{:S(2)}) collective-permute-start(f32[12,8,512]{2,1,0:T(8,128)S(1)} %collective-permute-done.15.refs_2_), channel_id=1, source_target_pairs={{0,1},{1,0},{2,3},{3,2},{4,5},{5,4},{6,7},{7,6},{8,9},{9,8},{10,11... | collective-permute-start | bytes 589832 | tf_op jit(solution)/shard_map/ppermute | solution.py:531

commit v7 on v6

--- a/solution.py
+++ b/solution.py
@@ -38,6 +38,7 @@
     width: int
     ny: int
     half: int
+    tiles: int
 
     def start(self, chip):
         place = jnp.clip(chip * self.part - LANES, 0, self.ny - self.width)
@@ -58,6 +59,10 @@
         _, core = self.here()
         own = 1 - lax.rem(self.odd() + core, 2)
         return own if mine else 1 - own
+
+    def inside(self, side):
+        tile = lax.axis_index("tile")
+        return jnp.where(side == 0, tile > 0, tile < self.tiles - 1).astype(F32)
 
     def rows(self, core):
         return pl.ds(pl.multiple_of(core * self.half, self.half), self.half)
@@ -347,7 +352,7 @@
     planes, nz, width = rim.shape
     n = planes * nz
     side = split.side(mine)
-    flat = rim[...].reshape(n, width)
+    flat = rim[...].reshape(n, width) * split.inside(side)
     for r0, count in chunks(n, 112):
         rows = slice(r0, r0 + count)
         blur_y(flat[rows, :], t.at[0], last.at[0], to_halves(dh, dl, rows))
@@ -381,6 +386,7 @@
     odd_start: int
     even: int
     even_start: int
+    outside: int | None = None
 
     def load(self, refs, odd, r0, n):
         if self.odd != self.even:
@@ -423,7 +429,10 @@
         lo, hi = max(q0, piece.at), min(q1, piece.at + piece.rows)
         for r0, n in chunks(max(0, hi - lo)):
             at = lo + r0
-            q = piece.load(record, odd, at - piece.at, n) / blurred[at : at + n, :]
+            q = piece.load(record, odd, at - piece.at, n)
+            if piece.outside is not None:
+                q = q * split.inside(piece.outside)
+            q = q / blurred[at : at + n, :]
             rows = slice(at - base, at - base + n)
             blur_y(q, t.at[1], last.at[1], to_halves(dh, dl, rows))
     if hands_on is not None:
@@ -522,7 +531,7 @@
     chips = views // cores
     part = ny // chips
     width = min(ny, part + (LANES if chips <= 2 else 2 * LANES))
-    split = Split(chips, cores, part, width, ny, nz // cores)
+    split = Split(chips, cores, part, width, ny, nz // cores, tiles)
     assert 2 * RADIUS * ITERS <= LANES and nx >= 2 * RADIUS
     flat = lambda a: a.reshape(-1, a.shape[-1])
 
@@ -534,21 +543,31 @@
         pairs = [(v, (v + r * cores) % views) for v in range(views)]
         return lax.ppermute(values, "view", pairs)
 
-    next_a = [(t, t ^ 1) for t in range(tiles) if t ^ 1 < tiles]
-    next_b = [(t, ((t + 1) ^ 1) - 1) for t in range(1, tiles)]
-    next_b = [(t, u) for t, u in next_b if u < tiles]
+    slabs = lax.axis_size("slab")
+    axes = ("slab", "tile", "view")
+
+    def partner(s, t, pair_b):
+        u = ((t + 1) ^ 1) - 1 if pair_b else t ^ 1
+        return (s, u) if 0 <= u < tiles else (s ^ 1, t)
+
+    def pairs_of(is_b):
+        pairs = []
+        for s in range(slabs):
+            for t in range(tiles):
+                for v in range(views):
+                    to, u = partner(s, t, is_b(v))
+                    if to < slabs:
+                        here = (s * tiles + t) * views + v
+                        pairs.append((here, (to * tiles + u) * views + v))
+        return pairs
 
     def pair_up(a, b):
-        b = lax.ppermute(b, "tile", next_b)
-        a = lax.ppermute(a, "tile", next_a)
+        b = lax.ppermute(b, axes, pairs_of(lambda v: True))
+        a = lax.ppermute(a, axes, pairs_of(lambda v: False))
         return a, b
 
-    both = []
-    for v in range(views):
-        both += [(t * views + v, u * views + v) for t, u in (next_b if v % cores else next_a)]
-
     def estimate_rims(values):
-        mine = lax.ppermute(values, ("tile", "view"), both)
+        mine = lax.ppermute(values, axes, pairs_of(lambda v: v % cores == 1))
         return mine, swap_core(mine)
 
     recorded = recorded[0]
@@ -579,7 +598,8 @@
     own_a, own_b = pair_up(own_a, own_b)
 
     record = [tuple(flat(a) for a in (own_a, own_b, own))]
-    before, after = Piece(0, rim, 0, 0, 1, 0), Piece(rim + end, rim, 1, 0, 0, 0)
+    before = Piece(0, rim, 0, 0, 1, 0, 0)
+    after = Piece(rim + end, rim, 1, 0, 0, 0, 1)
     pieces = [(before, Piece(rim, end, 2, 0, 2, 0), after)]
     for r in range(1, chips):
         pair_a, pair_b = pair_up(edges[r][:RADIUS], edges[r][RADIUS:])

time: 82.6 us -> 79.1 us (0.958)
  starting transfers between devices: 24.6 us -> 20 us
  waiting for transfers between devices: 28.1 us -> 29.2 us
    ppermute x6, starting transfers between devices: 16 us -> 11.5 us  [the longest x2 4.78 us: estimate_rims(): mine = lax.ppermute(values, axes, pairs_of(lambda v: v % cores == 1))]
    ppermute x5, waiting for transfers between devices: 9.24 us -> 10.4 us  [to_chip(): return lax.ppermute(values, 'view', pairs)]
  transfers between devices with their start and end apart: 21 -> 21, of which waited for: 9 -> 9; matrix products, arithmetic and copies ran while one was open for 0% -> 0% of each run, Pallas kernels for 20% -> 21%
where the time goes in v7:
time: 79.1 us; the launch traced here: 78.9 us
  Pallas kernels  29.3 us (37%)
  waiting for transfers between devices  29.2 us (37%)
  starting transfers between devices  20 us (25%)
    ppermute x2, waiting for transfers between devices, estimate_rims(): mine = lax.ppermute(values, axes, pairs_of(lambda v: v % cores == 1))  14.3 us
    ppermute x5, waiting for transfers between devices, to_chip(): return lax.ppermute(values, 'view', pairs)  10.4 us
    pallas_call x8, Pallas kernels, adjoint(): pl.pallas_call(kernel, out_shape=tuple(shapes), in_specs=[VMEM] * len(arg...  9.73 us
    pallas_call x8, Pallas kernels, rim_share(): pl.pallas_call(functools.partial(rim_kernel, split, mine), out_shape=jax....  7 us
    ppermute x5, starting transfers between devices, to_chip(): return lax.ppermute(values, 'view', pairs)  6.68 us
    pallas_call x4, Pallas kernels, own_share(): pl.pallas_call(own_kernel, out_shape=jax.ShapeDtypeStruct(((planes + 2 *...  6.37 us
    ppermute x2, starting transfers between devices, estimate_rims(): mine = lax.ppermute(values, axes, pairs_of(lambda v: v % cores == 1))  4.78 us
    ppermute x10, waiting for transfers between devices, swap_core(): return lax.ppermute(values, 'view', pairs)  4.48 us
  transfers between devices with their start and end apart: 21, of which 9 were waited for; matrix products, arithmetic and copies ran while one was open for 0% of the time, Pallas kernels for 21%

profile of v7, /device:TPU:0, one launch (start us, length us, event | category | flops | bytes accessed | tf_op | source)
XLA Modules:
  0.0 78.9 jit_solution(4547860152068800009)
XLA Ops:
  0.0 2.3 %cut.1 = (f32[14,16,640]{2,1,0:T(8,128)S(1)}, f32[10,16,640]{2,1,0:T(8,128)S(1)}, f32[24,16,640]{2,1,0:T(8,128)S(1)}, f32[7,16,640]{2,1,0:T(8,128)S(1)}, f32[7,1...) custom-call(f32[24,16,1024]{2,1,0:T(8,128)} %bitcast.36, f32[24,16,1024]{2,1,0:T(8,128)} %refs_1_.1), custom_call_target="tpu_custom_call" | custom-call | tf_op jit(solution)/shard_map/cut/pallas_call | solution.py:99
  2.3 3.2 %collective-permute-start.1 = (f32[14,16,640]{2,1,0:T(8,128)S(1)}, f32[14,16,640]{2,1,0:T(8,128)S(1)}, u32[]{:S(2)}, u32[]{:S(2)}) collective-permute-start(f32[14,16,640]{2,1,0:T(8,128)S(1)} %get-tuple-element.42), channel_id=1, source_target_pairs={{0,4},{1,17},{2,6},{3,19},{4,0},{5,9},{6,2},{7,11},{8,12},{9,5},{1... | collective-permute-start | bytes 1720328 | tf_op jit(solution)/shard_map/ppermute | solution.py:570
  5.4 1.5 %collective-permute-start.3 = (f32[14,16,640]{2,1,0:T(8,128)S(1)}, f32[14,16,640]{2,1,0:T(8,128)S(1)}, u32[]{:S(2)}, u32[]{:S(2)}) collective-permute-start(f32[14,16,640]{2,1,0:T(8,128)S(1)} %get-tuple-element.43), channel_id=1, source_target_pairs={{0,2},{1,3},{2,0},{3,1},{4,6},{5,7},{6,4},{7,5},{8,10},{9,11},{10,... | collective-permute-start | bytes 1720328 | tf_op jit(solution)/shard_map/ppermute | solution.py:544
  6.9 6.2 %collective-permute-done.1.rim = f32[14,16,640]{2,1,0:T(8,128)S(1)} collective-permute-done((f32[14,16,640]{2,1,0:T(8,128)S(1)}, f32[14,16,640]{2,1,0:T(8,128)S(1)}, u32[]{:S(2)}, u32[]{:S(2)}) %collective-permute-start.1) | collective-permute-done | bytes 573472 | tf_op jit(solution)/shard_map/ppermute | solution.py:570
  13.1 2.0 %collective-permute-start.7 = (f32[7,16,640]{2,1,0:T(8,128)S(1)}, f32[7,16,640]{2,1,0:T(8,128)S(1)}, u32[]{:S(2)}, u32[]{:S(2)}) collective-permute-start(f32[7,16,640]{2,1,0:T(8,128)S(1)} %get-tuple-element.49), channel_id=1, source_target_pairs={{0,4},{1,5},{2,6},{3,7},{4,0},{5,1},{6,2},{7,3},{8,12},{9,13},{10,... | collective-permute-start | bytes 860168 | tf_op jit(solution)/shard_map/ppermute | solution.py:566
  15.2 1.5 %collective-permute-start.8 = (f32[7,16,640]{2,1,0:T(8,128)S(1)}, f32[7,16,640]{2,1,0:T(8,128)S(1)}, u32[]{:S(2)}, u32[]{:S(2)}) collective-permute-start(f32[7,16,640]{2,1,0:T(8,128)S(1)} %get-tuple-element.50), channel_id=1, source_target_pairs={{0,16},{1,17},{2,18},{3,19},{4,8},{5,9},{6,10},{7,11},{8,4},{9,5},... | collective-permute-start | bytes 860168 | tf_op jit(solution)/shard_map/ppermute | solution.py:565
  16.7 1.5 %collective-permute-start = (f32[1,3,15]{2,1,0:T(4,128)S(1)}, f32[1,3,15]{2,1,0:T(4,128)S(1)}, u32[]{:S(2)}, u32[]{:S(2)}) collective-permute-start(f32[1,3,15]{2,1,0:T(4,128)S(1)} %copy.12.taps), channel_id=1, source_target_pairs={{0,2},{1,3},{2,0},{3,1},{4,6},{5,7},{6,4},{7,5},{8,10},{9,11},{10,... | collective-permute-start | bytes 548 | tf_op jit(solution)/shard_map/ppermute | solution.py:544
  18.2 1.6 %collective-permute-done.3 = f32[14,16,640]{2,1,0:T(8,128)S(1)} collective-permute-done((f32[14,16,640]{2,1,0:T(8,128)S(1)}, f32[14,16,640]{2,1,0:T(8,128)S(1)}, u32[]{:S(2)}, u32[]{:S(2)}) %collective-permute-start.3) | collective-permute-done | bytes 573472 | tf_op jit(solution)/shard_map/ppermute | solution.py:544
  19.8 1.5 %collective-permute-start.6 = (f32[10,16,640]{2,1,0:T(8,128)S(1)}, f32[10,16,640]{2,1,0:T(8,128)S(1)}, u32[]{:S(2)}, u32[]{:S(2)}) collective-permute-start(f32[10,16,640]{2,1,0:T(8,128)S(1)} %get-tuple-element.44), channel_id=1, source_target_pairs={{0,2},{1,3},{2,0},{3,1},{4,6},{5,7},{6,4},{7,5},{8,10},{9,11},{10,... | collective-permute-start | bytes 1228808 | tf_op jit(solution)/shard_map/ppermute | solution.py:544
  21.4 1.7 %collective-permute-start.4 = (f32[7,16,640]{2,1,0:T(8,128)S(1)}, f32[7,16,640]{2,1,0:T(8,128)S(1)}, u32[]{:S(2)}, u32[]{:S(2)}) collective-permute-start(f32[7,16,640]{2,1,0:T(8,128)S(1)} %get-tuple-element.70), channel_id=1, source_target_pairs={{0,4},{1,5},{2,6},{3,7},{4,0},{5,1},{6,2},{7,3},{8,12},{9,13},{10,... | collective-permute-start | bytes 860168 | tf_op jit(solution)/shard_map/ppermute | solution.py:566
  23.1 1.5 %collective-permute-start.5 = (f32[7,16,640]{2,1,0:T(8,128)S(1)}, f32[7,16,640]{2,1,0:T(8,128)S(1)}, u32[]{:S(2)}, u32[]{:S(2)}) collective-permute-start(f32[7,16,640]{2,1,0:T(8,128)S(1)} %get-tuple-element.69), channel_id=1, source_target_pairs={{0,16},{1,17},{2,18},{3,19},{4,8},{5,9},{6,10},{7,11},{8,4},{9,5},... | collective-permute-start | bytes 860168 | tf_op jit(solution)/shard_map/ppermute | solution.py:565
  25.7 1.6 %own_share.5.before = f32[608,640]{1,0:T(8,128)S(1)} custom-call(f32[24,16,640]{2,1,0:T(8,128)S(1)} %get-tuple-element.37.est.refs_4_, bf16[2,896,256]{2,1,0:T(8,128)(2,1)S(1)} %get-tuple-element.45.t.refs_4_, bf16[2,256,256]{2,1,0:T(8,128)(2,1)S(1)} %get-tuple-element.46.last.refs_5_, bf16[2,2,256,512]{3,2,1,0:T(8,128)(2,1)S(1)} %get-tuple-element.47.w.refs_6_, ...), custom_call_target="tpu_custom_call" | custom-call | tf_op jit(solution)/shard_map/own_share/pallas_call | solution.py:340
  28.4 1.6 %own_share.4.before = f32[608,640]{1,0:T(8,128)S(1)} custom-call(f32[24,16,640]{2,1,0:T(8,128)S(1)} %get-tuple-element.37.est.refs_4_, bf16[2,896,256]{2,1,0:T(8,128)(2,1)S(1)} %get-tuple-element.38.t.refs_5_, bf16[2,256,256]{2,1,0:T(8,128)(2,1)S(1)} %get-tuple-element.39.last.refs_6_, bf16[2,2,256,512]{3,2,1,0:T(8,128)(2,1)S(1)} %get-tuple-element.40.w.refs_7_, ...), custom_call_target="tpu_custom_call" | custom-call | tf_op jit(solution)/shard_map/own_share/pallas_call | solution.py:340
  35.9 1.5 %adjoint.9 = (f32[12,16,640]{2,1,0:T(8,128)S(1)}, bf16[224,640]{1,0:T(8,128)(2,1)S(1)}, bf16[224,640]{1,0:T(8,128)(2,1)S(1)}) custom-call(f32[608,640]{1,0:T(8,128)S(1)} %rim_share.9.refs_0_, f32[112,640]{1,0:T(8,128)S(1)} %bitcast.20, f32[112,640]{1,0:T(8,128)S(1)} %bitcast.24, f32[224,640]{1,0:T(8,128)S(1)} %bitcast.12, f32[160,640]{1,0:T(8,128)S(1)} %bitcast.16, ...), custom_call_target="tpu_custom_call" | custom-call | tf_op jit(solution)/shard_map/adjoint/pallas_call | solution.py:475
  39.0 1.4 %collective-permute-done.10.refs_3_ = f32[12,16,640]{2,1,0:T(8,128)S(1)} collective-permute-done((f32[12,16,640]{2,1,0:T(8,128)S(1)}, f32[12,16,640]{2,1,0:T(8,128)S(1)}, u32[]{:S(2)}, u32[]{:S(2)}) %collective-permute-start.10) | collective-permute-done | bytes 491552 | tf_op jit(solution)/shard_map/ppermute | solution.py:540
  41.6 1.6 %collective-permute-start.11 = (f32[14,16,640]{2,1,0:T(8,128)S(1)}, f32[14,16,640]{2,1,0:T(8,128)S(1)}, u32[]{:S(2)}, u32[]{:S(2)}) collective-permute-start(f32[14,16,640]{2,1,0:T(8,128)S(1)} %get-tuple-element.59), channel_id=1, source_target_pairs={{0,4},{1,17},{2,6},{3,19},{4,0},{5,9},{6,2},{7,11},{8,12},{9,5},{1... | collective-permute-start | bytes 1720328 | tf_op jit(solution)/shard_map/ppermute | solution.py:570
  43.2 8.2 %collective-permute-done.11.rim = f32[14,16,640]{2,1,0:T(8,128)S(1)} collective-permute-done((f32[14,16,640]{2,1,0:T(8,128)S(1)}, f32[14,16,640]{2,1,0:T(8,128)S(1)}, u32[]{:S(2)}, u32[]{:S(2)}) %collective-permute-start.11) | collective-permute-done | bytes 573472 | tf_op jit(solution)/shard_map/ppermute | solution.py:570
  51.4 1.6 %own_share.7.before = f32[608,640]{1,0:T(8,128)S(1)} custom-call(f32[24,16,640]{2,1,0:T(8,128)S(1)} %get-tuple-element.58.est, bf16[2,896,256]{2,1,0:T(8,128)(2,1)S(1)} %get-tuple-element.45.t.refs_4_, bf16[2,256,256]{2,1,0:T(8,128)(2,1)S(1)} %get-tuple-element.46.last.refs_5_, bf16[2,2,256,512]{3,2,1,0:T(8,128)(2,1)S(1)} %get-tuple-element.47.w.refs_6_, ...), custom_call_target="tpu_custom_call" | custom-call | tf_op jit(solution)/shard_map/own_share/pallas_call | solution.py:340
  52.9 1.6 %own_share.6.before = f32[608,640]{1,0:T(8,128)S(1)} custom-call(f32[24,16,640]{2,1,0:T(8,128)S(1)} %get-tuple-element.58.est, bf16[2,896,256]{2,1,0:T(8,128)(2,1)S(1)} %get-tuple-element.38.t.refs_5_, bf16[2,256,256]{2,1,0:T(8,128)(2,1)S(1)} %get-tuple-element.39.last.refs_6_, bf16[2,2,256,512]{3,2,1,0:T(8,128)(2,1)S(1)} %get-tuple-element.40.w.refs_7_, ...), custom_call_target="tpu_custom_call" | custom-call | tf_op jit(solution)/shard_map/own_share/pallas_call | solution.py:340
  60.4 1.5 %adjoint.13 = (f32[12,8,512]{2,1,0:T(8,128)S(1)}, f32[12,8,512]{2,1,0:T(8,128)S(1)}, bf16[224,640]{1,0:T(8,128)(2,1)S(1)}, bf16[224,640]{1,0:T(8,128)(2,1)S(1)}) custom-call(f32[608,640]{1,0:T(8,128)S(1)} %rim_share.13.refs_0_, f32[112,640]{1,0:T(8,128)S(1)} %bitcast.22, f32[112,640]{1,0:T(8,128)S(1)} %bitcast.26, f32[224,640]{1,0:T(8,128)S(1)} %bitcast.14, ...), custom_call_target="tpu_custom_call" | custom-call | tf_op jit(solution)/shard_map/adjoint/pallas_call | solution.py:475
  65.3 1.6 %collective-permute-start.15 = (f32[12,8,512]{2,1,0:T(8,128)S(1)}, f32[12,8,512]{2,1,0:T(8,128)S(1)}, u32[]{:S(2)}, u32[]{:S(2)}) collective-permute-start(f32[12,8,512]{2,1,0:T(8,128)S(1)} %finish.2.refs_0_), channel_id=1, source_target_pairs={{0,2},{1,3},{2,0},{3,1},{4,6},{5,7},{6,4},{7,5},{8,10},{9,11},{10,... | collective-permute-start | bytes 589832 | tf_op jit(solution)/shard_map/ppermute | solution.py:544
  67.4 5.1 %collective-permute-done.19.refs_6_ = f32[12,8,512]{2,1,0:T(8,128)S(1)} collective-permute-done((f32[12,8,512]{2,1,0:T(8,128)S(1)}, f32[12,8,512]{2,1,0:T(8,128)S(1)}, u32[]{:S(2)}, u32[]{:S(2)}) %collective-permute-start.19) | collective-permute-done | bytes 196640 | tf_op jit(solution)/shard_map/ppermute | solution.py:544
  72.5 3.6 %collective-permute-done.15.refs_2_ = f32[12,8,512]{2,1,0:T(8,128)S(1)} collective-permute-done((f32[12,8,512]{2,1,0:T(8,128)S(1)}, f32[12,8,512]{2,1,0:T(8,128)S(1)}, u32[]{:S(2)}, u32[]{:S(2)}) %collective-permute-start.15) | collective-permute-done | bytes 196640 | tf_op jit(solution)/shard_map/ppermute | solution.py:544
  76.2 1.4 %collective-permute-done.16.refs_3_ = f32[12,8,512]{2,1,0:T(8,128)S(1)} collective-permute-done((f32[12,8,512]{2,1,0:T(8,128)S(1)}, f32[12,8,512]{2,1,0:T(8,128)S(1)}, u32[]{:S(2)}, u32[]{:S(2)}) %collective-permute-start.16) | collective-permute-done | bytes 196640 | tf_op jit(solution)/shard_map/ppermute | solution.py:540
  (49 shorter events, 21.7 us)
Async XLA Ops:
  0.0 16.7 %copy-start = (f32[1,3,15]{2,0,1:T(1,128)S(1)}, f32[1,3,15]{2,0,1:T(1,128)}, u32[]{:S(2)}) copy-start(f32[1,3,15]{2,0,1:T(1,128)} %param.4) | copy-start | bytes 544
  2.3 10.9 %collective-permute-start.1 = (f32[14,16,640]{2,1,0:T(8,128)S(1)}, f32[14,16,640]{2,1,0:T(8,128)S(1)}, u32[]{:S(2)}, u32[]{:S(2)}) collective-permute-start(f32[14,16,640]{2,1,0:T(8,128)S(1)} %get-tuple-element.42), channel_id=1, source_target_pairs={{0,4},{1,17},{2,6},{3,19},{4,0},{5,9},{6,2},{7,11},{8,12},{9,5},{1... | collective-permute-start | bytes 1720328 | tf_op jit(solution)/shard_map/ppermute | solution.py:570
  5.4 14.4 %collective-permute-start.3 = (f32[14,16,640]{2,1,0:T(8,128)S(1)}, f32[14,16,640]{2,1,0:T(8,128)S(1)}, u32[]{:S(2)}, u32[]{:S(2)}) collective-permute-start(f32[14,16,640]{2,1,0:T(8,128)S(1)} %get-tuple-element.43), channel_id=1, source_target_pairs={{0,2},{1,3},{2,0},{3,1},{4,6},{5,7},{6,4},{7,5},{8,10},{9,11},{10,... | collective-permute-start | bytes 1720328 | tf_op jit(solution)/shard_map/ppermute | solution.py:544
  13.1 10.0 %collective-permute-start.2 = (f32[14,16,640]{2,1,0:T(8,128)S(1)}, f32[14,16,640]{2,1,0:T(8,128)S(1)}, u32[]{:S(2)}, u32[]{:S(2)}) collective-permute-start(f32[14,16,640]{2,1,0:T(8,128)S(1)} %collective-permute-done.1.rim), channel_id=1, source_target_pairs={{0,1},{1,0},{2,3},{3,2},{4,5},{5,4},{6,7},{7,6},{8,9},{9,8},{10,11... | collective-permute-start | bytes 1720328 | tf_op jit(solution)/shard_map/ppermute | solution.py:540
  13.1 19.5 %collective-permute-start.7 = (f32[7,16,640]{2,1,0:T(8,128)S(1)}, f32[7,16,640]{2,1,0:T(8,128)S(1)}, u32[]{:S(2)}, u32[]{:S(2)}) collective-permute-start(f32[7,16,640]{2,1,0:T(8,128)S(1)} %get-tuple-element.49), channel_id=1, source_target_pairs={{0,4},{1,5},{2,6},{3,7},{4,0},{5,1},{6,2},{7,3},{8,12},{9,13},{10,... | collective-permute-start | bytes 860168 | tf_op jit(solution)/shard_map/ppermute | solution.py:566
  15.2 17.5 %collective-permute-start.8 = (f32[7,16,640]{2,1,0:T(8,128)S(1)}, f32[7,16,640]{2,1,0:T(8,128)S(1)}, u32[]{:S(2)}, u32[]{:S(2)}) collective-permute-start(f32[7,16,640]{2,1,0:T(8,128)S(1)} %get-tuple-element.50), channel_id=1, source_target_pairs={{0,16},{1,17},{2,18},{3,19},{4,8},{5,9},{6,10},{7,11},{8,4},{9,5},... | collective-permute-start | bytes 860168 | tf_op jit(solution)/shard_map/ppermute | solution.py:565
  16.7 4.7 %collective-permute-start = (f32[1,3,15]{2,1,0:T(4,128)S(1)}, f32[1,3,15]{2,1,0:T(4,128)S(1)}, u32[]{:S(2)}, u32[]{:S(2)}) collective-permute-start(f32[1,3,15]{2,1,0:T(4,128)S(1)} %copy.12.taps), channel_id=1, source_target_pairs={{0,2},{1,3},{2,0},{3,1},{4,6},{5,7},{6,4},{7,5},{8,10},{9,11},{10,... | collective-permute-start | bytes 548 | tf_op jit(solution)/shard_map/ppermute | solution.py:544
  19.8 16.0 %collective-permute-start.6 = (f32[10,16,640]{2,1,0:T(8,128)S(1)}, f32[10,16,640]{2,1,0:T(8,128)S(1)}, u32[]{:S(2)}, u32[]{:S(2)}) collective-permute-start(f32[10,16,640]{2,1,0:T(8,128)S(1)} %get-tuple-element.44), channel_id=1, source_target_pairs={{0,2},{1,3},{2,0},{3,1},{4,6},{5,7},{6,4},{7,5},{8,10},{9,11},{10,... | collective-permute-start | bytes 1228808 | tf_op jit(solution)/shard_map/ppermute | solution.py:544
  21.4 14.5 %collective-permute-start.4 = (f32[7,16,640]{2,1,0:T(8,128)S(1)}, f32[7,16,640]{2,1,0:T(8,128)S(1)}, u32[]{:S(2)}, u32[]{:S(2)}) collective-permute-start(f32[7,16,640]{2,1,0:T(8,128)S(1)} %get-tuple-element.70), channel_id=1, source_target_pairs={{0,4},{1,5},{2,6},{3,7},{4,0},{5,1},{6,2},{7,3},{8,12},{9,13},{10,... | collective-permute-start | bytes 860168 | tf_op jit(solution)/shard_map/ppermute | solution.py:566
  23.1 12.8 %collective-permute-start.5 = (f32[7,16,640]{2,1,0:T(8,128)S(1)}, f32[7,16,640]{2,1,0:T(8,128)S(1)}, u32[]{:S(2)}, u32[]{:S(2)}) collective-permute-start(f32[7,16,640]{2,1,0:T(8,128)S(1)} %get-tuple-element.69), channel_id=1, source_target_pairs={{0,16},{1,17},{2,18},{3,19},{4,8},{5,9},{6,10},{7,11},{8,4},{9,5},... | collective-permute-start | bytes 860168 | tf_op jit(solution)/shard_map/ppermute | solution.py:565
  38.4 1.9 %collective-permute-start.10 = (f32[12,16,640]{2,1,0:T(8,128)S(1)}, f32[12,16,640]{2,1,0:T(8,128)S(1)}, u32[]{:S(2)}, u32[]{:S(2)}) collective-permute-start(f32[12,16,640]{2,1,0:T(8,128)S(1)} %adjoint.11.refs_2_), channel_id=1, source_target_pairs={{0,1},{1,0},{2,3},{3,2},{4,5},{5,4},{6,7},{7,6},{8,9},{9,8},{10,11... | collective-permute-start | bytes 1474568 | tf_op jit(solution)/shard_map/ppermute | solution.py:540
  38.5 2.6 %collective-permute-start.9 = (f32[12,16,640]{2,1,0:T(8,128)S(1)}, f32[12,16,640]{2,1,0:T(8,128)S(1)}, u32[]{:S(2)}, u32[]{:S(2)}) collective-permute-start(f32[12,16,640]{2,1,0:T(8,128)S(1)} %get-tuple-element.53.refs_0_), channel_id=1, source_target_pairs={{0,1},{1,0},{2,3},{3,2},{4,5},{5,4},{6,7},{7,6},{8,9},{9,8},{10,11... | collective-permute-start | bytes 1474568 | tf_op jit(solution)/shard_map/ppermute | solution.py:540
  41.6 9.8 %collective-permute-start.11 = (f32[14,16,640]{2,1,0:T(8,128)S(1)}, f32[14,16,640]{2,1,0:T(8,128)S(1)}, u32[]{:S(2)}, u32[]{:S(2)}) collective-permute-start(f32[14,16,640]{2,1,0:T(8,128)S(1)} %get-tuple-element.59), channel_id=1, source_target_pairs={{0,4},{1,17},{2,6},{3,19},{4,0},{5,9},{6,2},{7,11},{8,12},{9,5},{1... | collective-permute-start | bytes 1720328 | tf_op jit(solution)/shard_map/ppermute | solution.py:570
  51.3 5.0 %collective-permute-start.12 = (f32[14,16,640]{2,1,0:T(8,128)S(1)}, f32[14,16,640]{2,1,0:T(8,128)S(1)}, u32[]{:S(2)}, u32[]{:S(2)}) collective-permute-start(f32[14,16,640]{2,1,0:T(8,128)S(1)} %collective-permute-done.11.rim), channel_id=1, source_target_pairs={{0,1},{1,0},{2,3},{3,2},{4,5},{5,4},{6,7},{7,6},{8,9},{9,8},{10,11... | collective-permute-start | bytes 1720328 | tf_op jit(solution)/shard_map/ppermute | solution.py:540
  63.0 1.7 %collective-permute-start.17 = (f32[12,8,512]{2,1,0:T(8,128)S(1)}, f32[12,8,512]{2,1,0:T(8,128)S(1)}, u32[]{:S(2)}, u32[]{:S(2)}) collective-permute-start(f32[12,8,512]{2,1,0:T(8,128)S(1)} %get-tuple-element.68), channel_id=1, source_target_pairs={{0,1},{1,0},{2,3},{3,2},{4,5},{5,4},{6,7},{7,6},{8,9},{9,8},{10,11... | collective-permute-start | bytes 589832 | tf_op jit(solution)/shard_map/ppermute | solution.py:540
  63.6 1.7 %collective-permute-start.13 = (f32[12,8,512]{2,1,0:T(8,128)S(1)}, f32[12,8,512]{2,1,0:T(8,128)S(1)}, u32[]{:S(2)}, u32[]{:S(2)}) collective-permute-start(f32[12,8,512]{2,1,0:T(8,128)S(1)} %get-tuple-element.62), channel_id=1, source_target_pairs={{0,1},{1,0},{2,3},{3,2},{4,5},{5,4},{6,7},{7,6},{8,9},{9,8},{10,11... | collective-permute-start | bytes 589832 | tf_op jit(solution)/shard_map/ppermute | solution.py:540
  64.7 7.8 %collective-permute-start.19 = (f32[12,8,512]{2,1,0:T(8,128)S(1)}, f32[12,8,512]{2,1,0:T(8,128)S(1)}, u32[]{:S(2)}, u32[]{:S(2)}) collective-permute-start(f32[12,8,512]{2,1,0:T(8,128)S(1)} %finish.3.refs_4_), channel_id=1, source_target_pairs={{0,2},{1,3},{2,0},{3,1},{4,6},{5,7},{6,4},{7,5},{8,10},{9,11},{10,... | collective-permute-start | bytes 589832 | tf_op jit(solution)/shard_map/ppermute | solution.py:544
  65.3 10.8 %collective-permute-start.15 = (f32[12,8,512]{2,1,0:T(8,128)S(1)}, f32[12,8,512]{2,1,0:T(8,128)S(1)}, u32[]{:S(2)}, u32[]{:S(2)}) collective-permute-start(f32[12,8,512]{2,1,0:T(8,128)S(1)} %finish.2.refs_0_), channel_id=1, source_target_pairs={{0,2},{1,3},{2,0},{3,1},{4,6},{5,7},{6,4},{7,5},{8,10},{9,11},{10,... | collective-permute-start | bytes 589832 | tf_op jit(solution)/shard_map/ppermute | solution.py:544
  66.9 9.3 %collective-permute-start.18 = (f32[12,8,512]{2,1,0:T(8,128)S(1)}, f32[12,8,512]{2,1,0:T(8,128)S(1)}, u32[]{:S(2)}, u32[]{:S(2)}) collective-permute-start(f32[12,8,512]{2,1,0:T(8,128)S(1)} %finish.3.refs_4_), channel_id=1, source_target_pairs={{0,1},{1,0},{2,3},{3,2},{4,5},{5,4},{6,7},{7,6},{8,9},{9,8},{10,11... | collective-permute-start | bytes 589832 | tf_op jit(solution)/shard_map/ppermute | solution.py:540
  66.9 9.3 %collective-permute-start.14 = (f32[12,8,512]{2,1,0:T(8,128)S(1)}, f32[12,8,512]{2,1,0:T(8,128)S(1)}, u32[]{:S(2)}, u32[]{:S(2)}) collective-permute-start(f32[12,8,512]{2,1,0:T(8,128)S(1)} %finish.2.refs_0_), channel_id=1, source_target_pairs={{0,1},{1,0},{2,3},{3,2},{4,5},{5,4},{6,7},{7,6},{8,9},{9,8},{10,11... | collective-permute-start | bytes 589832 | tf_op jit(solution)/shard_map/ppermute | solution.py:540
  72.5 3.6 %collective-permute-start.20 = (f32[12,8,512]{2,1,0:T(8,128)S(1)}, f32[12,8,512]{2,1,0:T(8,128)S(1)}, u32[]{:S(2)}, u32[]{:S(2)}) collective-permute-start(f32[12,8,512]{2,1,0:T(8,128)S(1)} %collective-permute-done.19.refs_6_), channel_id=1, source_target_pairs={{0,1},{1,0},{2,3},{3,2},{4,5},{5,4},{6,7},{7,6},{8,9},{9,8},{10,11... | collective-permute-start | bytes 589832 | tf_op jit(solution)/shard_map/ppermute | solution.py:540
  76.1 1.4 %collective-permute-start.16 = (f32[12,8,512]{2,1,0:T(8,128)S(1)}, f32[12,8,512]{2,1,0:T(8,128)S(1)}, u32[]{:S(2)}, u32[]{:S(2)}) collective-permute-start(f32[12,8,512]{2,1,0:T(8,128)S(1)} %collective-permute-done.15.refs_2_), channel_id=1, source_target_pairs={{0,1},{1,0},{2,3},{3,2},{4,5},{5,4},{6,7},{7,6},{8,9},{9,8},{10,11... | collective-permute-start | bytes 589832 | tf_op jit(solution)/shard_map/ppermute | solution.py:540

commit v8 on v7

--- a/solution.py
+++ b/solution.py
@@ -348,35 +348,48 @@
     )(est, *ops)
 
 
-def rim_kernel(split, mine, before, rim, t, last, wr, blurred, dh, dl):
+def rim_kernel(split, mine, views, rim, *refs):
     planes, nz, width = rim.shape
     n = planes * nz
     side = split.side(mine)
     flat = rim[...].reshape(n, width) * split.inside(side)
-    for r0, count in chunks(n, 112):
-        rows = slice(r0, r0 + count)
-        blur_y(flat[rows, :], t.at[0], last.at[0], to_halves(dh, dl, rows))
-    rows = pl.ds(pl.multiple_of(side * (blurred.shape[0] - n), nz), n)
-
-    def store(o0, size, value):
-        blurred[rows, o0 : o0 + size] = before[rows, o0 : o0 + size] + value
-
-    product((wr[side, 0, :n, :n], wr[side, 1, :n, :n]), dh, dl, slice(0, n), store)
-
-
-def rim_share(split, mine, before, rim, ops):
+    befores, refs = refs[:views], refs[views:]
+    ops, refs = refs[: 3 * views], refs[3 * views :]
+    blurreds, halves_of = refs[:views], refs[views:]
+    for r in range(views):
+        t, last, wr = ops[3 * r : 3 * r + 3]
+        dh, dl = halves_of[2 * r : 2 * r + 2]
+        for r0, count in chunks(n, 112):
+            rows = slice(r0, r0 + count)
+            blur_y(flat[rows, :], t.at[0], last.at[0], to_halves(dh, dl, rows))
+    for r in range(views):
+        wr = ops[3 * r + 2]
+        before, blurred = befores[r], blurreds[r]
+        dh, dl = halves_of[2 * r : 2 * r + 2]
+        rows = pl.ds(pl.multiple_of(side * (blurred.shape[0] - n), nz), n)
+
+        def store(o0, size, value):
+            blurred[rows, o0 : o0 + size] = before[rows, o0 : o0 + size] + value
+
+        product((wr[side, 0, :n, :n], wr[side, 1, :n, :n]), dh, dl, slice(0, n), store)
+
+
+def rim_share(split, mine, befores, rim, ops):
     planes, nz, width = rim.shape
     half = pltpu.VMEM((planes * nz, width), BF)
-    return pl.pallas_call(
-        functools.partial(rim_kernel, split, mine),
-        out_shape=jax.ShapeDtypeStruct(before.shape, F32),
-        in_specs=[VMEM] * 5,
-        out_specs=VMEM,
-        scratch_shapes=[half, half],
-        input_output_aliases={0: 0},
-        compiler_params=PARAMS,
-        name="rim_share",
-    )(before, rim, ops.t, ops.last, ops.wr)
+    views = len(befores)
+    return list(
+        pl.pallas_call(
+            functools.partial(rim_kernel, split, mine, views),
+            out_shape=tuple(jax.ShapeDtypeStruct(b.shape, F32) for b in befores),
+            in_specs=[VMEM] * (1 + 4 * views),
+            out_specs=(VMEM,) * views,
+            scratch_shapes=[half] * (2 * views),
+            input_output_aliases={1 + r: r for r in range(views)},
+            compiler_params=PARAMS,
+            name="rim_share",
+        )(rim, *befores, *[x for o in ops for x in (o.t, o.last, o.wr)])
+    )
 
 
 class Piece(NamedTuple):
@@ -495,32 +508,32 @@
     return out
 
 
-def join_kernel(split, planes, *refs):
-    parts, out, sem = refs[:-2], refs[-2], refs[-1]
+def join_kernel(split, places, *refs):
+    parts, out, sem = refs[: len(places)], refs[-2], refs[-1]
     chip, core = split.here()
     copies = []
-    for p0, p1 in planes:
-        for r in range(split.chips):
-            owner = lax.rem(chip + split.chips - r, split.chips)
-            lanes = pl.ds(pl.multiple_of(owner * split.part, LANES), split.part)
-            for whose in (core, 1 - core):
-                to = out.at[p0:p1, split.rows(whose), lanes]
-                copies.append(pltpu.make_async_copy(parts[len(copies)], to, sem.at[len(copies)]))
-                copies[-1].start()
+    for part, (p0, p1, r, mine) in zip(parts, places):
+        owner = lax.rem(chip + split.chips - r, split.chips)
+        lanes = pl.ds(pl.multiple_of(owner * split.part, LANES), split.part)
+        to = out.at[p0:p1, split.rows(core if mine else 1 - core), lanes]
+        copies.append(pltpu.make_async_copy(part, to, sem.at[len(copies)]))
+        copies[-1].start()
     for copy in copies:
         copy.wait()
 
 
-def join(split, planes, parts, nx, nz):
+def join(split, pieces, out, nx, nz):
+    places, parts = zip(*pieces)
     return pl.pallas_call(
-        functools.partial(join_kernel, split, planes),
+        functools.partial(join_kernel, split, places),
         out_shape=jax.ShapeDtypeStruct((nx, nz, split.ny), F32),
-        in_specs=[VMEM] * len(parts),
+        in_specs=[VMEM] * len(parts) + ([] if out is None else [ANY]),
         out_specs=ANY,
         scratch_shapes=[pltpu.SemaphoreType.DMA((len(parts),))],
+        input_output_aliases={} if out is None else {len(parts): 0},
         compiler_params=PARAMS,
         name="join",
-    )(*parts)
+    )(*parts, *([] if out is None else [out]))
 
 
 def steps(recorded, psf_taps, estimate):
@@ -571,7 +584,6 @@
         return mine, swap_core(mine)
 
     recorded = recorded[0]
-    taps = [psf_taps] + [to_chip(psf_taps, r) for r in range(1, chips)]
 
     def to_a(n, by_core=False):
         return (nx - n, 0, n, by_core)
@@ -581,19 +593,17 @@
 
     rim, body = RADIUS * nz, (nx - 2 * RADIUS) * nz
     end = 2 * rim + body
-    outs = []
-    for r in range(1, chips):
-        outs.append((0, r, (to_a(RADIUS), to_b(RADIUS))))
-        outs.append((0, r, ((RADIUS, RADIUS, nx - 2 * RADIUS, False),)))
+    outs = [(0, r, (to_a(RADIUS), to_b(RADIUS))) for r in range(1, chips)]
+    outs.append((1, 0, (to_a(2 * RADIUS, True),)))
+    *cuts, est_rim = cut((recorded, estimate), split, outs)
+    taps = [psf_taps] + [to_chip(psf_taps, r) for r in range(1, chips)]
+    edges = [None] + [to_chip(cuts[r - 1], r) for r in range(1, chips)]
+
+    outs = [(0, r, ((RADIUS, RADIUS, nx - 2 * RADIUS, False),)) for r in range(1, chips)]
     outs += [(0, 0, ((0, 0, nx, False),)), (0, 0, (to_a(RADIUS),)), (0, 0, (to_b(RADIUS),))]
-    outs += [(1, 0, ((0, 0, nx, False),)), (1, 0, (to_a(2 * RADIUS, True),))]
-    cuts = cut((recorded, estimate), split, outs)
-    own, own_a, own_b, est, est_rim = cuts[2 * (chips - 1) :]
-
-    edges, middles = [None], [None]
-    for r in range(1, chips):
-        edges.append(to_chip(cuts[2 * r - 2], r))
-        middles.append(to_chip(cuts[2 * r - 1], r))
+    outs += [(1, 0, ((0, 0, nx, False),))]
+    *cuts, own, own_a, own_b, est = cut((recorded, estimate), split, outs)
+    middles = [None] + [to_chip(cuts[r - 1], r) for r in range(1, chips)]
     rims = estimate_rims(est_rim)
     own_a, own_b = pair_up(own_a, own_b)
 
@@ -619,9 +629,8 @@
         for r in range(chips):
             blurred.append(own_share(est, ops[r]))
         for mine in (True, False):
-            for r in range(chips):
-                rim_planes = rims[0] if mine else rims[1]
-                blurred[r] = rim_share(split, mine, blurred[r], rim_planes, ops[r])
+            rim_planes = rims[0] if mine else rims[1]
+            blurred = rim_share(split, mine, blurred, rim_planes, ops)
         plan = spans(nx, 2)
         handed = [None] * chips
         sums = []
@@ -648,13 +657,17 @@
             est, est_rim = update(split, views, planes, sum(sums, ()), est)
             rims = estimate_rims(est_rim)
 
-    parts = []
-    for span, pair in zip(plan, sums):
+    early, late = [], []
+    for c, (span, pair) in enumerate(zip(plan, sums)):
         done = finish(split, views, span.planes, *pair, est)
         for r in range(chips):
             mine = to_chip(done, r) if r else done
-            parts += [mine, swap_core(mine)]
-    return join(split, [span.planes for span in plan], parts, nx, nz)
+            sibling = swap_core(mine)
+            pieces = late if r and c == len(plan) - 1 else early
+            pieces.append(((*span.planes, r, True), mine))
+            pieces.append(((*span.planes, r, False), sibling))
+    out = join(split, early, None, nx, nz)
+    return join(split, late, out, nx, nz)
 
 
 def solution(mesh):

time: 79.1 us -> 75.4 us (0.953)
  waiting for transfers between devices: 29.2 us -> 25.9 us
    ppermute x5, waiting for transfers between devices: 10.4 us -> 8.72 us  [to_chip(): return lax.ppermute(values, 'view', pairs)]
    ppermute x10, waiting for transfers between devices: 4.48 us -> 2.85 us  [swap_core(): return lax.ppermute(values, 'view', pairs)]
    pallas_call x1 -> x2, Pallas kernels: 2.26 us -> 3.11 us  [cut(): pl.pallas_call(functools.partial(cut_kernel, split, len(sources), tuple(m...]
    pallas_call x9 -> x6, Pallas kernels: 8.2 us -> 7.45 us  [the longest x4 5.62 us: rim_share(): pl.pallas_call(functools.partial(rim_kernel, split, mine, views), out_sha...]
  transfers between devices with their start and end apart: 21 -> 21, of which waited for: 9 -> 8; matrix products, arithmetic and copies ran while one was open for 0% -> 0% of each run, Pallas kernels for 21% -> 27%
where the time goes in v8:
time: 75.4 us; the launch traced here: 75.2 us
  Pallas kernels  29.3 us (39%)
  waiting for transfers between devices  25.9 us (34%)
  starting transfers between devices  19.6 us (26%)
    ppermute x2, waiting for transfers between devices, estimate_rims(): mine = lax.ppermute(values, axes, pairs_of(lambda v: v % cores == 1))  14.3 us
    pallas_call x8, Pallas kernels, adjoint(): pl.pallas_call(kernel, out_shape=tuple(shapes), in_specs=[VMEM] * len(arg...  9.77 us
    ppermute x5, waiting for transfers between devices, to_chip(): return lax.ppermute(values, 'view', pairs)  8.72 us
    ppermute x5, starting transfers between devices, to_chip(): return lax.ppermute(values, 'view', pairs)  6.52 us
    pallas_call x4, Pallas kernels, own_share(): pl.pallas_call(own_kernel, out_shape=jax.ShapeDtypeStruct(((planes + 2 *...  6.37 us
    pallas_call x4, Pallas kernels, rim_share(): pl.pallas_call(functools.partial(rim_kernel, split, mine, views), out_sha...  5.62 us
    ppermute x2, starting transfers between devices, estimate_rims(): mine = lax.ppermute(values, axes, pairs_of(lambda v: v % cores == 1))  4.93 us
    ppermute x2, starting transfers between devices, pair_up(): a = lax.ppermute(a, axes, pairs_of(lambda v: False))  3.34 us
  transfers between devices with their start and end apart: 21, of which 8 were waited for; matrix products, arithmetic and copies ran while one was open for 0% of the time, Pallas kernels for 27%

profile of v8, /device:TPU:0, one launch (start us, length us, event | category | flops | bytes accessed | tf_op | source)
XLA Modules:
  0.0 75.2 jit_solution(16476195908322751642)
XLA Ops:
  1.3 3.1 %collective-permute-start = (f32[14,16,640]{2,1,0:T(8,128)S(1)}, f32[14,16,640]{2,1,0:T(8,128)S(1)}, u32[]{:S(2)}, u32[]{:S(2)}) collective-permute-start(f32[14,16,640]{2,1,0:T(8,128)S(1)} %get-tuple-element.45), channel_id=1, source_target_pairs={{0,4},{1,17},{2,6},{3,19},{4,0},{5,9},{6,2},{7,11},{8,12},{9,5},{1... | collective-permute-start | bytes 1720328 | tf_op jit(solution)/shard_map/ppermute | solution.py:583
  4.4 1.5 %collective-permute-start.3 = (f32[14,16,640]{2,1,0:T(8,128)S(1)}, f32[14,16,640]{2,1,0:T(8,128)S(1)}, u32[]{:S(2)}, u32[]{:S(2)}) collective-permute-start(f32[14,16,640]{2,1,0:T(8,128)S(1)} %get-tuple-element.58), channel_id=1, source_target_pairs={{0,2},{1,3},{2,0},{3,1},{4,6},{5,7},{6,4},{7,5},{8,10},{9,11},{10,... | collective-permute-start | bytes 1720328 | tf_op jit(solution)/shard_map/ppermute | solution.py:557
  5.9 6.2 %collective-permute-done.rim = f32[14,16,640]{2,1,0:T(8,128)S(1)} collective-permute-done((f32[14,16,640]{2,1,0:T(8,128)S(1)}, f32[14,16,640]{2,1,0:T(8,128)S(1)}, u32[]{:S(2)}, u32[]{:S(2)}) %collective-permute-start) | collective-permute-done | bytes 573472 | tf_op jit(solution)/shard_map/ppermute | solution.py:583
  12.1 2.0 %collective-permute-start.2 = (f32[1,3,15]{2,1,0:T(4,128)S(1)}, f32[1,3,15]{2,1,0:T(4,128)S(1)}, u32[]{:S(2)}, u32[]{:S(2)}) collective-permute-start(f32[1,3,15]{2,1,0:T(4,128)S(1)} %copy.13.taps), channel_id=1, source_target_pairs={{0,2},{1,3},{2,0},{3,1},{4,6},{5,7},{6,4},{7,5},{8,10},{9,11},{10,... | collective-permute-start | bytes 548 | tf_op jit(solution)/shard_map/ppermute | solution.py:557
  14.1 1.8 %cut.3 = (f32[10,16,640]{2,1,0:T(8,128)S(1)}, f32[24,16,640]{2,1,0:T(8,128)S(1)}, f32[7,16,640]{2,1,0:T(8,128)S(1)}, f32[7,16,640]{2,1,0:T(8,128)S(1)}, f32[24,16,640]{2,1,0:T(8,128)S(1)}) custom-call(f32[24,16,1024]{2,1,0:T(8,128)} %bitcast.37, f32[24,16,1024]{2,1,0:T(8,128)} %refs_1_.3), custom_call_target="tpu_custom_call" | custom-call | tf_op jit(solution)/shard_map/cut/pallas_call | solution.py:99
  15.9 1.6 %collective-permute-start.7 = (f32[7,16,640]{2,1,0:T(8,128)S(1)}, f32[7,16,640]{2,1,0:T(8,128)S(1)}, u32[]{:S(2)}, u32[]{:S(2)}) collective-permute-start(f32[7,16,640]{2,1,0:T(8,128)S(1)} %get-tuple-element.61), channel_id=1, source_target_pairs={{0,4},{1,5},{2,6},{3,7},{4,0},{5,1},{6,2},{7,3},{8,12},{9,13},{10,... | collective-permute-start | bytes 860168 | tf_op jit(solution)/shard_map/ppermute | solution.py:579
  17.6 1.5 %collective-permute-start.8 = (f32[7,16,640]{2,1,0:T(8,128)S(1)}, f32[7,16,640]{2,1,0:T(8,128)S(1)}, u32[]{:S(2)}, u32[]{:S(2)}) collective-permute-start(f32[7,16,640]{2,1,0:T(8,128)S(1)} %get-tuple-element.62), channel_id=1, source_target_pairs={{0,16},{1,17},{2,18},{3,19},{4,8},{5,9},{6,10},{7,11},{8,4},{9,5},... | collective-permute-start | bytes 860168 | tf_op jit(solution)/shard_map/ppermute | solution.py:578
  20.3 1.7 %collective-permute-start.4 = (f32[7,16,640]{2,1,0:T(8,128)S(1)}, f32[7,16,640]{2,1,0:T(8,128)S(1)}, u32[]{:S(2)}, u32[]{:S(2)}) collective-permute-start(f32[7,16,640]{2,1,0:T(8,128)S(1)} %get-tuple-element.86), channel_id=1, source_target_pairs={{0,4},{1,5},{2,6},{3,7},{4,0},{5,1},{6,2},{7,3},{8,12},{9,13},{10,... | collective-permute-start | bytes 860168 | tf_op jit(solution)/shard_map/ppermute | solution.py:579
  22.0 1.5 %collective-permute-start.5 = (f32[7,16,640]{2,1,0:T(8,128)S(1)}, f32[7,16,640]{2,1,0:T(8,128)S(1)}, u32[]{:S(2)}, u32[]{:S(2)}) collective-permute-start(f32[7,16,640]{2,1,0:T(8,128)S(1)} %get-tuple-element.85), channel_id=1, source_target_pairs={{0,16},{1,17},{2,18},{3,19},{4,8},{5,9},{6,10},{7,11},{8,4},{9,5},... | collective-permute-start | bytes 860168 | tf_op jit(solution)/shard_map/ppermute | solution.py:578
  24.6 1.6 %own_share.4.refs_0_ = f32[608,640]{1,0:T(8,128)S(1)} custom-call(f32[24,16,640]{2,1,0:T(8,128)S(1)} %get-tuple-element.46.est.refs_4_, bf16[2,896,256]{2,1,0:T(8,128)(2,1)S(1)} %get-tuple-element.47.t.refs_2_.refs_4_, bf16[2,256,256]{2,1,0:T(8,128)(2,1)S(1)} %get-tuple-element.48.last.refs_3_.refs_5_, ...), custom_call_target="tpu_custom_call" | custom-call | tf_op jit(solution)/shard_map/own_share/pallas_call | solution.py:340
  27.3 1.6 %own_share.5.refs_1_ = f32[608,640]{1,0:T(8,128)S(1)} custom-call(f32[24,16,640]{2,1,0:T(8,128)S(1)} %get-tuple-element.46.est.refs_4_, bf16[2,896,256]{2,1,0:T(8,128)(2,1)S(1)} %get-tuple-element.51.t.refs_5_, bf16[2,256,256]{2,1,0:T(8,128)(2,1)S(1)} %get-tuple-element.52.last.refs_6_, bf16[2,2,256,512]{3,2,1,0:T(8,128)(2,1)S(1)} %get-tuple-element.53.w.refs_7_, ...), custom_call_target="tpu_custom_call" | custom-call | tf_op jit(solution)/shard_map/own_share/pallas_call | solution.py:340
  28.9 1.4 %rim_share.4 = (f32[608,640]{1,0:T(8,128)S(1)}, f32[608,640]{1,0:T(8,128)S(1)}) custom-call(f32[14,16,640]{2,1,0:T(8,128)S(1)} %collective-permute-done.rim, f32[608,640]{1,0:T(8,128)S(1)} %own_share.4.refs_0_, f32[608,640]{1,0:T(8,128)S(1)} %own_share.5.refs_1_, ...), custom_call_target="tpu_custom_call", output_to_operand_aliasing={{0}: (1, {}), {1}: (2, {})} | custom-call | tf_op jit(solution)/shard_map/rim_share/pallas_call | solution.py:382
  30.3 1.4 %rim_share.5 = (f32[608,640]{1,0:T(8,128)S(1)}, f32[608,640]{1,0:T(8,128)S(1)}) custom-call(f32[14,16,640]{2,1,0:T(8,128)S(1)} %collective-permute-done.1.rim, f32[608,640]{1,0:T(8,128)S(1)} %get-tuple-element.55.refs_0_, f32[608,640]{1,0:T(8,128)S(1)} %get-tuple-element.56.refs_1_, ...), custom_call_target="tpu_custom_call", output_to_operand_aliasing={{0}: (1, {}), {1}: (2, {})} | custom-call | tf_op jit(solution)/shard_map/rim_share/pallas_call | solution.py:382
  34.2 1.5 %adjoint.9 = (f32[12,16,640]{2,1,0:T(8,128)S(1)}, bf16[224,640]{1,0:T(8,128)(2,1)S(1)}, bf16[224,640]{1,0:T(8,128)(2,1)S(1)}) custom-call(f32[608,640]{1,0:T(8,128)S(1)} %get-tuple-element.57.refs_0_, f32[112,640]{1,0:T(8,128)S(1)} %bitcast.20, f32[112,640]{1,0:T(8,128)S(1)} %bitcast.24, f32[224,640]{1,0:T(8,128)S(1)} %bitcast.12, f32[160,640]{1,0:T(8,128)S(1)} %bitcast.16, ...), custom_call_target="tpu_custom_call" | custom-call | tf_op jit(solution)/shard_map/adjoint/pallas_call | solution.py:488
  37.3 1.4 %collective-permute-done.10.refs_3_ = f32[12,16,640]{2,1,0:T(8,128)S(1)} collective-permute-done((f32[12,16,640]{2,1,0:T(8,128)S(1)}, f32[12,16,640]{2,1,0:T(8,128)S(1)}, u32[]{:S(2)}, u32[]{:S(2)}) %collective-permute-start.10) | collective-permute-done | bytes 491552 | tf_op jit(solution)/shard_map/ppermute | solution.py:553
  39.7 1.8 %collective-permute-start.11 = (f32[14,16,640]{2,1,0:T(8,128)S(1)}, f32[14,16,640]{2,1,0:T(8,128)S(1)}, u32[]{:S(2)}, u32[]{:S(2)}) collective-permute-start(f32[14,16,640]{2,1,0:T(8,128)S(1)} %get-tuple-element.70), channel_id=1, source_target_pairs={{0,4},{1,17},{2,6},{3,19},{4,0},{5,9},{6,2},{7,11},{8,12},{9,5},{1... | collective-permute-start | bytes 1720328 | tf_op jit(solution)/shard_map/ppermute | solution.py:583
  41.5 8.1 %collective-permute-done.11.rim = f32[14,16,640]{2,1,0:T(8,128)S(1)} collective-permute-done((f32[14,16,640]{2,1,0:T(8,128)S(1)}, f32[14,16,640]{2,1,0:T(8,128)S(1)}, u32[]{:S(2)}, u32[]{:S(2)}) %collective-permute-start.11) | collective-permute-done | bytes 573472 | tf_op jit(solution)/shard_map/ppermute | solution.py:583
  49.6 1.6 %own_share.7.refs_1_ = f32[608,640]{1,0:T(8,128)S(1)} custom-call(f32[24,16,640]{2,1,0:T(8,128)S(1)} %get-tuple-element.71.est, bf16[2,896,256]{2,1,0:T(8,128)(2,1)S(1)} %get-tuple-element.51.t.refs_5_, bf16[2,256,256]{2,1,0:T(8,128)(2,1)S(1)} %get-tuple-element.52.last.refs_6_, bf16[2,2,256,512]{3,2,1,0:T(8,128)(2,1)S(1)} %get-tuple-element.53.w.refs_7_, ...), custom_call_target="tpu_custom_call" | custom-call | tf_op jit(solution)/shard_map/own_share/pallas_call | solution.py:340
  51.2 1.6 %own_share.6.refs_0_ = f32[608,640]{1,0:T(8,128)S(1)} custom-call(f32[24,16,640]{2,1,0:T(8,128)S(1)} %get-tuple-element.71.est, bf16[2,896,256]{2,1,0:T(8,128)(2,1)S(1)} %get-tuple-element.47.t.refs_2_.refs_4_, bf16[2,256,256]{2,1,0:T(8,128)(2,1)S(1)} %get-tuple-element.48.last.refs_3_.refs_5_, bf16[2,2,256,512]{3,2,1,0:T(8,128)(2,1)S(1)} %get-tuple-element.49.w.refs_6_, ...), custom_call_target="tpu_custom_call" | custom-call | tf_op jit(solution)/shard_map/own_share/pallas_call | solution.py:340
  52.8 1.4 %rim_share.6 = (f32[608,640]{1,0:T(8,128)S(1)}, f32[608,640]{1,0:T(8,128)S(1)}) custom-call(f32[14,16,640]{2,1,0:T(8,128)S(1)} %collective-permute-done.11.rim, f32[608,640]{1,0:T(8,128)S(1)} %own_share.6.refs_0_, f32[608,640]{1,0:T(8,128)S(1)} %own_share.7.refs_1_, ...), custom_call_target="tpu_custom_call", output_to_operand_aliasing={{0}: (1, {}), {1}: (2, {})} | custom-call | tf_op jit(solution)/shard_map/rim_share/pallas_call | solution.py:382
  54.3 1.4 %rim_share.7 = (f32[608,640]{1,0:T(8,128)S(1)}, f32[608,640]{1,0:T(8,128)S(1)}) custom-call(f32[14,16,640]{2,1,0:T(8,128)S(1)} %collective-permute-done.12.rim, f32[608,640]{1,0:T(8,128)S(1)} %get-tuple-element.72.refs_0_, f32[608,640]{1,0:T(8,128)S(1)} %get-tuple-element.73.refs_1_, ...), custom_call_target="tpu_custom_call", output_to_operand_aliasing={{0}: (1, {}), {1}: (2, {})} | custom-call | tf_op jit(solution)/shard_map/rim_share/pallas_call | solution.py:382
  57.0 1.6 %adjoint.14 = (f32[12,8,512]{2,1,0:T(8,128)S(1)}, f32[12,8,512]{2,1,0:T(8,128)S(1)}, bf16[224,640]{1,0:T(8,128)(2,1)S(1)}, bf16[224,640]{1,0:T(8,128)(2,1)S(1)}) custom-call(f32[608,640]{1,0:T(8,128)S(1)} %get-tuple-element.74.refs_0_, f32[112,640]{1,0:T(8,128)S(1)} %bitcast.22, f32[112,640]{1,0:T(8,128)S(1)} %bitcast.26, f32[224,640]{1,0:T(8,128)S(1)} %bitcast.14, ...), custom_call_target="tpu_custom_call" | custom-call | tf_op jit(solution)/shard_map/adjoint/pallas_call | solution.py:488
  64.2 5.0 %collective-permute-done.18.refs_2_ = f32[12,8,512]{2,1,0:T(8,128)S(1)} collective-permute-done((f32[12,8,512]{2,1,0:T(8,128)S(1)}, f32[12,8,512]{2,1,0:T(8,128)S(1)}, u32[]{:S(2)}, u32[]{:S(2)}) %collective-permute-start.18) | collective-permute-done | bytes 196640 | tf_op jit(solution)/shard_map/ppermute | solution.py:557
  69.2 3.7 %collective-permute-done.14.refs_0_ = f32[12,8,512]{2,1,0:T(8,128)S(1)} collective-permute-done((f32[12,8,512]{2,1,0:T(8,128)S(1)}, f32[12,8,512]{2,1,0:T(8,128)S(1)}, u32[]{:S(2)}, u32[]{:S(2)}) %collective-permute-start.14) | collective-permute-done | bytes 196640 | tf_op jit(solution)/shard_map/ppermute | solution.py:557
  (47 shorter events, 18.7 us)
Async XLA Ops:
  0.0 12.1 %copy-start = (f32[1,3,15]{2,0,1:T(1,128)S(1)}, f32[1,3,15]{2,0,1:T(1,128)}, u32[]{:S(2)}) copy-start(f32[1,3,15]{2,0,1:T(1,128)} %param.4) | copy-start | bytes 544
  1.3 10.8 %collective-permute-start = (f32[14,16,640]{2,1,0:T(8,128)S(1)}, f32[14,16,640]{2,1,0:T(8,128)S(1)}, u32[]{:S(2)}, u32[]{:S(2)}) collective-permute-start(f32[14,16,640]{2,1,0:T(8,128)S(1)} %get-tuple-element.45), channel_id=1, source_target_pairs={{0,4},{1,17},{2,6},{3,19},{4,0},{5,9},{6,2},{7,11},{8,12},{9,5},{1... | collective-permute-start | bytes 1720328 | tf_op jit(solution)/shard_map/ppermute | solution.py:583
  4.4 14.7 %collective-permute-start.3 = (f32[14,16,640]{2,1,0:T(8,128)S(1)}, f32[14,16,640]{2,1,0:T(8,128)S(1)}, u32[]{:S(2)}, u32[]{:S(2)}) collective-permute-start(f32[14,16,640]{2,1,0:T(8,128)S(1)} %get-tuple-element.58), channel_id=1, source_target_pairs={{0,2},{1,3},{2,0},{3,1},{4,6},{5,7},{6,4},{7,5},{8,10},{9,11},{10,... | collective-permute-start | bytes 1720328 | tf_op jit(solution)/shard_map/ppermute | solution.py:557
  12.1 10.0 %collective-permute-start.1 = (f32[14,16,640]{2,1,0:T(8,128)S(1)}, f32[14,16,640]{2,1,0:T(8,128)S(1)}, u32[]{:S(2)}, u32[]{:S(2)}) collective-permute-start(f32[14,16,640]{2,1,0:T(8,128)S(1)} %collective-permute-done.rim), channel_id=1, source_target_pairs={{0,1},{1,0},{2,3},{3,2},{4,5},{5,4},{6,7},{7,6},{8,9},{9,8},{10,11... | collective-permute-start | bytes 1720328 | tf_op jit(solution)/shard_map/ppermute | solution.py:553
  12.1 8.2 %collective-permute-start.2 = (f32[1,3,15]{2,1,0:T(4,128)S(1)}, f32[1,3,15]{2,1,0:T(4,128)S(1)}, u32[]{:S(2)}, u32[]{:S(2)}) collective-permute-start(f32[1,3,15]{2,1,0:T(4,128)S(1)} %copy.13.taps), channel_id=1, source_target_pairs={{0,2},{1,3},{2,0},{3,1},{4,6},{5,7},{6,4},{7,5},{8,10},{9,11},{10,... | collective-permute-start | bytes 548 | tf_op jit(solution)/shard_map/ppermute | solution.py:557
  15.9 15.8 %collective-permute-start.7 = (f32[7,16,640]{2,1,0:T(8,128)S(1)}, f32[7,16,640]{2,1,0:T(8,128)S(1)}, u32[]{:S(2)}, u32[]{:S(2)}) collective-permute-start(f32[7,16,640]{2,1,0:T(8,128)S(1)} %get-tuple-element.61), channel_id=1, source_target_pairs={{0,4},{1,5},{2,6},{3,7},{4,0},{5,1},{6,2},{7,3},{8,12},{9,13},{10,... | collective-permute-start | bytes 860168 | tf_op jit(solution)/shard_map/ppermute | solution.py:579
  17.6 14.2 %collective-permute-start.8 = (f32[7,16,640]{2,1,0:T(8,128)S(1)}, f32[7,16,640]{2,1,0:T(8,128)S(1)}, u32[]{:S(2)}, u32[]{:S(2)}) collective-permute-start(f32[7,16,640]{2,1,0:T(8,128)S(1)} %get-tuple-element.62), channel_id=1, source_target_pairs={{0,16},{1,17},{2,18},{3,19},{4,8},{5,9},{6,10},{7,11},{8,4},{9,5},... | collective-permute-start | bytes 860168 | tf_op jit(solution)/shard_map/ppermute | solution.py:578
  19.1 15.0 %collective-permute-start.6 = (f32[10,16,640]{2,1,0:T(8,128)S(1)}, f32[10,16,640]{2,1,0:T(8,128)S(1)}, u32[]{:S(2)}, u32[]{:S(2)}) collective-permute-start(f32[10,16,640]{2,1,0:T(8,128)S(1)} %get-tuple-element.59), channel_id=1, source_target_pairs={{0,2},{1,3},{2,0},{3,1},{4,6},{5,7},{6,4},{7,5},{8,10},{9,11},{10,... | collective-permute-start | bytes 1228808 | tf_op jit(solution)/shard_map/ppermute | solution.py:557
  20.3 13.8 %collective-permute-start.4 = (f32[7,16,640]{2,1,0:T(8,128)S(1)}, f32[7,16,640]{2,1,0:T(8,128)S(1)}, u32[]{:S(2)}, u32[]{:S(2)}) collective-permute-start(f32[7,16,640]{2,1,0:T(8,128)S(1)} %get-tuple-element.86), channel_id=1, source_target_pairs={{0,4},{1,5},{2,6},{3,7},{4,0},{5,1},{6,2},{7,3},{8,12},{9,13},{10,... | collective-permute-start | bytes 860168 | tf_op jit(solution)/shard_map/ppermute | solution.py:579
  22.0 12.1 %collective-permute-start.5 = (f32[7,16,640]{2,1,0:T(8,128)S(1)}, f32[7,16,640]{2,1,0:T(8,128)S(1)}, u32[]{:S(2)}, u32[]{:S(2)}) collective-permute-start(f32[7,16,640]{2,1,0:T(8,128)S(1)} %get-tuple-element.85), channel_id=1, source_target_pairs={{0,16},{1,17},{2,18},{3,19},{4,8},{5,9},{6,10},{7,11},{8,4},{9,5},... | collective-permute-start | bytes 860168 | tf_op jit(solution)/shard_map/ppermute | solution.py:578
  36.7 1.9 %collective-permute-start.10 = (f32[12,16,640]{2,1,0:T(8,128)S(1)}, f32[12,16,640]{2,1,0:T(8,128)S(1)}, u32[]{:S(2)}, u32[]{:S(2)}) collective-permute-start(f32[12,16,640]{2,1,0:T(8,128)S(1)} %adjoint.11.refs_2_), channel_id=1, source_target_pairs={{0,1},{1,0},{2,3},{3,2},{4,5},{5,4},{6,7},{7,6},{8,9},{9,8},{10,11... | collective-permute-start | bytes 1474568 | tf_op jit(solution)/shard_map/ppermute | solution.py:553
  36.8 2.6 %collective-permute-start.9 = (f32[12,16,640]{2,1,0:T(8,128)S(1)}, f32[12,16,640]{2,1,0:T(8,128)S(1)}, u32[]{:S(2)}, u32[]{:S(2)}) collective-permute-start(f32[12,16,640]{2,1,0:T(8,128)S(1)} %get-tuple-element.65.refs_0_), channel_id=1, source_target_pairs={{0,1},{1,0},{2,3},{3,2},{4,5},{5,4},{6,7},{7,6},{8,9},{9,8},{10,11... | collective-permute-start | bytes 1474568 | tf_op jit(solution)/shard_map/ppermute | solution.py:553
  39.7 10.0 %collective-permute-start.11 = (f32[14,16,640]{2,1,0:T(8,128)S(1)}, f32[14,16,640]{2,1,0:T(8,128)S(1)}, u32[]{:S(2)}, u32[]{:S(2)}) collective-permute-start(f32[14,16,640]{2,1,0:T(8,128)S(1)} %get-tuple-element.70), channel_id=1, source_target_pairs={{0,4},{1,17},{2,6},{3,19},{4,0},{5,9},{6,2},{7,11},{8,12},{9,5},{1... | collective-permute-start | bytes 1720328 | tf_op jit(solution)/shard_map/ppermute | solution.py:583
  49.6 4.6 %collective-permute-start.12 = (f32[14,16,640]{2,1,0:T(8,128)S(1)}, f32[14,16,640]{2,1,0:T(8,128)S(1)}, u32[]{:S(2)}, u32[]{:S(2)}) collective-permute-start(f32[14,16,640]{2,1,0:T(8,128)S(1)} %collective-permute-done.11.rim), channel_id=1, source_target_pairs={{0,1},{1,0},{2,3},{3,2},{4,5},{5,4},{6,7},{7,6},{8,9},{9,8},{10,11... | collective-permute-start | bytes 1720328 | tf_op jit(solution)/shard_map/ppermute | solution.py:553
  58.6 2.7 %collective-permute-start.16 = (f32[12,8,512]{2,1,0:T(8,128)S(1)}, f32[12,8,512]{2,1,0:T(8,128)S(1)}, u32[]{:S(2)}, u32[]{:S(2)}) collective-permute-start(f32[12,8,512]{2,1,0:T(8,128)S(1)} %get-tuple-element.84), channel_id=1, source_target_pairs={{0,1},{1,0},{2,3},{3,2},{4,5},{5,4},{6,7},{7,6},{8,9},{9,8},{10,11... | collective-permute-start | bytes 589832 | tf_op jit(solution)/shard_map/ppermute | solution.py:553
  61.2 1.5 %collective-permute-start.13 = (f32[12,8,512]{2,1,0:T(8,128)S(1)}, f32[12,8,512]{2,1,0:T(8,128)S(1)}, u32[]{:S(2)}, u32[]{:S(2)}) collective-permute-start(f32[12,8,512]{2,1,0:T(8,128)S(1)} %get-tuple-element.82), channel_id=1, source_target_pairs={{0,1},{1,0},{2,3},{3,2},{4,5},{5,4},{6,7},{7,6},{8,9},{9,8},{10,11... | collective-permute-start | bytes 589832 | tf_op jit(solution)/shard_map/ppermute | solution.py:553
  61.3 7.8 %collective-permute-start.18 = (f32[12,8,512]{2,1,0:T(8,128)S(1)}, f32[12,8,512]{2,1,0:T(8,128)S(1)}, u32[]{:S(2)}, u32[]{:S(2)}) collective-permute-start(f32[12,8,512]{2,1,0:T(8,128)S(1)} %finish.3.refs_0_), channel_id=1, source_target_pairs={{0,2},{1,3},{2,0},{3,1},{4,6},{5,7},{6,4},{7,5},{8,10},{9,11},{10,... | collective-permute-start | bytes 589832 | tf_op jit(solution)/shard_map/ppermute | solution.py:557
  62.7 10.2 %collective-permute-start.14 = (f32[12,8,512]{2,1,0:T(8,128)S(1)}, f32[12,8,512]{2,1,0:T(8,128)S(1)}, u32[]{:S(2)}, u32[]{:S(2)}) collective-permute-start(f32[12,8,512]{2,1,0:T(8,128)S(1)} %finish.2.refs_4_), channel_id=1, source_target_pairs={{0,2},{1,3},{2,0},{3,1},{4,6},{5,7},{6,4},{7,5},{8,10},{9,11},{10,... | collective-permute-start | bytes 589832 | tf_op jit(solution)/shard_map/ppermute | solution.py:557
  63.7 9.2 %collective-permute-start.17 = (f32[12,8,512]{2,1,0:T(8,128)S(1)}, f32[12,8,512]{2,1,0:T(8,128)S(1)}, u32[]{:S(2)}, u32[]{:S(2)}) collective-permute-start(f32[12,8,512]{2,1,0:T(8,128)S(1)} %finish.3.refs_0_), channel_id=1, source_target_pairs={{0,1},{1,0},{2,3},{3,2},{4,5},{5,4},{6,7},{7,6},{8,9},{9,8},{10,11... | collective-permute-start | bytes 589832 | tf_op jit(solution)/shard_map/ppermute | solution.py:553
  63.7 9.2 %collective-permute-start.20 = (f32[12,8,512]{2,1,0:T(8,128)S(1)}, f32[12,8,512]{2,1,0:T(8,128)S(1)}, u32[]{:S(2)}, u32[]{:S(2)}) collective-permute-start(f32[12,8,512]{2,1,0:T(8,128)S(1)} %finish.2.refs_4_), channel_id=1, source_target_pairs={{0,1},{1,0},{2,3},{3,2},{4,5},{5,4},{6,7},{7,6},{8,9},{9,8},{10,11... | collective-permute-start | bytes 589832 | tf_op jit(solution)/shard_map/ppermute | solution.py:553
  69.2 3.8 %collective-permute-start.19 = (f32[12,8,512]{2,1,0:T(8,128)S(1)}, f32[12,8,512]{2,1,0:T(8,128)S(1)}, u32[]{:S(2)}, u32[]{:S(2)}) collective-permute-start(f32[12,8,512]{2,1,0:T(8,128)S(1)} %collective-permute-done.18.refs_2_), channel_id=1, source_target_pairs={{0,1},{1,0},{2,3},{3,2},{4,5},{5,4},{6,7},{7,6},{8,9},{9,8},{10,11... | collective-permute-start | bytes 589832 | tf_op jit(solution)/shard_map/ppermute | solution.py:553
  72.9 1.4 %collective-permute-start.15 = (f32[12,8,512]{2,1,0:T(8,128)S(1)}, f32[12,8,512]{2,1,0:T(8,128)S(1)}, u32[]{:S(2)}, u32[]{:S(2)}) collective-permute-start(f32[12,8,512]{2,1,0:T(8,128)S(1)} %collective-permute-done.14.refs_0_), channel_id=1, source_target_pairs={{0,1},{1,0},{2,3},{3,2},{4,5},{5,4},{6,7},{7,6},{8,9},{9,8},{10,11... | collective-permute-start | bytes 589832 | tf_op jit(solution)/shard_map/ppermute | solution.py:553

commit v9 on v8

--- a/solution.py
+++ b/solution.py
@@ -48,9 +48,21 @@
         place = lax.axis_index("view")
         return place // self.cores, lax.rem(place, self.cores)
 
-    def inner(self):
-        chip, _ = self.here()
+    def inner(self, chip):
         return pl.multiple_of(chip * self.part - self.start(chip), LANES)
+
+    def halo(self, chip):
+        return pl.multiple_of(jnp.where(chip == 0, self.part, 0), LANES)
+
+    def packs(self, planes, nz):
+        padded = -(-planes * nz // LANES) * LANES
+        one = self.chips == 2 and self.width == self.part + LANES
+        return one and SLIVER // nz * padded <= self.part
+
+    def rim(self, planes, nz):
+        if self.packs(planes, nz):
+            return (planes + 1, nz, self.part)
+        return (planes, nz, self.width)
 
     def odd(self):
         return lax.rem(lax.axis_index("tile"), 2)
@@ -68,8 +80,71 @@
         return pl.ds(pl.multiple_of(core * self.half, self.half), self.half)
 
 
-def cut_kernel(split, sources, moves, *refs):
-    outs, sem = refs[sources:-1], refs[-1]
+SLIVER = 32
+
+
+def pack(split, chip, window, first, planes, out, to):
+    nz = out.shape[1]
+    at = pl.ds(first, planes)
+    out[to : to + planes] = window[at, :, pl.ds(split.inner(chip), split.part)]
+    rows = planes * nz
+    padded = -(-rows // LANES) * LANES
+    tile = window[at, :, pl.ds(split.halo(chip), LANES)].reshape(rows, LANES)
+    if padded > rows:
+        tile = jnp.concatenate([tile, jnp.zeros((padded - rows, LANES), F32)], 0)
+    turned = tile.T
+    kept = jnp.where(chip == 0, turned[:SLIVER], turned[LANES - SLIVER :])
+    for g in range(SLIVER // nz):
+        out[to + planes, :, g * padded : (g + 1) * padded] = kept[g * nz : (g + 1) * nz]
+    rest = SLIVER // nz * padded
+    if rest < split.part:
+        out[to + planes, :, rest:] = jnp.zeros((nz, split.part - rest), F32)
+
+
+def unpack(split, packed, first, planes, window, to):
+    nz = packed.shape[1]
+    chip, _ = split.here()
+    rows = planes * nz
+    padded = -(-rows // LANES) * LANES
+    at = slice(to, to + rows)
+    own = packed[first : first + planes].reshape(rows, split.part)
+    window[at, pl.ds(split.inner(chip), split.part)] = own
+    extra = first + planes
+    kept = [packed[extra, :, g * padded : (g + 1) * padded] for g in range(SLIVER // nz)]
+    none = jnp.ones((LANES - SLIVER, padded), F32)
+    turned = jnp.where(
+        chip == 0, jnp.concatenate([*kept, none], 0), jnp.concatenate([none, *kept], 0)
+    )
+    window[at, pl.ds(split.halo(chip), LANES)] = turned.T[:rows]
+
+
+def unpack_kernel(split, packs, *refs):
+    for packed, window, counts in zip(refs[: len(packs)], refs[len(packs) :], packs):
+        first = to = 0
+        for planes in counts:
+            unpack(split, packed, first, planes, window, to)
+            first, to = first + planes + 1, to + planes * packed.shape[1]
+
+
+def unpacked(split, arrays, packs):
+    nz = arrays[0].shape[1]
+    if not split.packs(packs[0][0], nz):
+        return tuple(a.reshape(-1, a.shape[-1]) for a in arrays)
+    return pl.pallas_call(
+        functools.partial(unpack_kernel, split, packs),
+        out_shape=tuple(jax.ShapeDtypeStruct((sum(p) * nz, split.width), F32) for p in packs),
+        in_specs=[VMEM] * len(arrays),
+        out_specs=(VMEM,) * len(arrays),
+        compiler_params=PARAMS,
+        name="unpack",
+    )(*arrays)
+
+
+def cut_kernel(split, sources, moves, packed, *refs):
+    outs, sem = list(refs[sources : len(refs) - 1 - len(packed)]), refs[-1]
+    finals = [outs[k] for k, _, _ in packed]
+    for (k, _, _), scratch in zip(packed, refs[len(refs) - 1 - len(packed) : -1]):
+        outs[k] = scratch
     chip, _ = split.here()
     copies = []
     for source, ahead, out, at, even, odd, n, by_core in moves:
@@ -86,22 +161,34 @@
         copies[-1].start()
     for copy in copies:
         copy.wait()
-
-
-def cut(sources, split, outs):
-    moves, shapes = [], []
+    for (k, ahead, counts), final in zip(packed, finals):
+        first = to = 0
+        for planes in counts:
+            pack(split, lax.rem(chip + ahead, split.chips), outs[k], first, planes, final, to)
+            first, to = first + planes, to + planes + 1
+
+
+def cut(sources, split, outs, whole):
+    moves, shapes, scratch, packed = [], [], [], []
     for index, (source, ahead, ranges) in enumerate(outs):
         at = 0
         for even, odd, n, by_core in ranges:
             moves.append((source, ahead, index, at, even, odd, n, by_core))
             at += n
-        shapes.append(jax.ShapeDtypeStruct((at, sources[source].shape[1], split.width), F32))
+        nz = sources[source].shape[1]
+        shape = (at, nz, split.width)
+        counts = tuple(n for _, _, n, _ in ranges)
+        if index not in whole and split.packs(max(counts), nz):
+            scratch.append(pltpu.VMEM(shape, F32))
+            packed.append((index, ahead, counts))
+            shape = (at + len(counts), nz, split.part)
+        shapes.append(jax.ShapeDtypeStruct(shape, F32))
     return pl.pallas_call(
-        functools.partial(cut_kernel, split, len(sources), tuple(moves)),
+        functools.partial(cut_kernel, split, len(sources), tuple(moves), tuple(packed)),
         out_shape=tuple(shapes),
         in_specs=[ANY] * len(sources),
         out_specs=(VMEM,) * len(shapes),
-        scratch_shapes=[pltpu.SemaphoreType.DMA((len(moves),))],
+        scratch_shapes=[*scratch, pltpu.SemaphoreType.DMA((len(moves),))],
         compiler_params=PARAMS,
         name="cut",
     )(*[pltpu.with_memory_space_constraint(a, pltpu.HBM) for a in sources])
@@ -112,8 +199,12 @@
     for c, (p0, p1) in enumerate(planes):
         total = refs[2 * c][...] + refs[2 * c + 1][...]
         out[p0:p1] = est[p0:p1] * jnp.exp(total / views)
-    n = rim.shape[0]
-    rim[...] = out[pl.ds(split.side(True) * (out.shape[0] - n), n)]
+    n = 2 * RADIUS
+    first = split.side(True) * (out.shape[0] - n)
+    if split.packs(n, out.shape[1]):
+        pack(split, split.here()[0], out, first, n, rim, 0)
+    else:
+        rim[...] = out[pl.ds(first, n)]
 
 
 def update(split, views, planes, sums, est):
@@ -121,7 +212,7 @@
         functools.partial(update_kernel, split, views, planes),
         out_shape=(
             jax.ShapeDtypeStruct(est.shape, F32),
-            jax.ShapeDtypeStruct((2 * RADIUS, *est.shape[1:]), F32),
+            jax.ShapeDtypeStruct(split.rim(2 * RADIUS, est.shape[1]), F32),
         ),
         in_specs=[VMEM] * (len(sums) + 1),
         out_specs=(VMEM,) * 2,
@@ -131,8 +222,8 @@
 
 
 def finish_kernel(split, views, planes, mine, sibling, est, out):
-    _, core = split.here()
-    old = est[planes[0] : planes[1], split.rows(core), pl.ds(split.inner(), split.part)]
+    chip, core = split.here()
+    old = est[planes[0] : planes[1], split.rows(core), pl.ds(split.inner(chip), split.part)]
     out[...] = old * jnp.exp((mine[...] + sibling[...]) / views)
 
 
@@ -349,10 +440,15 @@
 
 
 def rim_kernel(split, mine, views, rim, *refs):
-    planes, nz, width = rim.shape
-    n = planes * nz
+    nz, width = rim.shape[1], split.width
+    n = 2 * RADIUS * nz
     side = split.side(mine)
-    flat = rim[...].reshape(n, width) * split.inside(side)
+    if split.packs(2 * RADIUS, nz):
+        *refs, window = refs
+        unpack(split, rim, 0, 2 * RADIUS, window, 0)
+        flat = window[...] * split.inside(side)
+    else:
+        flat = rim[...].reshape(n, width) * split.inside(side)
     befores, refs = refs[:views], refs[views:]
     ops, refs = refs[: 3 * views], refs[3 * views :]
     blurreds, halves_of = refs[:views], refs[views:]
@@ -375,8 +471,9 @@
 
 
 def rim_share(split, mine, befores, rim, ops):
-    planes, nz, width = rim.shape
-    half = pltpu.VMEM((planes * nz, width), BF)
+    rows, nz = 2 * RADIUS * rim.shape[1], rim.shape[1]
+    half = pltpu.VMEM((rows, split.width), BF)
+    window = [pltpu.VMEM((rows, split.width), F32)] if split.packs(2 * RADIUS, nz) else []
     views = len(befores)
     return list(
         pl.pallas_call(
@@ -384,7 +481,7 @@
             out_shape=tuple(jax.ShapeDtypeStruct(b.shape, F32) for b in befores),
             in_specs=[VMEM] * (1 + 4 * views),
             out_specs=(VMEM,) * views,
-            scratch_shapes=[half] * (2 * views),
+            scratch_shapes=[half] * (2 * views) + window,
             input_output_aliases={1 + r: r for r in range(views)},
             compiler_params=PARAMS,
             name="rim_share",
@@ -462,8 +559,8 @@
 
     blur_xz(dh, dl, w.at[1], nz, p1 - p0, store)
     if ends is not None:
-        _, core = split.here()
-        lanes = slice(None) if ends == split.width else pl.ds(split.inner(), ends)
+        chip, core = split.here()
+        lanes = slice(None) if ends == split.width else pl.ds(split.inner(chip), ends)
         keep[...] = out[:, split.rows(core), lanes]
         send[...] = out[:, split.rows(1 - core), lanes]
 
@@ -545,7 +642,7 @@
     part = ny // chips
     width = min(ny, part + (LANES if chips <= 2 else 2 * LANES))
     split = Split(chips, cores, part, width, ny, nz // cores, tiles)
-    assert 2 * RADIUS * ITERS <= LANES and nx >= 2 * RADIUS
+    assert 2 * RADIUS * ITERS <= SLIVER and nx >= 2 * RADIUS
     flat = lambda a: a.reshape(-1, a.shape[-1])
 
     def swap_core(values):
@@ -595,25 +692,30 @@
     end = 2 * rim + body
     outs = [(0, r, (to_a(RADIUS), to_b(RADIUS))) for r in range(1, chips)]
     outs.append((1, 0, (to_a(2 * RADIUS, True),)))
-    *cuts, est_rim = cut((recorded, estimate), split, outs)
+    *cuts, est_rim = cut((recorded, estimate), split, outs, ())
     taps = [psf_taps] + [to_chip(psf_taps, r) for r in range(1, chips)]
     edges = [None] + [to_chip(cuts[r - 1], r) for r in range(1, chips)]
 
     outs = [(0, r, ((RADIUS, RADIUS, nx - 2 * RADIUS, False),)) for r in range(1, chips)]
     outs += [(0, 0, ((0, 0, nx, False),)), (0, 0, (to_a(RADIUS),)), (0, 0, (to_b(RADIUS),))]
     outs += [(1, 0, ((0, 0, nx, False),))]
-    *cuts, own, own_a, own_b, est = cut((recorded, estimate), split, outs)
+    whole = (chips - 1, chips + 2)
+    *cuts, own, own_a, own_b, est = cut((recorded, estimate), split, outs, whole)
     middles = [None] + [to_chip(cuts[r - 1], r) for r in range(1, chips)]
     rims = estimate_rims(est_rim)
     own_a, own_b = pair_up(own_a, own_b)
 
-    record = [tuple(flat(a) for a in (own_a, own_b, own))]
+    own_a, own_b = unpacked(split, (own_a, own_b), ((RADIUS,), (RADIUS,)))
+    record = [(own_a, own_b, flat(own))]
     before = Piece(0, rim, 0, 0, 1, 0, 0)
     after = Piece(rim + end, rim, 1, 0, 0, 0, 1)
     pieces = [(before, Piece(rim, end, 2, 0, 2, 0), after)]
     for r in range(1, chips):
-        pair_a, pair_b = pair_up(edges[r][:RADIUS], edges[r][RADIUS:])
-        record.append(tuple(flat(a) for a in (pair_a, pair_b, edges[r], middles[r])))
+        one = edges[r].shape[0] // 2
+        pair_a, pair_b = pair_up(edges[r][:one], edges[r][one:])
+        arrays = (pair_a, pair_b, edges[r], middles[r])
+        packs = ((RADIUS,), (RADIUS,), (RADIUS, RADIUS), (nx - 2 * RADIUS,))
+        record.append(unpacked(split, arrays, packs))
         first = Piece(rim, rim, 2, 0, 2, rim)
         inner = Piece(2 * rim, body, 3, 0, 3, 0)
         last = Piece(2 * rim + body, rim, 2, rim, 2, 0)

time: 75.4 us -> 72.7 us (0.964)
  starting transfers between devices: 19.6 us -> 17.3 us
  waiting for transfers between devices: 25.9 us -> 24.2 us
  Pallas kernels: 29.3 us -> 30.5 us
    ppermute x2, waiting for transfers between devices: 14.3 us -> 12.6 us  [estimate_rims(): mine = lax.ppermute(values, axes, pairs_of(lambda v: v % cores == 1))]
    ppermute x2, starting transfers between devices: 4.93 us -> 3.26 us  [estimate_rims(): mine = lax.ppermute(values, axes, pairs_of(lambda v: v % cores == 1))]
  transfers between devices with their start and end apart: 21 -> 21, of which waited for: 8 -> 8; matrix products, arithmetic and copies ran while one was open for 0% -> 0% of each run, Pallas kernels for 27% -> 24%
where the time goes in v9:
time: 72.7 us; the launch traced here: 72.5 us
  Pallas kernels  30.5 us (42%)
  waiting for transfers between devices  24.2 us (33%)
  starting transfers between devices  17.3 us (24%)
    ppermute x2, waiting for transfers between devices, estimate_rims(): mine = lax.ppermute(values, axes, pairs_of(lambda v: v % cores == 1))  12.6 us
    pallas_call x8, Pallas kernels, adjoint(): pl.pallas_call(kernel, out_shape=tuple(shapes), in_specs=[VMEM] * len(arg...  9.93 us
    ppermute x5, waiting for transfers between devices, to_chip(): return lax.ppermute(values, 'view', pairs)  9.13 us
    pallas_call x4, Pallas kernels, own_share(): pl.pallas_call(own_kernel, out_shape=jax.ShapeDtypeStruct(((planes + 2 *...  6.36 us
    ppermute x5, starting transfers between devices, to_chip(): return lax.ppermute(values, 'view', pairs)  6.23 us
    pallas_call x4, Pallas kernels, rim_share(): pl.pallas_call(functools.partial(rim_kernel, split, mine, views), out_sha...  6 us
    pallas_call x2, Pallas kernels, cut(): pl.pallas_call(functools.partial(cut_kernel, split, len(sources), tuple(m...  3.49 us
    ppermute x2, starting transfers between devices, pair_up(): b = lax.ppermute(b, axes, pairs_of(lambda v: True))  3.41 us
  transfers between devices with their start and end apart: 21, of which 8 were waited for; matrix products, arithmetic and copies ran while one was open for 0% of the time, Pallas kernels for 24%

profile of v9, /device:TPU:0, one launch (start us, length us, event | category | flops | bytes accessed | tf_op | source)
XLA Modules:
  0.0 72.5 jit_solution(3921506886812148915)
XLA Ops:
  0.0 1.5 %cut.2 = (f32[16,16,512]{2,1,0:T(8,128)S(1)}, f32[15,16,512]{2,1,0:T(8,128)S(1)}) custom-call(f32[24,16,1024]{2,1,0:T(8,128)} %bitcast.6, f32[24,16,1024]{2,1,0:T(8,128)} %refs_1_.3), custom_call_target="tpu_custom_call" | custom-call | tf_op jit(solution)/shard_map/cut/pallas_call | solution.py:186
  1.5 3.0 %collective-permute-start.3 = (f32[16,16,512]{2,1,0:T(8,128)S(1)}, f32[16,16,512]{2,1,0:T(8,128)S(1)}, u32[]{:S(2)}, u32[]{:S(2)}) collective-permute-start(f32[16,16,512]{2,1,0:T(8,128)S(1)} %get-tuple-element.64), channel_id=1, source_target_pairs={{0,2},{1,3},{2,0},{3,1},{4,6},{5,7},{6,4},{7,5},{8,10},{9,11},{10,... | collective-permute-start | bytes 1572872 | tf_op jit(solution)/shard_map/ppermute | solution.py:654
  4.5 1.6 %collective-permute-start = (f32[15,16,512]{2,1,0:T(8,128)S(1)}, f32[15,16,512]{2,1,0:T(8,128)S(1)}, u32[]{:S(2)}, u32[]{:S(2)}) collective-permute-start(f32[15,16,512]{2,1,0:T(8,128)S(1)} %get-tuple-element.51), channel_id=1, source_target_pairs={{0,4},{1,17},{2,6},{3,19},{4,0},{5,9},{6,2},{7,11},{8,12},{9,5},{1... | collective-permute-start | bytes 1474568 | tf_op jit(solution)/shard_map/ppermute | solution.py:680
  6.1 2.0 %cut.3 = (f32[11,16,512]{2,1,0:T(8,128)S(1)}, f32[24,16,640]{2,1,0:T(8,128)S(1)}, f32[8,16,512]{2,1,0:T(8,128)S(1)}, f32[8,16,512]{2,1,0:T(8,128)S(1)}, f32[24,16,640]{2,1,0:T(8,128)S(1)}) custom-call(f32[24,16,1024]{2,1,0:T(8,128)} %bitcast.7, f32[24,16,1024]{2,1,0:T(8,128)} %refs_1_.3), custom_call_target="tpu_custom_call" | custom-call | tf_op jit(solution)/shard_map/cut/pallas_call | solution.py:186
  8.8 1.9 %collective-permute-start.8 = (f32[8,16,512]{2,1,0:T(8,128)S(1)}, f32[8,16,512]{2,1,0:T(8,128)S(1)}, u32[]{:S(2)}, u32[]{:S(2)}) collective-permute-start(f32[8,16,512]{2,1,0:T(8,128)S(1)} %get-tuple-element.72), channel_id=1, source_target_pairs={{0,16},{1,17},{2,18},{3,19},{4,8},{5,9},{6,10},{7,11},{8,4},{9,5},... | collective-permute-start | bytes 786440 | tf_op jit(solution)/shard_map/ppermute | solution.py:675
  10.7 5.4 %collective-permute-done.rim = f32[15,16,512]{2,1,0:T(8,128)S(1)} collective-permute-done((f32[15,16,512]{2,1,0:T(8,128)S(1)}, f32[15,16,512]{2,1,0:T(8,128)S(1)}, u32[]{:S(2)}, u32[]{:S(2)}) %collective-permute-start) | collective-permute-done | bytes 491552 | tf_op jit(solution)/shard_map/ppermute | solution.py:680
  17.3 2.2 %collective-permute-start.4 = (f32[8,16,512]{2,1,0:T(8,128)S(1)}, f32[8,16,512]{2,1,0:T(8,128)S(1)}, u32[]{:S(2)}, u32[]{:S(2)}) collective-permute-start(f32[8,16,512]{2,1,0:T(8,128)S(1)} %get-tuple-element.98), channel_id=1, source_target_pairs={{0,4},{1,5},{2,6},{3,7},{4,0},{5,1},{6,2},{7,3},{8,12},{9,13},{10,... | collective-permute-start | bytes 786440 | tf_op jit(solution)/shard_map/ppermute | solution.py:676
  19.5 1.5 %collective-permute-start.5 = (f32[8,16,512]{2,1,0:T(8,128)S(1)}, f32[8,16,512]{2,1,0:T(8,128)S(1)}, u32[]{:S(2)}, u32[]{:S(2)}) collective-permute-start(f32[8,16,512]{2,1,0:T(8,128)S(1)} %get-tuple-element.97), channel_id=1, source_target_pairs={{0,16},{1,17},{2,18},{3,19},{4,8},{5,9},{6,10},{7,11},{8,4},{9,5},... | collective-permute-start | bytes 786440 | tf_op jit(solution)/shard_map/ppermute | solution.py:675
  22.1 1.6 %own_share.4.refs_0_ = f32[608,640]{1,0:T(8,128)S(1)} custom-call(f32[24,16,640]{2,1,0:T(8,128)S(1)} %get-tuple-element.52.est.refs_4_, bf16[2,896,256]{2,1,0:T(8,128)(2,1)S(1)} %get-tuple-element.53.t.refs_2_.refs_4_, bf16[2,256,256]{2,1,0:T(8,128)(2,1)S(1)} %get-tuple-element.54.last.refs_3_.refs_5_, ...), custom_call_target="tpu_custom_call" | custom-call | tf_op jit(solution)/shard_map/own_share/pallas_call | solution.py:431
  24.8 1.6 %own_share.5.refs_1_ = f32[608,640]{1,0:T(8,128)S(1)} custom-call(f32[24,16,640]{2,1,0:T(8,128)S(1)} %get-tuple-element.52.est.refs_4_, bf16[2,896,256]{2,1,0:T(8,128)(2,1)S(1)} %get-tuple-element.57.t.refs_5_, bf16[2,256,256]{2,1,0:T(8,128)(2,1)S(1)} %get-tuple-element.58.last.refs_6_, bf16[2,2,256,512]{3,2,1,0:T(8,128)(2,1)S(1)} %get-tuple-element.59.w.refs_7_, ...), custom_call_target="tpu_custom_call" | custom-call | tf_op jit(solution)/shard_map/own_share/pallas_call | solution.py:431
  26.5 1.5 %rim_share.4 = (f32[608,640]{1,0:T(8,128)S(1)}, f32[608,640]{1,0:T(8,128)S(1)}) custom-call(f32[15,16,512]{2,1,0:T(8,128)S(1)} %collective-permute-done.rim, f32[608,640]{1,0:T(8,128)S(1)} %own_share.4.refs_0_, f32[608,640]{1,0:T(8,128)S(1)} %own_share.5.refs_1_, ...), custom_call_target="tpu_custom_call", output_to_operand_aliasing={{0}: (1, {}), {1}: (2, {})} | custom-call | tf_op jit(solution)/shard_map/rim_share/pallas_call | solution.py:479
  28.3 1.5 %rim_share.5 = (f32[608,640]{1,0:T(8,128)S(1)}, f32[608,640]{1,0:T(8,128)S(1)}) custom-call(f32[15,16,512]{2,1,0:T(8,128)S(1)} %collective-permute-done.1.rim, f32[608,640]{1,0:T(8,128)S(1)} %get-tuple-element.61.refs_0_, f32[608,640]{1,0:T(8,128)S(1)} %get-tuple-element.62.refs_1_, ...), custom_call_target="tpu_custom_call", output_to_operand_aliasing={{0}: (1, {}), {1}: (2, {})} | custom-call | tf_op jit(solution)/shard_map/rim_share/pallas_call | solution.py:479
  32.2 1.5 %adjoint.9 = (f32[12,16,640]{2,1,0:T(8,128)S(1)}, bf16[224,640]{1,0:T(8,128)(2,1)S(1)}, bf16[224,640]{1,0:T(8,128)(2,1)S(1)}) custom-call(f32[608,640]{1,0:T(8,128)S(1)} %get-tuple-element.63.refs_0_, f32[112,640]{1,0:T(8,128)S(1)} %get-tuple-element.66.refs_1_, f32[112,640]{1,0:T(8,128)S(1)} %get-tuple-element.67.refs_2_, ...), custom_call_target="tpu_custom_call" | custom-call | tf_op jit(solution)/shard_map/adjoint/pallas_call | solution.py:585
  37.8 1.7 %collective-permute-start.11 = (f32[15,16,512]{2,1,0:T(8,128)S(1)}, f32[15,16,512]{2,1,0:T(8,128)S(1)}, u32[]{:S(2)}, u32[]{:S(2)}) collective-permute-start(f32[15,16,512]{2,1,0:T(8,128)S(1)} %get-tuple-element.82), channel_id=1, source_target_pairs={{0,4},{1,17},{2,6},{3,19},{4,0},{5,9},{6,2},{7,11},{8,12},{9,5},{1... | collective-permute-start | bytes 1474568 | tf_op jit(solution)/shard_map/ppermute | solution.py:680
  39.5 7.2 %collective-permute-done.11.rim = f32[15,16,512]{2,1,0:T(8,128)S(1)} collective-permute-done((f32[15,16,512]{2,1,0:T(8,128)S(1)}, f32[15,16,512]{2,1,0:T(8,128)S(1)}, u32[]{:S(2)}, u32[]{:S(2)}) %collective-permute-start.11) | collective-permute-done | bytes 491552 | tf_op jit(solution)/shard_map/ppermute | solution.py:680
  46.7 1.6 %own_share.7.refs_1_ = f32[608,640]{1,0:T(8,128)S(1)} custom-call(f32[24,16,640]{2,1,0:T(8,128)S(1)} %get-tuple-element.83.est, bf16[2,896,256]{2,1,0:T(8,128)(2,1)S(1)} %get-tuple-element.57.t.refs_5_, bf16[2,256,256]{2,1,0:T(8,128)(2,1)S(1)} %get-tuple-element.58.last.refs_6_, bf16[2,2,256,512]{3,2,1,0:T(8,128)(2,1)S(1)} %get-tuple-element.59.w.refs_7_, ...), custom_call_target="tpu_custom_call" | custom-call | tf_op jit(solution)/shard_map/own_share/pallas_call | solution.py:431
  48.3 1.6 %own_share.6.refs_0_ = f32[608,640]{1,0:T(8,128)S(1)} custom-call(f32[24,16,640]{2,1,0:T(8,128)S(1)} %get-tuple-element.83.est, bf16[2,896,256]{2,1,0:T(8,128)(2,1)S(1)} %get-tuple-element.53.t.refs_2_.refs_4_, bf16[2,256,256]{2,1,0:T(8,128)(2,1)S(1)} %get-tuple-element.54.last.refs_3_.refs_5_, bf16[2,2,256,512]{3,2,1,0:T(8,128)(2,1)S(1)} %get-tuple-element.55.w.refs_6_, ...), custom_call_target="tpu_custom_call" | custom-call | tf_op jit(solution)/shard_map/own_share/pallas_call | solution.py:431
  49.9 1.5 %rim_share.6 = (f32[608,640]{1,0:T(8,128)S(1)}, f32[608,640]{1,0:T(8,128)S(1)}) custom-call(f32[15,16,512]{2,1,0:T(8,128)S(1)} %collective-permute-done.11.rim, f32[608,640]{1,0:T(8,128)S(1)} %own_share.6.refs_0_, f32[608,640]{1,0:T(8,128)S(1)} %own_share.7.refs_1_, ...), custom_call_target="tpu_custom_call", output_to_operand_aliasing={{0}: (1, {}), {1}: (2, {})} | custom-call | tf_op jit(solution)/shard_map/rim_share/pallas_call | solution.py:479
  51.4 1.5 %rim_share.7 = (f32[608,640]{1,0:T(8,128)S(1)}, f32[608,640]{1,0:T(8,128)S(1)}) custom-call(f32[15,16,512]{2,1,0:T(8,128)S(1)} %collective-permute-done.12.rim, f32[608,640]{1,0:T(8,128)S(1)} %get-tuple-element.84.refs_0_, f32[608,640]{1,0:T(8,128)S(1)} %get-tuple-element.85.refs_1_, ...), custom_call_target="tpu_custom_call", output_to_operand_aliasing={{0}: (1, {}), {1}: (2, {})} | custom-call | tf_op jit(solution)/shard_map/rim_share/pallas_call | solution.py:479
  54.3 1.5 %adjoint.14 = (f32[12,8,512]{2,1,0:T(8,128)S(1)}, f32[12,8,512]{2,1,0:T(8,128)S(1)}, bf16[224,640]{1,0:T(8,128)(2,1)S(1)}, bf16[224,640]{1,0:T(8,128)(2,1)S(1)}) custom-call(f32[608,640]{1,0:T(8,128)S(1)} %get-tuple-element.86.refs_0_, f32[112,640]{1,0:T(8,128)S(1)} %get-tuple-element.66.refs_1_, f32[112,640]{1,0:T(8,128)S(1)} %get-tuple-element.67.refs_2_, ...), custom_call_target="tpu_custom_call" | custom-call | tf_op jit(solution)/shard_map/adjoint/pallas_call | solution.py:585
  58.6 1.6 %collective-permute-start.18 = (f32[12,8,512]{2,1,0:T(8,128)S(1)}, f32[12,8,512]{2,1,0:T(8,128)S(1)}, u32[]{:S(2)}, u32[]{:S(2)}) collective-permute-start(f32[12,8,512]{2,1,0:T(8,128)S(1)} %finish.3.refs_0_), channel_id=1, source_target_pairs={{0,2},{1,3},{2,0},{3,1},{4,6},{5,7},{6,4},{7,5},{8,10},{9,11},{10,... | collective-permute-start | bytes 589832 | tf_op jit(solution)/shard_map/ppermute | solution.py:654
  60.2 1.4 %collective-permute-start.14 = (f32[12,8,512]{2,1,0:T(8,128)S(1)}, f32[12,8,512]{2,1,0:T(8,128)S(1)}, u32[]{:S(2)}, u32[]{:S(2)}) collective-permute-start(f32[12,8,512]{2,1,0:T(8,128)S(1)} %finish.2.refs_4_), channel_id=1, source_target_pairs={{0,2},{1,3},{2,0},{3,1},{4,6},{5,7},{6,4},{7,5},{8,10},{9,11},{10,... | collective-permute-start | bytes 589832 | tf_op jit(solution)/shard_map/ppermute | solution.py:654
  62.0 4.3 %collective-permute-done.18.refs_2_ = f32[12,8,512]{2,1,0:T(8,128)S(1)} collective-permute-done((f32[12,8,512]{2,1,0:T(8,128)S(1)}, f32[12,8,512]{2,1,0:T(8,128)S(1)}, u32[]{:S(2)}, u32[]{:S(2)}) %collective-permute-start.18) | collective-permute-done | bytes 196640 | tf_op jit(solution)/shard_map/ppermute | solution.py:654
  66.4 3.7 %collective-permute-done.14.refs_0_ = f32[12,8,512]{2,1,0:T(8,128)S(1)} collective-permute-done((f32[12,8,512]{2,1,0:T(8,128)S(1)}, f32[12,8,512]{2,1,0:T(8,128)S(1)}, u32[]{:S(2)}, u32[]{:S(2)}) %collective-permute-start.14) | collective-permute-done | bytes 196640 | tf_op jit(solution)/shard_map/ppermute | solution.py:654
  (49 shorter events, 17.6 us)
Async XLA Ops:
  1.5 15.8 %collective-permute-start.3 = (f32[16,16,512]{2,1,0:T(8,128)S(1)}, f32[16,16,512]{2,1,0:T(8,128)S(1)}, u32[]{:S(2)}, u32[]{:S(2)}) collective-permute-start(f32[16,16,512]{2,1,0:T(8,128)S(1)} %get-tuple-element.64), channel_id=1, source_target_pairs={{0,2},{1,3},{2,0},{3,1},{4,6},{5,7},{6,4},{7,5},{8,10},{9,11},{10,... | collective-permute-start | bytes 1572872 | tf_op jit(solution)/shard_map/ppermute | solution.py:654
  4.5 4.1 %copy-start = (f32[1,3,15]{2,0,1:T(1,128)S(1)}, f32[1,3,15]{2,0,1:T(1,128)}, u32[]{:S(2)}) copy-start(f32[1,3,15]{2,0,1:T(1,128)} %param.4) | copy-start | bytes 544
  4.5 11.6 %collective-permute-start = (f32[15,16,512]{2,1,0:T(8,128)S(1)}, f32[15,16,512]{2,1,0:T(8,128)S(1)}, u32[]{:S(2)}, u32[]{:S(2)}) collective-permute-start(f32[15,16,512]{2,1,0:T(8,128)S(1)} %get-tuple-element.51), channel_id=1, source_target_pairs={{0,4},{1,17},{2,6},{3,19},{4,0},{5,9},{6,2},{7,11},{8,12},{9,5},{1... | collective-permute-start | bytes 1474568 | tf_op jit(solution)/shard_map/ppermute | solution.py:680
  8.1 11.4 %collective-permute-start.7 = (f32[8,16,512]{2,1,0:T(8,128)S(1)}, f32[8,16,512]{2,1,0:T(8,128)S(1)}, u32[]{:S(2)}, u32[]{:S(2)}) collective-permute-start(f32[8,16,512]{2,1,0:T(8,128)S(1)} %get-tuple-element.71), channel_id=1, source_target_pairs={{0,4},{1,5},{2,6},{3,7},{4,0},{5,1},{6,2},{7,3},{8,12},{9,13},{10,... | collective-permute-start | bytes 786440 | tf_op jit(solution)/shard_map/ppermute | solution.py:676
  8.6 8.7 %collective-permute-start.2 = (f32[1,3,15]{2,1,0:T(4,128)S(1)}, f32[1,3,15]{2,1,0:T(4,128)S(1)}, u32[]{:S(2)}, u32[]{:S(2)}) collective-permute-start(f32[1,3,15]{2,1,0:T(4,128)S(1)} %copy.13.taps), channel_id=1, source_target_pairs={{0,2},{1,3},{2,0},{3,1},{4,6},{5,7},{6,4},{7,5},{8,10},{9,11},{10,... | collective-permute-start | bytes 548 | tf_op jit(solution)/shard_map/ppermute | solution.py:654
  8.8 17.6 %collective-permute-start.8 = (f32[8,16,512]{2,1,0:T(8,128)S(1)}, f32[8,16,512]{2,1,0:T(8,128)S(1)}, u32[]{:S(2)}, u32[]{:S(2)}) collective-permute-start(f32[8,16,512]{2,1,0:T(8,128)S(1)} %get-tuple-element.72), channel_id=1, source_target_pairs={{0,16},{1,17},{2,18},{3,19},{4,8},{5,9},{6,10},{7,11},{8,4},{9,5},... | collective-permute-start | bytes 786440 | tf_op jit(solution)/shard_map/ppermute | solution.py:675
  16.1 11.9 %collective-permute-start.6 = (f32[11,16,512]{2,1,0:T(8,128)S(1)}, f32[11,16,512]{2,1,0:T(8,128)S(1)}, u32[]{:S(2)}, u32[]{:S(2)}) collective-permute-start(f32[11,16,512]{2,1,0:T(8,128)S(1)} %get-tuple-element.65), channel_id=1, source_target_pairs={{0,2},{1,3},{2,0},{3,1},{4,6},{5,7},{6,4},{7,5},{8,10},{9,11},{10,... | collective-permute-start | bytes 1081352 | tf_op jit(solution)/shard_map/ppermute | solution.py:654
  17.3 11.0 %collective-permute-start.1 = (f32[15,16,512]{2,1,0:T(8,128)S(1)}, f32[15,16,512]{2,1,0:T(8,128)S(1)}, u32[]{:S(2)}, u32[]{:S(2)}) collective-permute-start(f32[15,16,512]{2,1,0:T(8,128)S(1)} %collective-permute-done.rim), channel_id=1, source_target_pairs={{0,1},{1,0},{2,3},{3,2},{4,5},{5,4},{6,7},{7,6},{8,9},{9,8},{10,11... | collective-permute-start | bytes 1474568 | tf_op jit(solution)/shard_map/ppermute | solution.py:650
  17.3 10.7 %collective-permute-start.4 = (f32[8,16,512]{2,1,0:T(8,128)S(1)}, f32[8,16,512]{2,1,0:T(8,128)S(1)}, u32[]{:S(2)}, u32[]{:S(2)}) collective-permute-start(f32[8,16,512]{2,1,0:T(8,128)S(1)} %get-tuple-element.98), channel_id=1, source_target_pairs={{0,4},{1,5},{2,6},{3,7},{4,0},{5,1},{6,2},{7,3},{8,12},{9,13},{10,... | collective-permute-start | bytes 786440 | tf_op jit(solution)/shard_map/ppermute | solution.py:676
  19.5 8.6 %collective-permute-start.5 = (f32[8,16,512]{2,1,0:T(8,128)S(1)}, f32[8,16,512]{2,1,0:T(8,128)S(1)}, u32[]{:S(2)}, u32[]{:S(2)}) collective-permute-start(f32[8,16,512]{2,1,0:T(8,128)S(1)} %get-tuple-element.97), channel_id=1, source_target_pairs={{0,16},{1,17},{2,18},{3,19},{4,8},{5,9},{6,10},{7,11},{8,4},{9,5},... | collective-permute-start | bytes 786440 | tf_op jit(solution)/shard_map/ppermute | solution.py:675
  34.9 1.9 %collective-permute-start.10 = (f32[12,16,640]{2,1,0:T(8,128)S(1)}, f32[12,16,640]{2,1,0:T(8,128)S(1)}, u32[]{:S(2)}, u32[]{:S(2)}) collective-permute-start(f32[12,16,640]{2,1,0:T(8,128)S(1)} %adjoint.11.refs_2_), channel_id=1, source_target_pairs={{0,1},{1,0},{2,3},{3,2},{4,5},{5,4},{6,7},{7,6},{8,9},{9,8},{10,11... | collective-permute-start | bytes 1474568 | tf_op jit(solution)/shard_map/ppermute | solution.py:650
  34.9 2.6 %collective-permute-start.9 = (f32[12,16,640]{2,1,0:T(8,128)S(1)}, f32[12,16,640]{2,1,0:T(8,128)S(1)}, u32[]{:S(2)}, u32[]{:S(2)}) collective-permute-start(f32[12,16,640]{2,1,0:T(8,128)S(1)} %get-tuple-element.77.refs_0_), channel_id=1, source_target_pairs={{0,1},{1,0},{2,3},{3,2},{4,5},{5,4},{6,7},{7,6},{8,9},{9,8},{10,11... | collective-permute-start | bytes 1474568 | tf_op jit(solution)/shard_map/ppermute | solution.py:650
  37.8 8.9 %collective-permute-start.11 = (f32[15,16,512]{2,1,0:T(8,128)S(1)}, f32[15,16,512]{2,1,0:T(8,128)S(1)}, u32[]{:S(2)}, u32[]{:S(2)}) collective-permute-start(f32[15,16,512]{2,1,0:T(8,128)S(1)} %get-tuple-element.82), channel_id=1, source_target_pairs={{0,4},{1,17},{2,6},{3,19},{4,0},{5,9},{6,2},{7,11},{8,12},{9,5},{1... | collective-permute-start | bytes 1474568 | tf_op jit(solution)/shard_map/ppermute | solution.py:680
  46.7 4.7 %collective-permute-start.12 = (f32[15,16,512]{2,1,0:T(8,128)S(1)}, f32[15,16,512]{2,1,0:T(8,128)S(1)}, u32[]{:S(2)}, u32[]{:S(2)}) collective-permute-start(f32[15,16,512]{2,1,0:T(8,128)S(1)} %collective-permute-done.11.rim), channel_id=1, source_target_pairs={{0,1},{1,0},{2,3},{3,2},{4,5},{5,4},{6,7},{7,6},{8,9},{9,8},{10,11... | collective-permute-start | bytes 1474568 | tf_op jit(solution)/shard_map/ppermute | solution.py:650
  55.8 2.7 %collective-permute-start.16 = (f32[12,8,512]{2,1,0:T(8,128)S(1)}, f32[12,8,512]{2,1,0:T(8,128)S(1)}, u32[]{:S(2)}, u32[]{:S(2)}) collective-permute-start(f32[12,8,512]{2,1,0:T(8,128)S(1)} %get-tuple-element.96), channel_id=1, source_target_pairs={{0,1},{1,0},{2,3},{3,2},{4,5},{5,4},{6,7},{7,6},{8,9},{9,8},{10,11... | collective-permute-start | bytes 589832 | tf_op jit(solution)/shard_map/ppermute | solution.py:650
  58.4 1.7 %collective-permute-start.13 = (f32[12,8,512]{2,1,0:T(8,128)S(1)}, f32[12,8,512]{2,1,0:T(8,128)S(1)}, u32[]{:S(2)}, u32[]{:S(2)}) collective-permute-start(f32[12,8,512]{2,1,0:T(8,128)S(1)} %get-tuple-element.94), channel_id=1, source_target_pairs={{0,1},{1,0},{2,3},{3,2},{4,5},{5,4},{6,7},{7,6},{8,9},{9,8},{10,11... | collective-permute-start | bytes 589832 | tf_op jit(solution)/shard_map/ppermute | solution.py:650
  58.6 7.8 %collective-permute-start.18 = (f32[12,8,512]{2,1,0:T(8,128)S(1)}, f32[12,8,512]{2,1,0:T(8,128)S(1)}, u32[]{:S(2)}, u32[]{:S(2)}) collective-permute-start(f32[12,8,512]{2,1,0:T(8,128)S(1)} %finish.3.refs_0_), channel_id=1, source_target_pairs={{0,2},{1,3},{2,0},{3,1},{4,6},{5,7},{6,4},{7,5},{8,10},{9,11},{10,... | collective-permute-start | bytes 589832 | tf_op jit(solution)/shard_map/ppermute | solution.py:654
  60.2 10.0 %collective-permute-start.14 = (f32[12,8,512]{2,1,0:T(8,128)S(1)}, f32[12,8,512]{2,1,0:T(8,128)S(1)}, u32[]{:S(2)}, u32[]{:S(2)}) collective-permute-start(f32[12,8,512]{2,1,0:T(8,128)S(1)} %finish.2.refs_4_), channel_id=1, source_target_pairs={{0,2},{1,3},{2,0},{3,1},{4,6},{5,7},{6,4},{7,5},{8,10},{9,11},{10,... | collective-permute-start | bytes 589832 | tf_op jit(solution)/shard_map/ppermute | solution.py:654
  61.5 8.6 %collective-permute-start.17 = (f32[12,8,512]{2,1,0:T(8,128)S(1)}, f32[12,8,512]{2,1,0:T(8,128)S(1)}, u32[]{:S(2)}, u32[]{:S(2)}) collective-permute-start(f32[12,8,512]{2,1,0:T(8,128)S(1)} %finish.3.refs_0_), channel_id=1, source_target_pairs={{0,1},{1,0},{2,3},{3,2},{4,5},{5,4},{6,7},{7,6},{8,9},{9,8},{10,11... | collective-permute-start | bytes 589832 | tf_op jit(solution)/shard_map/ppermute | solution.py:650
  61.5 8.6 %collective-permute-start.20 = (f32[12,8,512]{2,1,0:T(8,128)S(1)}, f32[12,8,512]{2,1,0:T(8,128)S(1)}, u32[]{:S(2)}, u32[]{:S(2)}) collective-permute-start(f32[12,8,512]{2,1,0:T(8,128)S(1)} %finish.2.refs_4_), channel_id=1, source_target_pairs={{0,1},{1,0},{2,3},{3,2},{4,5},{5,4},{6,7},{7,6},{8,9},{9,8},{10,11... | collective-permute-start | bytes 589832 | tf_op jit(solution)/shard_map/ppermute | solution.py:650
  66.4 3.8 %collective-permute-start.19 = (f32[12,8,512]{2,1,0:T(8,128)S(1)}, f32[12,8,512]{2,1,0:T(8,128)S(1)}, u32[]{:S(2)}, u32[]{:S(2)}) collective-permute-start(f32[12,8,512]{2,1,0:T(8,128)S(1)} %collective-permute-done.18.refs_2_), channel_id=1, source_target_pairs={{0,1},{1,0},{2,3},{3,2},{4,5},{5,4},{6,7},{7,6},{8,9},{9,8},{10,11... | collective-permute-start | bytes 589832 | tf_op jit(solution)/shard_map/ppermute | solution.py:650
  70.1 1.4 %collective-permute-start.15 = (f32[12,8,512]{2,1,0:T(8,128)S(1)}, f32[12,8,512]{2,1,0:T(8,128)S(1)}, u32[]{:S(2)}, u32[]{:S(2)}) collective-permute-start(f32[12,8,512]{2,1,0:T(8,128)S(1)} %collective-permute-done.14.refs_0_), channel_id=1, source_target_pairs={{0,1},{1,0},{2,3},{3,2},{4,5},{5,4},{6,7},{7,6},{8,9},{9,8},{10,11... | collective-permute-start | bytes 589832 | tf_op jit(solution)/shard_map/ppermute | solution.py:650

commit v10 on v9

--- a/solution.py
+++ b/solution.py
@@ -393,7 +393,7 @@
     return store
 
 
-def chunks(rows, step=128):
+def chunks(rows, step=256):
     return [(r, min(step, rows - r)) for r in range(0, rows, step)]
 
 
@@ -595,14 +595,12 @@
     return total, (out[-2:] if span.hands_on else None)
 
 
-def spans(nx, count):
-    out, done = [], 0
-    for c in range(count):
-        p0, p1 = c * nx // count, (c + 1) * nx // count
-        q1 = p1 + 2 * RADIUS
-        out.append(Span((p0, p1), (done, q1), c > 0, c < count - 1))
-        done = q1
-    return out
+def spans(nx, cut):
+    reach = cut + 2 * RADIUS
+    return [
+        Span((0, cut), (0, reach), False, True),
+        Span((cut, nx), (reach, nx + 2 * RADIUS), True, False),
+    ]
 
 
 def join_kernel(split, places, *refs):
@@ -733,7 +731,7 @@
         for mine in (True, False):
             rim_planes = rims[0] if mine else rims[1]
             blurred = rim_share(split, mine, blurred, rim_planes, ops)
-        plan = spans(nx, 2)
+        plan = spans(nx, nx // 2 if final else 2 * nx // 3)
         handed = [None] * chips
         sums = []
         for span in plan:

time: 72.7 us -> 71.7 us (0.986)
  waiting for transfers between devices: 24.2 us -> 23.4 us
    ppermute x10, waiting for transfers between devices: 2.41 us -> 1.62 us  [swap_core(): return lax.ppermute(values, 'view', pairs)]
  transfers between devices with their start and end apart: 21 -> 21, of which waited for: 8 -> 7; matrix products, arithmetic and copies ran while one was open for 0% -> 0% of each run, Pallas kernels for 24% -> 26%
where the time goes in v10:
time: 71.7 us; the launch traced here: 71.5 us
  Pallas kernels  30.3 us (42%)
  waiting for transfers between devices  23.4 us (33%)
  starting transfers between devices  17.4 us (24%)
    ppermute x2, waiting for transfers between devices, estimate_rims(): mine = lax.ppermute(values, axes, pairs_of(lambda v: v % cores == 1))  12.6 us
    pallas_call x8, Pallas kernels, adjoint(): pl.pallas_call(kernel, out_shape=tuple(shapes), in_specs=[VMEM] * len(arg...  9.67 us
    ppermute x5, waiting for transfers between devices, to_chip(): return lax.ppermute(values, 'view', pairs)  9.13 us
    pallas_call x4, Pallas kernels, own_share(): pl.pallas_call(own_kernel, out_shape=jax.ShapeDtypeStruct(((planes + 2 *...  6.37 us
    ppermute x5, starting transfers between devices, to_chip(): return lax.ppermute(values, 'view', pairs)  6.23 us
    pallas_call x4, Pallas kernels, rim_share(): pl.pallas_call(functools.partial(rim_kernel, split, mine, views), out_sha...  6 us
    pallas_call x2, Pallas kernels, cut(): pl.pallas_call(functools.partial(cut_kernel, split, len(sources), tuple(m...  3.49 us
    ppermute x2, starting transfers between devices, pair_up(): b = lax.ppermute(b, axes, pairs_of(lambda v: True))  3.41 us
  transfers between devices with their start and end apart: 21, of which 7 were waited for; matrix products, arithmetic and copies ran while one was open for 0% of the time, Pallas kernels for 26%

profile of v10, /device:TPU:0, one launch (start us, length us, event | category | flops | bytes accessed | tf_op | source)
XLA Modules:
  0.0 71.5 jit_solution(17536144208810237292)
XLA Ops:
  0.0 1.5 %cut.2 = (f32[16,16,512]{2,1,0:T(8,128)S(1)}, f32[15,16,512]{2,1,0:T(8,128)S(1)}) custom-call(f32[24,16,1024]{2,1,0:T(8,128)} %bitcast.6, f32[24,16,1024]{2,1,0:T(8,128)} %refs_1_.3), custom_call_target="tpu_custom_call" | custom-call | tf_op jit(solution)/shard_map/cut/pallas_call | solution.py:186
  1.5 3.0 %collective-permute-start.3 = (f32[16,16,512]{2,1,0:T(8,128)S(1)}, f32[16,16,512]{2,1,0:T(8,128)S(1)}, u32[]{:S(2)}, u32[]{:S(2)}) collective-permute-start(f32[16,16,512]{2,1,0:T(8,128)S(1)} %get-tuple-element.64), channel_id=1, source_target_pairs={{0,2},{1,3},{2,0},{3,1},{4,6},{5,7},{6,4},{7,5},{8,10},{9,11},{10,... | collective-permute-start | bytes 1572872 | tf_op jit(solution)/shard_map/ppermute | solution.py:652
  4.5 1.6 %collective-permute-start = (f32[15,16,512]{2,1,0:T(8,128)S(1)}, f32[15,16,512]{2,1,0:T(8,128)S(1)}, u32[]{:S(2)}, u32[]{:S(2)}) collective-permute-start(f32[15,16,512]{2,1,0:T(8,128)S(1)} %get-tuple-element.51), channel_id=1, source_target_pairs={{0,4},{1,17},{2,6},{3,19},{4,0},{5,9},{6,2},{7,11},{8,12},{9,5},{1... | collective-permute-start | bytes 1474568 | tf_op jit(solution)/shard_map/ppermute | solution.py:678
  6.1 2.0 %cut.3 = (f32[11,16,512]{2,1,0:T(8,128)S(1)}, f32[24,16,640]{2,1,0:T(8,128)S(1)}, f32[8,16,512]{2,1,0:T(8,128)S(1)}, f32[8,16,512]{2,1,0:T(8,128)S(1)}, f32[24,16,640]{2,1,0:T(8,128)S(1)}) custom-call(f32[24,16,1024]{2,1,0:T(8,128)} %bitcast.7, f32[24,16,1024]{2,1,0:T(8,128)} %refs_1_.3), custom_call_target="tpu_custom_call" | custom-call | tf_op jit(solution)/shard_map/cut/pallas_call | solution.py:186
  8.8 1.9 %collective-permute-start.8 = (f32[8,16,512]{2,1,0:T(8,128)S(1)}, f32[8,16,512]{2,1,0:T(8,128)S(1)}, u32[]{:S(2)}, u32[]{:S(2)}) collective-permute-start(f32[8,16,512]{2,1,0:T(8,128)S(1)} %get-tuple-element.72), channel_id=1, source_target_pairs={{0,16},{1,17},{2,18},{3,19},{4,8},{5,9},{6,10},{7,11},{8,4},{9,5},... | collective-permute-start | bytes 786440 | tf_op jit(solution)/shard_map/ppermute | solution.py:673
  10.7 5.4 %collective-permute-done.rim = f32[15,16,512]{2,1,0:T(8,128)S(1)} collective-permute-done((f32[15,16,512]{2,1,0:T(8,128)S(1)}, f32[15,16,512]{2,1,0:T(8,128)S(1)}, u32[]{:S(2)}, u32[]{:S(2)}) %collective-permute-start) | collective-permute-done | bytes 491552 | tf_op jit(solution)/shard_map/ppermute | solution.py:678
  17.3 2.2 %collective-permute-start.4 = (f32[8,16,512]{2,1,0:T(8,128)S(1)}, f32[8,16,512]{2,1,0:T(8,128)S(1)}, u32[]{:S(2)}, u32[]{:S(2)}) collective-permute-start(f32[8,16,512]{2,1,0:T(8,128)S(1)} %get-tuple-element.98), channel_id=1, source_target_pairs={{0,4},{1,5},{2,6},{3,7},{4,0},{5,1},{6,2},{7,3},{8,12},{9,13},{10,... | collective-permute-start | bytes 786440 | tf_op jit(solution)/shard_map/ppermute | solution.py:674
  19.5 1.5 %collective-permute-start.5 = (f32[8,16,512]{2,1,0:T(8,128)S(1)}, f32[8,16,512]{2,1,0:T(8,128)S(1)}, u32[]{:S(2)}, u32[]{:S(2)}) collective-permute-start(f32[8,16,512]{2,1,0:T(8,128)S(1)} %get-tuple-element.97), channel_id=1, source_target_pairs={{0,16},{1,17},{2,18},{3,19},{4,8},{5,9},{6,10},{7,11},{8,4},{9,5},... | collective-permute-start | bytes 786440 | tf_op jit(solution)/shard_map/ppermute | solution.py:673
  22.1 1.6 %own_share.4.refs_0_ = f32[608,640]{1,0:T(8,128)S(1)} custom-call(f32[24,16,640]{2,1,0:T(8,128)S(1)} %get-tuple-element.52.est.refs_4_, bf16[2,896,256]{2,1,0:T(8,128)(2,1)S(1)} %get-tuple-element.53.t.refs_2_.refs_4_, bf16[2,256,256]{2,1,0:T(8,128)(2,1)S(1)} %get-tuple-element.54.last.refs_3_.refs_5_, ...), custom_call_target="tpu_custom_call" | custom-call | tf_op jit(solution)/shard_map/own_share/pallas_call | solution.py:431
  24.8 1.6 %own_share.5.refs_1_ = f32[608,640]{1,0:T(8,128)S(1)} custom-call(f32[24,16,640]{2,1,0:T(8,128)S(1)} %get-tuple-element.52.est.refs_4_, bf16[2,896,256]{2,1,0:T(8,128)(2,1)S(1)} %get-tuple-element.57.t.refs_5_, bf16[2,256,256]{2,1,0:T(8,128)(2,1)S(1)} %get-tuple-element.58.last.refs_6_, bf16[2,2,256,512]{3,2,1,0:T(8,128)(2,1)S(1)} %get-tuple-element.59.w.refs_7_, ...), custom_call_target="tpu_custom_call" | custom-call | tf_op jit(solution)/shard_map/own_share/pallas_call | solution.py:431
  26.5 1.5 %rim_share.4 = (f32[608,640]{1,0:T(8,128)S(1)}, f32[608,640]{1,0:T(8,128)S(1)}) custom-call(f32[15,16,512]{2,1,0:T(8,128)S(1)} %collective-permute-done.rim, f32[608,640]{1,0:T(8,128)S(1)} %own_share.4.refs_0_, f32[608,640]{1,0:T(8,128)S(1)} %own_share.5.refs_1_, ...), custom_call_target="tpu_custom_call", output_to_operand_aliasing={{0}: (1, {}), {1}: (2, {})} | custom-call | tf_op jit(solution)/shard_map/rim_share/pallas_call | solution.py:479
  28.3 1.5 %rim_share.5 = (f32[608,640]{1,0:T(8,128)S(1)}, f32[608,640]{1,0:T(8,128)S(1)}) custom-call(f32[15,16,512]{2,1,0:T(8,128)S(1)} %collective-permute-done.1.rim, f32[608,640]{1,0:T(8,128)S(1)} %get-tuple-element.61.refs_0_, f32[608,640]{1,0:T(8,128)S(1)} %get-tuple-element.62.refs_1_, ...), custom_call_target="tpu_custom_call", output_to_operand_aliasing={{0}: (1, {}), {1}: (2, {})} | custom-call | tf_op jit(solution)/shard_map/rim_share/pallas_call | solution.py:479
  29.8 1.5 %adjoint.8 = (f32[16,16,640]{2,1,0:T(8,128)S(1)}, bf16[224,640]{1,0:T(8,128)(2,1)S(1)}, bf16[224,640]{1,0:T(8,128)(2,1)S(1)}) custom-call(f32[608,640]{1,0:T(8,128)S(1)} %get-tuple-element.70.refs_0_, f32[112,640]{1,0:T(8,128)S(1)} %get-tuple-element.73.refs_1_, f32[112,640]{1,0:T(8,128)S(1)} %get-tuple-element.74.refs_2_, f32[384,640]{1,0:T(8,128)S(1)} %bitcast.2, ...), custom_call_target="tpu_custom_call" | custom-call | tf_op jit(solution)/shard_map/adjoint/pallas_call | solution.py:585
  31.3 1.5 %adjoint.9 = (f32[16,16,640]{2,1,0:T(8,128)S(1)}, bf16[224,640]{1,0:T(8,128)(2,1)S(1)}, bf16[224,640]{1,0:T(8,128)(2,1)S(1)}) custom-call(f32[608,640]{1,0:T(8,128)S(1)} %get-tuple-element.63.refs_0_, f32[112,640]{1,0:T(8,128)S(1)} %get-tuple-element.66.refs_1_, f32[112,640]{1,0:T(8,128)S(1)} %get-tuple-element.67.refs_2_, ...), custom_call_target="tpu_custom_call" | custom-call | tf_op jit(solution)/shard_map/adjoint/pallas_call | solution.py:585
  36.9 1.7 %collective-permute-start.11 = (f32[15,16,512]{2,1,0:T(8,128)S(1)}, f32[15,16,512]{2,1,0:T(8,128)S(1)}, u32[]{:S(2)}, u32[]{:S(2)}) collective-permute-start(f32[15,16,512]{2,1,0:T(8,128)S(1)} %get-tuple-element.82), channel_id=1, source_target_pairs={{0,4},{1,17},{2,6},{3,19},{4,0},{5,9},{6,2},{7,11},{8,12},{9,5},{1... | collective-permute-start | bytes 1474568 | tf_op jit(solution)/shard_map/ppermute | solution.py:678
  38.6 7.2 %collective-permute-done.11.rim = f32[15,16,512]{2,1,0:T(8,128)S(1)} collective-permute-done((f32[15,16,512]{2,1,0:T(8,128)S(1)}, f32[15,16,512]{2,1,0:T(8,128)S(1)}, u32[]{:S(2)}, u32[]{:S(2)}) %collective-permute-start.11) | collective-permute-done | bytes 491552 | tf_op jit(solution)/shard_map/ppermute | solution.py:678
  45.8 1.6 %own_share.7.refs_1_ = f32[608,640]{1,0:T(8,128)S(1)} custom-call(f32[24,16,640]{2,1,0:T(8,128)S(1)} %get-tuple-element.83.est, bf16[2,896,256]{2,1,0:T(8,128)(2,1)S(1)} %get-tuple-element.57.t.refs_5_, bf16[2,256,256]{2,1,0:T(8,128)(2,1)S(1)} %get-tuple-element.58.last.refs_6_, bf16[2,2,256,512]{3,2,1,0:T(8,128)(2,1)S(1)} %get-tuple-element.59.w.refs_7_, ...), custom_call_target="tpu_custom_call" | custom-call | tf_op jit(solution)/shard_map/own_share/pallas_call | solution.py:431
  47.4 1.6 %own_share.6.refs_0_ = f32[608,640]{1,0:T(8,128)S(1)} custom-call(f32[24,16,640]{2,1,0:T(8,128)S(1)} %get-tuple-element.83.est, bf16[2,896,256]{2,1,0:T(8,128)(2,1)S(1)} %get-tuple-element.53.t.refs_2_.refs_4_, bf16[2,256,256]{2,1,0:T(8,128)(2,1)S(1)} %get-tuple-element.54.last.refs_3_.refs_5_, bf16[2,2,256,512]{3,2,1,0:T(8,128)(2,1)S(1)} %get-tuple-element.55.w.refs_6_, ...), custom_call_target="tpu_custom_call" | custom-call | tf_op jit(solution)/shard_map/own_share/pallas_call | solution.py:431
  49.0 1.5 %rim_share.6 = (f32[608,640]{1,0:T(8,128)S(1)}, f32[608,640]{1,0:T(8,128)S(1)}) custom-call(f32[15,16,512]{2,1,0:T(8,128)S(1)} %collective-permute-done.11.rim, f32[608,640]{1,0:T(8,128)S(1)} %own_share.6.refs_0_, f32[608,640]{1,0:T(8,128)S(1)} %own_share.7.refs_1_, ...), custom_call_target="tpu_custom_call", output_to_operand_aliasing={{0}: (1, {}), {1}: (2, {})} | custom-call | tf_op jit(solution)/shard_map/rim_share/pallas_call | solution.py:479
  50.5 1.5 %rim_share.7 = (f32[608,640]{1,0:T(8,128)S(1)}, f32[608,640]{1,0:T(8,128)S(1)}) custom-call(f32[15,16,512]{2,1,0:T(8,128)S(1)} %collective-permute-done.12.rim, f32[608,640]{1,0:T(8,128)S(1)} %get-tuple-element.84.refs_0_, f32[608,640]{1,0:T(8,128)S(1)} %get-tuple-element.85.refs_1_, ...), custom_call_target="tpu_custom_call", output_to_operand_aliasing={{0}: (1, {}), {1}: (2, {})} | custom-call | tf_op jit(solution)/shard_map/rim_share/pallas_call | solution.py:479
  53.4 1.4 %adjoint.14 = (f32[12,8,512]{2,1,0:T(8,128)S(1)}, f32[12,8,512]{2,1,0:T(8,128)S(1)}, bf16[224,640]{1,0:T(8,128)(2,1)S(1)}, bf16[224,640]{1,0:T(8,128)(2,1)S(1)}) custom-call(f32[608,640]{1,0:T(8,128)S(1)} %get-tuple-element.86.refs_0_, f32[112,640]{1,0:T(8,128)S(1)} %get-tuple-element.66.refs_1_, f32[112,640]{1,0:T(8,128)S(1)} %get-tuple-element.67.refs_2_, ...), custom_call_target="tpu_custom_call" | custom-call | tf_op jit(solution)/shard_map/adjoint/pallas_call | solution.py:585
  57.6 1.6 %collective-permute-start.18 = (f32[12,8,512]{2,1,0:T(8,128)S(1)}, f32[12,8,512]{2,1,0:T(8,128)S(1)}, u32[]{:S(2)}, u32[]{:S(2)}) collective-permute-start(f32[12,8,512]{2,1,0:T(8,128)S(1)} %finish.3.refs_0_), channel_id=1, source_target_pairs={{0,2},{1,3},{2,0},{3,1},{4,6},{5,7},{6,4},{7,5},{8,10},{9,11},{10,... | collective-permute-start | bytes 589832 | tf_op jit(solution)/shard_map/ppermute | solution.py:652
  61.1 4.3 %collective-permute-done.18.refs_2_ = f32[12,8,512]{2,1,0:T(8,128)S(1)} collective-permute-done((f32[12,8,512]{2,1,0:T(8,128)S(1)}, f32[12,8,512]{2,1,0:T(8,128)S(1)}, u32[]{:S(2)}, u32[]{:S(2)}) %collective-permute-start.18) | collective-permute-done | bytes 196640 | tf_op jit(solution)/shard_map/ppermute | solution.py:652
  65.4 3.7 %collective-permute-done.14.refs_0_ = f32[12,8,512]{2,1,0:T(8,128)S(1)} collective-permute-done((f32[12,8,512]{2,1,0:T(8,128)S(1)}, f32[12,8,512]{2,1,0:T(8,128)S(1)}, u32[]{:S(2)}, u32[]{:S(2)}) %collective-permute-start.14) | collective-permute-done | bytes 196640 | tf_op jit(solution)/shard_map/ppermute | solution.py:652
  (49 shorter events, 16.6 us)
Async XLA Ops:
  1.5 15.8 %collective-permute-start.3 = (f32[16,16,512]{2,1,0:T(8,128)S(1)}, f32[16,16,512]{2,1,0:T(8,128)S(1)}, u32[]{:S(2)}, u32[]{:S(2)}) collective-permute-start(f32[16,16,512]{2,1,0:T(8,128)S(1)} %get-tuple-element.64), channel_id=1, source_target_pairs={{0,2},{1,3},{2,0},{3,1},{4,6},{5,7},{6,4},{7,5},{8,10},{9,11},{10,... | collective-permute-start | bytes 1572872 | tf_op jit(solution)/shard_map/ppermute | solution.py:652
  4.5 4.1 %copy-start = (f32[1,3,15]{2,0,1:T(1,128)S(1)}, f32[1,3,15]{2,0,1:T(1,128)}, u32[]{:S(2)}) copy-start(f32[1,3,15]{2,0,1:T(1,128)} %param.4) | copy-start | bytes 544
  4.5 11.6 %collective-permute-start = (f32[15,16,512]{2,1,0:T(8,128)S(1)}, f32[15,16,512]{2,1,0:T(8,128)S(1)}, u32[]{:S(2)}, u32[]{:S(2)}) collective-permute-start(f32[15,16,512]{2,1,0:T(8,128)S(1)} %get-tuple-element.51), channel_id=1, source_target_pairs={{0,4},{1,17},{2,6},{3,19},{4,0},{5,9},{6,2},{7,11},{8,12},{9,5},{1... | collective-permute-start | bytes 1474568 | tf_op jit(solution)/shard_map/ppermute | solution.py:678
  8.1 11.4 %collective-permute-start.7 = (f32[8,16,512]{2,1,0:T(8,128)S(1)}, f32[8,16,512]{2,1,0:T(8,128)S(1)}, u32[]{:S(2)}, u32[]{:S(2)}) collective-permute-start(f32[8,16,512]{2,1,0:T(8,128)S(1)} %get-tuple-element.71), channel_id=1, source_target_pairs={{0,4},{1,5},{2,6},{3,7},{4,0},{5,1},{6,2},{7,3},{8,12},{9,13},{10,... | collective-permute-start | bytes 786440 | tf_op jit(solution)/shard_map/ppermute | solution.py:674
  8.6 8.7 %collective-permute-start.2 = (f32[1,3,15]{2,1,0:T(4,128)S(1)}, f32[1,3,15]{2,1,0:T(4,128)S(1)}, u32[]{:S(2)}, u32[]{:S(2)}) collective-permute-start(f32[1,3,15]{2,1,0:T(4,128)S(1)} %copy.13.taps), channel_id=1, source_target_pairs={{0,2},{1,3},{2,0},{3,1},{4,6},{5,7},{6,4},{7,5},{8,10},{9,11},{10,... | collective-permute-start | bytes 548 | tf_op jit(solution)/shard_map/ppermute | solution.py:652
  8.8 17.6 %collective-permute-start.8 = (f32[8,16,512]{2,1,0:T(8,128)S(1)}, f32[8,16,512]{2,1,0:T(8,128)S(1)}, u32[]{:S(2)}, u32[]{:S(2)}) collective-permute-start(f32[8,16,512]{2,1,0:T(8,128)S(1)} %get-tuple-element.72), channel_id=1, source_target_pairs={{0,16},{1,17},{2,18},{3,19},{4,8},{5,9},{6,10},{7,11},{8,4},{9,5},... | collective-permute-start | bytes 786440 | tf_op jit(solution)/shard_map/ppermute | solution.py:673
  16.1 11.9 %collective-permute-start.6 = (f32[11,16,512]{2,1,0:T(8,128)S(1)}, f32[11,16,512]{2,1,0:T(8,128)S(1)}, u32[]{:S(2)}, u32[]{:S(2)}) collective-permute-start(f32[11,16,512]{2,1,0:T(8,128)S(1)} %get-tuple-element.65), channel_id=1, source_target_pairs={{0,2},{1,3},{2,0},{3,1},{4,6},{5,7},{6,4},{7,5},{8,10},{9,11},{10,... | collective-permute-start | bytes 1081352 | tf_op jit(solution)/shard_map/ppermute | solution.py:652
  17.3 11.0 %collective-permute-start.1 = (f32[15,16,512]{2,1,0:T(8,128)S(1)}, f32[15,16,512]{2,1,0:T(8,128)S(1)}, u32[]{:S(2)}, u32[]{:S(2)}) collective-permute-start(f32[15,16,512]{2,1,0:T(8,128)S(1)} %collective-permute-done.rim), channel_id=1, source_target_pairs={{0,1},{1,0},{2,3},{3,2},{4,5},{5,4},{6,7},{7,6},{8,9},{9,8},{10,11... | collective-permute-start | bytes 1474568 | tf_op jit(solution)/shard_map/ppermute | solution.py:648
  17.3 10.7 %collective-permute-start.4 = (f32[8,16,512]{2,1,0:T(8,128)S(1)}, f32[8,16,512]{2,1,0:T(8,128)S(1)}, u32[]{:S(2)}, u32[]{:S(2)}) collective-permute-start(f32[8,16,512]{2,1,0:T(8,128)S(1)} %get-tuple-element.98), channel_id=1, source_target_pairs={{0,4},{1,5},{2,6},{3,7},{4,0},{5,1},{6,2},{7,3},{8,12},{9,13},{10,... | collective-permute-start | bytes 786440 | tf_op jit(solution)/shard_map/ppermute | solution.py:674
  19.5 8.6 %collective-permute-start.5 = (f32[8,16,512]{2,1,0:T(8,128)S(1)}, f32[8,16,512]{2,1,0:T(8,128)S(1)}, u32[]{:S(2)}, u32[]{:S(2)}) collective-permute-start(f32[8,16,512]{2,1,0:T(8,128)S(1)} %get-tuple-element.97), channel_id=1, source_target_pairs={{0,16},{1,17},{2,18},{3,19},{4,8},{5,9},{6,10},{7,11},{8,4},{9,5},... | collective-permute-start | bytes 786440 | tf_op jit(solution)/shard_map/ppermute | solution.py:673
  32.8 3.8 %collective-permute-start.9 = (f32[16,16,640]{2,1,0:T(8,128)S(1)}, f32[16,16,640]{2,1,0:T(8,128)S(1)}, u32[]{:S(2)}, u32[]{:S(2)}) collective-permute-start(f32[16,16,640]{2,1,0:T(8,128)S(1)} %get-tuple-element.77.refs_0_), channel_id=1, source_target_pairs={{0,1},{1,0},{2,3},{3,2},{4,5},{5,4},{6,7},{7,6},{8,9},{9,8},{10,11... | collective-permute-start | bytes 1966088 | tf_op jit(solution)/shard_map/ppermute | solution.py:648
  34.8 1.8 %collective-permute-start.10 = (f32[8,16,640]{2,1,0:T(8,128)S(1)}, f32[8,16,640]{2,1,0:T(8,128)S(1)}, u32[]{:S(2)}, u32[]{:S(2)}) collective-permute-start(f32[8,16,640]{2,1,0:T(8,128)S(1)} %adjoint.11.refs_2_), channel_id=1, source_target_pairs={{0,1},{1,0},{2,3},{3,2},{4,5},{5,4},{6,7},{7,6},{8,9},{9,8},{10,11... | collective-permute-start | bytes 983048 | tf_op jit(solution)/shard_map/ppermute | solution.py:648
  36.9 8.9 %collective-permute-start.11 = (f32[15,16,512]{2,1,0:T(8,128)S(1)}, f32[15,16,512]{2,1,0:T(8,128)S(1)}, u32[]{:S(2)}, u32[]{:S(2)}) collective-permute-start(f32[15,16,512]{2,1,0:T(8,128)S(1)} %get-tuple-element.82), channel_id=1, source_target_pairs={{0,4},{1,17},{2,6},{3,19},{4,0},{5,9},{6,2},{7,11},{8,12},{9,5},{1... | collective-permute-start | bytes 1474568 | tf_op jit(solution)/shard_map/ppermute | solution.py:678
  45.8 4.7 %collective-permute-start.12 = (f32[15,16,512]{2,1,0:T(8,128)S(1)}, f32[15,16,512]{2,1,0:T(8,128)S(1)}, u32[]{:S(2)}, u32[]{:S(2)}) collective-permute-start(f32[15,16,512]{2,1,0:T(8,128)S(1)} %collective-permute-done.11.rim), channel_id=1, source_target_pairs={{0,1},{1,0},{2,3},{3,2},{4,5},{5,4},{6,7},{7,6},{8,9},{9,8},{10,11... | collective-permute-start | bytes 1474568 | tf_op jit(solution)/shard_map/ppermute | solution.py:648
  54.8 2.7 %collective-permute-start.16 = (f32[12,8,512]{2,1,0:T(8,128)S(1)}, f32[12,8,512]{2,1,0:T(8,128)S(1)}, u32[]{:S(2)}, u32[]{:S(2)}) collective-permute-start(f32[12,8,512]{2,1,0:T(8,128)S(1)} %get-tuple-element.96), channel_id=1, source_target_pairs={{0,1},{1,0},{2,3},{3,2},{4,5},{5,4},{6,7},{7,6},{8,9},{9,8},{10,11... | collective-permute-start | bytes 589832 | tf_op jit(solution)/shard_map/ppermute | solution.py:648
  57.4 1.7 %collective-permute-start.13 = (f32[12,8,512]{2,1,0:T(8,128)S(1)}, f32[12,8,512]{2,1,0:T(8,128)S(1)}, u32[]{:S(2)}, u32[]{:S(2)}) collective-permute-start(f32[12,8,512]{2,1,0:T(8,128)S(1)} %get-tuple-element.94), channel_id=1, source_target_pairs={{0,1},{1,0},{2,3},{3,2},{4,5},{5,4},{6,7},{7,6},{8,9},{9,8},{10,11... | collective-permute-start | bytes 589832 | tf_op jit(solution)/shard_map/ppermute | solution.py:648
  57.6 7.8 %collective-permute-start.18 = (f32[12,8,512]{2,1,0:T(8,128)S(1)}, f32[12,8,512]{2,1,0:T(8,128)S(1)}, u32[]{:S(2)}, u32[]{:S(2)}) collective-permute-start(f32[12,8,512]{2,1,0:T(8,128)S(1)} %finish.3.refs_0_), channel_id=1, source_target_pairs={{0,2},{1,3},{2,0},{3,1},{4,6},{5,7},{6,4},{7,5},{8,10},{9,11},{10,... | collective-permute-start | bytes 589832 | tf_op jit(solution)/shard_map/ppermute | solution.py:652
  59.2 10.0 %collective-permute-start.14 = (f32[12,8,512]{2,1,0:T(8,128)S(1)}, f32[12,8,512]{2,1,0:T(8,128)S(1)}, u32[]{:S(2)}, u32[]{:S(2)}) collective-permute-start(f32[12,8,512]{2,1,0:T(8,128)S(1)} %finish.2.refs_4_), channel_id=1, source_target_pairs={{0,2},{1,3},{2,0},{3,1},{4,6},{5,7},{6,4},{7,5},{8,10},{9,11},{10,... | collective-permute-start | bytes 589832 | tf_op jit(solution)/shard_map/ppermute | solution.py:652
  60.6 8.6 %collective-permute-start.17 = (f32[12,8,512]{2,1,0:T(8,128)S(1)}, f32[12,8,512]{2,1,0:T(8,128)S(1)}, u32[]{:S(2)}, u32[]{:S(2)}) collective-permute-start(f32[12,8,512]{2,1,0:T(8,128)S(1)} %finish.3.refs_0_), channel_id=1, source_target_pairs={{0,1},{1,0},{2,3},{3,2},{4,5},{5,4},{6,7},{7,6},{8,9},{9,8},{10,11... | collective-permute-start | bytes 589832 | tf_op jit(solution)/shard_map/ppermute | solution.py:648
  60.6 8.6 %collective-permute-start.20 = (f32[12,8,512]{2,1,0:T(8,128)S(1)}, f32[12,8,512]{2,1,0:T(8,128)S(1)}, u32[]{:S(2)}, u32[]{:S(2)}) collective-permute-start(f32[12,8,512]{2,1,0:T(8,128)S(1)} %finish.2.refs_4_), channel_id=1, source_target_pairs={{0,1},{1,0},{2,3},{3,2},{4,5},{5,4},{6,7},{7,6},{8,9},{9,8},{10,11... | collective-permute-start | bytes 589832 | tf_op jit(solution)/shard_map/ppermute | solution.py:648
  65.4 3.8 %collective-permute-start.19 = (f32[12,8,512]{2,1,0:T(8,128)S(1)}, f32[12,8,512]{2,1,0:T(8,128)S(1)}, u32[]{:S(2)}, u32[]{:S(2)}) collective-permute-start(f32[12,8,512]{2,1,0:T(8,128)S(1)} %collective-permute-done.18.refs_2_), channel_id=1, source_target_pairs={{0,1},{1,0},{2,3},{3,2},{4,5},{5,4},{6,7},{7,6},{8,9},{9,8},{10,11... | collective-permute-start | bytes 589832 | tf_op jit(solution)/shard_map/ppermute | solution.py:648
  69.1 1.4 %collective-permute-start.15 = (f32[12,8,512]{2,1,0:T(8,128)S(1)}, f32[12,8,512]{2,1,0:T(8,128)S(1)}, u32[]{:S(2)}, u32[]{:S(2)}) collective-permute-start(f32[12,8,512]{2,1,0:T(8,128)S(1)} %collective-permute-done.14.refs_0_), channel_id=1, source_target_pairs={{0,1},{1,0},{2,3},{3,2},{4,5},{5,4},{6,7},{7,6},{8,9},{9,8},{10,11... | collective-permute-start | bytes 589832 | tf_op jit(solution)/shard_map/ppermute | solution.py:648
